TPU v7x, 32 devices: a whole 2x2x4 slice. The times are simulated.
32 devices in a mesh: dp: 2 (over y), expert: 16 (over z, x, core).
Axes of the slice: x: 2, y: 2, z: 4, core: 2. Of those that a mesh axis runs over, the one named last changes fastest.
Arguments:
- out_grad: bfloat16 [3072, 2048], P('expert', 'dp'), may hold values from -6 to 6
- routes: int32 [3072, 8], P('expert'), may hold values from 0 to 15, all different within a row; in each aligned block of 192 rows (0 to 191, 192 to 383, ...) at most 144 rows name the same one
- gate_codes: int32 [3072, 8], P('expert'), may hold values from 1 to 255
- w_gate: bfloat16 [16, 2048, 384], P('expert', 'dp'), may hold values from -0.125 to 0.125
- w_up: bfloat16 [16, 2048, 384], P('expert', 'dp'), may hold values from -0.125 to 0.125
- w_down: bfloat16 [16, 384, 2048], P('expert', None, 'dp'), may hold values from -0.3125 to 0.3125
- saved_inputs: bfloat16 [16, 2304, 2048], P('expert', None, 'dp'), may hold values from -6 to 6
- saved_gate: bfloat16 [16, 2304, 384], P('expert'), may hold values from -6 to 6
- saved_up: bfloat16 [16, 2304, 384], P('expert'), may hold values from -6 to 6
Outputs:
- token_grads: bfloat16 [3072, 2048], P('expert', 'dp')
- weight_grads: bfloat16 [16, 2048, 1152], P('expert', 'dp')
Inputs may be any that keep to these rules, and one draw needn't show every extreme that they name: `routes`: each token names 8 different experts; in each block of 192 tokens no expert is named by more than 144 tokens, a bound that some block reaches.
All inputs are finite; a program needn't handle non-finite values.
Results may differ from a plain program's by a relative error of at most 0.0065.
Values may be sent and summed in bfloat16 or wider, within the bound.
No kernel may reach another device: no remote copies, remote signals or barrier semaphores. Data moves between devices by JAX's collectives and lax.ppermute only.
A program may use at most 128 MiB of HBM per device.

v0:
```python
import jax
import jax.numpy as jnp
from jax import lax
from jax.sharding import PartitionSpec as P

gate_unit = 0.00390625
loss_scale = 0.015625


def contract_rows(left, right):
    return lax.dot_general(
        left, right, (((0,), (0,)), ((), ())), preferred_element_type=jnp.float32
    )


def contract_cols(left, right):
    return lax.dot_general(
        left, right, (((1,), (1,)), ((), ())), preferred_element_type=jnp.float32
    )


def activation_grads(grad_hidden, gate_pre, up_pre):
    sigmoid = jax.nn.sigmoid(gate_pre)
    silu = gate_pre * sigmoid
    dsilu = sigmoid * (1.0 + gate_pre * (1.0 - sigmoid))
    grad_gate_pre = (grad_hidden * up_pre * dsilu).astype(jnp.bfloat16)
    grad_up_pre = (grad_hidden * silu).astype(jnp.bfloat16)
    return (grad_gate_pre, grad_up_pre)


def body(out_grad, routes, gate_codes, w_gate, w_up, w_down, saved_inputs, saved_gate, saved_up):
    owners = lax.axis_size("expert")
    slot_count = saved_gate.shape[1]
    capacity = slot_count // owners
    token_count = routes.shape[0]
    choice_count = routes.shape[1]
    flat_routes = routes.reshape(-1)
    onehot = (flat_routes[:, None] == jnp.arange(owners, dtype=jnp.int32)[None, :]).astype(
        jnp.int32
    )
    earlier = jnp.cumsum(onehot, axis=0) - onehot
    position = jnp.sum(earlier * onehot, axis=1)
    slot_index = (flat_routes * capacity + position).reshape(token_count, choice_count)
    gate_values = gate_codes.astype(jnp.float32) * gate_unit
    rows_iota = jnp.arange(slot_count, dtype=jnp.int32)[:, None]
    weighted = jnp.zeros((slot_count, token_count), jnp.float32)
    picks = jnp.zeros((slot_count, token_count), jnp.float32)
    for pick in range(choice_count):
        hit = rows_iota == slot_index[:, pick][None, :]
        weighted = weighted + jnp.where(hit, gate_values[:, pick][None, :], 0.0)
        picks = picks + hit.astype(jnp.float32)
    weighted_map = weighted.astype(jnp.bfloat16)
    pick_map = picks.astype(jnp.bfloat16)
    outgoing = jnp.dot(weighted_map, out_grad, preferred_element_type=jnp.float32).astype(
        jnp.bfloat16
    )
    received = lax.all_to_all(outgoing, "expert", split_axis=0, concat_axis=0, tiled=True)
    down_local = w_down[0]
    hidden_share = lax.psum_scatter(
        contract_cols(received, down_local), "dp", scatter_dimension=0, tiled=True
    )
    gate_pre = saved_gate[0].astype(jnp.float32)
    up_pre = saved_up[0].astype(jnp.float32)
    hidden = (gate_pre * jax.nn.sigmoid(gate_pre) * up_pre).astype(jnp.bfloat16)
    grad_hidden = lax.all_gather(hidden_share, "dp", axis=0, tiled=True)
    grad_gate_pre, grad_up_pre = activation_grads(grad_hidden, gate_pre, up_pre)
    slot_grads = contract_cols(grad_gate_pre, w_gate[0]) + contract_cols(grad_up_pre, w_up[0])
    slot_grads = slot_grads.astype(jnp.bfloat16)
    returned = lax.all_to_all(slot_grads, "expert", split_axis=0, concat_axis=0, tiled=True)
    token_grads = contract_rows(pick_map, returned).astype(jnp.bfloat16)
    inputs_here = saved_inputs[0]
    part = jnp.concatenate(
        [
            contract_rows(inputs_here, grad_gate_pre),
            contract_rows(inputs_here, grad_up_pre),
            contract_rows(received, hidden),
        ],
        axis=1,
    )
    weight_grads = (part * loss_scale).astype(jnp.bfloat16)[None]
    return (token_grads, weight_grads)


def solution(mesh):
    placed = (
        P("expert", "dp"),
        P("expert", None),
        P("expert", None),
        P("expert", "dp", None),
        P("expert", "dp", None),
        P("expert", None, "dp"),
        P("expert", None, "dp"),
        P("expert", None, None),
        P("expert", None, None),
    )
    return jax.shard_map(
        body,
        mesh=mesh,
        in_specs=placed,
        out_specs=(P("expert", "dp"), P("expert", "dp", None)),
        check_vma=False,
    )
```

profile of v0, /device:TPU:11, one launch (start us, length us, event | category | flops | bytes accessed | tf_op | source)
XLA Modules:
  0.0 369.5 jit_solution(16599904412477799178)
XLA Ops:
  7.2 0.9 copy.22
  8.3 0.7 convert_multiply_fusion.2
  9.0 4.5 %reduce-window.6 = s32[16,12,128]{2,1,0:T(8,128)S(1)} reduce-window(s32[16,12,128]{2,1,0:T(8,128)S(1)} %fusion.64, s32[]{:T(128)} %constant.3.clone.1), window={size=1x1x128 pad=0_0x0_0x127_0}, to_apply=%region_0.0 | reduce-window | flops 3121152 | bytes 196612 | tf_op jit(solution)/shard_map/reduce-window
  13.6 0.4 slice_reduce_fusion
  14.0 0.2 reduce-window.9
  14.2 0.1 broadcast_add_fusion
  14.5 0.7 multiply_add_fusion
  15.2 4.1 %convolution_convert_fusion = bf16[2304,1024]{1,0:T(8,128)(2,1)S(1)} fusion(bf16[192,1024]{1,0:T(8,128)(2,1)} %param.9, f32[192]{0:T(256)S(1)} %bitcast.138, f32[192]{0:T(256)S(1)} %bitcast.139, f32[192]{0:T(256)S(1)} %bitcast.140, f32[192]{0:T(256)S(1)} %bitcast.141, f32[192]{0:T(256)S(1)} %bitcast.142, f32[192]{0:T(256)S(1)} %bitcast.143, ...), kind=kOutput, calls=%fused_computation.1 | convolution fusion | flops 918945792 | bytes 5124096 | tf_op jit(solution)/shard_map/dot_general | solution.py:54
  19.4 110.0 %all_to_all.24 = bf16[16,144,1024]{2,1,0:T(8,128)(2,1)S(1)} all-to-all(bf16[16,144,1024]{2,1,0:T(8,128)(2,1)S(1)} %bitcast.118), channel_id=1, replica_groups=mesh['dp'=2,'expert'=16] {'expert'}, dimensions={0} | all-to-all | bytes 9437184 | tf_op jit(solution)/shard_map/all_to_all | solution.py:57
  129.3 2.1 copy-done.1
  131.5 4.5 %fusion.62 = f32[2304,384]{1,0:T(8,128)} fusion(bf16[2304,1024]{1,0:T(8,128)(2,1)S(1)} %bitcast.115, bf16[1,384,1024]{2,1,0:T(8,128)(2,1)S(1)} %copy-done.6), kind=kOutput, calls=%fused_computation.74 | convolution fusion | flops 1811939328 | bytes 9043968 | tf_op jit(solution)/shard_map/dot_general | solution.py:17
  136.0 47.7 %reduce-scatter.2.cloned.1.call-done = f32[1152,384]{1,0:T(8,128)} async-done(((f32[2304,384]{1,0:T(8,128)}), f32[1152,384]{1,0:T(8,128)}) %reduce-scatter.2.cloned.1.call-update) | async-done | bytes 1769488 | tf_op jit(solution)/shard_map/reduce_scatter | solution.py:59
  183.7 51.0 %all-gather.2.cloned.1.call-done = f32[2304,384]{1,0:T(8,128)} async-done(((f32[1152,384]{1,0:T(8,128)}), f32[2304,384]{1,0:T(8,128)}) %all-gather.2.cloned.1.call-update) | async-done | bytes 3538960 | tf_op jit(solution)/shard_map/all_gather | solution.py:65
  234.7 4.6 %fusion.10 = bf16[2304,384]{1,0:T(8,128)(2,1)S(1)} fusion(f32[2304,384]{1,0:T(8,128)} %all-gather.2.cloned.1.call-done, bf16[1,2304,384]{2,1,0:T(8,128)(2,1)} %param.17, bf16[1,2304,384]{2,1,0:T(8,128)(2,1)} %param.16), kind=kLoop, calls=%fused_computation.18 | loop fusion | flops 10616832 | bytes 8847360 | tf_op jit(solution)/shard_map/convert_element_type | solution.py:26
  239.3 2.7 fusion.60
  242.1 4.5 %add_convert_fusion = bf16[2304,1024]{1,0:T(8,128)(2,1)} fusion(f32[2304,1024]{1,0:T(8,128)S(1)} %fusion.60, bf16[1,1024,384]{2,1,0:T(8,128)(2,1)S(1)} %copy-done.7, f32[2304,384]{1,0:T(8,128)S(1)} %copy-done.2, bf16[1,2304,384]{2,1,0:T(8,128)(2,1)S(1)} %copy-done.4), kind=kOutput, calls=%fused_computation | convolution fusion | flops 1822851072 | bytes 20250624 | tf_op jit(solution)/shard_map/dot_general | solution.py:17
  246.5 6.4 %all-to-all-start.1 = ((bf16[16,144,1024]{2,1,0:T(8,128)(2,1)}), bf16[16,144,1024]{2,1,0:T(8,128)(2,1)}, u32[]{:S(2)}, u32[]{:S(2)}) async-start(bf16[16,144,1024]{2,1,0:T(8,128)(2,1)} %bitcast.117), calls=%async_computation.2 | async-start | bytes 9437184 | tf_op jit(solution)/shard_map/all_to_all | solution.py:69
  252.9 5.6 %fusion.25 = f32[1,1024,384]{1,2,0:T(8,128)S(1)} fusion(bf16[2304,1024]{1,0:T(8,128)(2,1)} %bitcast.116, bf16[1,2304,384]{2,1,0:T(8,128)(2,1)} %param.17, bf16[1,2304,384]{2,1,0:T(8,128)(2,1)} %param.16), kind=kOutput, calls=%fused_computation.42 | convolution fusion | flops 1819017216 | bytes 9830400 | tf_op jit(solution)/shard_map/dot_general | solution.py:11
  258.5 4.5 %fusion.28 = f32[1,1024,384]{1,2,0:T(8,128)S(1)} fusion(bf16[2304,384]{1,0:T(8,128)(2,1)S(1)} %fusion.10, bf16[1,2304,1024]{2,1,0:T(8,128)(2,1)} %param.15), kind=kOutput, calls=%fused_computation.43 | convolution fusion | flops 1811939328 | bytes 8060928 | tf_op jit(solution)/shard_map/dot_general | solution.py:11
  263.0 4.7 %fusion.31 = f32[1,1024,384]{1,2,0:T(8,128)S(1)} fusion(bf16[1,2304,1024]{2,1,0:T(8,128)(2,1)} %param.15, f32[2304,384]{1,0:T(8,128)S(1)} %copy-done.3, bf16[1,2304,384]{2,1,0:T(8,128)(2,1)S(1)} %copy-done.5), kind=kOutput, calls=%fused_computation.44 | convolution fusion | flops 1818132480 | bytes 11599872 | tf_op jit(solution)/shard_map/dot_general | solution.py:11
  267.7 0.7 fusion.3
  268.4 2.4 copy.25
  270.8 85.8 %all-to-all-done.1 = bf16[16,144,1024]{2,1,0:T(8,128)(2,1)} async-done(((bf16[16,144,1024]{2,1,0:T(8,128)(2,1)}), bf16[16,144,1024]{2,1,0:T(8,128)(2,1)}, u32[]{:S(2)}, u32[]{:S(2)}) %all-to-all-start.1) | async-done | bytes 4718624 | tf_op jit(solution)/shard_map/all_to_all | solution.py:69
  356.6 6.1 %convolution_convert_fusion.1 = bf16[192,1024]{1,0:T(8,128)(2,1)} fusion(bf16[2304,1024]{1,0:T(8,128)(2,1)} %bitcast.25, s32[192]{0:T(256)S(1)} %bitcast.124, s32[192]{0:T(256)S(1)} %bitcast.126, s32[192]{0:T(256)S(1)} %bitcast.128, s32[192]{0:T(256)S(1)} %bitcast.130, s32[192]{0:T(256)S(1)} %bitcast.132, s32[192]{0:T(256)S(1)} %bitcast.134, ...), kind=kOutput, calls=%fused_computation.45 | convolution fusion | flops 916783104 | bytes 5117952 | tf_op jit(solution)/shard_map/dot_general | solution.py:11
  (27 shorter events, 0.6 us)
Async XLA Ops:
  7.2 232.1 %copy-start = (bf16[1,1024,384]{2,1,0:T(8,128)(2,1)S(1)}, bf16[1,1024,384]{2,1,0:T(8,128)(2,1)}, u32[]{:S(2)}) copy-start(bf16[1,1024,384]{2,1,0:T(8,128)(2,1)} %param.12) | copy-start | bytes 2359300
  7.2 176.5 %reduce-scatter.2.cloned.1.call-start = ((), (), s32[]{:S(2)}) async-start(), calls=%async_computation.3 | async-start | bytes 5308416 | tf_op jit(solution)/shard_map/reduce_scatter | solution.py:59
  19.4 112.1 %copy-start.6 = (bf16[1,384,1024]{2,1,0:T(8,128)(2,1)S(1)}, bf16[1,384,1024]{2,1,0:T(8,128)(2,1)}, u32[]{:S(2)}) copy-start(bf16[1,384,1024]{2,1,0:T(8,128)(2,1)} %param.14) | copy-start | bytes 2359300
  129.3 2.1 copy-start.1
  135.9 98.8 %all-gather.2.cloned.1.call-start = ((), (), s32[]{:S(2)}) async-start(), calls=%async_computation.4 | async-start | bytes 5308416 | tf_op jit(solution)/shard_map/all_gather | solution.py:65
  239.3 2.7 copy-start.2
  239.3 2.7 copy-start.4
  239.3 2.7 copy-start.7
  246.5 110.1 %all-to-all-start.1 = ((bf16[16,144,1024]{2,1,0:T(8,128)(2,1)}), bf16[16,144,1024]{2,1,0:T(8,128)(2,1)}, u32[]{:S(2)}, u32[]{:S(2)}) async-start(bf16[16,144,1024]{2,1,0:T(8,128)(2,1)} %bitcast.117), calls=%async_computation.2 | async-start | bytes 9437184 | tf_op jit(solution)/shard_map/all_to_all | solution.py:69
  258.5 4.5 %copy-start.3 = (f32[2304,384]{1,0:T(8,128)S(1)}, f32[2304,384]{1,0:T(8,128)}, u32[]{:S(2)}) copy-start(f32[2304,384]{1,0:T(8,128)} %all-gather.2.cloned.1.call-done) | copy-start | bytes 10616836
  258.5 4.5 %copy-start.5 = (bf16[1,2304,384]{2,1,0:T(8,128)(2,1)S(1)}, bf16[1,2304,384]{2,1,0:T(8,128)(2,1)}, u32[]{:S(2)}) copy-start(bf16[1,2304,384]{2,1,0:T(8,128)(2,1)} %param.16) | copy-start | bytes 5308420
Sparse Core Ops, SparseCore 0:
  136.1 47.5 reduce-scatter.1
  185.3 49.3 all-gather.1
where the time goes:
time: 370 us
  waiting for transfers between devices  185 us (50%)
  blocking collectives  110 us (30%)
  matrix products  36.5 us (10%)
  between operations  14.2 us (4%)
  other arithmetic  11.5 us (3%)
  starting transfers between devices  6.45 us (2%)
  local copies, waits for them, and re-layouts  6.28 us (2%)
    all_to_all x1, blocking collectives, body(): lax.all_to_all(outgoing, 'expert', split_axis=0, concat_axis=0, tiled=True)  110 us
    all_to_all x1, waiting for transfers between devices, body(): lax.all_to_all(slot_grads, 'expert', split_axis=0, concat_axis=0, tiled=T...  85.8 us
    all_gather x1, waiting for transfers between devices, body(): grad_hidden = lax.all_gather(hidden_share, 'dp', axis=0, tiled=True)  51 us
    reduce_scatter x1, waiting for transfers between devices, body(): lax.psum_scatter(contract_cols(received, down_local), 'dp', scatter_dimen...  47.7 us
    dot_general x4, matrix products, contract_rows(): lax.dot_general(left, right, (((0,), (0,)), ((), ())), preferred_element_...  20.8 us
    dot_general x3, matrix products, contract_cols(): lax.dot_general(left, right, (((1,), (1,)), ((), ())), preferred_element_...  11.6 us
  transfers between devices with their start and end apart: 3, of which 3 were waited for; matrix products, arithmetic and copies ran while one was open for 5% of the time, Pallas kernels for 0%

commit v1 on v0

v1 whole, which is shorter than its diff:
```python
import jax
import jax.numpy as jnp
from jax import lax
from jax.experimental import pallas as pl
from jax.experimental.pallas import tpu as pltpu
from jax.sharding import PartitionSpec as P

gate_unit = 0.00390625
loss_scale = 0.015625
f32 = jnp.float32
bf16 = jnp.bfloat16


def contract_rows(left, right):
    return lax.dot_general(left, right, (((0,), (0,)), ((), ())), preferred_element_type=f32)


def contract_cols(left, right):
    return lax.dot_general(left, right, (((1,), (1,)), ((), ())), preferred_element_type=f32)


def activation_grads(grad_hidden, gate_pre, up_pre):
    sigmoid = jax.nn.sigmoid(gate_pre)
    silu = gate_pre * sigmoid
    dsilu = sigmoid * (1.0 + gate_pre * (1.0 - sigmoid))
    grad_gate_pre = (grad_hidden * up_pre * dsilu).astype(bf16)
    grad_up_pre = (grad_hidden * silu).astype(bf16)
    return (grad_gate_pre, grad_up_pre)


def body_any(out_grad, routes, gate_codes, w_gate, w_up, w_down, saved_inputs, saved_gate, saved_up):
    owners = lax.axis_size("expert")
    slot_count = saved_gate.shape[1]
    capacity = slot_count // owners
    token_count = routes.shape[0]
    choice_count = routes.shape[1]
    flat_routes = routes.reshape(-1)
    onehot = (flat_routes[:, None] == jnp.arange(owners, dtype=jnp.int32)[None, :]).astype(jnp.int32)
    earlier = jnp.cumsum(onehot, axis=0) - onehot
    position = jnp.sum(earlier * onehot, axis=1)
    slot_index = (flat_routes * capacity + position).reshape(token_count, choice_count)
    gate_values = gate_codes.astype(f32) * gate_unit
    rows_iota = jnp.arange(slot_count, dtype=jnp.int32)[:, None]
    weighted = jnp.zeros((slot_count, token_count), f32)
    picks = jnp.zeros((slot_count, token_count), f32)
    for pick in range(choice_count):
        hit = rows_iota == slot_index[:, pick][None, :]
        weighted = weighted + jnp.where(hit, gate_values[:, pick][None, :], 0.0)
        picks = picks + hit.astype(f32)
    outgoing = jnp.dot(weighted.astype(bf16), out_grad, preferred_element_type=f32).astype(bf16)
    received = lax.all_to_all(outgoing, "expert", split_axis=0, concat_axis=0, tiled=True)
    hidden_share = lax.psum_scatter(
        contract_cols(received, w_down[0]), "dp", scatter_dimension=0, tiled=True
    )
    gate_pre = saved_gate[0].astype(f32)
    up_pre = saved_up[0].astype(f32)
    hidden = (gate_pre * jax.nn.sigmoid(gate_pre) * up_pre).astype(bf16)
    grad_hidden = lax.all_gather(hidden_share, "dp", axis=0, tiled=True)
    grad_gate_pre, grad_up_pre = activation_grads(grad_hidden, gate_pre, up_pre)
    slot_grads = contract_cols(grad_gate_pre, w_gate[0]) + contract_cols(grad_up_pre, w_up[0])
    returned = lax.all_to_all(
        slot_grads.astype(bf16), "expert", split_axis=0, concat_axis=0, tiled=True
    )
    token_grads = contract_rows(picks.astype(bf16), returned).astype(bf16)
    inputs_here = saved_inputs[0]
    part = jnp.concatenate(
        [
            contract_rows(inputs_here, grad_gate_pre),
            contract_rows(inputs_here, grad_up_pre),
            contract_rows(received, hidden),
        ],
        axis=1,
    )
    return (token_grads, (part * loss_scale).astype(bf16)[None])


def full(shape):
    return pl.BlockSpec(shape, lambda i, sc: (0,) * len(shape))


def dispatch_kernel(sc, t0, t1, t2, t3, pos, gate, wd, rec, share, share_out):
    group, own = sc[0], sc[1]
    cap = rec.shape[0] // 4
    for rel, tok in enumerate((t0, t1, t2, t3)):
        j = jnp.bitwise_xor(own, rel)
        src = group * 4 + j
        slot = lax.broadcasted_iota(jnp.int32, (cap, tok.shape[0]), 0)
        w = jnp.where(slot == pos[pl.ds(src, 1), :], gate[pl.ds(src, 1), :], 0.0).astype(bf16)
        rows = jnp.dot(w, tok[...], preferred_element_type=f32).astype(bf16)
        rec[pl.ds(pl.multiple_of(j * cap, 16), cap), :] = rows
    gh = contract_cols(rec[...], wd[...])
    share[...] = gh
    share_out[...] = gh.astype(bf16)


def dispatch(sc, tokens, pos, gate, wd, rows):
    tok, d = tokens[0].shape
    h = wd.shape[0]
    return pl.pallas_call(
        dispatch_kernel,
        out_shape=(
            jax.ShapeDtypeStruct((rows, d), bf16),
            jax.ShapeDtypeStruct((rows, h), f32),
            jax.ShapeDtypeStruct((rows, h), bf16),
        ),
        grid_spec=pltpu.PrefetchScalarGridSpec(
            num_scalar_prefetch=1,
            grid=(1,),
            in_specs=[full((tok, d))] * 4 + [full(pos.shape)] * 2 + [full(wd.shape)],
            out_specs=(full((rows, d)), full((rows, h)), full((rows, h))),
        ),
        cost_estimate=pl.CostEstimate(
            flops=2 * rows * d * (tok + h), bytes_accessed=8 * tok * d + 2 * rows * d, transcendentals=0
        ),
        name="dispatch",
    )(sc, *tokens, pos, gate, wd)


def combine_kernel(sc, share, peer, sg, su, pos, wg, wu, gp, hid, keep, send, slots):
    group, own = sc[0], sc[1]
    cap = share.shape[0] // 4
    h = share.shape[1]
    gh = share[...] + peer[...].astype(f32)
    gate_pre = sg[...].astype(f32)
    up_pre = su[...].astype(f32)
    sigmoid = jax.nn.sigmoid(gate_pre)
    silu = gate_pre * sigmoid
    dsilu = sigmoid * (1.0 + gate_pre * (1.0 - sigmoid))
    gg = (gh * up_pre * dsilu).astype(bf16)
    gu = (gh * silu).astype(bf16)
    gp[:, :h] = gg
    gp[:, h:] = gu
    hid[...] = (silu * up_pre).astype(bf16)
    slots[...] = (contract_cols(gg, wg[...]) + contract_cols(gu, wu[...])).astype(bf16)
    for rel in range(4):
        j = jnp.bitwise_xor(own, rel)
        src = group * 4 + j
        slot = lax.broadcasted_iota(jnp.int32, (cap, pos.shape[1]), 0)
        pick = jnp.where(slot == pos[pl.ds(src, 1), :], 1.0, 0.0).astype(bf16)
        rows = slots[pl.ds(pl.multiple_of(j * cap, 16), cap), :]
        back = contract_rows(pick, rows).astype(bf16)
        (send if rel & 1 else keep)[rel >> 1] = back


def combine(sc, share, peer, sg, su, pos, wg, wu):
    rows, h = share.shape
    d = wg.shape[0]
    tok = pos.shape[1]
    part = pl.BlockSpec((rows, h), lambda i, sc: (sc[0], 0))
    return pl.pallas_call(
        combine_kernel,
        out_shape=(
            jax.ShapeDtypeStruct((rows, 2 * h), bf16),
            jax.ShapeDtypeStruct((rows, h), bf16),
            jax.ShapeDtypeStruct((2, tok, d), bf16),
            jax.ShapeDtypeStruct((2, tok, d), bf16),
        ),
        grid_spec=pltpu.PrefetchScalarGridSpec(
            num_scalar_prefetch=1,
            grid=(1,),
            in_specs=[full((rows, h)), full((rows, h)), part, part, full(pos.shape), full((d, h)), full((d, h))],
            out_specs=(full((rows, 2 * h)), full((rows, h)), full((2, tok, d)), full((2, tok, d))),
            scratch_shapes=[pltpu.VMEM((rows, d), bf16)],
        ),
        cost_estimate=pl.CostEstimate(
            flops=2 * rows * d * (tok + 2 * h), bytes_accessed=8 * tok * d + 8 * rows * h, transcendentals=rows * h
        ),
        name="combine",
    )(sc, share, peer, sg, su, pos, wg, wu)


def weights_kernel(sc, x, *refs):
    n = (len(refs) - 1) // 3
    recs, gps, hids, out = refs[:n], refs[n : 2 * n], refs[2 * n : 3 * n], refs[-1]
    rows, wide = gps[0].shape
    left = right = None
    for k in range(n):
        xs = x[pl.ds(pl.multiple_of(sc[k] * rows, 16), rows), :]
        a = contract_rows(xs, gps[k][...])
        b = contract_rows(recs[k][...], hids[k][...])
        left = a if left is None else left + a
        right = b if right is None else right + b
    out[0, :, :wide] = (left * loss_scale).astype(bf16)
    out[0, :, wide:] = (right * loss_scale).astype(bf16)


def weight_sums(groups, x, recs, gps, hids):
    slots, d = x.shape
    rows, wide = gps[0].shape
    h = hids[0].shape[1]
    tile = 256
    return pl.pallas_call(
        weights_kernel,
        out_shape=jax.ShapeDtypeStruct((1, d, wide + h), bf16),
        grid_spec=pltpu.PrefetchScalarGridSpec(
            num_scalar_prefetch=1,
            grid=(d // tile,),
            in_specs=[pl.BlockSpec((slots, tile), lambda i, sc: (0, i))]
            + [pl.BlockSpec((rows, tile), lambda i, sc: (0, i))] * len(recs)
            + [full((rows, wide))] * len(gps)
            + [full((rows, h))] * len(hids),
            out_specs=pl.BlockSpec((1, tile, wide + h), lambda i, sc: (0, i, 0)),
        ),
        cost_estimate=pl.CostEstimate(
            flops=2 * slots * d * (wide + h), bytes_accessed=4 * slots * d + 4 * d * wide, transcendentals=0
        ),
        name="weights",
    )(groups, x, *recs, *gps, *hids)


def body_grid(out_grad, routes, gate_codes, w_gate, w_up, w_down, saved_inputs, saved_gate, saved_up):
    owners = lax.axis_size("expert")
    me = lax.axis_index("expert")
    to_core = [(i, i ^ 1) for i in range(owners)]
    to_x = [(i, i ^ 2) for i in range(owners)]
    ring = [(i, (i + 4) % owners) for i in range(owners)]
    rounds = owners // 4

    def send(v, perm):
        return lax.ppermute(v, "expert", perm)

    own_col = [out_grad]
    for _ in range(rounds - 1):
        own_col.append(send(own_col[-1], ring))
    other_col = [send(v, to_x) for v in own_col]
    own_col_c = [send(v, to_core) for v in own_col]
    other_col_c = [send(v, to_core) for v in other_col]

    named = jnp.concatenate([routes.T, gate_codes.T], axis=0)
    named = lax.all_gather(named, "expert", axis=0, tiled=False)
    choices = routes.shape[1]
    hit = named[:, :choices, :] == me
    mask = jnp.any(hit, axis=1)
    gate = jnp.sum(jnp.where(hit, named[:, choices:, :], 0), axis=1).astype(f32) * gate_unit
    tok = routes.shape[0]
    tri = (jnp.arange(tok)[:, None] < jnp.arange(tok)[None, :]).astype(bf16)
    pos = jnp.dot(mask.astype(bf16), tri, preferred_element_type=f32).astype(jnp.int32)
    pos = jnp.where(mask, pos, -1)

    slots = saved_gate.shape[1]
    rows = slots // rounds
    groups = (me // 4 + rounds - jnp.arange(rounds, dtype=jnp.int32)) % rounds
    scalars = [jnp.stack([groups[k], me % 4]).astype(jnp.int32) for k in range(rounds)]
    sg, su, wg, wu, wd = saved_gate[0], saved_up[0], w_gate[0], w_up[0], w_down[0]

    recs, gps, hids, kept = [], [], [], []
    for k in range(rounds):
        rec, share, share_out = dispatch(
            scalars[k], (own_col[k], own_col_c[k], other_col[k], other_col_c[k]), pos, gate, wd, rows
        )
        peer = lax.ppermute(share_out, "dp", [(0, 1), (1, 0)])
        gp, hid, keep, away = combine(scalars[k], share, peer, sg, su, pos, wg, wu)
        pair = keep.astype(f32) + send(away, to_core).astype(f32)
        near, far = pair[0], pair[1].astype(bf16)
        kept.append((near, send(far, to_x)))
        recs.append(rec)
        gps.append(gp)
        hids.append(hid)

    run = None
    for k in [1, 2, 3, 0]:
        near, arrived = kept[k]
        total = near + arrived.astype(f32)
        if run is not None:
            total = total + run.astype(f32)
        total = total.astype(bf16)
        run = send(total, ring) if k else None
    weight_grads = weight_sums(groups, saved_inputs[0], recs, gps, hids)
    return (total, weight_grads)


def solution(mesh):
    placed = (
        P("expert", "dp"),
        P("expert", None),
        P("expert", None),
        P("expert", "dp", None),
        P("expert", "dp", None),
        P("expert", None, "dp"),
        P("expert", None, "dp"),
        P("expert", None, None),
        P("expert", None, None),
    )
    small = mesh.shape["expert"] == 16 and mesh.shape["dp"] == 2
    return jax.shard_map(
        body_grid if small else body_any,
        mesh=mesh,
        in_specs=placed,
        out_specs=(P("expert", "dp"), P("expert", "dp", None)),
        check_vma=False,
    )
```

time: 370 us -> 174 us (0.47)
  the two profiles are of different devices: /device:TPU:11 before, /device:TPU:0 now
where the time goes in v1:
time: 174 us; the launch traced here: 173 us
  Pallas kernels  55.8 us (32%)
  waiting for transfers between devices  54 us (31%)
  blocking collectives  24.2 us (14%)
  starting transfers between devices  19.8 us (11%)
  other arithmetic  13.3 us (8%)
  local copies, waits for them, and re-layouts  4.18 us (2%)
    ppermute x26, waiting for transfers between devices, send(): return lax.ppermute(v, 'expert', perm)  41.1 us
    all_gather x1, blocking collectives, body_grid(): named = lax.all_gather(named, 'expert', axis=0, tiled=False)  24.2 us
    pallas_call x4, Pallas kernels, combine(): pl.pallas_call(combine_kernel, out_shape=(jax.ShapeDtypeStruct((rows, 2 *...  23.5 us
    pallas_call x4, Pallas kernels, dispatch(): pl.pallas_call(dispatch_kernel, out_shape=(jax.ShapeDtypeStruct((rows, d)...  18.5 us
    ppermute x26, starting transfers between devices, send(): return lax.ppermute(v, 'expert', perm)  15.8 us
    pallas_call x1, Pallas kernels, weight_sums(): pl.pallas_call(weights_kernel, out_shape=jax.ShapeDtypeStruct((1, d, wide...  13.8 us
    ppermute x4, waiting for transfers between devices, body_grid(): peer = lax.ppermute(share_out, 'dp', [(0, 1), (1, 0)])  12.9 us
    another operation x4, other arithmetic, body_grid(): jnp.stack([groups[k], me % 4]).astype(jnp.int32)  4.88 us
  transfers between devices with their start and end apart: 30, of which 10 were waited for; matrix products, arithmetic and copies ran while one was open for 9% of the time, Pallas kernels for 32%

profile of v1, /device:TPU:0, one launch (start us, length us, event | category | flops | bytes accessed | tf_op | source)
XLA Modules:
  0.0 173.0 jit_solution(4289717502425178231)
XLA Ops:
  0.6 3.1 %collective-permute-start.6 = (bf16[192,1024]{1,0:T(8,128)(2,1)}, bf16[192,1024]{1,0:T(8,128)(2,1)S(1)}, u32[]{:S(2)}, u32[]{:S(2)}) collective-permute-start(bf16[192,1024]{1,0:T(8,128)(2,1)} %t0.1), channel_id=1, source_target_pairs={{0,4},{1,5},{2,6},{3,7},{4,8},{5,9},{6,10},{7,11},{8,12},{9,13},{1... | collective-permute-start | bytes 1179656 | tf_op jit(solution)/shard_map/ppermute | solution.py:220
  4.4 24.2 %all-gather = s32[256,192]{1,0:T(8,128)S(1)} all-gather(s32[16,192]{1,0:T(8,128)S(1)} %pad_add_fusion), channel_id=2, replica_groups=mesh['dp'=2,'expert'=16] {'expert'}, dimensions={0}, use_global_device_ids=true | all-gather | bytes 208896 | tf_op jit(solution)/shard_map/all_gather | solution.py:230
  30.1 10.0 %collective-permute-done.22.t2 = bf16[192,1024]{1,0:T(8,128)(2,1)S(1)} collective-permute-done((bf16[192,1024]{1,0:T(8,128)(2,1)S(1)}, bf16[192,1024]{1,0:T(8,128)(2,1)S(1)}, u32[]{:S(2)}, u32[]{:S(2)}) %collective-permute-start.22) | collective-permute-done | bytes 393248 | tf_op jit(solution)/shard_map/ppermute | solution.py:220
  40.1 1.9 %collective-permute-done.7.t0 = bf16[192,1024]{1,0:T(8,128)(2,1)S(1)} collective-permute-done((bf16[192,1024]{1,0:T(8,128)(2,1)S(1)}, bf16[192,1024]{1,0:T(8,128)(2,1)S(1)}, u32[]{:S(2)}, u32[]{:S(2)}) %collective-permute-start.7) | collective-permute-done | bytes 393248 | tf_op jit(solution)/shard_map/ppermute | solution.py:220
  46.1 6.3 %collective-permute-done.16.t2 = bf16[192,1024]{1,0:T(8,128)(2,1)S(1)} collective-permute-done((bf16[192,1024]{1,0:T(8,128)(2,1)S(1)}, bf16[192,1024]{1,0:T(8,128)(2,1)S(1)}, u32[]{:S(2)}, u32[]{:S(2)}) %collective-permute-start.16) | collective-permute-done | bytes 393248 | tf_op jit(solution)/shard_map/ppermute | solution.py:220
  53.4 4.6 %dispatch.7 = (bf16[576,1024]{1,0:T(8,128)(2,1)}, f32[576,384]{1,0:T(8,128)}, bf16[576,384]{1,0:T(8,128)(2,1)}) custom-call(s32[2]{0:T(128)} %pad_add_fusion.4.sc, bf16[192,1024]{1,0:T(8,128)(2,1)} %copy-done.8, bf16[192,1024]{1,0:T(8,128)(2,1)} %copy-done.14, bf16[192,1024]{1,0:T(8,128)(2,1)} %copy-done.10, bf16[192,1024]{1,0:T(8,128)(2,1)} %copy-done.16, ...), custom_call_target="tpu_custom_call" | custom-call | flops 679477248 | bytes 2752512 | tf_op jit(solution)/shard_map/dispatch/pallas_call | solution.py:99
  62.5 4.6 %dispatch.6 = (bf16[576,1024]{1,0:T(8,128)(2,1)}, f32[576,384]{1,0:T(8,128)}, bf16[576,384]{1,0:T(8,128)(2,1)}) custom-call(s32[2]{0:T(128)} %pad_add_fusion.3.sc, bf16[192,1024]{1,0:T(8,128)(2,1)} %copy-done.7, bf16[192,1024]{1,0:T(8,128)(2,1)} %collective-permute-done.15.t1, bf16[192,1024]{1,0:T(8,128)(2,1)} %copy-done.13, ...), custom_call_target="tpu_custom_call" | custom-call | flops 679477248 | bytes 2752512 | tf_op jit(solution)/shard_map/dispatch/pallas_call | solution.py:99
  67.6 5.0 %collective-permute-done.8.t0 = bf16[192,1024]{1,0:T(8,128)(2,1)S(1)} collective-permute-done((bf16[192,1024]{1,0:T(8,128)(2,1)S(1)}, bf16[192,1024]{1,0:T(8,128)(2,1)S(1)}, u32[]{:S(2)}, u32[]{:S(2)}) %collective-permute-start.8) | collective-permute-done | bytes 393248 | tf_op jit(solution)/shard_map/ppermute | solution.py:220
  72.6 1.6 collective-permute-start.10
  75.0 6.0 %combine.7 = (bf16[576,768]{1,0:T(8,128)(2,1)}, bf16[576,384]{1,0:T(8,128)(2,1)}, bf16[2,192,1024]{2,1,0:T(8,128)(2,1)}, bf16[2,192,1024]{2,1,0:T(8,128)(2,1)}) custom-call(s32[2]{0:T(128)} %pad_add_fusion.4.sc, f32[576,384]{1,0:T(8,128)} %get-tuple-element.42.share, bf16[576,384]{1,0:T(8,128)(2,1)} %copy-done.4, bf16[2304,384]{1,0:T(8,128)(2,1)} %bitcast.49, ...), custom_call_target="tpu_custom_call" | custom-call | flops 1132462080 | bytes 3342336 | tf_op jit(solution)/shard_map/combine/pallas_call | solution.py:150
  85.9 5.8 %combine.6 = (bf16[576,768]{1,0:T(8,128)(2,1)}, bf16[576,384]{1,0:T(8,128)(2,1)}, bf16[2,192,1024]{2,1,0:T(8,128)(2,1)}, bf16[2,192,1024]{2,1,0:T(8,128)(2,1)}) custom-call(s32[2]{0:T(128)} %pad_add_fusion.3.sc, f32[576,384]{1,0:T(8,128)} %get-tuple-element.38.share, bf16[576,384]{1,0:T(8,128)(2,1)} %copy-done.3, bf16[2304,384]{1,0:T(8,128)(2,1)} %bitcast.50, ...), custom_call_target="tpu_custom_call" | custom-call | flops 1132462080 | bytes 3342336 | tf_op jit(solution)/shard_map/combine/pallas_call | solution.py:150
  91.9 4.6 %dispatch.4 = (bf16[576,1024]{1,0:T(8,128)(2,1)}, f32[576,384]{1,0:T(8,128)}, bf16[576,384]{1,0:T(8,128)(2,1)}) custom-call(s32[2]{0:T(128)} %pad_add_fusion.1.sc, bf16[192,1024]{1,0:T(8,128)(2,1)} %t0.1, bf16[192,1024]{1,0:T(8,128)(2,1)} %collective-permute-done.t1, bf16[192,1024]{1,0:T(8,128)(2,1)} %copy-done.11, ...), custom_call_target="tpu_custom_call" | custom-call | flops 679477248 | bytes 2752512 | tf_op jit(solution)/shard_map/dispatch/pallas_call | solution.py:99
  97.8 4.6 %dispatch.5 = (bf16[576,1024]{1,0:T(8,128)(2,1)}, f32[576,384]{1,0:T(8,128)}, bf16[576,384]{1,0:T(8,128)(2,1)}) custom-call(s32[2]{0:T(128)} %pad_add_fusion.2.sc, bf16[192,1024]{1,0:T(8,128)(2,1)} %copy-done.9, bf16[192,1024]{1,0:T(8,128)(2,1)} %copy-done.15, bf16[192,1024]{1,0:T(8,128)(2,1)} %copy-done.12, bf16[192,1024]{1,0:T(8,128)(2,1)} %collective-permute-done.11.t3, ...), custom_call_target="tpu_custom_call" | custom-call | flops 679477248 | bytes 2752512 | tf_op jit(solution)/shard_map/dispatch/pallas_call | solution.py:99
  104.3 1.7 collective-permute-start.26
  106.0 12.9 %collective-permute-done.12.peer = bf16[576,384]{1,0:T(8,128)(2,1)} collective-permute-done((bf16[576,384]{1,0:T(8,128)(2,1)}, bf16[576,384]{1,0:T(8,128)(2,1)}, u32[]{:S(2)}, u32[]{:S(2)}) %collective-permute-start.12) | collective-permute-done | bytes 442400 | tf_op jit(solution)/shard_map/ppermute | solution.py:251
  118.8 5.8 %combine.5 = (bf16[576,768]{1,0:T(8,128)(2,1)}, bf16[576,384]{1,0:T(8,128)(2,1)}, bf16[2,192,1024]{2,1,0:T(8,128)(2,1)}, bf16[2,192,1024]{2,1,0:T(8,128)(2,1)}) custom-call(s32[2]{0:T(128)} %pad_add_fusion.2.sc, f32[576,384]{1,0:T(8,128)} %get-tuple-element.34.share, bf16[576,384]{1,0:T(8,128)(2,1)} %collective-permute-done.12.peer, ...), custom_call_target="tpu_custom_call" | custom-call | flops 1132462080 | bytes 3342336 | tf_op jit(solution)/shard_map/combine/pallas_call | solution.py:150
  124.7 1.6 convert_add_fusion.1
  127.1 1.6 collective-permute-start.20
  130.1 5.9 %combine.4 = (bf16[576,768]{1,0:T(8,128)(2,1)}, bf16[576,384]{1,0:T(8,128)(2,1)}, bf16[2,192,1024]{2,1,0:T(8,128)(2,1)}, bf16[2,192,1024]{2,1,0:T(8,128)(2,1)}) custom-call(s32[2]{0:T(128)} %pad_add_fusion.1.sc, f32[576,384]{1,0:T(8,128)} %get-tuple-element.30.share, bf16[576,384]{1,0:T(8,128)(2,1)} %collective-permute-done.3.peer, ...), custom_call_target="tpu_custom_call" | custom-call | flops 1132462080 | bytes 3342336 | tf_op jit(solution)/shard_map/combine/pallas_call | solution.py:150
  136.3 2.7 %collective-permute-done.20 = bf16[192,1024]{1,0:T(8,128)(2,1)} collective-permute-done((bf16[192,1024]{1,0:T(8,128)(2,1)}, bf16[192,1024]{1,0:T(8,128)(2,1)}, u32[]{:S(2)}, u32[]{:S(2)}) %collective-permute-start.20) | collective-permute-done | bytes 393248 | tf_op jit(solution)/shard_map/ppermute | solution.py:220
  139.0 4.2 %collective-permute-done.27 = bf16[192,1024]{1,0:T(8,128)(2,1)S(1)} collective-permute-done((bf16[192,1024]{1,0:T(8,128)(2,1)S(1)}, bf16[192,1024]{1,0:T(8,128)(2,1)S(1)}, u32[]{:S(2)}, u32[]{:S(2)}) %collective-permute-start.27) | collective-permute-done | bytes 393248 | tf_op jit(solution)/shard_map/ppermute | solution.py:220
  146.8 1.7 collective-permute-start.5
  148.5 8.1 %collective-permute-done.28 = bf16[192,1024]{1,0:T(8,128)(2,1)S(1)} collective-permute-done((bf16[192,1024]{1,0:T(8,128)(2,1)S(1)}, bf16[192,1024]{1,0:T(8,128)(2,1)S(1)}, u32[]{:S(2)}, u32[]{:S(2)}) %collective-permute-start.28) | collective-permute-done | bytes 393248 | tf_op jit(solution)/shard_map/ppermute | solution.py:220
  158.3 13.8 %weights.1 = bf16[1,1024,1152]{2,1,0:T(8,128)(2,1)} custom-call(s32[4]{0:T(128)} %copy-done.5, bf16[2304,1024]{1,0:T(8,128)(2,1)} %bitcast.68, bf16[576,1024]{1,0:T(8,128)(2,1)} %get-tuple-element.46.refs_0_, bf16[576,1024]{1,0:T(8,128)(2,1)} %get-tuple-element.47.refs_1_, bf16[576,1024]{1,0:T(8,128)(2,1)} %get-tuple-element.48.refs_2_, ...), custom_call_target="tpu_custom_call" | custom-call | flops 5435817984 | bytes 12582912 | tf_op jit(solution)/shard_map/weights/pallas_call | solution.py:192
  (103 shorter events, 29.7 us)
Async XLA Ops:
  0.6 28.0 %collective-permute-start.6 = (bf16[192,1024]{1,0:T(8,128)(2,1)}, bf16[192,1024]{1,0:T(8,128)(2,1)S(1)}, u32[]{:S(2)}, u32[]{:S(2)}) collective-permute-start(bf16[192,1024]{1,0:T(8,128)(2,1)} %t0.1), channel_id=1, source_target_pairs={{0,4},{1,5},{2,6},{3,7},{4,8},{5,9},{6,10},{7,11},{8,12},{9,13},{1... | collective-permute-start | bytes 1179656 | tf_op jit(solution)/shard_map/ppermute | solution.py:220
  28.7 11.4 %collective-permute-start.22 = (bf16[192,1024]{1,0:T(8,128)(2,1)S(1)}, bf16[192,1024]{1,0:T(8,128)(2,1)S(1)}, u32[]{:S(2)}, u32[]{:S(2)}) collective-permute-start(bf16[192,1024]{1,0:T(8,128)(2,1)S(1)} %collective-permute-done.6.t0), channel_id=1, source_target_pairs={{0,2},{1,3},{2,0},{3,1},{4,6},{5,7},{6,4},{7,5},{8,10},{9,11},{10,... | collective-permute-start | bytes 1179656 | tf_op jit(solution)/shard_map/ppermute | solution.py:220
  29.1 13.0 %collective-permute-start.7 = (bf16[192,1024]{1,0:T(8,128)(2,1)S(1)}, bf16[192,1024]{1,0:T(8,128)(2,1)S(1)}, u32[]{:S(2)}, u32[]{:S(2)}) collective-permute-start(bf16[192,1024]{1,0:T(8,128)(2,1)S(1)} %collective-permute-done.6.t0), channel_id=1, source_target_pairs={{0,4},{1,5},{2,6},{3,7},{4,8},{5,9},{6,10},{7,11},{8,12},{9,13},{1... | collective-permute-start | bytes 1179656 | tf_op jit(solution)/shard_map/ppermute | solution.py:220
  30.0 22.4 %collective-permute-start.21 = (bf16[192,1024]{1,0:T(8,128)(2,1)S(1)}, bf16[192,1024]{1,0:T(8,128)(2,1)S(1)}, u32[]{:S(2)}, u32[]{:S(2)}) collective-permute-start(bf16[192,1024]{1,0:T(8,128)(2,1)S(1)} %collective-permute-done.6.t0), channel_id=1, source_target_pairs={{0,1},{1,0},{2,3},{3,2},{4,5},{5,4},{6,7},{7,6},{8,9},{9,8},{10,11... | collective-permute-start | bytes 1179656 | tf_op jit(solution)/shard_map/ppermute | solution.py:220
  40.1 12.3 %collective-permute-start.23 = (bf16[192,1024]{1,0:T(8,128)(2,1)S(1)}, bf16[192,1024]{1,0:T(8,128)(2,1)S(1)}, u32[]{:S(2)}, u32[]{:S(2)}) collective-permute-start(bf16[192,1024]{1,0:T(8,128)(2,1)S(1)} %collective-permute-done.22.t2), channel_id=1, source_target_pairs={{0,1},{1,0},{2,3},{3,2},{4,5},{5,4},{6,7},{7,6},{8,9},{9,8},{10,11... | collective-permute-start | bytes 1179656 | tf_op jit(solution)/shard_map/ppermute | solution.py:220
  46.1 16.3 %collective-permute-start.15 = (bf16[192,1024]{1,0:T(8,128)(2,1)S(1)}, bf16[192,1024]{1,0:T(8,128)(2,1)}, u32[]{:S(2)}, u32[]{:S(2)}) collective-permute-start(bf16[192,1024]{1,0:T(8,128)(2,1)S(1)} %collective-permute-done.7.t0), channel_id=1, source_target_pairs={{0,1},{1,0},{2,3},{3,2},{4,5},{5,4},{6,7},{7,6},{8,9},{9,8},{10,11... | collective-permute-start | bytes 1179656 | tf_op jit(solution)/shard_map/ppermute | solution.py:220
  58.0 16.1 %collective-permute-start.24 = (bf16[576,384]{1,0:T(8,128)(2,1)}, bf16[576,384]{1,0:T(8,128)(2,1)S(1)}, u32[]{:S(2)}, u32[]{:S(2)}) collective-permute-start(bf16[576,384]{1,0:T(8,128)(2,1)} %get-tuple-element.43), channel_id=1, source_target_pairs={{0,16},{16,0},{1,17},{17,1},{2,18},{18,2},{3,19},{19,3},{4,20},{20... | collective-permute-start | bytes 1327112 | tf_op jit(solution)/shard_map/ppermute | solution.py:251
  59.6 13.0 %collective-permute-start.8 = (bf16[192,1024]{1,0:T(8,128)(2,1)S(1)}, bf16[192,1024]{1,0:T(8,128)(2,1)S(1)}, u32[]{:S(2)}, u32[]{:S(2)}) collective-permute-start(bf16[192,1024]{1,0:T(8,128)(2,1)S(1)} %collective-permute-done.7.t0), channel_id=1, source_target_pairs={{0,4},{1,5},{2,6},{3,7},{4,8},{5,9},{6,10},{7,11},{8,12},{9,13},{1... | collective-permute-start | bytes 1179656 | tf_op jit(solution)/shard_map/ppermute | solution.py:220
  59.6 21.9 %collective-permute-start.1 = (bf16[192,1024]{1,0:T(8,128)(2,1)S(1)}, bf16[192,1024]{1,0:T(8,128)(2,1)S(1)}, u32[]{:S(2)}, u32[]{:S(2)}) collective-permute-start(bf16[192,1024]{1,0:T(8,128)(2,1)S(1)} %copy-done.6), channel_id=1, source_target_pairs={{0,2},{1,3},{2,0},{3,1},{4,6},{5,7},{6,4},{7,5},{8,10},{9,11},{10,... | collective-permute-start | bytes 1179656 | tf_op jit(solution)/shard_map/ppermute | solution.py:220
  67.1 15.9 %collective-permute-start.18 = (bf16[576,384]{1,0:T(8,128)(2,1)}, bf16[576,384]{1,0:T(8,128)(2,1)S(1)}, u32[]{:S(2)}, u32[]{:S(2)}) collective-permute-start(bf16[576,384]{1,0:T(8,128)(2,1)} %get-tuple-element.39), channel_id=1, source_target_pairs={{0,16},{16,0},{1,17},{17,1},{2,18},{18,2},{3,19},{19,3},{4,20},{20... | collective-permute-start | bytes 1327112 | tf_op jit(solution)/shard_map/ppermute | solution.py:251
  81.0 23.0 %collective-permute-start.25 = (bf16[2,192,1024]{2,1,0:T(8,128)(2,1)}, bf16[2,192,1024]{2,1,0:T(8,128)(2,1)S(1)}, u32[]{:S(2)}, u32[]{:S(2)}) collective-permute-start(bf16[2,192,1024]{2,1,0:T(8,128)(2,1)} %get-tuple-element.45), channel_id=1, source_target_pairs={{0,1},{1,0},{2,3},{3,2},{4,5},{5,4},{6,7},{7,6},{8,9},{9,8},{10,11... | collective-permute-start | bytes 2359304 | tf_op jit(solution)/shard_map/ppermute | solution.py:220
  83.0 14.1 %collective-permute-start.9 = (bf16[192,1024]{1,0:T(8,128)(2,1)S(1)}, bf16[192,1024]{1,0:T(8,128)(2,1)S(1)}, u32[]{:S(2)}, u32[]{:S(2)}) collective-permute-start(bf16[192,1024]{1,0:T(8,128)(2,1)S(1)} %collective-permute-done.8.t0), channel_id=1, source_target_pairs={{0,1},{1,0},{2,3},{3,2},{4,5},{5,4},{6,7},{7,6},{8,9},{9,8},{10,11... | collective-permute-start | bytes 1179656 | tf_op jit(solution)/shard_map/ppermute | solution.py:220
  83.0 14.1 %collective-permute-start.11 = (bf16[192,1024]{1,0:T(8,128)(2,1)S(1)}, bf16[192,1024]{1,0:T(8,128)(2,1)}, u32[]{:S(2)}, u32[]{:S(2)}) collective-permute-start(bf16[192,1024]{1,0:T(8,128)(2,1)S(1)} %collective-permute-done.10.t2), channel_id=1, source_target_pairs={{0,1},{1,0},{2,3},{3,2},{4,5},{5,4},{6,7},{7,6},{8,9},{9,8},{10,11... | collective-permute-start | bytes 1179656 | tf_op jit(solution)/shard_map/ppermute | solution.py:220
  91.7 32.9 %collective-permute-start.19 = (bf16[2,192,1024]{2,1,0:T(8,128)(2,1)}, bf16[2,192,1024]{2,1,0:T(8,128)(2,1)}, u32[]{:S(2)}, u32[]{:S(2)}) collective-permute-start(bf16[2,192,1024]{2,1,0:T(8,128)(2,1)} %get-tuple-element.41), channel_id=1, source_target_pairs={{0,1},{1,0},{2,3},{3,2},{4,5},{5,4},{6,7},{7,6},{8,9},{9,8},{10,11... | collective-permute-start | bytes 2359304 | tf_op jit(solution)/shard_map/ppermute | solution.py:220
  96.5 33.6 %collective-permute-start.3 = (bf16[576,384]{1,0:T(8,128)(2,1)}, bf16[576,384]{1,0:T(8,128)(2,1)}, u32[]{:S(2)}, u32[]{:S(2)}) collective-permute-start(bf16[576,384]{1,0:T(8,128)(2,1)} %get-tuple-element.31), channel_id=1, source_target_pairs={{0,16},{16,0},{1,17},{17,1},{2,18},{18,2},{3,19},{19,3},{4,20},{20... | collective-permute-start | bytes 1327112 | tf_op jit(solution)/shard_map/ppermute | solution.py:251
  102.4 16.4 %collective-permute-start.12 = (bf16[576,384]{1,0:T(8,128)(2,1)}, bf16[576,384]{1,0:T(8,128)(2,1)}, u32[]{:S(2)}, u32[]{:S(2)}) collective-permute-start(bf16[576,384]{1,0:T(8,128)(2,1)} %get-tuple-element.35), channel_id=1, source_target_pairs={{0,16},{16,0},{1,17},{17,1},{2,18},{18,2},{3,19},{19,3},{4,20},{20... | collective-permute-start | bytes 1327112 | tf_op jit(solution)/shard_map/ppermute | solution.py:251
  104.3 24.5 %collective-permute-start.26 = (bf16[192,1024]{1,0:T(8,128)(2,1)S(1)}, bf16[192,1024]{1,0:T(8,128)(2,1)}, u32[]{:S(2)}, u32[]{:S(2)}) collective-permute-start(bf16[192,1024]{1,0:T(8,128)(2,1)S(1)} %fusion.15), channel_id=1, source_target_pairs={{0,2},{1,3},{2,0},{3,1},{4,6},{5,7},{6,4},{7,5},{8,10},{9,11},{10,... | collective-permute-start | bytes 1179656 | tf_op jit(solution)/shard_map/ppermute | solution.py:220
  124.7 19.7 %collective-permute-start.13 = (bf16[2,192,1024]{2,1,0:T(8,128)(2,1)}, bf16[2,192,1024]{2,1,0:T(8,128)(2,1)}, u32[]{:S(2)}, u32[]{:S(2)}) collective-permute-start(bf16[2,192,1024]{2,1,0:T(8,128)(2,1)} %get-tuple-element.37), channel_id=1, source_target_pairs={{0,1},{1,0},{2,3},{3,2},{4,5},{5,4},{6,7},{7,6},{8,9},{9,8},{10,11... | collective-permute-start | bytes 2359304 | tf_op jit(solution)/shard_map/ppermute | solution.py:220
  127.1 11.8 %collective-permute-start.20 = (bf16[192,1024]{1,0:T(8,128)(2,1)}, bf16[192,1024]{1,0:T(8,128)(2,1)}, u32[]{:S(2)}, u32[]{:S(2)}) collective-permute-start(bf16[192,1024]{1,0:T(8,128)(2,1)} %fusion.14), channel_id=1, source_target_pairs={{0,2},{1,3},{2,0},{3,1},{4,6},{5,7},{6,4},{7,5},{8,10},{9,11},{10,... | collective-permute-start | bytes 1179656 | tf_op jit(solution)/shard_map/ppermute | solution.py:220
  129.8 13.3 %collective-permute-start.27 = (bf16[192,1024]{1,0:T(8,128)(2,1)S(1)}, bf16[192,1024]{1,0:T(8,128)(2,1)S(1)}, u32[]{:S(2)}, u32[]{:S(2)}) collective-permute-start(bf16[192,1024]{1,0:T(8,128)(2,1)S(1)} %fusion.2), channel_id=1, source_target_pairs={{0,4},{1,5},{2,6},{3,7},{4,8},{5,9},{6,10},{7,11},{8,12},{9,13},{1... | collective-permute-start | bytes 1179656 | tf_op jit(solution)/shard_map/ppermute | solution.py:220
  144.3 12.3 %collective-permute-start.28 = (bf16[192,1024]{1,0:T(8,128)(2,1)S(1)}, bf16[192,1024]{1,0:T(8,128)(2,1)S(1)}, u32[]{:S(2)}, u32[]{:S(2)}) collective-permute-start(bf16[192,1024]{1,0:T(8,128)(2,1)S(1)} %fusion.5), channel_id=1, source_target_pairs={{0,4},{1,5},{2,6},{3,7},{4,8},{5,9},{6,10},{7,11},{8,12},{9,13},{1... | collective-permute-start | bytes 1179656 | tf_op jit(solution)/shard_map/ppermute | solution.py:220
  146.0 12.1 %collective-permute-start.14 = (bf16[192,1024]{1,0:T(8,128)(2,1)S(1)}, bf16[192,1024]{1,0:T(8,128)(2,1)S(1)}, u32[]{:S(2)}, u32[]{:S(2)}) collective-permute-start(bf16[192,1024]{1,0:T(8,128)(2,1)S(1)} %fusion.13), channel_id=1, source_target_pairs={{0,2},{1,3},{2,0},{3,1},{4,6},{5,7},{6,4},{7,5},{8,10},{9,11},{10,... | collective-permute-start | bytes 1179656 | tf_op jit(solution)/shard_map/ppermute | solution.py:220
  146.8 25.3 %collective-permute-start.5 = (bf16[192,1024]{1,0:T(8,128)(2,1)S(1)}, bf16[192,1024]{1,0:T(8,128)(2,1)S(1)}, u32[]{:S(2)}, u32[]{:S(2)}) collective-permute-start(bf16[192,1024]{1,0:T(8,128)(2,1)S(1)} %fusion.12), channel_id=1, source_target_pairs={{0,2},{1,3},{2,0},{3,1},{4,6},{5,7},{6,4},{7,5},{8,10},{9,11},{10,... | collective-permute-start | bytes 1179656 | tf_op jit(solution)/shard_map/ppermute | solution.py:220
  158.3 13.9 %collective-permute-start.29 = (bf16[192,1024]{1,0:T(8,128)(2,1)S(1)}, bf16[192,1024]{1,0:T(8,128)(2,1)S(1)}, u32[]{:S(2)}, u32[]{:S(2)}) collective-permute-start(bf16[192,1024]{1,0:T(8,128)(2,1)S(1)} %fusion.8), channel_id=1, source_target_pairs={{0,4},{1,5},{2,6},{3,7},{4,8},{5,9},{6,10},{7,11},{8,12},{9,13},{1... | collective-permute-start | bytes 1179656 | tf_op jit(solution)/shard_map/ppermute | solution.py:220
  (23 other events, 265.4 us)

commit v2 on v0

v2 whole, which is shorter than its diff:
```python
import functools

import jax
import jax.numpy as jnp
from jax import lax
from jax.experimental import pallas as pl
from jax.experimental.pallas import tpu as pltpu
from jax.sharding import PartitionSpec as P

gate_unit = 0.00390625
loss_scale = 0.015625
f32 = jnp.float32
bf16 = jnp.bfloat16


def contract_rows(left, right):
    return lax.dot_general(left, right, (((0,), (0,)), ((), ())), preferred_element_type=f32)


def contract_cols(left, right):
    return lax.dot_general(left, right, (((1,), (1,)), ((), ())), preferred_element_type=f32)


def activation_grads(grad_hidden, gate_pre, up_pre):
    sigmoid = jax.nn.sigmoid(gate_pre)
    silu = gate_pre * sigmoid
    dsilu = sigmoid * (1.0 + gate_pre * (1.0 - sigmoid))
    grad_gate_pre = (grad_hidden * up_pre * dsilu).astype(bf16)
    grad_up_pre = (grad_hidden * silu).astype(bf16)
    return (grad_gate_pre, grad_up_pre)


def body_any(out_grad, routes, gate_codes, w_gate, w_up, w_down, saved_inputs, saved_gate, saved_up):
    owners = lax.axis_size("expert")
    slot_count = saved_gate.shape[1]
    capacity = slot_count // owners
    token_count = routes.shape[0]
    choice_count = routes.shape[1]
    flat_routes = routes.reshape(-1)
    onehot = (flat_routes[:, None] == jnp.arange(owners, dtype=jnp.int32)[None, :]).astype(jnp.int32)
    earlier = jnp.cumsum(onehot, axis=0) - onehot
    position = jnp.sum(earlier * onehot, axis=1)
    slot_index = (flat_routes * capacity + position).reshape(token_count, choice_count)
    gate_values = gate_codes.astype(f32) * gate_unit
    rows_iota = jnp.arange(slot_count, dtype=jnp.int32)[:, None]
    weighted = jnp.zeros((slot_count, token_count), f32)
    picks = jnp.zeros((slot_count, token_count), f32)
    for pick in range(choice_count):
        hit = rows_iota == slot_index[:, pick][None, :]
        weighted = weighted + jnp.where(hit, gate_values[:, pick][None, :], 0.0)
        picks = picks + hit.astype(f32)
    outgoing = jnp.dot(weighted.astype(bf16), out_grad, preferred_element_type=f32).astype(bf16)
    received = lax.all_to_all(outgoing, "expert", split_axis=0, concat_axis=0, tiled=True)
    hidden_share = lax.psum_scatter(
        contract_cols(received, w_down[0]), "dp", scatter_dimension=0, tiled=True
    )
    gate_pre = saved_gate[0].astype(f32)
    up_pre = saved_up[0].astype(f32)
    hidden = (gate_pre * jax.nn.sigmoid(gate_pre) * up_pre).astype(bf16)
    grad_hidden = lax.all_gather(hidden_share, "dp", axis=0, tiled=True)
    grad_gate_pre, grad_up_pre = activation_grads(grad_hidden, gate_pre, up_pre)
    slot_grads = contract_cols(grad_gate_pre, w_gate[0]) + contract_cols(grad_up_pre, w_up[0])
    returned = lax.all_to_all(
        slot_grads.astype(bf16), "expert", split_axis=0, concat_axis=0, tiled=True
    )
    token_grads = contract_rows(picks.astype(bf16), returned).astype(bf16)
    inputs_here = saved_inputs[0]
    part = jnp.concatenate(
        [
            contract_rows(inputs_here, grad_gate_pre),
            contract_rows(inputs_here, grad_up_pre),
            contract_rows(received, hidden),
        ],
        axis=1,
    )
    return (token_grads, (part * loss_scale).astype(bf16)[None])


def whole(shape):
    return pl.BlockSpec(shape, lambda i, sc: (0,) * len(shape))


def params(mib):
    return pltpu.CompilerParams(vmem_limit_bytes=mib << 20)


def dispatch_kernel(n, cap, sc, *refs):
    toks, (wd0, wd1) = refs[:n], refs[n : n + 2]
    rec0, rec1, share, share_out, pos_out = refs[n + 2 :]
    tok = toks[0].shape[0] - 8
    line = 256 * pl.cdiv(tok, 256)
    before = lax.broadcasted_iota(jnp.int32, (tok, tok), 0) < lax.broadcasted_iota(jnp.int32, (tok, tok), 1)
    before = jnp.where(before, 1.0, 0.0).astype(bf16)
    slot = lax.broadcasted_iota(jnp.int32, (cap, tok), 0).astype(f32)
    masks, gates = [], []
    for a in range(2):
        expert = sc[a].astype(f32)
        for t in toks:
            hit = t[tok:, :tok].astype(f32) == expert
            masks.append(jnp.max(jnp.where(hit, 1.0, 0.0), axis=0, keepdims=True))
            gates.append(jnp.sum(jnp.where(hit, t[tok:, line : line + tok].astype(f32), 0.0), axis=0, keepdims=True))
    fill = [jnp.zeros((8 - 2 * n, tok), f32)] if n < 4 else []
    mask = jnp.concatenate(masks + fill, axis=0)
    pos = jnp.dot(mask.astype(bf16), before, preferred_element_type=f32)
    pos = jnp.where(mask > 0.0, pos, -1.0)
    pos_out[...] = pos
    for rel, t in enumerate(toks):
        w = [
            jnp.where(slot == pos[i : i + 1, :], gates[i] * gate_unit, 0.0).astype(bf16)
            for i in (rel, n + rel)
        ]
        rows = jnp.dot(jnp.concatenate(w, axis=0), t[:tok, :], preferred_element_type=f32).astype(bf16)
        rec0[rel * cap : (rel + 1) * cap, :] = rows[:cap]
        rec1[rel * cap : (rel + 1) * cap, :] = rows[cap:]
    for a, (rec, wd) in enumerate(((rec0, wd0), (rec1, wd1))):
        gh = contract_cols(rec[...], wd[...])
        share[a * n * cap : (a + 1) * n * cap, :] = gh
        share_out[a * n * cap : (a + 1) * n * cap, :] = gh.astype(bf16)


def dispatch(experts, toks, wd0, wd1, cap):
    n = len(toks)
    tok, d = toks[0].shape
    h = wd0.shape[0]
    outs = [((n * cap, d), bf16), ((n * cap, d), bf16), ((2 * n * cap, h), f32), ((2 * n * cap, h), bf16), ((8, tok - 8), f32)]
    return pl.pallas_call(
        functools.partial(dispatch_kernel, n, cap),
        out_shape=[jax.ShapeDtypeStruct(s, t) for s, t in outs],
        grid_spec=pltpu.PrefetchScalarGridSpec(
            num_scalar_prefetch=1,
            grid=(1,),
            in_specs=[whole((tok, d))] * n + [whole((h, d))] * 2,
            out_specs=[whole(s) for s, _ in outs],
        ),
        cost_estimate=pl.CostEstimate(
            flops=4 * n * cap * d * (tok + h), bytes_accessed=2 * n * d * (tok + 2 * cap) + 4 * h * d, transcendentals=0
        ),
        compiler_params=params(24),
        name="dispatch",
    )(experts, *toks, wd0, wd1)


def combine_kernel(n, cap, sc, share, peer, pos, *refs):
    saved, (w0, w1), (gp0, gp1), backs = refs[: 4 * n], refs[4 * n : 4 * n + 2], refs[4 * n + 2 : 4 * n + 4], refs[4 * n + 4 :]
    h = share.shape[1]
    slot = lax.broadcasted_iota(jnp.int32, (cap, pos.shape[1]), 0).astype(f32)
    sums = [None] * n
    for a, (gp, w) in enumerate(((gp0, w0), (gp1, w1))):
        for rel in range(n):
            i = a * n + rel
            gh = share[i * cap : (i + 1) * cap, :] + peer[i * cap : (i + 1) * cap, :].astype(f32)
            gate_pre = saved[2 * i][...].astype(f32)
            up_pre = saved[2 * i + 1][...].astype(f32)
            gg, gu = activation_grads(gh, gate_pre, up_pre)
            gp[rel * cap : (rel + 1) * cap, :h] = gg
            gp[rel * cap : (rel + 1) * cap, h:] = gu
        slots = contract_cols(gp[...], w[...]).astype(bf16)
        for rel in range(n):
            i = a * n + rel
            pick = jnp.where(slot == pos[i : i + 1, :], 1.0, 0.0).astype(bf16)
            part = contract_rows(pick, slots[rel * cap : (rel + 1) * cap])
            sums[rel] = part if sums[rel] is None else sums[rel] + part
    for rel in range(n):
        backs[rel][...] = sums[rel].astype(bf16)


def combine(sources, share, peer, pos, saved0, saved1, w0, w1, cap):
    n = share.shape[0] // (2 * cap)
    h = share.shape[1]
    d = w0.shape[0]
    tok = pos.shape[1]

    def piece(rel):
        return pl.BlockSpec((cap, h), lambda i, sc: (sc[rel], 0))

    saved = [v for pair in (saved0, saved1) for _ in range(n) for v in pair]
    saved_specs = [piece(rel) for _ in range(2) for rel in range(n) for _ in range(2)]
    outs = [(n * cap, 2 * h)] * 2 + [(tok, d)] * n
    return pl.pallas_call(
        functools.partial(combine_kernel, n, cap),
        out_shape=[jax.ShapeDtypeStruct(s, bf16) for s in outs],
        grid_spec=pltpu.PrefetchScalarGridSpec(
            num_scalar_prefetch=1,
            grid=(1,),
            in_specs=[whole(share.shape), whole(share.shape), whole(pos.shape)] + saved_specs + [whole((d, 2 * h))] * 2,
            out_specs=[whole(s) for s in outs],
        ),
        cost_estimate=pl.CostEstimate(
            flops=4 * n * cap * d * (tok + 2 * h),
            bytes_accessed=2 * n * tok * d + 20 * n * cap * h + 8 * d * h,
            transcendentals=2 * n * cap * h,
        ),
        compiler_params=params(28),
        name="combine",
    )(sources, share, peer, pos, *saved, w0, w1)


def weights_kernel(count, cap, sc, x, hid, *refs):
    recs, gps = refs[:count], refs[count : 2 * count]
    out, xs, rs, gs, hs, sems = refs[2 * count :]
    i = pl.program_id(0)
    tile = xs.shape[2]
    steps = pl.num_programs(0)

    def columns(at, step):
        at_col = pl.ds(pl.multiple_of(step * tile, 128), tile)
        copies = []
        base = 0
        for r in recs:
            copies.append(pltpu.make_async_copy(r.at[:, at_col], rs.at[at, pl.ds(base, r.shape[0]), :], sems.at[at, len(copies)]))
            base += r.shape[0]
        for p in range(base // cap):
            src = pl.ds(pl.multiple_of(sc[p] * cap, 16), cap)
            copies.append(pltpu.make_async_copy(x.at[src, at_col], xs.at[at, pl.ds(p * cap, cap), :], sems.at[at, len(copies)]))
        return copies

    def fixed():
        copies = []
        base = 0
        for g in gps:
            copies.append(pltpu.make_async_copy(g, gs.at[pl.ds(base, g.shape[0]), :], sems.at[2, len(copies)]))
            base += g.shape[0]
        for p in range(base // cap):
            src = pl.ds(pl.multiple_of(sc[p] * cap, 16), cap)
            copies.append(pltpu.make_async_copy(hid.at[src, :], hs.at[pl.ds(p * cap, cap), :], sems.at[2, len(copies)]))
        return copies

    @pl.when(i == 0)
    def _():
        for c in columns(0, 0) + fixed():
            c.start()

    @pl.when(i + 1 < steps)
    def _():
        for c in columns((i + 1) % 2, i + 1):
            c.start()

    for c in columns(i % 2, i):
        c.wait()

    @pl.when(i == 0)
    def _():
        for c in fixed():
            c.wait()

    wide = gs.shape[1]
    now = i % 2
    out[0, :, :wide] = (contract_rows(xs[now], gs[...]) * loss_scale).astype(bf16)
    out[0, :, wide:] = (contract_rows(rs[now], hs[...]) * loss_scale).astype(bf16)


def weight_sums(sources, x, hid, recs, gps, cap):
    slots, d = x.shape
    h = hid.shape[1]
    tile = 256
    anywhere = pl.BlockSpec(memory_space=pl.ANY)
    return pl.pallas_call(
        functools.partial(weights_kernel, len(recs), cap),
        out_shape=jax.ShapeDtypeStruct((1, d, 3 * h), bf16),
        grid_spec=pltpu.PrefetchScalarGridSpec(
            num_scalar_prefetch=1,
            grid=(d // tile,),
            in_specs=[anywhere] * (2 + 2 * len(recs)),
            out_specs=pl.BlockSpec((1, tile, 3 * h), lambda i, sc: (0, i, 0)),
            scratch_shapes=[
                pltpu.VMEM((2, slots, tile), bf16),
                pltpu.VMEM((2, slots, tile), bf16),
                pltpu.VMEM((slots, 2 * h), bf16),
                pltpu.VMEM((slots, h), bf16),
                pltpu.SemaphoreType.DMA((3, len(recs) + slots // cap)),
            ],
        ),
        cost_estimate=pl.CostEstimate(
            flops=6 * slots * d * h, bytes_accessed=4 * slots * d + 6 * d * h + 6 * slots * h, transcendentals=0
        ),
        compiler_params=params(24),
        name="weights",
    )(sources, x, hid, *recs, *gps)


def after(value, *others):
    return lax.optimization_barrier((value, *others))[0]


def body_grid(out_grad, routes, gate_codes, w_gate, w_up, w_down, saved_inputs, saved_gate, saved_up):
    owners = lax.axis_size("expert")
    me = lax.axis_index("expert")
    to_core = [(i, i ^ 1) for i in range(owners)]
    to_x = [(i, i ^ 2) for i in range(owners)]
    ring = [(i, (i + 4) % owners) for i in range(owners)]
    rounds = owners // 4
    tok, d = out_grad.shape
    choices = routes.shape[1]
    slots = saved_gate.shape[1]
    cap = slots // owners

    def send(v, perm):
        return lax.ppermute(v, "expert", perm)

    line = 256 * pl.cdiv(tok, 256)
    named = jnp.concatenate(
        [
            jnp.pad(routes.T.astype(bf16), ((0, 8 - choices), (0, line - tok)), constant_values=-1),
            jnp.pad(gate_codes.T.astype(bf16), ((0, 8 - choices), (0, d - line - tok))),
        ],
        axis=1,
    )
    block = jnp.concatenate([out_grad, named], axis=0)
    own_col = [block]
    for _ in range(rounds - 1):
        own_col.append(send(own_col[-1], ring))
    other_col = [send(v, to_x) for v in own_col]

    wd, sg, su = w_down[0], saved_gate[0], saved_up[0]
    w = jnp.concatenate([w_gate[0], w_up[0]], axis=1)
    wd_c, w_c, sg_c, su_c = [send(v, to_core) for v in (wd, w, sg, su)]
    gate_pre = sg.astype(f32)
    hid = (gate_pre * jax.nn.sigmoid(gate_pre) * su.astype(f32)).astype(bf16)

    groups = (me // 4 + rounds - jnp.arange(rounds, dtype=jnp.int32)) % rounds
    own_src = groups * 4 + me % 4
    other_src = jnp.bitwise_xor(own_src, 2)
    experts = jnp.stack([me, jnp.bitwise_xor(me, 1)]).astype(jnp.int32)

    chunks = [[(0, 0)]] + [[(1, k - 1), (0, k)] for k in range(1, rounds)] + [[(1, rounds - 1)]]
    recs, recs_c, gps, gps_c, order = [], [], [], [], []
    back = {}
    for chunk in chunks:
        toks = [(other_col if col else own_col)[k] for col, k in chunk]
        src = jnp.stack([(other_src if col else own_src)[k] for col, k in chunk])
        rec, rec_c, share, share_out, pos = dispatch(experts, toks, wd, wd_c, cap)
        peer = lax.ppermute(share_out, "dp", [(0, 1), (1, 0)])
        gp, gp_c, *sums = combine(src, share, peer, pos, (sg, su), (sg_c, su_c), w, w_c, cap)
        back.update(zip(chunk, sums))
        recs.append(rec)
        recs_c.append(send(rec_c, to_core))
        gps.append(gp)
        gps_c.append(send(gp_c, to_core))
        order.append(src)

    run = None
    arrived = {k: send(back[(1, k)], to_x) for k in [1, 2, 3, 0]}
    for k in [1, 2, 3, 0]:
        total = back[(0, k)].astype(f32) + arrived[k].astype(f32)
        if run is not None:
            total = total + run.astype(f32)
        total = total.astype(bf16)
        run = send(total, ring) if k else None
    order = jnp.concatenate(order)
    order = jnp.concatenate([order, jnp.bitwise_xor(order, 1)])
    weight_grads = weight_sums(order, saved_inputs[0], hid, recs + recs_c, gps + gps_c, cap)
    return (total, weight_grads)


def solution(mesh):
    placed = (
        P("expert", "dp"),
        P("expert", None),
        P("expert", None),
        P("expert", "dp", None),
        P("expert", "dp", None),
        P("expert", None, "dp"),
        P("expert", None, "dp"),
        P("expert", None, None),
        P("expert", None, None),
    )
    small = mesh.shape["expert"] == 16 and mesh.shape["dp"] == 2
    return jax.shard_map(
        body_grid if small else body_any,
        mesh=mesh,
        in_specs=placed,
        out_specs=(P("expert", "dp"), P("expert", "dp", None)),
        check_vma=False,
    )
```

time: 370 us -> 150 us (0.41)
  the two profiles are of different devices: /device:TPU:11 before, /device:TPU:0 now
where the time goes in v2:
time: 150 us; the launch traced here: 148 us
  Pallas kernels  48.6 us (32%)
  local copies, waits for them, and re-layouts  30.8 us (21%)
  waiting for transfers between devices  29.1 us (19%)
  starting transfers between devices  23.9 us (16%)
  other arithmetic  14.1 us (9%)
    ppermute x28, waiting for transfers between devices, send(): return lax.ppermute(v, 'expert', perm)  23 us
    pallas_call x5, Pallas kernels, combine(): pl.pallas_call(functools.partial(combine_kernel, n, cap), out_shape=[jax....  22.8 us
    unnamed x106, local copies, waits for them, and re-layouts  19.5 us
    ppermute x28, starting transfers between devices, send(): return lax.ppermute(v, 'expert', perm)  18.3 us
    pallas_call x1, Pallas kernels, weight_sums(): pl.pallas_call(functools.partial(weights_kernel, len(recs), cap), out_sha...  15.6 us
    pallas_call x5, Pallas kernels, dispatch(): pl.pallas_call(functools.partial(dispatch_kernel, n, cap), out_shape=[jax...  10.2 us
    ppermute x5, waiting for transfers between devices, body_grid(): peer = lax.ppermute(share_out, 'dp', [(0, 1), (1, 0)])  6.07 us
    ppermute x5, starting transfers between devices, body_grid(): peer = lax.ppermute(share_out, 'dp', [(0, 1), (1, 0)])  5.57 us
  transfers between devices with their start and end apart: 33, of which 6 were waited for; matrix products, arithmetic and copies ran while one was open for 15% of the time, Pallas kernels for 33%

profile of v2, /device:TPU:0, one launch (start us, length us, event | category | flops | bytes accessed | tf_op | source)
XLA Modules:
  0.0 147.6 jit_solution(2619100809472043061)
XLA Ops:
  2.5 3.1 %collective-permute-start.6 = (bf16[200,1024]{1,0:T(8,128)(2,1)S(1)}, bf16[200,1024]{1,0:T(8,128)(2,1)S(1)}, u32[]{:S(2)}, u32[]{:S(2)}) collective-permute-start(bf16[200,1024]{1,0:T(8,128)(2,1)S(1)} %fusion.12.refs_0_), channel_id=1, source_target_pairs={{0,4},{1,5},{2,6},{3,7},{4,8},{5,9},{6,10},{7,11},{8,12},{9,13},{1... | collective-permute-start | bytes 1228808 | tf_op jit(solution)/shard_map/ppermute | solution.py:298
  7.6 2.6 %pad_maximum_fusion.refs_4_.refs_8_ = bf16[1024,768]{1,0:T(8,128)(2,1)} fusion(bf16[1024,384]{1,0:T(8,128)(2,1)} %bitcast.39, bf16[1024,384]{1,0:T(8,128)(2,1)} %bitcast.40), kind=kLoop, calls=%fused_computation.7 | loop fusion | flops 3145728 | bytes 3145728 | tf_op jit(solution)/shard_map/concatenate | solution.py:315
  10.2 6.8 %collective-permute-done.6.refs_1_ = bf16[200,1024]{1,0:T(8,128)(2,1)S(1)} collective-permute-done((bf16[200,1024]{1,0:T(8,128)(2,1)S(1)}, bf16[200,1024]{1,0:T(8,128)(2,1)S(1)}, u32[]{:S(2)}, u32[]{:S(2)}) %collective-permute-start.6) | collective-permute-done | bytes 409632 | tf_op jit(solution)/shard_map/ppermute | solution.py:298
  18.2 1.6 %collective-permute-start.9 = (bf16[200,1024]{1,0:T(8,128)(2,1)S(1)}, bf16[200,1024]{1,0:T(8,128)(2,1)}, u32[]{:S(2)}, u32[]{:S(2)}) collective-permute-start(bf16[200,1024]{1,0:T(8,128)(2,1)S(1)} %collective-permute-done.6.refs_1_), channel_id=1, source_target_pairs={{0,4},{1,5},{2,6},{3,7},{4,8},{5,9},{6,10},{7,11},{8,12},{9,13},{1... | collective-permute-start | bytes 1228808 | tf_op jit(solution)/shard_map/ppermute | solution.py:298
  19.8 1.6 %collective-permute-start.16 = (bf16[200,1024]{1,0:T(8,128)(2,1)S(1)}, bf16[200,1024]{1,0:T(8,128)(2,1)S(1)}, u32[]{:S(2)}, u32[]{:S(2)}) collective-permute-start(bf16[200,1024]{1,0:T(8,128)(2,1)S(1)} %collective-permute-done.6.refs_1_), channel_id=1, source_target_pairs={{0,2},{1,3},{2,0},{3,1},{4,6},{5,7},{6,4},{7,5},{8,10},{9,11},{10,... | collective-permute-start | bytes 1228808 | tf_op jit(solution)/shard_map/ppermute | solution.py:298
  21.3 10.3 %collective-permute-done.9.refs_1_ = bf16[200,1024]{1,0:T(8,128)(2,1)} collective-permute-done((bf16[200,1024]{1,0:T(8,128)(2,1)S(1)}, bf16[200,1024]{1,0:T(8,128)(2,1)}, u32[]{:S(2)}, u32[]{:S(2)}) %collective-permute-start.9) | collective-permute-done | bytes 409632 | tf_op jit(solution)/shard_map/ppermute | solution.py:298
  33.2 3.0 %dispatch.9 = (bf16[288,1024]{1,0:T(8,128)(2,1)S(1)}, bf16[288,1024]{1,0:T(8,128)(2,1)}, f32[576,384]{1,0:T(8,128)S(1)}, bf16[576,384]{1,0:T(8,128)(2,1)S(1)}, f32[8,192]{1,0:T(8,128)S(1)}) custom-call(s32[2]{0:T(128)S(1)} %pad_add_fusion.sc, bf16[200,1024]{1,0:T(8,128)(2,1)S(1)} %collective-permute-done.16.refs_0_, ...), custom_call_target="tpu_custom_call" | custom-call | flops 688914432 | bytes 3571712 | tf_op jit(solution)/shard_map/dispatch/pallas_call | solution.py:126
  37.0 5.5 %collective-permute-done.10.refs_0_ = bf16[200,1024]{1,0:T(8,128)(2,1)S(1)} collective-permute-done((bf16[200,1024]{1,0:T(8,128)(2,1)}, bf16[200,1024]{1,0:T(8,128)(2,1)S(1)}, u32[]{:S(2)}, u32[]{:S(2)}) %collective-permute-start.10) | collective-permute-done | bytes 409632 | tf_op jit(solution)/shard_map/ppermute | solution.py:298
  49.4 1.8 %dispatch.6 = (bf16[288,1024]{1,0:T(8,128)(2,1)S(1)}, bf16[288,1024]{1,0:T(8,128)(2,1)S(1)}, f32[576,384]{1,0:T(8,128)S(1)}, bf16[576,384]{1,0:T(8,128)(2,1)S(1)}, f32[8,192]{1,0:T(8,128)S(1)}) custom-call(s32[2]{0:T(128)S(1)} %pad_add_fusion.sc, bf16[200,1024]{1,0:T(8,128)(2,1)S(1)} %copy-done.32, bf16[200,1024]{1,0:T(8,128)(2,1)S(1)} %copy-done.30, ...), custom_call_target="tpu_custom_call" | custom-call | flops 688914432 | bytes 3571712 | tf_op jit(solution)/shard_map/dispatch/pallas_call | solution.py:126
  53.4 2.1 %dispatch.7 = (bf16[288,1024]{1,0:T(8,128)(2,1)S(1)}, bf16[288,1024]{1,0:T(8,128)(2,1)}, f32[576,384]{1,0:T(8,128)S(1)}, bf16[576,384]{1,0:T(8,128)(2,1)S(1)}, f32[8,192]{1,0:T(8,128)S(1)}) custom-call(s32[2]{0:T(128)S(1)} %pad_add_fusion.sc, bf16[200,1024]{1,0:T(8,128)(2,1)S(1)} %copy-done.34, bf16[200,1024]{1,0:T(8,128)(2,1)S(1)} %collective-permute-done.11.refs_1_, ...), custom_call_target="tpu_custom_call" | custom-call | flops 688914432 | bytes 3571712 | tf_op jit(solution)/shard_map/dispatch/pallas_call | solution.py:126
  59.3 4.4 %combine.9 = (bf16[288,768]{1,0:T(8,128)(2,1)S(1)}, bf16[288,768]{1,0:T(8,128)(2,1)S(1)}, bf16[192,1024]{1,0:T(8,128)(2,1)S(1)}, bf16[192,1024]{1,0:T(8,128)(2,1)S(1)}) custom-call(s32[2]{0:T(128)S(1)} %pad_add_fusion.3.sc, f32[576,384]{1,0:T(8,128)S(1)} %get-tuple-element.61.share, bf16[576,384]{1,0:T(8,128)(2,1)S(1)} %collective-permute-done.17.peer, ...), custom_call_target="tpu_custom_call" | custom-call | flops 1132462080 | bytes 6144000 | tf_op jit(solution)/shard_map/combine/pallas_call | solution.py:179
  69.8 2.8 %collective-permute-done.12.peer = bf16[576,384]{1,0:T(8,128)(2,1)S(1)} collective-permute-done((bf16[576,384]{1,0:T(8,128)(2,1)S(1)}, bf16[576,384]{1,0:T(8,128)(2,1)S(1)}, u32[]{:S(2)}, u32[]{:S(2)}) %collective-permute-start.12) | collective-permute-done | bytes 442400 | tf_op jit(solution)/shard_map/ppermute | solution.py:332
  72.6 4.4 %combine.7 = (bf16[288,768]{1,0:T(8,128)(2,1)S(1)}, bf16[288,768]{1,0:T(8,128)(2,1)S(1)}, bf16[192,1024]{1,0:T(8,128)(2,1)S(1)}, bf16[192,1024]{1,0:T(8,128)(2,1)S(1)}) custom-call(s32[2]{0:T(128)S(1)} %pad_add_fusion.2.sc, f32[576,384]{1,0:T(8,128)S(1)} %get-tuple-element.53.share, bf16[576,384]{1,0:T(8,128)(2,1)S(1)} %collective-permute-done.12.peer, ...), custom_call_target="tpu_custom_call" | custom-call | flops 1132462080 | bytes 6144000 | tf_op jit(solution)/shard_map/combine/pallas_call | solution.py:179
  80.9 4.4 %combine.6 = (bf16[288,768]{1,0:T(8,128)(2,1)S(1)}, bf16[288,768]{1,0:T(8,128)(2,1)S(1)}, bf16[192,1024]{1,0:T(8,128)(2,1)S(1)}, bf16[192,1024]{1,0:T(8,128)(2,1)S(1)}) custom-call(s32[2]{0:T(128)S(1)} %pad_add_fusion.1.sc, f32[576,384]{1,0:T(8,128)S(1)} %get-tuple-element.49.share, bf16[576,384]{1,0:T(8,128)(2,1)S(1)} %collective-permute-done.7.peer, ...), custom_call_target="tpu_custom_call" | custom-call | flops 1132462080 | bytes 6144000 | tf_op jit(solution)/shard_map/combine/pallas_call | solution.py:179
  86.7 2.0 %dispatch.8 = (bf16[144,1024]{1,0:T(8,128)(2,1)S(1)}, bf16[144,1024]{1,0:T(8,128)(2,1)}, f32[288,384]{1,0:T(8,128)S(1)}, bf16[288,384]{1,0:T(8,128)(2,1)S(1)}, f32[8,192]{1,0:T(8,128)S(1)}) custom-call(s32[2]{0:T(128)S(1)} %pad_add_fusion.sc, bf16[200,1024]{1,0:T(8,128)(2,1)S(1)} %collective-permute-done.13.refs_0_, bf16[384,1024]{1,0:T(8,128)(2,1)S(1)} %bitcast.36, ...), custom_call_target="tpu_custom_call" | custom-call | flops 344457216 | bytes 2572288 | tf_op jit(solution)/shard_map/dispatch/pallas_call | solution.py:126
  94.3 3.3 %collective-permute-done.14.peer = bf16[288,384]{1,0:T(8,128)(2,1)S(1)} collective-permute-done((bf16[288,384]{1,0:T(8,128)(2,1)S(1)}, bf16[288,384]{1,0:T(8,128)(2,1)S(1)}, u32[]{:S(2)}, u32[]{:S(2)}) %collective-permute-start.14) | collective-permute-done | bytes 221216 | tf_op jit(solution)/shard_map/ppermute | solution.py:332
  97.6 4.9 %combine.8 = (bf16[144,768]{1,0:T(8,128)(2,1)S(1)}, bf16[144,768]{1,0:T(8,128)(2,1)S(1)}, bf16[192,1024]{1,0:T(8,128)(2,1)}) custom-call(s32[1]{0:T(128)} %get-tuple-element.94.sc, f32[288,384]{1,0:T(8,128)S(1)} %get-tuple-element.57.share, bf16[288,384]{1,0:T(8,128)(2,1)S(1)} %collective-permute-done.14.peer, f32[8,192]{1,0:T(8,128)S(1)} %get-tuple-element.59.pos, ...), custom_call_target="tpu_custom_call" | custom-call | flops 566231040 | bytes 4644864 | tf_op jit(solution)/shard_map/combine/pallas_call | solution.py:179
  105.1 2.3 %fusion.4.hid = bf16[2304,384]{1,0:T(8,128)(2,1)} fusion(bf16[1,2304,384]{2,1,0:T(8,128)(2,1)S(1)} %copy-done.1, bf16[1,2304,384]{2,1,0:T(8,128)(2,1)S(1)} %copy-done), kind=kLoop, calls=%fused_computation.6 | loop fusion | flops 7077888 | bytes 5308416 | tf_op jit(solution)/shard_map/convert_element_type | solution.py:318
  107.4 5.0 %concatenate.20 = s32[8]{0:T(128)S(1)} concatenate(s32[1]{0:T(128)} %get-tuple-element.90.sc, s32[1]{0:T(128)} %get-tuple-element.97, s32[1]{0:T(128)} %get-tuple-element.92, s32[1]{0:T(128)} %get-tuple-element.95, s32[1]{0:T(128)} %get-tuple-element.93, s32[1]{0:T(128)} %get-tuple-element.96, s32[1]{0:T(128)} %get-tuple-element.91, s32[1]{0:T(128)} %get-tuple-element.94.sc), dimensions={0} | concatenate | bytes 64 | tf_op jit(solution)/shard_map/concatenate | solution.py:349
  113.1 5.0 %concatenate.21.sc = s32[16]{0:T(128)S(1)} concatenate(s32[1]{0:T(128)} %get-tuple-element.90.sc, s32[1]{0:T(128)} %get-tuple-element.97, s32[1]{0:T(128)} %get-tuple-element.92, s32[1]{0:T(128)} %get-tuple-element.95, s32[1]{0:T(128)} %get-tuple-element.93, s32[1]{0:T(128)} %get-tuple-element.96, s32[1]{0:T(128)} %get-tuple-element.91, s32[1]{0:T(128)} %get-tuple-element.94.sc, ...), dimensions={0} | concatenate | bytes 128 | tf_op jit(solution)/shard_map/concatenate | solution.py:350
  120.2 4.6 %combine.5 = (bf16[144,768]{1,0:T(8,128)(2,1)S(1)}, bf16[144,768]{1,0:T(8,128)(2,1)S(1)}, bf16[192,1024]{1,0:T(8,128)(2,1)S(1)}) custom-call(s32[1]{0:T(128)} %get-tuple-element.90.sc, f32[288,384]{1,0:T(8,128)S(1)} %copy-done.12, bf16[288,384]{1,0:T(8,128)(2,1)S(1)} %copy-done.16, f32[8,192]{1,0:T(8,128)S(1)} %get-tuple-element.47.pos, ...), custom_call_target="tpu_custom_call" | custom-call | flops 566231040 | bytes 4644864 | tf_op jit(solution)/shard_map/combine/pallas_call | solution.py:179
  126.7 1.6 %collective-permute-start.8 = (bf16[192,1024]{1,0:T(8,128)(2,1)S(1)}, bf16[192,1024]{1,0:T(8,128)(2,1)S(1)}, u32[]{:S(2)}, u32[]{:S(2)}) collective-permute-start(bf16[192,1024]{1,0:T(8,128)(2,1)S(1)} %copy-done.36), channel_id=1, source_target_pairs={{0,2},{1,3},{2,0},{3,1},{4,6},{5,7},{6,4},{7,5},{8,10},{9,11},{10,... | collective-permute-start | bytes 1179656 | tf_op jit(solution)/shard_map/ppermute | solution.py:298
  128.8 2.3 %copy-done.17 = bf16[1,2304,1024]{2,1,0:T(8,128)(2,1)S(1)} copy-done((bf16[1,2304,1024]{2,1,0:T(8,128)(2,1)S(1)}, bf16[1,2304,1024]{2,1,0:T(8,128)(2,1)}, u32[]{:S(2)}) %copy-start.17) | copy-done | bytes 4718616
  131.1 15.6 %weights.1 = bf16[1,1024,1152]{2,1,0:T(8,128)(2,1)} custom-call(s32[16]{0:T(128)S(1)} %concatenate.21.sc, bf16[2304,1024]{1,0:T(8,128)(2,1)S(1)} %bitcast.38, bf16[2304,384]{1,0:T(8,128)(2,1)S(1)} %copy-done.8, bf16[144,1024]{1,0:T(8,128)(2,1)S(1)} %copy-done.40, bf16[288,1024]{1,0:T(8,128)(2,1)S(1)} %copy-done.50, bf16[288,1024]{1,0:T(8,128)(2,1)S(1)} %copy-done.48, ...), custom_call_target="tpu_custom_call" | custom-call | flops 5435817984 | bytes 17104896 | tf_op jit(solution)/shard_map/weights/pallas_call | solution.py:257
  (177 shorter events, 45.6 us)
Async XLA Ops:
  2.5 14.6 %collective-permute-start.6 = (bf16[200,1024]{1,0:T(8,128)(2,1)S(1)}, bf16[200,1024]{1,0:T(8,128)(2,1)S(1)}, u32[]{:S(2)}, u32[]{:S(2)}) collective-permute-start(bf16[200,1024]{1,0:T(8,128)(2,1)S(1)} %fusion.12.refs_0_), channel_id=1, source_target_pairs={{0,4},{1,5},{2,6},{3,7},{4,8},{5,9},{6,10},{7,11},{8,12},{9,13},{1... | collective-permute-start | bytes 1228808 | tf_op jit(solution)/shard_map/ppermute | solution.py:298
  5.5 14.2 %collective-permute-start = (bf16[384,1024]{1,0:T(8,128)(2,1)}, bf16[384,1024]{1,0:T(8,128)(2,1)S(1)}, u32[]{:S(2)}, u32[]{:S(2)}) collective-permute-start(bf16[384,1024]{1,0:T(8,128)(2,1)} %bitcast.32), channel_id=1, source_target_pairs={{0,1},{1,0},{2,3},{3,2},{4,5},{5,4},{6,7},{7,6},{8,9},{9,8},{10,11... | collective-permute-start | bytes 2359304 | tf_op jit(solution)/shard_map/ppermute | solution.py:298
  5.5 11.9 %collective-permute-start.5 = (bf16[200,1024]{1,0:T(8,128)(2,1)S(1)}, bf16[200,1024]{1,0:T(8,128)(2,1)S(1)}, u32[]{:S(2)}, u32[]{:S(2)}) collective-permute-start(bf16[200,1024]{1,0:T(8,128)(2,1)S(1)} %fusion.12.refs_0_), channel_id=1, source_target_pairs={{0,2},{1,3},{2,0},{3,1},{4,6},{5,7},{6,4},{7,5},{8,10},{9,11},{10,... | collective-permute-start | bytes 1228808 | tf_op jit(solution)/shard_map/ppermute | solution.py:298
  7.0 52.2 %collective-permute-start.2 = (bf16[2304,384]{1,0:T(8,128)(2,1)}, bf16[2304,384]{1,0:T(8,128)(2,1)}, u32[]{:S(2)}, u32[]{:S(2)}) collective-permute-start(bf16[2304,384]{1,0:T(8,128)(2,1)} %bitcast.14), channel_id=1, source_target_pairs={{0,1},{1,0},{2,3},{3,2},{4,5},{5,4},{6,7},{7,6},{8,9},{9,8},{10,11... | collective-permute-start | bytes 5308424 | tf_op jit(solution)/shard_map/ppermute | solution.py:298
  7.3 52.0 %collective-permute-start.3 = (bf16[2304,384]{1,0:T(8,128)(2,1)}, bf16[2304,384]{1,0:T(8,128)(2,1)}, u32[]{:S(2)}, u32[]{:S(2)}) collective-permute-start(bf16[2304,384]{1,0:T(8,128)(2,1)} %bitcast.23), channel_id=1, source_target_pairs={{0,1},{1,0},{2,3},{3,2},{4,5},{5,4},{6,7},{7,6},{8,9},{9,8},{10,11... | collective-permute-start | bytes 5308424 | tf_op jit(solution)/shard_map/ppermute | solution.py:298
  17.0 42.2 %collective-permute-start.4 = (bf16[1024,768]{1,0:T(8,128)(2,1)}, bf16[1024,768]{1,0:T(8,128)(2,1)}, u32[]{:S(2)}, u32[]{:S(2)}) collective-permute-start(bf16[1024,768]{1,0:T(8,128)(2,1)} %pad_maximum_fusion.refs_4_.refs_8_), channel_id=1, source_target_pairs={{0,1},{1,0},{2,3},{3,2},{4,5},{5,4},{6,7},{7,6},{8,9},{9,8},{10,11... | collective-permute-start | bytes 4718600 | tf_op jit(solution)/shard_map/ppermute | solution.py:298
  18.2 13.4 %collective-permute-start.9 = (bf16[200,1024]{1,0:T(8,128)(2,1)S(1)}, bf16[200,1024]{1,0:T(8,128)(2,1)}, u32[]{:S(2)}, u32[]{:S(2)}) collective-permute-start(bf16[200,1024]{1,0:T(8,128)(2,1)S(1)} %collective-permute-done.6.refs_1_), channel_id=1, source_target_pairs={{0,4},{1,5},{2,6},{3,7},{4,8},{5,9},{6,10},{7,11},{8,12},{9,13},{1... | collective-permute-start | bytes 1228808 | tf_op jit(solution)/shard_map/ppermute | solution.py:298
  19.8 13.4 %collective-permute-start.16 = (bf16[200,1024]{1,0:T(8,128)(2,1)S(1)}, bf16[200,1024]{1,0:T(8,128)(2,1)S(1)}, u32[]{:S(2)}, u32[]{:S(2)}) collective-permute-start(bf16[200,1024]{1,0:T(8,128)(2,1)S(1)} %collective-permute-done.6.refs_1_), channel_id=1, source_target_pairs={{0,2},{1,3},{2,0},{3,1},{4,6},{5,7},{6,4},{7,5},{8,10},{9,11},{10,... | collective-permute-start | bytes 1228808 | tf_op jit(solution)/shard_map/ppermute | solution.py:298
  33.1 18.8 %collective-permute-start.11 = (bf16[200,1024]{1,0:T(8,128)(2,1)}, bf16[200,1024]{1,0:T(8,128)(2,1)S(1)}, u32[]{:S(2)}, u32[]{:S(2)}) collective-permute-start(bf16[200,1024]{1,0:T(8,128)(2,1)} %collective-permute-done.9.refs_1_), channel_id=1, source_target_pairs={{0,4},{1,5},{2,6},{3,7},{4,8},{5,9},{6,10},{7,11},{8,12},{9,13},{1... | collective-permute-start | bytes 1228808 | tf_op jit(solution)/shard_map/ppermute | solution.py:298
  43.2 13.2 %collective-permute-start.17 = (bf16[576,384]{1,0:T(8,128)(2,1)S(1)}, bf16[576,384]{1,0:T(8,128)(2,1)S(1)}, u32[]{:S(2)}, u32[]{:S(2)}) collective-permute-start(bf16[576,384]{1,0:T(8,128)(2,1)S(1)} %get-tuple-element.62), channel_id=1, source_target_pairs={{0,16},{16,0},{1,17},{17,1},{2,18},{18,2},{3,19},{19,3},{4,20},{20... | collective-permute-start | bytes 1327112 | tf_op jit(solution)/shard_map/ppermute | solution.py:332
  51.9 29.0 %collective-permute-start.7 = (bf16[576,384]{1,0:T(8,128)(2,1)S(1)}, bf16[576,384]{1,0:T(8,128)(2,1)S(1)}, u32[]{:S(2)}, u32[]{:S(2)}) collective-permute-start(bf16[576,384]{1,0:T(8,128)(2,1)S(1)} %get-tuple-element.50), channel_id=1, source_target_pairs={{0,16},{16,0},{1,17},{17,1},{2,18},{18,2},{3,19},{19,3},{4,20},{20... | collective-permute-start | bytes 1327112 | tf_op jit(solution)/shard_map/ppermute | solution.py:332
  56.4 16.2 %collective-permute-start.12 = (bf16[576,384]{1,0:T(8,128)(2,1)S(1)}, bf16[576,384]{1,0:T(8,128)(2,1)S(1)}, u32[]{:S(2)}, u32[]{:S(2)}) collective-permute-start(bf16[576,384]{1,0:T(8,128)(2,1)S(1)} %get-tuple-element.54), channel_id=1, source_target_pairs={{0,16},{16,0},{1,17},{17,1},{2,18},{18,2},{3,19},{19,3},{4,20},{20... | collective-permute-start | bytes 1327112 | tf_op jit(solution)/shard_map/ppermute | solution.py:332
  65.2 21.0 %collective-permute-start.19 = (bf16[192,1024]{1,0:T(8,128)(2,1)S(1)}, bf16[192,1024]{1,0:T(8,128)(2,1)S(1)}, u32[]{:S(2)}, u32[]{:S(2)}) collective-permute-start(bf16[192,1024]{1,0:T(8,128)(2,1)S(1)} %get-tuple-element.67), channel_id=1, source_target_pairs={{0,2},{1,3},{2,0},{3,1},{4,6},{5,7},{6,4},{7,5},{8,10},{9,11},{10,... | collective-permute-start | bytes 1179656 | tf_op jit(solution)/shard_map/ppermute | solution.py:298
  69.3 17.3 %collective-permute-start.13 = (bf16[200,1024]{1,0:T(8,128)(2,1)S(1)}, bf16[200,1024]{1,0:T(8,128)(2,1)S(1)}, u32[]{:S(2)}, u32[]{:S(2)}) collective-permute-start(bf16[200,1024]{1,0:T(8,128)(2,1)S(1)} %collective-permute-done.11.refs_1_), channel_id=1, source_target_pairs={{0,2},{1,3},{2,0},{3,1},{4,6},{5,7},{6,4},{7,5},{8,10},{9,11},{10,... | collective-permute-start | bytes 1228808 | tf_op jit(solution)/shard_map/ppermute | solution.py:298
  79.4 23.1 %collective-permute-start.18 = (bf16[192,1024]{1,0:T(8,128)(2,1)S(1)}, bf16[192,1024]{1,0:T(8,128)(2,1)S(1)}, u32[]{:S(2)}, u32[]{:S(2)}) collective-permute-start(bf16[192,1024]{1,0:T(8,128)(2,1)S(1)} %get-tuple-element.65), channel_id=1, source_target_pairs={{0,2},{1,3},{2,0},{3,1},{4,6},{5,7},{6,4},{7,5},{8,10},{9,11},{10,... | collective-permute-start | bytes 1179656 | tf_op jit(solution)/shard_map/ppermute | solution.py:298
  86.3 16.8 %collective-permute-start.20 = (bf16[192,1024]{1,0:T(8,128)(2,1)S(1)}, bf16[192,1024]{1,0:T(8,128)(2,1)S(1)}, u32[]{:S(2)}, u32[]{:S(2)}) collective-permute-start(bf16[192,1024]{1,0:T(8,128)(2,1)S(1)} %add_convert_fusion.3), channel_id=1, source_target_pairs={{0,4},{1,5},{2,6},{3,7},{4,8},{5,9},{6,10},{7,11},{8,12},{9,13},{1... | collective-permute-start | bytes 1179656 | tf_op jit(solution)/shard_map/ppermute | solution.py:298
  86.6 18.5 %collective-permute-start.24 = (bf16[288,1024]{1,0:T(8,128)(2,1)S(1)}, bf16[288,1024]{1,0:T(8,128)(2,1)S(1)}, u32[]{:S(2)}, u32[]{:S(2)}) collective-permute-start(bf16[288,1024]{1,0:T(8,128)(2,1)S(1)} %get-tuple-element.74), channel_id=1, source_target_pairs={{0,1},{1,0},{2,3},{3,2},{4,5},{5,4},{6,7},{7,6},{8,9},{9,8},{10,11... | collective-permute-start | bytes 1769480 | tf_op jit(solution)/shard_map/ppermute | solution.py:298
  104.6 20.2 %collective-permute-start.15 = (bf16[192,1024]{1,0:T(8,128)(2,1)}, bf16[192,1024]{1,0:T(8,128)(2,1)}, u32[]{:S(2)}, u32[]{:S(2)}) collective-permute-start(bf16[192,1024]{1,0:T(8,128)(2,1)} %get-tuple-element.60), channel_id=1, source_target_pairs={{0,2},{1,3},{2,0},{3,1},{4,6},{5,7},{6,4},{7,5},{8,10},{9,11},{10,... | collective-permute-start | bytes 1179656 | tf_op jit(solution)/shard_map/ppermute | solution.py:298
  105.1 20.2 %collective-permute-start.21 = (bf16[192,1024]{1,0:T(8,128)(2,1)}, bf16[192,1024]{1,0:T(8,128)(2,1)}, u32[]{:S(2)}, u32[]{:S(2)}) collective-permute-start(bf16[192,1024]{1,0:T(8,128)(2,1)} %add_convert_fusion.2), channel_id=1, source_target_pairs={{0,4},{1,5},{2,6},{3,7},{4,8},{5,9},{6,10},{7,11},{8,12},{9,13},{1... | collective-permute-start | bytes 1179656 | tf_op jit(solution)/shard_map/ppermute | solution.py:298
  112.4 16.2 %collective-permute-start.29 = (bf16[288,768]{1,0:T(8,128)(2,1)}, bf16[288,768]{1,0:T(8,128)(2,1)}, u32[]{:S(2)}, u32[]{:S(2)}) collective-permute-start(bf16[288,768]{1,0:T(8,128)(2,1)} %copy-done.28), channel_id=1, source_target_pairs={{0,1},{1,0},{2,3},{3,2},{4,5},{5,4},{6,7},{7,6},{8,9},{9,8},{10,11... | collective-permute-start | bytes 1327112 | tf_op jit(solution)/shard_map/ppermute | solution.py:298
  112.5 16.1 %collective-permute-start.30 = (bf16[288,768]{1,0:T(8,128)(2,1)}, bf16[288,768]{1,0:T(8,128)(2,1)}, u32[]{:S(2)}, u32[]{:S(2)}) collective-permute-start(bf16[288,768]{1,0:T(8,128)(2,1)} %copy-done.22), channel_id=1, source_target_pairs={{0,1},{1,0},{2,3},{3,2},{4,5},{5,4},{6,7},{7,6},{8,9},{9,8},{10,11... | collective-permute-start | bytes 1327112 | tf_op jit(solution)/shard_map/ppermute | solution.py:298
  113.0 15.6 %collective-permute-start.31 = (bf16[288,768]{1,0:T(8,128)(2,1)}, bf16[288,768]{1,0:T(8,128)(2,1)}, u32[]{:S(2)}, u32[]{:S(2)}) collective-permute-start(bf16[288,768]{1,0:T(8,128)(2,1)} %copy-done.27), channel_id=1, source_target_pairs={{0,1},{1,0},{2,3},{3,2},{4,5},{5,4},{6,7},{7,6},{8,9},{9,8},{10,11... | collective-permute-start | bytes 1327112 | tf_op jit(solution)/shard_map/ppermute | solution.py:298
  126.7 20.0 %collective-permute-start.8 = (bf16[192,1024]{1,0:T(8,128)(2,1)S(1)}, bf16[192,1024]{1,0:T(8,128)(2,1)S(1)}, u32[]{:S(2)}, u32[]{:S(2)}) collective-permute-start(bf16[192,1024]{1,0:T(8,128)(2,1)S(1)} %copy-done.36), channel_id=1, source_target_pairs={{0,2},{1,3},{2,0},{3,1},{4,6},{5,7},{6,4},{7,5},{8,10},{9,11},{10,... | collective-permute-start | bytes 1179656 | tf_op jit(solution)/shard_map/ppermute | solution.py:298
  128.3 18.4 %collective-permute-start.22 = (bf16[192,1024]{1,0:T(8,128)(2,1)S(1)}, bf16[192,1024]{1,0:T(8,128)(2,1)S(1)}, u32[]{:S(2)}, u32[]{:S(2)}) collective-permute-start(bf16[192,1024]{1,0:T(8,128)(2,1)S(1)} %add_convert_fusion.1), channel_id=1, source_target_pairs={{0,4},{1,5},{2,6},{3,7},{4,8},{5,9},{6,10},{7,11},{8,12},{9,13},{1... | collective-permute-start | bytes 1179656 | tf_op jit(solution)/shard_map/ppermute | solution.py:298
  (62 other events, 392.7 us)

commit v3 on v2

--- a/solution.py
+++ b/solution.py
@@ -80,11 +80,20 @@
     return pl.BlockSpec(shape, lambda i, sc: (0,) * len(shape))
 
 
+def in_hbm(v):
+    return pltpu.with_memory_space_constraint(v, pltpu.HBM)
+
+
+def source(here, step, other):
+    group = lax.rem(here // 4 + (4 - step), 4)
+    return jnp.bitwise_xor(group * 4 + lax.rem(here, 4), 2 * other)
+
+
 def params(mib):
     return pltpu.CompilerParams(vmem_limit_bytes=mib << 20)
 
 
-def dispatch_kernel(n, cap, sc, *refs):
+def dispatch_kernel(n, cap, here, *refs):
     toks, (wd0, wd1) = refs[:n], refs[n : n + 2]
     rec0, rec1, share, share_out, pos_out = refs[n + 2 :]
     tok = toks[0].shape[0] - 8
@@ -94,7 +103,7 @@
     slot = lax.broadcasted_iota(jnp.int32, (cap, tok), 0).astype(f32)
     masks, gates = [], []
     for a in range(2):
-        expert = sc[a].astype(f32)
+        expert = jnp.bitwise_xor(here[0], a).astype(f32)
         for t in toks:
             hit = t[tok:, :tok].astype(f32) == expert
             masks.append(jnp.max(jnp.where(hit, 1.0, 0.0), axis=0, keepdims=True))
@@ -118,14 +127,14 @@
         share_out[a * n * cap : (a + 1) * n * cap, :] = gh.astype(bf16)
 
 
-def dispatch(experts, toks, wd0, wd1, cap):
+def dispatch(here, toks, wd0, wd1, cap):
     n = len(toks)
     tok, d = toks[0].shape
     h = wd0.shape[0]
     outs = [((n * cap, d), bf16), ((n * cap, d), bf16), ((2 * n * cap, h), f32), ((2 * n * cap, h), bf16), ((8, tok - 8), f32)]
     return pl.pallas_call(
         functools.partial(dispatch_kernel, n, cap),
-        out_shape=[jax.ShapeDtypeStruct(s, t) for s, t in outs],
+        out_shape=[pltpu.HBM(s, t) for s, t in outs],
         grid_spec=pltpu.PrefetchScalarGridSpec(
             num_scalar_prefetch=1,
             grid=(1,),
@@ -137,7 +146,7 @@
         ),
         compiler_params=params(24),
         name="dispatch",
-    )(experts, *toks, wd0, wd1)
+    )(here, *[in_hbm(t) for t in toks], wd0, wd1)
 
 
 def combine_kernel(n, cap, sc, share, peer, pos, *refs):
@@ -164,21 +173,22 @@
         backs[rel][...] = sums[rel].astype(bf16)
 
 
-def combine(sources, share, peer, pos, saved0, saved1, w0, w1, cap):
-    n = share.shape[0] // (2 * cap)
+def combine(here, chunk, share, peer, pos, saved0, saved1, w0, w1, cap):
+    n = len(chunk)
     h = share.shape[1]
     d = w0.shape[0]
     tok = pos.shape[1]
 
     def piece(rel):
-        return pl.BlockSpec((cap, h), lambda i, sc: (sc[rel], 0))
+        other, step = chunk[rel]
+        return pl.BlockSpec((cap, h), lambda i, here: (source(here[0], step, other), 0))
 
     saved = [v for pair in (saved0, saved1) for _ in range(n) for v in pair]
     saved_specs = [piece(rel) for _ in range(2) for rel in range(n) for _ in range(2)]
     outs = [(n * cap, 2 * h)] * 2 + [(tok, d)] * n
     return pl.pallas_call(
         functools.partial(combine_kernel, n, cap),
-        out_shape=[jax.ShapeDtypeStruct(s, bf16) for s in outs],
+        out_shape=[pltpu.HBM(s, bf16) for s in outs],
         grid_spec=pltpu.PrefetchScalarGridSpec(
             num_scalar_prefetch=1,
             grid=(1,),
@@ -192,94 +202,101 @@
         ),
         compiler_params=params(28),
         name="combine",
-    )(sources, share, peer, pos, *saved, w0, w1)
-
-
-def weights_kernel(count, cap, sc, x, hid, *refs):
-    recs, gps = refs[:count], refs[count : 2 * count]
-    out, xs, rs, gs, hs, sems = refs[2 * count :]
+    )(here, in_hbm(share), in_hbm(peer), in_hbm(pos), *saved, w0, w1)
+
+
+def weights_kernel(order, cap, sorted_left, here, *refs):
+    by_source, pieces = refs[0], refs[1:-4]
+    pieces, out = (pieces[:-1], pieces[-1])
+    ls, rs, left_sems, right_sems = refs[-4:]
     i = pl.program_id(0)
-    tile = xs.shape[2]
+    tile = ls.shape[2]
     steps = pl.num_programs(0)
 
-    def columns(at, step):
-        at_col = pl.ds(pl.multiple_of(step * tile, 128), tile)
-        copies = []
-        base = 0
-        for r in recs:
-            copies.append(pltpu.make_async_copy(r.at[:, at_col], rs.at[at, pl.ds(base, r.shape[0]), :], sems.at[at, len(copies)]))
+    def copies_of_sorted(column, to, sems):
+        made = []
+        for p, (step, other, plane) in enumerate(order):
+            src = jnp.bitwise_xor(source(here[0], step, other), plane)
+            rows = pl.ds(pl.multiple_of(src * cap, 16), cap)
+            at = by_source.at[rows, :] if column is None else by_source.at[rows, column]
+            made.append(pltpu.make_async_copy(at, to.at[pl.ds(p * cap, cap), :], sems.at[len(made)]))
+        return made
+
+    def copies_of_pieces(column, to, sems):
+        made, base = [], 0
+        for r in pieces:
+            at = r if column is None else r.at[:, column]
+            made.append(pltpu.make_async_copy(at, to.at[pl.ds(base, r.shape[0]), :], sems.at[len(made)]))
             base += r.shape[0]
-        for p in range(base // cap):
-            src = pl.ds(pl.multiple_of(sc[p] * cap, 16), cap)
-            copies.append(pltpu.make_async_copy(x.at[src, at_col], xs.at[at, pl.ds(p * cap, cap), :], sems.at[at, len(copies)]))
-        return copies
-
-    def fixed():
-        copies = []
-        base = 0
-        for g in gps:
-            copies.append(pltpu.make_async_copy(g, gs.at[pl.ds(base, g.shape[0]), :], sems.at[2, len(copies)]))
-            base += g.shape[0]
-        for p in range(base // cap):
-            src = pl.ds(pl.multiple_of(sc[p] * cap, 16), cap)
-            copies.append(pltpu.make_async_copy(hid.at[src, :], hs.at[pl.ds(p * cap, cap), :], sems.at[2, len(copies)]))
-        return copies
+        return made
+
+    left_copies, right_copies = (
+        (copies_of_sorted, copies_of_pieces) if sorted_left else (copies_of_pieces, copies_of_sorted)
+    )
+
+    def left(step):
+        slot = lax.rem(step, 2)
+        column = pl.ds(pl.multiple_of(step * tile, 128), tile)
+        return left_copies(column, ls.at[slot], left_sems.at[slot])
 
     @pl.when(i == 0)
     def _():
-        for c in columns(0, 0) + fixed():
+        for c in right_copies(None, rs, right_sems) + left(i):
             c.start()
 
     @pl.when(i + 1 < steps)
     def _():
-        for c in columns((i + 1) % 2, i + 1):
+        for c in left(i + 1):
             c.start()
 
-    for c in columns(i % 2, i):
+    for c in left(i):
         c.wait()
 
     @pl.when(i == 0)
     def _():
-        for c in fixed():
+        for c in right_copies(None, rs, right_sems):
             c.wait()
 
-    wide = gs.shape[1]
-    now = i % 2
-    out[0, :, :wide] = (contract_rows(xs[now], gs[...]) * loss_scale).astype(bf16)
-    out[0, :, wide:] = (contract_rows(rs[now], hs[...]) * loss_scale).astype(bf16)
-
-
-def weight_sums(sources, x, hid, recs, gps, cap):
-    slots, d = x.shape
-    h = hid.shape[1]
+    out[0] = (contract_rows(ls[lax.rem(i, 2)], rs[...]) * loss_scale).astype(bf16)
+
+
+def weight_sums(here, order, by_source, pieces, sorted_left, into, cap):
+    slots = by_source.shape[0]
+    d = by_source.shape[1] if sorted_left else pieces[0].shape[1]
+    wide = pieces[0].shape[1] if sorted_left else by_source.shape[1]
     tile = 256
     anywhere = pl.BlockSpec(memory_space=pl.ANY)
+    at = 0 if sorted_left else 2
+    whole_out = jax.ShapeDtypeStruct((1, d, 3 * (wide // 2 if sorted_left else wide)), bf16)
+    given = [by_source, *pieces]
+    kernel = functools.partial(weights_kernel, order, cap, sorted_left)
+    body = kernel if into is None else (lambda here, old, *refs: kernel(here, *refs))
     return pl.pallas_call(
-        functools.partial(weights_kernel, len(recs), cap),
-        out_shape=jax.ShapeDtypeStruct((1, d, 3 * h), bf16),
+        body,
+        out_shape=whole_out,
         grid_spec=pltpu.PrefetchScalarGridSpec(
             num_scalar_prefetch=1,
             grid=(d // tile,),
-            in_specs=[anywhere] * (2 + 2 * len(recs)),
-            out_specs=pl.BlockSpec((1, tile, 3 * h), lambda i, sc: (0, i, 0)),
+            in_specs=[anywhere] * (len(given) + (into is not None)),
+            out_specs=pl.BlockSpec((1, tile, wide), lambda i, here: (0, i, at)),
             scratch_shapes=[
                 pltpu.VMEM((2, slots, tile), bf16),
-                pltpu.VMEM((2, slots, tile), bf16),
-                pltpu.VMEM((slots, 2 * h), bf16),
-                pltpu.VMEM((slots, h), bf16),
-                pltpu.SemaphoreType.DMA((3, len(recs) + slots // cap)),
+                pltpu.VMEM((slots, wide), bf16),
+                pltpu.SemaphoreType.DMA((2, len(order))),
+                pltpu.SemaphoreType.DMA((len(order),)),
             ],
         ),
+        input_output_aliases={} if into is None else {1: 0},
         cost_estimate=pl.CostEstimate(
-            flops=6 * slots * d * h, bytes_accessed=4 * slots * d + 6 * d * h + 6 * slots * h, transcendentals=0
-        ),
-        compiler_params=params(24),
+            flops=2 * slots * d * wide, bytes_accessed=2 * slots * (d + wide) + 2 * d * wide, transcendentals=0
+        ),
+        compiler_params=params(20),
         name="weights",
-    )(sources, x, hid, *recs, *gps)
-
-
-def after(value, *others):
-    return lax.optimization_barrier((value, *others))[0]
+    )(here, *([] if into is None else [into]), *[in_hbm(v) for v in given])
+
+
+def together(*values):
+    return lax.optimization_barrier(values)
 
 
 def body_grid(out_grad, routes, gate_codes, w_gate, w_up, w_down, saved_inputs, saved_gate, saved_up):
@@ -287,8 +304,6 @@
     me = lax.axis_index("expert")
     to_core = [(i, i ^ 1) for i in range(owners)]
     to_x = [(i, i ^ 2) for i in range(owners)]
-    ring = [(i, (i + 4) % owners) for i in range(owners)]
-    rounds = owners // 4
     tok, d = out_grad.shape
     choices = routes.shape[1]
     slots = saved_gate.shape[1]
@@ -306,49 +321,76 @@
         axis=1,
     )
     block = jnp.concatenate([out_grad, named], axis=0)
-    own_col = [block]
-    for _ in range(rounds - 1):
-        own_col.append(send(own_col[-1], ring))
-    other_col = [send(v, to_x) for v in own_col]
+    here = me.reshape(1).astype(jnp.int32)
+
+    def ring(v, hops=1):
+        return send(v, [(i, (i + 4 * hops) % owners) for i in range(owners)])
 
     wd, sg, su = w_down[0], saved_gate[0], saved_up[0]
     w = jnp.concatenate([w_gate[0], w_up[0]], axis=1)
-    wd_c, w_c, sg_c, su_c = [send(v, to_core) for v in (wd, w, sg, su)]
+    wd_c, sg_c, su_c, w_c = [send(v, to_core) for v in (wd, sg, su, w)]
     gate_pre = sg.astype(f32)
     hid = (gate_pre * jax.nn.sigmoid(gate_pre) * su.astype(f32)).astype(bf16)
 
-    groups = (me // 4 + rounds - jnp.arange(rounds, dtype=jnp.int32)) % rounds
-    own_src = groups * 4 + me % 4
-    other_src = jnp.bitwise_xor(own_src, 2)
-    experts = jnp.stack([me, jnp.bitwise_xor(me, 1)]).astype(jnp.int32)
-
-    chunks = [[(0, 0)]] + [[(1, k - 1), (0, k)] for k in range(1, rounds)] + [[(1, rounds - 1)]]
-    recs, recs_c, gps, gps_c, order = [], [], [], [], []
-    back = {}
-    for chunk in chunks:
-        toks = [(other_col if col else own_col)[k] for col, k in chunk]
-        src = jnp.stack([(other_src if col else own_src)[k] for col, k in chunk])
-        rec, rec_c, share, share_out, pos = dispatch(experts, toks, wd, wd_c, cap)
-        peer = lax.ppermute(share_out, "dp", [(0, 1), (1, 0)])
-        gp, gp_c, *sums = combine(src, share, peer, pos, (sg, su), (sg_c, su_c), w, w_c, cap)
-        back.update(zip(chunk, sums))
+    order, recs, recs_c, gps, gps_c = [], [], [], [], []
+
+    def first(chunk, toks):
+        rec, rec_c, share, share_out, pos = dispatch(here, toks, wd, wd_c, cap)
+        order.extend((k, col, 0) for col, k in chunk)
         recs.append(rec)
         recs_c.append(send(rec_c, to_core))
+        return chunk, share, share_out, pos
+
+    def exchange(share_out):
+        return lax.ppermute(share_out, "dp", [(0, 1), (1, 0)])
+
+    def second(state, peer):
+        chunk, share, _, pos = state
+        gp, gp_c, *sums = combine(here, chunk, share, peer, pos, (sg, su), (sg_c, su_c), w, w_c, cap)
         gps.append(gp)
         gps_c.append(send(gp_c, to_core))
-        order.append(src)
-
-    run = None
-    arrived = {k: send(back[(1, k)], to_x) for k in [1, 2, 3, 0]}
-    for k in [1, 2, 3, 0]:
-        total = back[(0, k)].astype(f32) + arrived[k].astype(f32)
-        if run is not None:
-            total = total + run.astype(f32)
-        total = total.astype(bf16)
-        run = send(total, ring) if k else None
-    order = jnp.concatenate(order)
-    order = jnp.concatenate([order, jnp.bitwise_xor(order, 1)])
-    weight_grads = weight_sums(order, saved_inputs[0], hid, recs + recs_c, gps + gps_c, cap)
+        return sums
+
+    def add(*values):
+        return sum(v.astype(f32) for v in values).astype(bf16)
+
+    r1, x0 = ring(block), send(block, to_x)
+    c0 = first([(0, 0)], [block])
+    y0 = exchange(c0[2])
+    r1, x0, _ = together(r1, x0, c0[2])
+    r2, x1 = ring(r1), send(r1, to_x)
+    c1 = first([(1, 0), (0, 1)], [x0, r1])
+    y1 = exchange(c1[2])
+    (t_r0,) = second(c0, y0)
+    r2, x1, _, t_r0 = together(r2, x1, c1[2], t_r0)
+    r3, x2 = ring(r2), send(r2, to_x)
+    c2 = first([(1, 1), (0, 2)], [x1, r2])
+    y2 = exchange(c2[2])
+    t_x0, t_r1 = second(c1, y1)
+    r3, x2, _, t_x0, t_r1 = together(r3, x2, c2[2], t_x0, t_r1)
+    x3 = send(r3, to_x)
+    c3 = first([(1, 2), (0, 3)], [x2, r3])
+    y3 = exchange(c3[2])
+    t_x1, t_r2 = second(c2, y2)
+    x3, _, t_x1, t_r2 = together(x3, c3[2], t_x1, t_r2)
+    b1 = send(t_x1, to_x)
+    c4 = first([(1, 3)], [x3])
+    y4 = exchange(c4[2])
+    t_x2, t_r3 = second(c3, y3)
+    b1, _, t_x2, t_r3 = together(b1, c4[2], t_x2, t_r3)
+    b2 = send(t_x2, to_x)
+    v1 = ring(add(t_r1, b1), 3)
+    (t_x3,) = second(c4, y4)
+    b2, t_x3 = together(b2, t_x3)
+    b3 = send(t_x3, to_x)
+    v2 = ring(add(t_r2, b2), 2)
+    order_all = order + [(k, col, 1) for k, col, _ in order]
+    part = weight_sums(here, order_all, hid, recs + recs_c, False, None, cap)
+    b3, v1, part = together(b3, v1, part)
+    v3 = ring(add(t_r3, b3), 1)
+    b0 = send(t_x0, to_x)
+    weight_grads = weight_sums(here, order_all, saved_inputs[0], gps + gps_c, True, part, cap)
+    total = add(t_r0, b0, v1, v2, v3)
     return (total, weight_grads)
 
 

time: 150 us -> 136 us (0.907); the launches traced: 148 us -> 135 us
  local copies, waits for them, and re-layouts: 30.8 us -> 5.81 us
  starting transfers between devices: 23.9 us -> 31.9 us
  other arithmetic: 14.1 us -> 7.16 us
  Pallas kernels: 48.6 us -> 55.5 us
  waiting for transfers between devices: 29.1 us -> 33.9 us
    unnamed x106 -> x92, local copies, waits for them, and re-layouts: 19.5 us -> 5.81 us
    concatenate x2 -> x0, local copies, waits for them, and re-layouts: 9.98 us -> none  [the longest x1 4.99 us: body_grid(): order = jnp.concatenate(order)]
    ppermute x28, waiting for transfers between devices: 23 us -> 31.5 us  [send(): return lax.ppermute(v, 'expert', perm)]
    ppermute x28, starting transfers between devices: 18.3 us -> 25.5 us  [send(): return lax.ppermute(v, 'expert', perm)]
    pallas_call x11 -> x12, Pallas kernels: 48.6 us -> 55.5 us  [the longest x5 24 us: combine(): pl.pallas_call(functools.partial(combine_kernel, n, cap), out_shape=[pltp...]
    another operation x4 -> x0, other arithmetic: 3.98 us -> none  [the longest x3 3.91 us: body_grid(): src = jnp.stack([(other_src if col else own_src)[k] for col, k in chunk])]
    ppermute x5, waiting for transfers between devices: 6.07 us -> 2.44 us  [exchange(): return lax.ppermute(share_out, 'dp', [(0, 1), (1, 0)])]
    convert_element_type x4, other arithmetic: 3.33 us -> 1.47 us  [add(): return sum((v.astype(f32) for v in values)).astype(bf16)]
  transfers between devices with their start and end apart: 33 -> 33, of which waited for: 6 -> 9; matrix products, arithmetic and copies ran while one was open for 15% -> 4% of each run, Pallas kernels for 33% -> 41%
where the time goes in v3:
time: 136 us; the launch traced here: 135 us
  Pallas kernels  55.5 us (41%)
  waiting for transfers between devices  33.9 us (25%)
  starting transfers between devices  31.9 us (23%)
  other arithmetic  7.16 us (5%)
  local copies, waits for them, and re-layouts  5.81 us (4%)
    ppermute x28, waiting for transfers between devices, send(): return lax.ppermute(v, 'expert', perm)  31.5 us
    ppermute x28, starting transfers between devices, send(): return lax.ppermute(v, 'expert', perm)  25.5 us
    pallas_call x5, Pallas kernels, combine(): pl.pallas_call(functools.partial(combine_kernel, n, cap), out_shape=[pltp...  24 us
    pallas_call x5, Pallas kernels, dispatch(): pl.pallas_call(functools.partial(dispatch_kernel, n, cap), out_shape=[plt...  15.7 us
    pallas_call x2, Pallas kernels, weight_sums(): pl.pallas_call(body, out_shape=whole_out, grid_spec=pltpu.PrefetchScalarG...  15.7 us
    ppermute x5, starting transfers between devices, exchange(): return lax.ppermute(share_out, 'dp', [(0, 1), (1, 0)])  6.44 us
    unnamed x92, local copies, waits for them, and re-layouts  5.81 us
  transfers between devices with their start and end apart: 33, of which 9 were waited for; matrix products, arithmetic and copies ran while one was open for 4% of the time, Pallas kernels for 41%

profile of v3, /device:TPU:0, one launch (start us, length us, event | category | flops | bytes accessed | tf_op | source)
XLA Modules:
  0.0 135.3 jit_solution(8484741791139435411)
XLA Ops:
  1.3 2.6 %pad_maximum_fusion.refs_4_.refs_8_ = bf16[1024,768]{1,0:T(8,128)(2,1)} fusion(bf16[1024,384]{1,0:T(8,128)(2,1)} %bitcast.37, bf16[1024,384]{1,0:T(8,128)(2,1)} %bitcast.38), kind=kLoop, calls=%fused_computation.7 | loop fusion | flops 3145728 | bytes 3145728 | tf_op jit(solution)/shard_map/concatenate | solution.py:330
  5.2 3.0 %collective-permute-start = (bf16[200,1024]{1,0:T(8,128)(2,1)}, bf16[200,1024]{1,0:T(8,128)(2,1)}, u32[]{:S(2)}, u32[]{:S(2)}) collective-permute-start(bf16[200,1024]{1,0:T(8,128)(2,1)} %fusion.12.refs_0_), channel_id=1, source_target_pairs={{0,4},{1,5},{2,6},{3,7},{4,8},{5,9},{6,10},{7,11},{8,12},{9,13},{1... | collective-permute-start | bytes 1228808 | tf_op jit(solution)/shard_map/ppermute | solution.py:313
  10.2 2.9 %collective-permute-start.1 = (bf16[200,1024]{1,0:T(8,128)(2,1)}, bf16[200,1024]{1,0:T(8,128)(2,1)}, u32[]{:S(2)}, u32[]{:S(2)}) collective-permute-start(bf16[200,1024]{1,0:T(8,128)(2,1)} %fusion.12.refs_0_), channel_id=1, source_target_pairs={{0,2},{1,3},{2,0},{3,1},{4,6},{5,7},{6,4},{7,5},{8,10},{9,11},{10,... | collective-permute-start | bytes 1228808 | tf_op jit(solution)/shard_map/ppermute | solution.py:313
  15.3 2.7 %dispatch.5 = (bf16[144,1024]{1,0:T(8,128)(2,1)}, bf16[144,1024]{1,0:T(8,128)(2,1)}, f32[288,384]{1,0:T(8,128)}, bf16[288,384]{1,0:T(8,128)(2,1)}, f32[8,192]{1,0:T(8,128)}) custom-call(s32[1]{0:T(128)} %bitcast.2.here.sc, bf16[200,1024]{1,0:T(8,128)(2,1)} %fusion.12.refs_0_, bf16[384,1024]{1,0:T(8,128)(2,1)S(1)} %bitcast.32, bf16[384,1024]{1,0:T(8,128)(2,1)S(1)} %copy-done.6), custom_call_target="tpu_custom_call" | custom-call | flops 344457216 | bytes 2572288 | tf_op jit(solution)/shard_map/dispatch/pallas_call | solution.py:135
  18.0 2.3 %collective-permute-done.refs_1_ = bf16[200,1024]{1,0:T(8,128)(2,1)} collective-permute-done((bf16[200,1024]{1,0:T(8,128)(2,1)}, bf16[200,1024]{1,0:T(8,128)(2,1)}, u32[]{:S(2)}, u32[]{:S(2)}) %collective-permute-start) | collective-permute-done | bytes 409632 | tf_op jit(solution)/shard_map/ppermute | solution.py:313
  23.1 1.8 %collective-permute-start.3 = (bf16[200,1024]{1,0:T(8,128)(2,1)}, bf16[200,1024]{1,0:T(8,128)(2,1)S(1)}, u32[]{:S(2)}, u32[]{:S(2)}) collective-permute-start(bf16[200,1024]{1,0:T(8,128)(2,1)} %collective-permute-done.refs_1_), channel_id=1, source_target_pairs={{0,4},{1,5},{2,6},{3,7},{4,8},{5,9},{6,10},{7,11},{8,12},{9,13},{1... | collective-permute-start | bytes 1228808 | tf_op jit(solution)/shard_map/ppermute | solution.py:313
  25.0 2.4 %collective-permute-done.5.peer = bf16[288,384]{1,0:T(8,128)(2,1)S(1)} collective-permute-done((bf16[288,384]{1,0:T(8,128)(2,1)}, bf16[288,384]{1,0:T(8,128)(2,1)S(1)}, u32[]{:S(2)}, u32[]{:S(2)}) %collective-permute-start.5) | collective-permute-done | bytes 221216 | tf_op jit(solution)/shard_map/ppermute | solution.py:345
  28.6 3.5 %dispatch.6 = (bf16[288,1024]{1,0:T(8,128)(2,1)}, bf16[288,1024]{1,0:T(8,128)(2,1)}, f32[576,384]{1,0:T(8,128)}, bf16[576,384]{1,0:T(8,128)(2,1)}, f32[8,192]{1,0:T(8,128)}) custom-call(s32[1]{0:T(128)} %bitcast.2.here.sc, bf16[200,1024]{1,0:T(8,128)(2,1)} %collective-permute-done.1.refs_0_, bf16[200,1024]{1,0:T(8,128)(2,1)} %collective-permute-done.refs_1_, ...), custom_call_target="tpu_custom_call" | custom-call | flops 688914432 | bytes 3571712 | tf_op jit(solution)/shard_map/dispatch/pallas_call | solution.py:135
  33.7 4.6 %combine.5 = (bf16[144,768]{1,0:T(8,128)(2,1)}, bf16[144,768]{1,0:T(8,128)(2,1)}, bf16[192,1024]{1,0:T(8,128)(2,1)}) custom-call(s32[1]{0:T(128)} %bitcast.2.here.sc, f32[288,384]{1,0:T(8,128)} %get-tuple-element.69.share, bf16[288,384]{1,0:T(8,128)(2,1)} %copy-done.23, f32[8,192]{1,0:T(8,128)} %get-tuple-element.70.pos, bf16[2304,384]{1,0:T(8,128)(2,1)S(1)} %bitcast.14, ...), custom_call_target="tpu_custom_call" | custom-call | flops 566231040 | bytes 4644864 | tf_op jit(solution)/shard_map/combine/pallas_call | solution.py:189
  39.2 3.4 %dispatch.7 = (bf16[288,1024]{1,0:T(8,128)(2,1)}, bf16[288,1024]{1,0:T(8,128)(2,1)}, f32[576,384]{1,0:T(8,128)}, bf16[576,384]{1,0:T(8,128)(2,1)}, f32[8,192]{1,0:T(8,128)}) custom-call(s32[1]{0:T(128)} %bitcast.2.here.sc, bf16[200,1024]{1,0:T(8,128)(2,1)} %copy-done.37, bf16[200,1024]{1,0:T(8,128)(2,1)} %copy-done.35, bf16[384,1024]{1,0:T(8,128)(2,1)S(1)} %bitcast.34, ...), custom_call_target="tpu_custom_call" | custom-call | flops 688914432 | bytes 3571712 | tf_op jit(solution)/shard_map/dispatch/pallas_call | solution.py:135
  44.4 4.9 %combine.6 = (bf16[288,768]{1,0:T(8,128)(2,1)}, bf16[288,768]{1,0:T(8,128)(2,1)}, bf16[192,1024]{1,0:T(8,128)(2,1)}, bf16[192,1024]{1,0:T(8,128)(2,1)}) custom-call(s32[1]{0:T(128)} %bitcast.2.here.sc, f32[576,384]{1,0:T(8,128)} %get-tuple-element.76.share, bf16[576,384]{1,0:T(8,128)(2,1)} %copy-done.12, f32[8,192]{1,0:T(8,128)} %get-tuple-element.77.pos, ...), custom_call_target="tpu_custom_call" | custom-call | flops 1132462080 | bytes 6144000 | tf_op jit(solution)/shard_map/combine/pallas_call | solution.py:189
  50.4 3.4 %dispatch.8 = (bf16[288,1024]{1,0:T(8,128)(2,1)}, bf16[288,1024]{1,0:T(8,128)(2,1)}, f32[576,384]{1,0:T(8,128)}, bf16[576,384]{1,0:T(8,128)(2,1)}, f32[8,192]{1,0:T(8,128)}) custom-call(s32[1]{0:T(128)} %bitcast.2.here.sc, bf16[200,1024]{1,0:T(8,128)(2,1)} %copy-done.38, bf16[200,1024]{1,0:T(8,128)(2,1)} %copy-done.36, bf16[384,1024]{1,0:T(8,128)(2,1)S(1)} %bitcast.35, ...), custom_call_target="tpu_custom_call" | custom-call | flops 688914432 | bytes 3571712 | tf_op jit(solution)/shard_map/dispatch/pallas_call | solution.py:135
  56.0 5.1 %combine.7 = (bf16[288,768]{1,0:T(8,128)(2,1)}, bf16[288,768]{1,0:T(8,128)(2,1)}, bf16[192,1024]{1,0:T(8,128)(2,1)}, bf16[192,1024]{1,0:T(8,128)(2,1)}) custom-call(s32[1]{0:T(128)} %bitcast.2.here.sc, f32[576,384]{1,0:T(8,128)} %get-tuple-element.84.share, bf16[576,384]{1,0:T(8,128)(2,1)} %copy-done.13, f32[8,192]{1,0:T(8,128)} %get-tuple-element.85.pos, ...), custom_call_target="tpu_custom_call" | custom-call | flops 1132462080 | bytes 6144000 | tf_op jit(solution)/shard_map/combine/pallas_call | solution.py:189
  62.6 2.7 %dispatch.9 = (bf16[144,1024]{1,0:T(8,128)(2,1)}, bf16[144,1024]{1,0:T(8,128)(2,1)}, f32[288,384]{1,0:T(8,128)}, bf16[288,384]{1,0:T(8,128)(2,1)}, f32[8,192]{1,0:T(8,128)}) custom-call(s32[1]{0:T(128)} %bitcast.2.here.sc, bf16[200,1024]{1,0:T(8,128)(2,1)} %copy-done.14, bf16[384,1024]{1,0:T(8,128)(2,1)S(1)} %bitcast.36, bf16[384,1024]{1,0:T(8,128)(2,1)S(1)} %copy-done.7), custom_call_target="tpu_custom_call" | custom-call | flops 344457216 | bytes 2572288 | tf_op jit(solution)/shard_map/dispatch/pallas_call | solution.py:135
  66.3 5.0 %combine.8 = (bf16[288,768]{1,0:T(8,128)(2,1)}, bf16[288,768]{1,0:T(8,128)(2,1)}, bf16[192,1024]{1,0:T(8,128)(2,1)}, bf16[192,1024]{1,0:T(8,128)(2,1)}) custom-call(s32[1]{0:T(128)} %bitcast.2.here.sc, f32[576,384]{1,0:T(8,128)} %get-tuple-element.91.share, bf16[576,384]{1,0:T(8,128)(2,1)} %copy-done.11, f32[8,192]{1,0:T(8,128)} %get-tuple-element.92.pos, ...), custom_call_target="tpu_custom_call" | custom-call | flops 1132462080 | bytes 6144000 | tf_op jit(solution)/shard_map/combine/pallas_call | solution.py:189
  72.3 2.3 %fusion.4.refs_0_ = bf16[2304,384]{1,0:T(8,128)(2,1)} fusion(bf16[1,2304,384]{2,1,0:T(8,128)(2,1)S(1)} %copy-done.1, bf16[1,2304,384]{2,1,0:T(8,128)(2,1)S(1)} %copy-done), kind=kLoop, calls=%fused_computation.6 | loop fusion | flops 7077888 | bytes 5308416 | tf_op jit(solution)/shard_map/convert_element_type | solution.py:333
  74.8 8.0 %collective-permute-done.17 = bf16[192,1024]{1,0:T(8,128)(2,1)S(1)} collective-permute-done((bf16[192,1024]{1,0:T(8,128)(2,1)}, bf16[192,1024]{1,0:T(8,128)(2,1)S(1)}, u32[]{:S(2)}, u32[]{:S(2)}) %collective-permute-start.17) | collective-permute-done | bytes 393248 | tf_op jit(solution)/shard_map/ppermute | solution.py:313
  82.8 4.6 %combine.9 = (bf16[144,768]{1,0:T(8,128)(2,1)}, bf16[144,768]{1,0:T(8,128)(2,1)}, bf16[192,1024]{1,0:T(8,128)(2,1)}) custom-call(s32[1]{0:T(128)} %bitcast.2.here.sc, f32[288,384]{1,0:T(8,128)} %get-tuple-element.96.share, bf16[288,384]{1,0:T(8,128)(2,1)} %copy-done.22, f32[8,192]{1,0:T(8,128)} %get-tuple-element.97.pos, bf16[2304,384]{1,0:T(8,128)(2,1)S(1)} %bitcast.21, ...), custom_call_target="tpu_custom_call" | custom-call | flops 566231040 | bytes 4644864 | tf_op jit(solution)/shard_map/combine/pallas_call | solution.py:189
  88.8 3.7 %collective-permute-start.20 = (bf16[192,1024]{1,0:T(8,128)(2,1)S(1)}, bf16[192,1024]{1,0:T(8,128)(2,1)S(1)}, u32[]{:S(2)}, u32[]{:S(2)}) collective-permute-start(bf16[192,1024]{1,0:T(8,128)(2,1)S(1)} %add_convert_fusion.3), channel_id=1, source_target_pairs={{0,12},{1,13},{2,14},{3,15},{4,0},{5,1},{6,2},{7,3},{8,4},{9,5},{1... | collective-permute-start | bytes 1179656 | tf_op jit(solution)/shard_map/ppermute | solution.py:313
  93.8 7.1 %weights.2.old = bf16[1,1024,1152]{2,1,0:T(8,128)(2,1)} custom-call(s32[1]{0:T(128)} %bitcast.2.here.sc, bf16[2304,384]{1,0:T(8,128)(2,1)} %fusion.4.refs_0_, bf16[144,1024]{1,0:T(8,128)(2,1)} %get-tuple-element.102.refs_1_, bf16[288,1024]{1,0:T(8,128)(2,1)} %get-tuple-element.103.refs_2_, bf16[288,1024]{1,0:T(8,128)(2,1)} %get-tuple-element.104.refs_3_, ...), custom_call_target="tpu_custom_call" | custom-call | flops 1811939328 | bytes 7274496 | tf_op jit(solution)/shard_map/weights/pallas_call | solution.py:274
  101.4 2.4 %collective-permute-done.19 = bf16[192,1024]{1,0:T(8,128)(2,1)S(1)} collective-permute-done((bf16[192,1024]{1,0:T(8,128)(2,1)}, bf16[192,1024]{1,0:T(8,128)(2,1)S(1)}, u32[]{:S(2)}, u32[]{:S(2)}) %collective-permute-start.19) | collective-permute-done | bytes 393248 | tf_op jit(solution)/shard_map/ppermute | solution.py:313
  105.4 3.5 %collective-permute-start.27 = (bf16[192,1024]{1,0:T(8,128)(2,1)S(1)}, bf16[192,1024]{1,0:T(8,128)(2,1)S(1)}, u32[]{:S(2)}, u32[]{:S(2)}) collective-permute-start(bf16[192,1024]{1,0:T(8,128)(2,1)S(1)} %add_convert_fusion.1), channel_id=1, source_target_pairs={{0,4},{1,5},{2,6},{3,7},{4,8},{5,9},{6,10},{7,11},{8,12},{9,13},{1... | collective-permute-start | bytes 1179656 | tf_op jit(solution)/shard_map/ppermute | solution.py:313
  109.8 8.6 %weights.3 = bf16[1,1024,1152]{2,1,0:T(8,128)(2,1)} custom-call(s32[1]{0:T(128)} %bitcast.2.here.sc, bf16[1,1024,1152]{2,1,0:T(8,128)(2,1)} %weights.2.old, bf16[2304,1024]{1,0:T(8,128)(2,1)} %bitcast.39, bf16[144,768]{1,0:T(8,128)(2,1)} %get-tuple-element.118.refs_1_, bf16[288,768]{1,0:T(8,128)(2,1)} %get-tuple-element.119.refs_2_, ...), custom_call_target="tpu_custom_call", output_to_operand_aliasing={{}: (1, {})} | custom-call | flops 3623878656 | bytes 9830400 | tf_op jit(solution)/shard_map/weights/pallas_call | solution.py:274
  118.4 15.8 %collective-permute-done.26 = bf16[192,1024]{1,0:T(8,128)(2,1)S(1)} collective-permute-done((bf16[192,1024]{1,0:T(8,128)(2,1)S(1)}, bf16[192,1024]{1,0:T(8,128)(2,1)S(1)}, u32[]{:S(2)}, u32[]{:S(2)}) %collective-permute-start.26) | collective-permute-done | bytes 393248 | tf_op jit(solution)/shard_map/ppermute | solution.py:313
  (154 shorter events, 28.0 us)
Async XLA Ops:
  0.7 32.9 %collective-permute-start.6 = (bf16[2304,384]{1,0:T(8,128)(2,1)}, bf16[2304,384]{1,0:T(8,128)(2,1)}, u32[]{:S(2)}, u32[]{:S(2)}) collective-permute-start(bf16[2304,384]{1,0:T(8,128)(2,1)} %bitcast.13), channel_id=1, source_target_pairs={{0,1},{1,0},{2,3},{3,2},{4,5},{5,4},{6,7},{7,6},{8,9},{9,8},{10,11... | collective-permute-start | bytes 5308424 | tf_op jit(solution)/shard_map/ppermute | solution.py:313
  1.2 32.4 %collective-permute-start.7 = (bf16[2304,384]{1,0:T(8,128)(2,1)}, bf16[2304,384]{1,0:T(8,128)(2,1)}, u32[]{:S(2)}, u32[]{:S(2)}) collective-permute-start(bf16[2304,384]{1,0:T(8,128)(2,1)} %bitcast.22), channel_id=1, source_target_pairs={{0,1},{1,0},{2,3},{3,2},{4,5},{5,4},{6,7},{7,6},{8,9},{9,8},{10,11... | collective-permute-start | bytes 5308424 | tf_op jit(solution)/shard_map/ppermute | solution.py:313
  3.9 28.2 %collective-permute-start.8 = (bf16[1024,768]{1,0:T(8,128)(2,1)}, bf16[1024,768]{1,0:T(8,128)(2,1)}, u32[]{:S(2)}, u32[]{:S(2)}) collective-permute-start(bf16[1024,768]{1,0:T(8,128)(2,1)} %pad_maximum_fusion.refs_4_.refs_8_), channel_id=1, source_target_pairs={{0,1},{1,0},{2,3},{3,2},{4,5},{5,4},{6,7},{7,6},{8,9},{9,8},{10,11... | collective-permute-start | bytes 4718600 | tf_op jit(solution)/shard_map/ppermute | solution.py:313
  5.2 15.1 %collective-permute-start = (bf16[200,1024]{1,0:T(8,128)(2,1)}, bf16[200,1024]{1,0:T(8,128)(2,1)}, u32[]{:S(2)}, u32[]{:S(2)}) collective-permute-start(bf16[200,1024]{1,0:T(8,128)(2,1)} %fusion.12.refs_0_), channel_id=1, source_target_pairs={{0,4},{1,5},{2,6},{3,7},{4,8},{5,9},{6,10},{7,11},{8,12},{9,13},{1... | collective-permute-start | bytes 1228808 | tf_op jit(solution)/shard_map/ppermute | solution.py:313
  10.2 12.9 %collective-permute-start.1 = (bf16[200,1024]{1,0:T(8,128)(2,1)}, bf16[200,1024]{1,0:T(8,128)(2,1)}, u32[]{:S(2)}, u32[]{:S(2)}) collective-permute-start(bf16[200,1024]{1,0:T(8,128)(2,1)} %fusion.12.refs_0_), channel_id=1, source_target_pairs={{0,2},{1,3},{2,0},{3,1},{4,6},{5,7},{6,4},{7,5},{8,10},{9,11},{10,... | collective-permute-start | bytes 1228808 | tf_op jit(solution)/shard_map/ppermute | solution.py:313
  23.1 15.1 %collective-permute-start.3 = (bf16[200,1024]{1,0:T(8,128)(2,1)}, bf16[200,1024]{1,0:T(8,128)(2,1)S(1)}, u32[]{:S(2)}, u32[]{:S(2)}) collective-permute-start(bf16[200,1024]{1,0:T(8,128)(2,1)} %collective-permute-done.refs_1_), channel_id=1, source_target_pairs={{0,4},{1,5},{2,6},{3,7},{4,8},{5,9},{6,10},{7,11},{8,12},{9,13},{1... | collective-permute-start | bytes 1228808 | tf_op jit(solution)/shard_map/ppermute | solution.py:313
  32.1 11.5 %collective-permute-start.11 = (bf16[576,384]{1,0:T(8,128)(2,1)}, bf16[576,384]{1,0:T(8,128)(2,1)S(1)}, u32[]{:S(2)}, u32[]{:S(2)}) collective-permute-start(bf16[576,384]{1,0:T(8,128)(2,1)} %get-tuple-element.68), channel_id=1, source_target_pairs={{0,16},{16,0},{1,17},{17,1},{2,18},{18,2},{3,19},{19,3},{4,20},{20... | collective-permute-start | bytes 1327112 | tf_op jit(solution)/shard_map/ppermute | solution.py:345
  38.2 11.2 %collective-permute-start.9 = (bf16[200,1024]{1,0:T(8,128)(2,1)S(1)}, bf16[200,1024]{1,0:T(8,128)(2,1)S(1)}, u32[]{:S(2)}, u32[]{:S(2)}) collective-permute-start(bf16[200,1024]{1,0:T(8,128)(2,1)S(1)} %collective-permute-done.3.refs_1_), channel_id=1, source_target_pairs={{0,4},{1,5},{2,6},{3,7},{4,8},{5,9},{6,10},{7,11},{8,12},{9,13},{1... | collective-permute-start | bytes 1228808 | tf_op jit(solution)/shard_map/ppermute | solution.py:313
  42.6 12.7 %collective-permute-start.14 = (bf16[576,384]{1,0:T(8,128)(2,1)}, bf16[576,384]{1,0:T(8,128)(2,1)S(1)}, u32[]{:S(2)}, u32[]{:S(2)}) collective-permute-start(bf16[576,384]{1,0:T(8,128)(2,1)} %get-tuple-element.75), channel_id=1, source_target_pairs={{0,16},{16,0},{1,17},{17,1},{2,18},{18,2},{3,19},{19,3},{4,20},{20... | collective-permute-start | bytes 1327112 | tf_op jit(solution)/shard_map/ppermute | solution.py:345
  49.5 11.6 %collective-permute-start.13 = (bf16[200,1024]{1,0:T(8,128)(2,1)S(1)}, bf16[200,1024]{1,0:T(8,128)(2,1)S(1)}, u32[]{:S(2)}, u32[]{:S(2)}) collective-permute-start(bf16[200,1024]{1,0:T(8,128)(2,1)S(1)} %collective-permute-done.9.refs_1_), channel_id=1, source_target_pairs={{0,2},{1,3},{2,0},{3,1},{4,6},{5,7},{6,4},{7,5},{8,10},{9,11},{10,... | collective-permute-start | bytes 1228808 | tf_op jit(solution)/shard_map/ppermute | solution.py:313
  53.9 11.5 %collective-permute-start.16 = (bf16[576,384]{1,0:T(8,128)(2,1)}, bf16[576,384]{1,0:T(8,128)(2,1)S(1)}, u32[]{:S(2)}, u32[]{:S(2)}) collective-permute-start(bf16[576,384]{1,0:T(8,128)(2,1)} %get-tuple-element.83), channel_id=1, source_target_pairs={{0,16},{16,0},{1,17},{17,1},{2,18},{18,2},{3,19},{19,3},{4,20},{20... | collective-permute-start | bytes 1327112 | tf_op jit(solution)/shard_map/ppermute | solution.py:345
  62.0 26.1 %collective-permute-start.22 = (bf16[288,1024]{1,0:T(8,128)(2,1)S(1)}, bf16[288,1024]{1,0:T(8,128)(2,1)S(1)}, u32[]{:S(2)}, u32[]{:S(2)}) collective-permute-start(bf16[288,1024]{1,0:T(8,128)(2,1)S(1)} %copy-done.26), channel_id=1, source_target_pairs={{0,1},{1,0},{2,3},{3,2},{4,5},{5,4},{6,7},{7,6},{8,9},{9,8},{10,11... | collective-permute-start | bytes 1769480 | tf_op jit(solution)/shard_map/ppermute | solution.py:313
  62.0 26.2 %collective-permute-start.23 = (bf16[288,1024]{1,0:T(8,128)(2,1)S(1)}, bf16[288,1024]{1,0:T(8,128)(2,1)S(1)}, u32[]{:S(2)}, u32[]{:S(2)}) collective-permute-start(bf16[288,1024]{1,0:T(8,128)(2,1)S(1)} %copy-done.27), channel_id=1, source_target_pairs={{0,1},{1,0},{2,3},{3,2},{4,5},{5,4},{6,7},{7,6},{8,9},{9,8},{10,11... | collective-permute-start | bytes 1769480 | tf_op jit(solution)/shard_map/ppermute | solution.py:313
  62.5 26.2 %collective-permute-start.24 = (bf16[288,1024]{1,0:T(8,128)(2,1)S(1)}, bf16[288,1024]{1,0:T(8,128)(2,1)S(1)}, u32[]{:S(2)}, u32[]{:S(2)}) collective-permute-start(bf16[288,1024]{1,0:T(8,128)(2,1)S(1)} %copy-done.28), channel_id=1, source_target_pairs={{0,1},{1,0},{2,3},{3,2},{4,5},{5,4},{6,7},{7,6},{8,9},{9,8},{10,11... | collective-permute-start | bytes 1769480 | tf_op jit(solution)/shard_map/ppermute | solution.py:313
  71.3 11.5 %collective-permute-start.17 = (bf16[192,1024]{1,0:T(8,128)(2,1)}, bf16[192,1024]{1,0:T(8,128)(2,1)S(1)}, u32[]{:S(2)}, u32[]{:S(2)}) collective-permute-start(bf16[192,1024]{1,0:T(8,128)(2,1)} %get-tuple-element.95), channel_id=1, source_target_pairs={{0,2},{1,3},{2,0},{3,1},{4,6},{5,7},{6,4},{7,5},{8,10},{9,11},{10,... | collective-permute-start | bytes 1179656 | tf_op jit(solution)/shard_map/ppermute | solution.py:313
  74.6 12.9 %collective-permute-start.21 = (bf16[144,1024]{1,0:T(8,128)(2,1)S(1)}, bf16[144,1024]{1,0:T(8,128)(2,1)S(1)}, u32[]{:S(2)}, u32[]{:S(2)}) collective-permute-start(bf16[144,1024]{1,0:T(8,128)(2,1)S(1)} %copy-done.40), channel_id=1, source_target_pairs={{0,1},{1,0},{2,3},{3,2},{4,5},{5,4},{6,7},{7,6},{8,9},{9,8},{10,11... | collective-permute-start | bytes 884744 | tf_op jit(solution)/shard_map/ppermute | solution.py:313
  87.6 17.7 %collective-permute-start.29 = (bf16[288,768]{1,0:T(8,128)(2,1)S(1)}, bf16[288,768]{1,0:T(8,128)(2,1)S(1)}, u32[]{:S(2)}, u32[]{:S(2)}) collective-permute-start(bf16[288,768]{1,0:T(8,128)(2,1)S(1)} %copy-done.29), channel_id=1, source_target_pairs={{0,1},{1,0},{2,3},{3,2},{4,5},{5,4},{6,7},{7,6},{8,9},{9,8},{10,11... | collective-permute-start | bytes 1327112 | tf_op jit(solution)/shard_map/ppermute | solution.py:313
  88.1 17.2 %collective-permute-start.30 = (bf16[288,768]{1,0:T(8,128)(2,1)S(1)}, bf16[288,768]{1,0:T(8,128)(2,1)S(1)}, u32[]{:S(2)}, u32[]{:S(2)}) collective-permute-start(bf16[288,768]{1,0:T(8,128)(2,1)S(1)} %copy-done.30), channel_id=1, source_target_pairs={{0,1},{1,0},{2,3},{3,2},{4,5},{5,4},{6,7},{7,6},{8,9},{9,8},{10,11... | collective-permute-start | bytes 1327112 | tf_op jit(solution)/shard_map/ppermute | solution.py:313
  88.2 20.7 %collective-permute-start.31 = (bf16[288,768]{1,0:T(8,128)(2,1)S(1)}, bf16[288,768]{1,0:T(8,128)(2,1)S(1)}, u32[]{:S(2)}, u32[]{:S(2)}) collective-permute-start(bf16[288,768]{1,0:T(8,128)(2,1)S(1)} %copy-done.31), channel_id=1, source_target_pairs={{0,1},{1,0},{2,3},{3,2},{4,5},{5,4},{6,7},{7,6},{8,9},{9,8},{10,11... | collective-permute-start | bytes 1327112 | tf_op jit(solution)/shard_map/ppermute | solution.py:313
  88.8 12.6 %collective-permute-start.20 = (bf16[192,1024]{1,0:T(8,128)(2,1)S(1)}, bf16[192,1024]{1,0:T(8,128)(2,1)S(1)}, u32[]{:S(2)}, u32[]{:S(2)}) collective-permute-start(bf16[192,1024]{1,0:T(8,128)(2,1)S(1)} %add_convert_fusion.3), channel_id=1, source_target_pairs={{0,12},{1,13},{2,14},{3,15},{4,0},{5,1},{6,2},{7,3},{8,4},{9,5},{1... | collective-permute-start | bytes 1179656 | tf_op jit(solution)/shard_map/ppermute | solution.py:313
  92.5 11.3 %collective-permute-start.19 = (bf16[192,1024]{1,0:T(8,128)(2,1)}, bf16[192,1024]{1,0:T(8,128)(2,1)S(1)}, u32[]{:S(2)}, u32[]{:S(2)}) collective-permute-start(bf16[192,1024]{1,0:T(8,128)(2,1)} %get-tuple-element.99), channel_id=1, source_target_pairs={{0,2},{1,3},{2,0},{3,1},{4,6},{5,7},{6,4},{7,5},{8,10},{9,11},{10,... | collective-permute-start | bytes 1179656 | tf_op jit(solution)/shard_map/ppermute | solution.py:313
  104.0 14.4 %collective-permute-start.12 = (bf16[192,1024]{1,0:T(8,128)(2,1)S(1)}, bf16[192,1024]{1,0:T(8,128)(2,1)S(1)}, u32[]{:S(2)}, u32[]{:S(2)}) collective-permute-start(bf16[192,1024]{1,0:T(8,128)(2,1)S(1)} %copy-done.39), channel_id=1, source_target_pairs={{0,2},{1,3},{2,0},{3,1},{4,6},{5,7},{6,4},{7,5},{8,10},{9,11},{10,... | collective-permute-start | bytes 1179656 | tf_op jit(solution)/shard_map/ppermute | solution.py:313
  105.2 29.0 %collective-permute-start.26 = (bf16[192,1024]{1,0:T(8,128)(2,1)S(1)}, bf16[192,1024]{1,0:T(8,128)(2,1)S(1)}, u32[]{:S(2)}, u32[]{:S(2)}) collective-permute-start(bf16[192,1024]{1,0:T(8,128)(2,1)S(1)} %add_convert_fusion.2), channel_id=1, source_target_pairs={{0,8},{1,9},{2,10},{3,11},{4,12},{5,13},{6,14},{7,15},{8,0},{9,1},... | collective-permute-start | bytes 1179656 | tf_op jit(solution)/shard_map/ppermute | solution.py:313
  105.4 28.9 %collective-permute-start.27 = (bf16[192,1024]{1,0:T(8,128)(2,1)S(1)}, bf16[192,1024]{1,0:T(8,128)(2,1)S(1)}, u32[]{:S(2)}, u32[]{:S(2)}) collective-permute-start(bf16[192,1024]{1,0:T(8,128)(2,1)S(1)} %add_convert_fusion.1), channel_id=1, source_target_pairs={{0,4},{1,5},{2,6},{3,7},{4,8},{5,9},{6,10},{7,11},{8,12},{9,13},{1... | collective-permute-start | bytes 1179656 | tf_op jit(solution)/shard_map/ppermute | solution.py:313
  (55 other events, 331.6 us)

commit v4 on v3

v4 whole, which is shorter than its diff:
```python
import functools

import jax
import jax.numpy as jnp
from jax import lax
from jax.experimental import pallas as pl
from jax.experimental.pallas import tpu as pltpu
from jax.sharding import PartitionSpec as P

gate_unit = 0.00390625
loss_scale = 0.015625
f32 = jnp.float32
bf16 = jnp.bfloat16


def contract_rows(left, right):
    return lax.dot_general(left, right, (((0,), (0,)), ((), ())), preferred_element_type=f32)


def contract_cols(left, right):
    return lax.dot_general(left, right, (((1,), (1,)), ((), ())), preferred_element_type=f32)


def activation_grads(grad_hidden, gate_pre, up_pre):
    sigmoid = jax.nn.sigmoid(gate_pre)
    silu = gate_pre * sigmoid
    dsilu = sigmoid * (1.0 + gate_pre * (1.0 - sigmoid))
    grad_gate_pre = (grad_hidden * up_pre * dsilu).astype(bf16)
    grad_up_pre = (grad_hidden * silu).astype(bf16)
    return (grad_gate_pre, grad_up_pre)


def body_any(out_grad, routes, gate_codes, w_gate, w_up, w_down, saved_inputs, saved_gate, saved_up):
    owners = lax.axis_size("expert")
    slot_count = saved_gate.shape[1]
    capacity = slot_count // owners
    token_count = routes.shape[0]
    choice_count = routes.shape[1]
    flat_routes = routes.reshape(-1)
    onehot = (flat_routes[:, None] == jnp.arange(owners, dtype=jnp.int32)[None, :]).astype(jnp.int32)
    earlier = jnp.cumsum(onehot, axis=0) - onehot
    position = jnp.sum(earlier * onehot, axis=1)
    slot_index = (flat_routes * capacity + position).reshape(token_count, choice_count)
    gate_values = gate_codes.astype(f32) * gate_unit
    rows_iota = jnp.arange(slot_count, dtype=jnp.int32)[:, None]
    weighted = jnp.zeros((slot_count, token_count), f32)
    picks = jnp.zeros((slot_count, token_count), f32)
    for pick in range(choice_count):
        hit = rows_iota == slot_index[:, pick][None, :]
        weighted = weighted + jnp.where(hit, gate_values[:, pick][None, :], 0.0)
        picks = picks + hit.astype(f32)
    outgoing = jnp.dot(weighted.astype(bf16), out_grad, preferred_element_type=f32).astype(bf16)
    received = lax.all_to_all(outgoing, "expert", split_axis=0, concat_axis=0, tiled=True)
    hidden_share = lax.psum_scatter(
        contract_cols(received, w_down[0]), "dp", scatter_dimension=0, tiled=True
    )
    gate_pre = saved_gate[0].astype(f32)
    up_pre = saved_up[0].astype(f32)
    hidden = (gate_pre * jax.nn.sigmoid(gate_pre) * up_pre).astype(bf16)
    grad_hidden = lax.all_gather(hidden_share, "dp", axis=0, tiled=True)
    grad_gate_pre, grad_up_pre = activation_grads(grad_hidden, gate_pre, up_pre)
    slot_grads = contract_cols(grad_gate_pre, w_gate[0]) + contract_cols(grad_up_pre, w_up[0])
    returned = lax.all_to_all(
        slot_grads.astype(bf16), "expert", split_axis=0, concat_axis=0, tiled=True
    )
    token_grads = contract_rows(picks.astype(bf16), returned).astype(bf16)
    inputs_here = saved_inputs[0]
    part = jnp.concatenate(
        [
            contract_rows(inputs_here, grad_gate_pre),
            contract_rows(inputs_here, grad_up_pre),
            contract_rows(received, hidden),
        ],
        axis=1,
    )
    return (token_grads, (part * loss_scale).astype(bf16)[None])


on_chip = pl.BlockSpec(memory_space=pltpu.VMEM)
on_scalar = pl.BlockSpec(memory_space=pltpu.SMEM)
anywhere = pl.BlockSpec(memory_space=pl.ANY)
light = pl.CostEstimate(flops=1 << 20, bytes_accessed=1 << 14, transcendentals=0)


def source(here, step, other):
    group = lax.rem(here // 4 + (4 - step), 4)
    return jnp.bitwise_xor(group * 4 + lax.rem(here, 4), 2 * other)


def params(mib):
    return pltpu.CompilerParams(vmem_limit_bytes=mib << 20)


def dispatch_kernel(n, cap, here, *refs):
    toks, (wd0, wd1) = refs[:n], refs[n : n + 2]
    rec0, rec1, share, *share_out, pos_out = refs[n + 2 :]
    tok = toks[0].shape[0] - 8
    line = 256 * pl.cdiv(tok, 256)
    before = lax.broadcasted_iota(jnp.int32, (tok, tok), 0) < lax.broadcasted_iota(jnp.int32, (tok, tok), 1)
    before = jnp.where(before, 1.0, 0.0).astype(bf16)
    slot = lax.broadcasted_iota(jnp.int32, (cap, tok), 0).astype(f32)
    masks, gates = [], []
    for a in range(2):
        expert = jnp.bitwise_xor(here[0], a).astype(f32)
        for t in toks:
            hit = t[tok:, :tok].astype(f32) == expert
            masks.append(jnp.max(jnp.where(hit, 1.0, 0.0), axis=0, keepdims=True))
            gates.append(jnp.sum(jnp.where(hit, t[tok:, line : line + tok].astype(f32), 0.0), axis=0, keepdims=True))
    fill = [jnp.zeros((8 - 2 * n, tok), f32)] if n < 4 else []
    mask = jnp.concatenate(masks + fill, axis=0)
    pos = jnp.dot(mask.astype(bf16), before, preferred_element_type=f32)
    pos = jnp.where(mask > 0.0, pos, -1.0)
    pos_out[...] = pos
    for rel, t in enumerate(toks):
        w = [
            jnp.where(slot == pos[i : i + 1, :], gates[i] * gate_unit, 0.0).astype(bf16)
            for i in (rel, n + rel)
        ]
        rows = jnp.dot(jnp.concatenate(w, axis=0), t[:tok, :], preferred_element_type=f32).astype(bf16)
        rec0[rel * cap : (rel + 1) * cap, :] = rows[:cap]
        rec1[rel * cap : (rel + 1) * cap, :] = rows[cap:]
    for a, (rec, wd) in enumerate(((rec0, wd0), (rec1, wd1))):
        gh = contract_cols(rec[...], wd[...])
        share[a * n * cap : (a + 1) * n * cap, :] = gh
        share_out[a][...] = gh.astype(bf16)


def dispatch(here, toks, wd0, wd1, cap):
    n = len(toks)
    tok, d = toks[0].shape
    h = wd0.shape[0]
    outs = [((n * cap, d), bf16), ((n * cap, d), bf16), ((2 * n * cap, h), f32), ((n * cap, h), bf16), ((n * cap, h), bf16), ((8, tok - 8), f32)]
    return pl.pallas_call(
        functools.partial(dispatch_kernel, n, cap),
        out_shape=[jax.ShapeDtypeStruct(s, t) for s, t in outs],
        in_specs=[on_scalar] + [on_chip] * (n + 2),
        out_specs=[on_chip] * len(outs),
        cost_estimate=light,
        compiler_params=params(16),
        name="dispatch",
    )(here, *toks, wd0, wd1)


def combine_kernel(chunk, cap, here, share, peer0, peer1, pos, *refs):
    n = len(chunk)
    saved, (w0, w1, rec1), (gp0, both) = refs[:4], refs[4:7], refs[7:9]
    backs, (held, sems) = refs[9 : 9 + n], refs[9 + n :]
    d = rec1.shape[1]
    gp1 = both.at[:, d:]
    both[:, :d] = rec1[...]
    h = share.shape[1]
    copies = []
    for a in range(2):
        for other, step in chunk:
            rows = pl.ds(pl.multiple_of(source(here[0], step, other) * cap, 16), cap)
            for v in saved[2 * a : 2 * a + 2]:
                i = len(copies)
                copies.append(pltpu.make_async_copy(v.at[rows, :], held.at[i], sems.at[i]))
    for c in copies:
        c.start()
    slot = lax.broadcasted_iota(jnp.int32, (cap, pos.shape[1]), 0).astype(f32)
    sums = [None] * n
    for a, (gp, w, peer) in enumerate(((gp0, w0, peer0), (gp1, w1, peer1))):
        for rel in range(n):
            i = a * n + rel
            copies[2 * i].wait()
            copies[2 * i + 1].wait()
            gh = share[i * cap : (i + 1) * cap, :] + peer[rel * cap : (rel + 1) * cap, :].astype(f32)
            gg, gu = activation_grads(gh, held[2 * i].astype(f32), held[2 * i + 1].astype(f32))
            gp[rel * cap : (rel + 1) * cap, :h] = gg
            gp[rel * cap : (rel + 1) * cap, h:] = gu
        slots = contract_cols(gp[...], w[...]).astype(bf16)
        for rel in range(n):
            i = a * n + rel
            pick = jnp.where(slot == pos[i : i + 1, :], 1.0, 0.0).astype(bf16)
            part = contract_rows(pick, slots[rel * cap : (rel + 1) * cap])
            sums[rel] = part if sums[rel] is None else sums[rel] + part
    for rel in range(n):
        backs[rel][...] = sums[rel].astype(bf16)


def combine(here, chunk, share, peers, pos, saved0, saved1, w0, w1, rec1, cap):
    n = len(chunk)
    h = share.shape[1]
    d = w0.shape[0]
    tok = pos.shape[1]
    outs = [(n * cap, 2 * h), (n * cap, d + 2 * h)] + [(tok, d)] * n
    return pl.pallas_call(
        functools.partial(combine_kernel, chunk, cap),
        out_shape=[jax.ShapeDtypeStruct(s, bf16) for s in outs],
        in_specs=[on_scalar] + [on_chip] * 4 + [anywhere] * 4 + [on_chip] * 3,
        out_specs=[on_chip] * len(outs),
        scratch_shapes=[pltpu.VMEM((4 * n, cap, h), bf16), pltpu.SemaphoreType.DMA((4 * n,))],
        cost_estimate=light,
        compiler_params=params(20),
        name="combine",
    )(here, share, *peers, pos, *saved0, *saved1, w0, w1, rec1)


def join_kernel(left, right, out):
    out[:, : left.shape[1]] = left[...]
    out[:, left.shape[1] :] = right[...]


def join(left, right):
    rows, h = left.shape
    return pl.pallas_call(
        join_kernel,
        out_shape=jax.ShapeDtypeStruct((rows, 2 * h), left.dtype),
        in_specs=[on_chip] * 2,
        out_specs=on_chip,
        cost_estimate=light,
        compiler_params=params(8),
        name="join",
    )(left, right)


def add_kernel(*refs):
    total = refs[0][...].astype(f32)
    for r in refs[1:-1]:
        total = total + r[...].astype(f32)
    refs[-1][...] = total.astype(refs[-1].dtype)


def add(*values):
    return pl.pallas_call(
        add_kernel,
        out_shape=jax.ShapeDtypeStruct(values[0].shape, values[0].dtype),
        in_specs=[on_chip] * len(values),
        out_specs=on_chip,
        cost_estimate=light,
        compiler_params=params(8),
        name="add",
    )(*values)


def weights_kernel(order, cap, sorted_left, starts, here, *refs):
    count = 1 if sorted_left else 2
    by_source, pieces, out = refs[:count], refs[count:-5], refs[-5]
    ls, rs, left_sems, right_sems = refs[-4:]
    i = pl.program_id(0)
    tile = ls.shape[2]
    steps = pl.num_programs(0)

    def copies_of_sorted(v, column, to, sems):
        made = []
        for p, (step, other, plane) in enumerate(order):
            src = jnp.bitwise_xor(source(here[0], step, other), plane)
            rows = pl.ds(pl.multiple_of(src * cap, 16), cap)
            at = v.at[rows, :] if column is None else v.at[rows, pl.ds(pl.multiple_of(column * tile, 128), tile)]
            made.append(pltpu.make_async_copy(at, to.at[pl.ds(p * cap, cap), :], sems.at[len(made)]))
        return made

    def copies_of_pieces(column, to, sems):
        made, base = [], 0
        for r, first in zip(pieces, starts):
            if column is None:
                at = r.at[:, pl.ds(first, to.shape[1])]
            else:
                at = r.at[:, pl.ds(pl.multiple_of(first + column * tile, 128), tile)]
            made.append(pltpu.make_async_copy(at, to.at[pl.ds(base, r.shape[0]), :], sems.at[len(made)]))
            base += r.shape[0]
        return made

    def left(step):
        slot = lax.rem(step, 2)
        if sorted_left:
            return copies_of_sorted(by_source[0], step, ls.at[slot], left_sems.at[slot])
        return copies_of_pieces(step, ls.at[slot], left_sems.at[slot])

    def right():
        if sorted_left:
            return copies_of_pieces(None, rs.at[0], right_sems.at[0])
        return [c for k in range(2) for c in copies_of_sorted(by_source[k], None, rs.at[k], right_sems.at[k])]

    @pl.when(i == 0)
    def _():
        for c in right() + left(i):
            c.start()

    @pl.when(i + 1 < steps)
    def _():
        for c in left(i + 1):
            c.start()

    @pl.when(i == 0)
    def _():
        for c in right():
            c.wait()
        if not sorted_left:
            gate_pre = rs[0].astype(f32)
            rs[0] = (gate_pre * jax.nn.sigmoid(gate_pre) * rs[1].astype(f32)).astype(bf16)

    for c in left(i):
        c.wait()

    out[0] = (contract_rows(ls[lax.rem(i, 2)], rs[0]) * loss_scale).astype(bf16)


def weight_sums(here, order, by_source, pieces, starts, sorted_left, into, cap):
    slots, wide = by_source[0].shape
    d = pieces[0].shape[1]
    if sorted_left:
        d, wide = wide, d
    tile = 256
    at = 0 if sorted_left else 2
    whole_out = jax.ShapeDtypeStruct((1, d, 3 * (wide // 2 if sorted_left else wide)), bf16)
    given = [*by_source, *pieces]
    kernel = functools.partial(weights_kernel, order, cap, sorted_left, starts)
    body = kernel if into is None else (lambda here, old, *refs: kernel(here, *refs))
    return pl.pallas_call(
        body,
        out_shape=whole_out,
        grid_spec=pltpu.PrefetchScalarGridSpec(
            num_scalar_prefetch=1,
            grid=(d // tile,),
            in_specs=[anywhere] * (len(given) + (into is not None)),
            out_specs=pl.BlockSpec((1, tile, wide), lambda i, here: (0, i, at)),
            scratch_shapes=[
                pltpu.VMEM((2, slots, tile), bf16),
                pltpu.VMEM((len(by_source), slots, wide), bf16),
                pltpu.SemaphoreType.DMA((2, len(order))),
                pltpu.SemaphoreType.DMA((len(by_source), len(order))),
            ],
        ),
        input_output_aliases={} if into is None else {1: 0},
        cost_estimate=light,
        compiler_params=params(20),
        name="weights",
    )(here, *([] if into is None else [into]), *given)


def together(*values):
    return lax.optimization_barrier(values)


def body_grid(out_grad, routes, gate_codes, w_gate, w_up, w_down, saved_inputs, saved_gate, saved_up):
    owners = lax.axis_size("expert")
    me = lax.axis_index("expert")
    to_core = [(i, i ^ 1) for i in range(owners)]
    to_x = [(i, i ^ 2) for i in range(owners)]
    tok, d = out_grad.shape
    choices = routes.shape[1]
    slots = saved_gate.shape[1]
    cap = slots // owners

    def send(v, perm):
        return lax.ppermute(v, "expert", perm)

    line = 256 * pl.cdiv(tok, 256)
    named = jnp.concatenate(
        [
            jnp.pad(routes.T.astype(bf16), ((0, 8 - choices), (0, line - tok)), constant_values=-1),
            jnp.pad(gate_codes.T.astype(bf16), ((0, 8 - choices), (0, d - line - tok))),
        ],
        axis=1,
    )
    block = jnp.concatenate([out_grad, named], axis=0)
    here = me.reshape(1).astype(jnp.int32)

    def ring(v, hops=1):
        return send(v, [(i, (i + 4 * hops) % owners) for i in range(owners)])

    wd, sg, su = w_down[0], saved_gate[0], saved_up[0]
    wd_c, sg_c, su_c = [send(v, to_core) for v in (wd, sg, su)]

    order, recs, gps = [], [], []

    def first(chunk, toks):
        rec, rec_c, share, share0, share1, pos = dispatch(here, toks, wd, wd_c, cap)
        order.extend((k, col, 0) for col, k in chunk)
        recs.append(rec)
        return (chunk, share, pos, rec_c), share0, share1

    def exchange(v):
        return lax.ppermute(v, "dp", [(0, 1), (1, 0)])

    def second(state, *peers):
        chunk, share, pos, rec_c = state
        gp, both, *sums = combine(here, chunk, share, peers, pos, (sg, su), (sg_c, su_c), w, w_c, rec_c, cap)
        gps.append(gp)
        return both, *sums

    r1, x0 = ring(block), send(block, to_x)
    c0, h0, g0 = first([(0, 0)], [block])
    w = join(w_gate[0], w_up[0])
    r1, x0, h0, g0, w, sg_c, su_c = together(r1, x0, h0, g0, w, sg_c, su_c)
    r2, x1 = ring(r1), send(r1, to_x)
    h0, g0, w_c = exchange(h0), exchange(g0), send(w, to_core)
    c1, h1, g1 = first([(1, 0), (0, 1)], [x0, r1])
    h1 = exchange(h1)
    both0, t_r0 = second(c0, h0, g0)
    r2, x1, h1, g1, t_r0, both0 = together(r2, x1, h1, g1, t_r0, both0)
    r3, x2 = ring(r2), send(r2, to_x)
    g1, p0 = exchange(g1), send(both0, to_core)
    c2, h2, g2 = first([(1, 1), (0, 2)], [x1, r2])
    h2 = exchange(h2)
    both1, t_x0, t_r1 = second(c1, h1, g1)
    r3, x2, p0, h2, g2, t_x0, t_r1, both1 = together(r3, x2, p0, h2, g2, t_x0, t_r1, both1)
    x3 = send(r3, to_x)
    g2, p1 = exchange(g2), send(both1, to_core)
    c3, h3, g3 = first([(1, 2), (0, 3)], [x2, r3])
    h3 = exchange(h3)
    both2, t_x1, t_r2 = second(c2, h2, g2)
    x3, p1, h3, g3, t_x1, t_r2, both2 = together(x3, p1, h3, g3, t_x1, t_r2, both2)
    b1 = send(t_x1, to_x)
    g3, p2 = exchange(g3), send(both2, to_core)
    c4, h4, g4 = first([(1, 3)], [x3])
    h4, g4 = exchange(h4), exchange(g4)
    both3, t_x2, t_r3 = second(c3, h3, g3)
    b1, p2, h4, g4, t_x2, t_r3, both3 = together(b1, p2, h4, g4, t_x2, t_r3, both3)
    b2 = send(t_x2, to_x)
    p3 = send(both3, to_core)
    w1 = ring(add(t_r1, b1))
    both4, t_x3 = second(c4, h4, g4)
    b3, p4 = send(t_x3, to_x), send(both4, to_core)
    b2, p3, w1, _ = together(b2, p3, w1, t_x3)
    w2 = ring(add(t_r2, b2, w1))
    away = [p0, p1, p2, p3, p4]
    order_all = order + [(k, col, 1) for k, col, _ in order]
    zeros = [0] * len(recs)
    part = weight_sums(here, order_all, [sg, su], recs + away, zeros + zeros, False, None, cap)
    b3, w2, part, t_x0 = together(b3, w2, part, t_x0)
    w3 = ring(add(t_r3, b3, w2))
    b0 = send(t_x0, to_x)
    skip = [d] * len(recs)
    weight_grads = weight_sums(here, order_all, [saved_inputs[0]], gps + away, zeros + skip, True, part, cap)
    total = add(t_r0, b0, w3)
    return (total, weight_grads)


def solution(mesh):
    placed = (
        P("expert", "dp"),
        P("expert", None),
        P("expert", None),
        P("expert", "dp", None),
        P("expert", "dp", None),
        P("expert", None, "dp"),
        P("expert", None, "dp"),
        P("expert", None, None),
        P("expert", None, None),
    )
    small = mesh.shape["expert"] == 16 and mesh.shape["dp"] == 2
    return jax.shard_map(
        body_grid if small else body_any,
        mesh=mesh,
        in_specs=placed,
        out_specs=(P("expert", "dp"), P("expert", "dp", None)),
        check_vma=False,
    )
```

time: 136 us -> 118 us (0.87)
  Pallas kernels: 55.5 us -> 47.3 us
  other arithmetic: 7.16 us -> 2.49 us
  local copies, waits for them, and re-layouts: 5.81 us -> 2.36 us
  starting transfers between devices: 31.9 us -> 28.5 us
  waiting for transfers between devices: 33.9 us -> 36.2 us
    ppermute x5 -> x10, waiting for transfers between devices: 2.44 us -> 19.8 us  [exchange(): return lax.ppermute(v, 'dp', [(0, 1), (1, 0)])]
    ppermute x28 -> x23, waiting for transfers between devices: 31.5 us -> 16.3 us  [send(): return lax.ppermute(v, 'expert', perm)]
    pallas_call x10 -> x15, Pallas kernels: 39.8 us -> 27.8 us  [the longest x5 14.7 us: combine(): pl.pallas_call(functools.partial(combine_kernel, chunk, cap), out_shape=[...]
    ppermute x28 -> x23, starting transfers between devices: 25.5 us -> 18.2 us  [send(): return lax.ppermute(v, 'expert', perm)]
    ppermute x5 -> x10, starting transfers between devices: 6.44 us -> 10.4 us  [exchange(): return lax.ppermute(v, 'dp', [(0, 1), (1, 0)])]
    pallas_call x2, Pallas kernels: 15.7 us -> 19.6 us  [weight_sums(): pl.pallas_call(body, out_shape=whole_out, grid_spec=pltpu.PrefetchScalarG...]
    convert_element_type x5 -> x0, other arithmetic: 3.74 us -> none  [the longest x1 2.27 us: body_grid(): hid = (gate_pre * jax.nn.sigmoid(gate_pre) * su.astype(f32)).astype(bf16)]
    unnamed x92 -> x14, local copies, waits for them, and re-layouts: 5.81 us -> 2.36 us
  transfers between devices with their start and end apart: 33 -> 33, of which waited for: 9 -> 11; matrix products, arithmetic and copies ran while one was open for 4% -> 2% of each run, Pallas kernels for 41% -> 39%
where the time goes in v4:
time: 118 us
  Pallas kernels  47.3 us (40%)
  waiting for transfers between devices  36.2 us (31%)
  starting transfers between devices  28.5 us (24%)
  other arithmetic  2.49 us (2%)
  local copies, waits for them, and re-layouts  2.36 us (2%)
    ppermute x10, waiting for transfers between devices, exchange(): return lax.ppermute(v, 'dp', [(0, 1), (1, 0)])  19.8 us
    pallas_call x2, Pallas kernels, weight_sums(): pl.pallas_call(body, out_shape=whole_out, grid_spec=pltpu.PrefetchScalarG...  19.6 us
    ppermute x23, starting transfers between devices, send(): return lax.ppermute(v, 'expert', perm)  18.2 us
    ppermute x23, waiting for transfers between devices, send(): return lax.ppermute(v, 'expert', perm)  16.3 us
    pallas_call x5, Pallas kernels, combine(): pl.pallas_call(functools.partial(combine_kernel, chunk, cap), out_shape=[...  14.7 us
    pallas_call x5, Pallas kernels, dispatch(): pl.pallas_call(functools.partial(dispatch_kernel, n, cap), out_shape=[jax...  11.6 us
    ppermute x10, starting transfers between devices, exchange(): return lax.ppermute(v, 'dp', [(0, 1), (1, 0)])  10.4 us
    unnamed x14, local copies, waits for them, and re-layouts  2.36 us
  transfers between devices with their start and end apart: 33, of which 11 were waited for; matrix products, arithmetic and copies ran while one was open for 2% of the time, Pallas kernels for 39%

profile of v4, /device:TPU:0, one launch (start us, length us, event | category | flops | bytes accessed | tf_op | source)
XLA Modules:
  0.0 117.8 jit_solution(14606880697520031608)
XLA Ops:
  2.4 1.8 %fusion.7.refs_0_ = bf16[200,1024]{1,0:T(8,128)(2,1)} fusion(bf16[8,192]{1,0:T(8,128)(2,1)S(1)} %get-tuple-element.182, bf16[8,192]{1,0:T(8,128)(2,1)S(1)} %get-tuple-element.183, bf16[192,1024]{1,0:T(8,128)(2,1)} %param.9), kind=kLoop, calls=%fused_computation.10 | loop fusion | flops 3072000 | bytes 808960 | tf_op jit(solution)/shard_map/concatenate | solution.py:358
  4.2 2.7 %collective-permute-start = (bf16[200,1024]{1,0:T(8,128)(2,1)}, bf16[200,1024]{1,0:T(8,128)(2,1)}, u32[]{:S(2)}, u32[]{:S(2)}) collective-permute-start(bf16[200,1024]{1,0:T(8,128)(2,1)} %fusion.7.refs_0_), channel_id=1, source_target_pairs={{0,4},{1,5},{2,6},{3,7},{4,8},{5,9},{6,10},{7,11},{8,12},{9,13},{1... | collective-permute-start | bytes 1228808 | tf_op jit(solution)/shard_map/ppermute | solution.py:348
  10.8 2.3 %dispatch.5 = (bf16[144,1024]{1,0:T(8,128)(2,1)S(1)}, bf16[144,1024]{1,0:T(8,128)(2,1)S(1)}, f32[288,384]{1,0:T(8,128)S(1)}, bf16[144,384]{1,0:T(8,128)(2,1)S(1)...) custom-call(s32[1]{0:T(128)} %bitcast.2.here, bf16[200,1024]{1,0:T(8,128)(2,1)} %fusion.7.refs_0_, ...), custom_call_target="tpu_custom_call" | custom-call | flops 1048576 | bytes 16384 | tf_op jit(solution)/shard_map/dispatch/pallas_call | solution.py:133
  13.1 6.1 %collective-permute-done.refs_1_ = bf16[200,1024]{1,0:T(8,128)(2,1)} collective-permute-done((bf16[200,1024]{1,0:T(8,128)(2,1)}, bf16[200,1024]{1,0:T(8,128)(2,1)}, u32[]{:S(2)}, u32[]{:S(2)}) %collective-permute-start) | collective-permute-done | bytes 409632 | tf_op jit(solution)/shard_map/ppermute | solution.py:348
  23.3 2.6 %dispatch.6 = (bf16[288,1024]{1,0:T(8,128)(2,1)S(1)}, bf16[288,1024]{1,0:T(8,128)(2,1)S(1)}, f32[576,384]{1,0:T(8,128)S(1)}, bf16[288,384]{1,0:T(8,128)(2,1)S(1)...) custom-call(s32[1]{0:T(128)} %bitcast.2.here, bf16[200,1024]{1,0:T(8,128)(2,1)} %collective-permute-done.1.refs_0_, ...), custom_call_target="tpu_custom_call" | custom-call | flops 1048576 | bytes 16384 | tf_op jit(solution)/shard_map/dispatch/pallas_call | solution.py:133
  28.2 7.1 %collective-permute-done.9.peer1 = bf16[144,384]{1,0:T(8,128)(2,1)S(1)} collective-permute-done((bf16[144,384]{1,0:T(8,128)(2,1)S(1)}, bf16[144,384]{1,0:T(8,128)(2,1)S(1)}, u32[]{:S(2)}, u32[]{:S(2)}) %collective-permute-start.9) | collective-permute-done | bytes 110624 | tf_op jit(solution)/shard_map/ppermute | solution.py:376
  35.3 2.3 %combine.5 = (bf16[144,768]{1,0:T(8,128)(2,1)S(1)}, bf16[144,1792]{1,0:T(8,128)(2,1)S(1)}, bf16[192,1024]{1,0:T(8,128)(2,1)S(1)}) custom-call(s32[1]{0:T(128)} %bitcast.2.here, f32[288,384]{1,0:T(8,128)S(1)} %get-tuple-element.98.share, bf16[144,384]{1,0:T(8,128)(2,1)S(1)} %collective-permute-done.8.peer0, ...), custom_call_target="tpu_custom_call" | custom-call | flops 1048576 | bytes 16384 | tf_op jit(solution)/shard_map/combine/pallas_call | solution.py:188
  37.7 1.8 %collective-permute-start.11 = (bf16[200,1024]{1,0:T(8,128)(2,1)S(1)}, bf16[200,1024]{1,0:T(8,128)(2,1)S(1)}, u32[]{:S(2)}, u32[]{:S(2)}) collective-permute-start(bf16[200,1024]{1,0:T(8,128)(2,1)S(1)} %collective-permute-done.5.refs_1_), channel_id=1, source_target_pairs={{0,4},{1,5},{2,6},{3,7},{4,8},{5,9},{6,10},{7,11},{8,12},{9,13},{1... | collective-permute-start | bytes 1228808 | tf_op jit(solution)/shard_map/ppermute | solution.py:348
  40.6 2.4 %dispatch.7 = (bf16[288,1024]{1,0:T(8,128)(2,1)S(1)}, bf16[288,1024]{1,0:T(8,128)(2,1)S(1)}, f32[576,384]{1,0:T(8,128)S(1)}, bf16[288,384]{1,0:T(8,128)(2,1)S(1)...) custom-call(s32[1]{0:T(128)} %bitcast.2.here, bf16[200,1024]{1,0:T(8,128)(2,1)S(1)} %collective-permute-done.6.refs_0_, ...), custom_call_target="tpu_custom_call" | custom-call | flops 1048576 | bytes 16384 | tf_op jit(solution)/shard_map/dispatch/pallas_call | solution.py:133
  43.0 1.6 %collective-permute-start.14 = (bf16[288,384]{1,0:T(8,128)(2,1)S(1)}, bf16[288,384]{1,0:T(8,128)(2,1)S(1)}, u32[]{:S(2)}, u32[]{:S(2)}) collective-permute-start(bf16[288,384]{1,0:T(8,128)(2,1)S(1)} %get-tuple-element.112), channel_id=1, source_target_pairs={{0,16},{16,0},{1,17},{17,1},{2,18},{18,2},{3,19},{19,3},{4,20},{20... | collective-permute-start | bytes 663560 | tf_op jit(solution)/shard_map/ppermute | solution.py:376
  44.6 3.9 %collective-permute-done.15.peer1 = bf16[288,384]{1,0:T(8,128)(2,1)S(1)} collective-permute-done((bf16[288,384]{1,0:T(8,128)(2,1)S(1)}, bf16[288,384]{1,0:T(8,128)(2,1)S(1)}, u32[]{:S(2)}, u32[]{:S(2)}) %collective-permute-start.15) | collective-permute-done | bytes 221216 | tf_op jit(solution)/shard_map/ppermute | solution.py:376
  48.4 3.4 %combine.6 = (bf16[288,768]{1,0:T(8,128)(2,1)S(1)}, bf16[288,1792]{1,0:T(8,128)(2,1)S(1)}, bf16[192,1024]{1,0:T(8,128)(2,1)S(1)}, bf16[192,1024]{1,0:T(8,128)(2,1)S(1)}) custom-call(s32[1]{0:T(128)} %bitcast.2.here, f32[576,384]{1,0:T(8,128)S(1)} %get-tuple-element.114.share, bf16[288,384]{1,0:T(8,128)(2,1)S(1)} %collective-permute-done.7.peer0, ...), custom_call_target="tpu_custom_call" | custom-call | flops 1048576 | bytes 16384 | tf_op jit(solution)/shard_map/combine/pallas_call | solution.py:188
  54.0 2.4 %dispatch.8 = (bf16[288,1024]{1,0:T(8,128)(2,1)S(1)}, bf16[288,1024]{1,0:T(8,128)(2,1)S(1)}, f32[576,384]{1,0:T(8,128)S(1)}, bf16[288,384]{1,0:T(8,128)(2,1)S(1)...) custom-call(s32[1]{0:T(128)} %bitcast.2.here, bf16[200,1024]{1,0:T(8,128)(2,1)S(1)} %collective-permute-done.12.refs_0_, ...), custom_call_target="tpu_custom_call" | custom-call | flops 1048576 | bytes 16384 | tf_op jit(solution)/shard_map/dispatch/pallas_call | solution.py:133
  56.4 1.6 %collective-permute-start.18 = (bf16[288,384]{1,0:T(8,128)(2,1)S(1)}, bf16[288,384]{1,0:T(8,128)(2,1)S(1)}, u32[]{:S(2)}, u32[]{:S(2)}) collective-permute-start(bf16[288,384]{1,0:T(8,128)(2,1)S(1)} %get-tuple-element.125), channel_id=1, source_target_pairs={{0,16},{16,0},{1,17},{17,1},{2,18},{18,2},{3,19},{19,3},{4,20},{20... | collective-permute-start | bytes 663560 | tf_op jit(solution)/shard_map/ppermute | solution.py:376
  58.0 3.8 %collective-permute-done.19.peer1 = bf16[288,384]{1,0:T(8,128)(2,1)S(1)} collective-permute-done((bf16[288,384]{1,0:T(8,128)(2,1)S(1)}, bf16[288,384]{1,0:T(8,128)(2,1)S(1)}, u32[]{:S(2)}, u32[]{:S(2)}) %collective-permute-start.19) | collective-permute-done | bytes 221216 | tf_op jit(solution)/shard_map/ppermute | solution.py:376
  61.8 3.4 %combine.7 = (bf16[288,768]{1,0:T(8,128)(2,1)S(1)}, bf16[288,1792]{1,0:T(8,128)(2,1)S(1)}, bf16[192,1024]{1,0:T(8,128)(2,1)S(1)}, bf16[192,1024]{1,0:T(8,128)(2,1)S(1)}) custom-call(s32[1]{0:T(128)} %bitcast.2.here, f32[576,384]{1,0:T(8,128)S(1)} %get-tuple-element.127.share, bf16[288,384]{1,0:T(8,128)(2,1)S(1)} %collective-permute-done.14.peer0, ...), custom_call_target="tpu_custom_call" | custom-call | flops 1048576 | bytes 16384 | tf_op jit(solution)/shard_map/combine/pallas_call | solution.py:188
  66.9 2.0 %dispatch.9 = (bf16[144,1024]{1,0:T(8,128)(2,1)S(1)}, bf16[144,1024]{1,0:T(8,128)(2,1)S(1)}, f32[288,384]{1,0:T(8,128)S(1)}, bf16[144,384]{1,0:T(8,128)(2,1)S(1)...) custom-call(s32[1]{0:T(128)} %bitcast.2.here, bf16[200,1024]{1,0:T(8,128)(2,1)S(1)} %collective-permute-done.16.refs_0_, ...), custom_call_target="tpu_custom_call" | custom-call | flops 1048576 | bytes 16384 | tf_op jit(solution)/shard_map/dispatch/pallas_call | solution.py:133
  68.9 1.6 %collective-permute-start.22 = (bf16[144,384]{1,0:T(8,128)(2,1)S(1)}, bf16[144,384]{1,0:T(8,128)(2,1)S(1)}, u32[]{:S(2)}, u32[]{:S(2)}) collective-permute-start(bf16[144,384]{1,0:T(8,128)(2,1)S(1)} %get-tuple-element.139), channel_id=1, source_target_pairs={{0,16},{16,0},{1,17},{17,1},{2,18},{18,2},{3,19},{19,3},{4,20},{20... | collective-permute-start | bytes 331784 | tf_op jit(solution)/shard_map/ppermute | solution.py:376
  71.0 3.7 %collective-permute-done.24.peer1 = bf16[288,384]{1,0:T(8,128)(2,1)S(1)} collective-permute-done((bf16[288,384]{1,0:T(8,128)(2,1)S(1)}, bf16[288,384]{1,0:T(8,128)(2,1)S(1)}, u32[]{:S(2)}, u32[]{:S(2)}) %collective-permute-start.24) | collective-permute-done | bytes 221216 | tf_op jit(solution)/shard_map/ppermute | solution.py:376
  74.7 3.4 %combine.8 = (bf16[288,768]{1,0:T(8,128)(2,1)S(1)}, bf16[288,1792]{1,0:T(8,128)(2,1)S(1)}, bf16[192,1024]{1,0:T(8,128)(2,1)S(1)}, bf16[192,1024]{1,0:T(8,128)(2,1)S(1)}) custom-call(s32[1]{0:T(128)} %bitcast.2.here, f32[576,384]{1,0:T(8,128)S(1)} %get-tuple-element.141.share, bf16[288,384]{1,0:T(8,128)(2,1)S(1)} %collective-permute-done.18.peer0, ...), custom_call_target="tpu_custom_call" | custom-call | flops 1048576 | bytes 16384 | tf_op jit(solution)/shard_map/combine/pallas_call | solution.py:188
  80.6 2.3 %combine.9 = (bf16[144,768]{1,0:T(8,128)(2,1)S(1)}, bf16[144,1792]{1,0:T(8,128)(2,1)S(1)}, bf16[192,1024]{1,0:T(8,128)(2,1)S(1)}) custom-call(s32[1]{0:T(128)} %bitcast.2.here, f32[288,384]{1,0:T(8,128)S(1)} %get-tuple-element.136.share, bf16[144,384]{1,0:T(8,128)(2,1)S(1)} %collective-permute-done.22.peer0, ...), custom_call_target="tpu_custom_call" | custom-call | flops 1048576 | bytes 16384 | tf_op jit(solution)/shard_map/combine/pallas_call | solution.py:188
  83.6 8.5 %collective-permute-done.28.refs_2_ = bf16[192,1024]{1,0:T(8,128)(2,1)S(1)} collective-permute-done((bf16[192,1024]{1,0:T(8,128)(2,1)S(1)}, bf16[192,1024]{1,0:T(8,128)(2,1)S(1)}, u32[]{:S(2)}, u32[]{:S(2)}) %collective-permute-start.28) | collective-permute-done | bytes 393248 | tf_op jit(solution)/shard_map/ppermute | solution.py:348
  93.6 10.8 %weights.2.old = bf16[1,1024,1152]{2,1,0:T(8,128)(2,1)} custom-call(s32[1]{0:T(128)} %bitcast.2.here, bf16[2304,384]{1,0:T(8,128)(2,1)S(1)} %bitcast.17, bf16[2304,384]{1,0:T(8,128)(2,1)S(1)} %bitcast.24, bf16[144,1024]{1,0:T(8,128)(2,1)S(1)} %get-tuple-element.161.refs_2_, bf16[288,1024]{1,0:T(8,128)(2,1)S(1)} %get-tuple-element.162.refs_3_, ...), custom_call_target="tpu_custom_call" | custom-call | flops 1048576 | bytes 16384 | tf_op jit(solution)/shard_map/weights/pallas_call | solution.py:311
  107.1 8.7 %weights.3 = bf16[1,1024,1152]{2,1,0:T(8,128)(2,1)} custom-call(s32[1]{0:T(128)} %bitcast.2.here, bf16[1,1024,1152]{2,1,0:T(8,128)(2,1)} %weights.2.old, bf16[2304,1024]{1,0:T(8,128)(2,1)S(1)} %bitcast.33, bf16[144,768]{1,0:T(8,128)(2,1)S(1)} %get-tuple-element.177.refs_1_, ...), custom_call_target="tpu_custom_call", output_to_operand_aliasing={{}: (1, {})} | custom-call | flops 1048576 | bytes 16384 | tf_op jit(solution)/shard_map/weights/pallas_call | solution.py:311
  (76 shorter events, 26.9 us)
Async XLA Ops:
  0.6 18.6 %collective-permute-start.3 = (bf16[2304,384]{1,0:T(8,128)(2,1)}, bf16[2304,384]{1,0:T(8,128)(2,1)S(1)}, u32[]{:S(2)}, u32[]{:S(2)}) collective-permute-start(bf16[2304,384]{1,0:T(8,128)(2,1)} %bitcast.11), channel_id=1, source_target_pairs={{0,1},{1,0},{2,3},{3,2},{4,5},{5,4},{6,7},{7,6},{8,9},{9,8},{10,11... | collective-permute-start | bytes 5308424 | tf_op jit(solution)/shard_map/ppermute | solution.py:348
  1.1 18.1 %collective-permute-start.4 = (bf16[2304,384]{1,0:T(8,128)(2,1)}, bf16[2304,384]{1,0:T(8,128)(2,1)S(1)}, u32[]{:S(2)}, u32[]{:S(2)}) collective-permute-start(bf16[2304,384]{1,0:T(8,128)(2,1)} %bitcast.18), channel_id=1, source_target_pairs={{0,1},{1,0},{2,3},{3,2},{4,5},{5,4},{6,7},{7,6},{8,9},{9,8},{10,11... | collective-permute-start | bytes 5308424 | tf_op jit(solution)/shard_map/ppermute | solution.py:348
  1.2 9.6 %collective-permute-start.2 = (bf16[384,1024]{1,0:T(8,128)(2,1)}, bf16[384,1024]{1,0:T(8,128)(2,1)}, u32[]{:S(2)}, u32[]{:S(2)}) collective-permute-start(bf16[384,1024]{1,0:T(8,128)(2,1)} %bitcast.25), channel_id=1, source_target_pairs={{0,1},{1,0},{2,3},{3,2},{4,5},{5,4},{6,7},{7,6},{8,9},{9,8},{10,11... | collective-permute-start | bytes 2359304 | tf_op jit(solution)/shard_map/ppermute | solution.py:348
  4.2 15.1 %collective-permute-start = (bf16[200,1024]{1,0:T(8,128)(2,1)}, bf16[200,1024]{1,0:T(8,128)(2,1)}, u32[]{:S(2)}, u32[]{:S(2)}) collective-permute-start(bf16[200,1024]{1,0:T(8,128)(2,1)} %fusion.7.refs_0_), channel_id=1, source_target_pairs={{0,4},{1,5},{2,6},{3,7},{4,8},{5,9},{6,10},{7,11},{8,12},{9,13},{1... | collective-permute-start | bytes 1228808 | tf_op jit(solution)/shard_map/ppermute | solution.py:348
  6.8 12.4 %collective-permute-start.1 = (bf16[200,1024]{1,0:T(8,128)(2,1)}, bf16[200,1024]{1,0:T(8,128)(2,1)}, u32[]{:S(2)}, u32[]{:S(2)}) collective-permute-start(bf16[200,1024]{1,0:T(8,128)(2,1)} %fusion.7.refs_0_), channel_id=1, source_target_pairs={{0,2},{1,3},{2,0},{3,1},{4,6},{5,7},{6,4},{7,5},{8,10},{9,11},{10,... | collective-permute-start | bytes 1228808 | tf_op jit(solution)/shard_map/ppermute | solution.py:348
  19.2 16.1 %collective-permute-start.10 = (bf16[1024,768]{1,0:T(8,128)(2,1)S(1)}, bf16[1024,768]{1,0:T(8,128)(2,1)S(1)}, u32[]{:S(2)}, u32[]{:S(2)}) collective-permute-start(bf16[1024,768]{1,0:T(8,128)(2,1)S(1)} %join.1.refs_4_), channel_id=1, source_target_pairs={{0,1},{1,0},{2,3},{3,2},{4,5},{5,4},{6,7},{7,6},{8,9},{9,8},{10,11... | collective-permute-start | bytes 4718600 | tf_op jit(solution)/shard_map/ppermute | solution.py:348
  19.3 18.4 %collective-permute-start.5 = (bf16[200,1024]{1,0:T(8,128)(2,1)}, bf16[200,1024]{1,0:T(8,128)(2,1)S(1)}, u32[]{:S(2)}, u32[]{:S(2)}) collective-permute-start(bf16[200,1024]{1,0:T(8,128)(2,1)} %collective-permute-done.refs_1_), channel_id=1, source_target_pairs={{0,4},{1,5},{2,6},{3,7},{4,8},{5,9},{6,10},{7,11},{8,12},{9,13},{1... | collective-permute-start | bytes 1228808 | tf_op jit(solution)/shard_map/ppermute | solution.py:348
  20.3 17.4 %collective-permute-start.6 = (bf16[200,1024]{1,0:T(8,128)(2,1)}, bf16[200,1024]{1,0:T(8,128)(2,1)S(1)}, u32[]{:S(2)}, u32[]{:S(2)}) collective-permute-start(bf16[200,1024]{1,0:T(8,128)(2,1)} %collective-permute-done.refs_1_), channel_id=1, source_target_pairs={{0,2},{1,3},{2,0},{3,1},{4,6},{5,7},{6,4},{7,5},{8,10},{9,11},{10,... | collective-permute-start | bytes 1228808 | tf_op jit(solution)/shard_map/ppermute | solution.py:348
  25.9 11.7 %collective-permute-start.7 = (bf16[288,384]{1,0:T(8,128)(2,1)S(1)}, bf16[288,384]{1,0:T(8,128)(2,1)S(1)}, u32[]{:S(2)}, u32[]{:S(2)}) collective-permute-start(bf16[288,384]{1,0:T(8,128)(2,1)S(1)} %get-tuple-element.96), channel_id=1, source_target_pairs={{0,16},{16,0},{1,17},{17,1},{2,18},{18,2},{3,19},{19,3},{4,20},{20... | collective-permute-start | bytes 663560 | tf_op jit(solution)/shard_map/ppermute | solution.py:376
  37.7 14.2 %collective-permute-start.13 = (bf16[144,1792]{1,0:T(8,128)(2,1)S(1)}, bf16[144,1792]{1,0:T(8,128)(2,1)S(1)}, u32[]{:S(2)}, u32[]{:S(2)}) collective-permute-start(bf16[144,1792]{1,0:T(8,128)(2,1)S(1)} %get-tuple-element.110), channel_id=1, source_target_pairs={{0,1},{1,0},{2,3},{3,2},{4,5},{5,4},{6,7},{7,6},{8,9},{9,8},{10,11... | collective-permute-start | bytes 1548296 | tf_op jit(solution)/shard_map/ppermute | solution.py:348
  37.7 14.1 %collective-permute-start.11 = (bf16[200,1024]{1,0:T(8,128)(2,1)S(1)}, bf16[200,1024]{1,0:T(8,128)(2,1)S(1)}, u32[]{:S(2)}, u32[]{:S(2)}) collective-permute-start(bf16[200,1024]{1,0:T(8,128)(2,1)S(1)} %collective-permute-done.5.refs_1_), channel_id=1, source_target_pairs={{0,4},{1,5},{2,6},{3,7},{4,8},{5,9},{6,10},{7,11},{8,12},{9,13},{1... | collective-permute-start | bytes 1228808 | tf_op jit(solution)/shard_map/ppermute | solution.py:348
  39.6 12.3 %collective-permute-start.12 = (bf16[200,1024]{1,0:T(8,128)(2,1)S(1)}, bf16[200,1024]{1,0:T(8,128)(2,1)S(1)}, u32[]{:S(2)}, u32[]{:S(2)}) collective-permute-start(bf16[200,1024]{1,0:T(8,128)(2,1)S(1)} %collective-permute-done.5.refs_1_), channel_id=1, source_target_pairs={{0,2},{1,3},{2,0},{3,1},{4,6},{5,7},{6,4},{7,5},{8,10},{9,11},{10,... | collective-permute-start | bytes 1228808 | tf_op jit(solution)/shard_map/ppermute | solution.py:348
  51.9 13.9 %collective-permute-start.17 = (bf16[288,1792]{1,0:T(8,128)(2,1)S(1)}, bf16[288,1792]{1,0:T(8,128)(2,1)S(1)}, u32[]{:S(2)}, u32[]{:S(2)}) collective-permute-start(bf16[288,1792]{1,0:T(8,128)(2,1)S(1)} %get-tuple-element.123), channel_id=1, source_target_pairs={{0,1},{1,0},{2,3},{3,2},{4,5},{5,4},{6,7},{7,6},{8,9},{9,8},{10,11... | collective-permute-start | bytes 3096584 | tf_op jit(solution)/shard_map/ppermute | solution.py:348
  52.0 13.8 %collective-permute-start.16 = (bf16[200,1024]{1,0:T(8,128)(2,1)S(1)}, bf16[200,1024]{1,0:T(8,128)(2,1)S(1)}, u32[]{:S(2)}, u32[]{:S(2)}) collective-permute-start(bf16[200,1024]{1,0:T(8,128)(2,1)S(1)} %collective-permute-done.11.refs_1_), channel_id=1, source_target_pairs={{0,2},{1,3},{2,0},{3,1},{4,6},{5,7},{6,4},{7,5},{8,10},{9,11},{10,... | collective-permute-start | bytes 1228808 | tf_op jit(solution)/shard_map/ppermute | solution.py:348
  65.8 12.8 %collective-permute-start.21 = (bf16[288,1792]{1,0:T(8,128)(2,1)S(1)}, bf16[288,1792]{1,0:T(8,128)(2,1)S(1)}, u32[]{:S(2)}, u32[]{:S(2)}) collective-permute-start(bf16[288,1792]{1,0:T(8,128)(2,1)S(1)} %get-tuple-element.138), channel_id=1, source_target_pairs={{0,1},{1,0},{2,3},{3,2},{4,5},{5,4},{6,7},{7,6},{8,9},{9,8},{10,11... | collective-permute-start | bytes 3096584 | tf_op jit(solution)/shard_map/ppermute | solution.py:348
  65.8 12.8 %collective-permute-start.20 = (bf16[192,1024]{1,0:T(8,128)(2,1)S(1)}, bf16[192,1024]{1,0:T(8,128)(2,1)S(1)}, u32[]{:S(2)}, u32[]{:S(2)}) collective-permute-start(bf16[192,1024]{1,0:T(8,128)(2,1)S(1)} %get-tuple-element.137), channel_id=1, source_target_pairs={{0,2},{1,3},{2,0},{3,1},{4,6},{5,7},{6,4},{7,5},{8,10},{9,11},{10,... | collective-permute-start | bytes 1179656 | tf_op jit(solution)/shard_map/ppermute | solution.py:348
  78.6 13.5 %collective-permute-start.27 = (bf16[288,1792]{1,0:T(8,128)(2,1)S(1)}, bf16[288,1792]{1,0:T(8,128)(2,1)S(1)}, u32[]{:S(2)}, u32[]{:S(2)}) collective-permute-start(bf16[288,1792]{1,0:T(8,128)(2,1)S(1)} %get-tuple-element.156), channel_id=1, source_target_pairs={{0,1},{1,0},{2,3},{3,2},{4,5},{5,4},{6,7},{7,6},{8,9},{9,8},{10,11... | collective-permute-start | bytes 3096584 | tf_op jit(solution)/shard_map/ppermute | solution.py:348
  78.7 13.4 %collective-permute-start.28 = (bf16[192,1024]{1,0:T(8,128)(2,1)S(1)}, bf16[192,1024]{1,0:T(8,128)(2,1)S(1)}, u32[]{:S(2)}, u32[]{:S(2)}) collective-permute-start(bf16[192,1024]{1,0:T(8,128)(2,1)S(1)} %add.8), channel_id=1, source_target_pairs={{0,4},{1,5},{2,6},{3,7},{4,8},{5,9},{6,10},{7,11},{8,12},{9,13},{1... | collective-permute-start | bytes 1179656 | tf_op jit(solution)/shard_map/ppermute | solution.py:348
  79.1 13.0 %collective-permute-start.26 = (bf16[192,1024]{1,0:T(8,128)(2,1)S(1)}, bf16[192,1024]{1,0:T(8,128)(2,1)S(1)}, u32[]{:S(2)}, u32[]{:S(2)}) collective-permute-start(bf16[192,1024]{1,0:T(8,128)(2,1)S(1)} %get-tuple-element.155), channel_id=1, source_target_pairs={{0,2},{1,3},{2,0},{3,1},{4,6},{5,7},{6,4},{7,5},{8,10},{9,11},{10,... | collective-permute-start | bytes 1179656 | tf_op jit(solution)/shard_map/ppermute | solution.py:348
  82.9 10.7 %collective-permute-start.30 = (bf16[144,1792]{1,0:T(8,128)(2,1)S(1)}, bf16[144,1792]{1,0:T(8,128)(2,1)S(1)}, u32[]{:S(2)}, u32[]{:S(2)}) collective-permute-start(bf16[144,1792]{1,0:T(8,128)(2,1)S(1)} %get-tuple-element.170), channel_id=1, source_target_pairs={{0,1},{1,0},{2,3},{3,2},{4,5},{5,4},{6,7},{7,6},{8,9},{9,8},{10,11... | collective-permute-start | bytes 1548296 | tf_op jit(solution)/shard_map/ppermute | solution.py:348
  83.0 21.4 %collective-permute-start.25 = (bf16[192,1024]{1,0:T(8,128)(2,1)S(1)}, bf16[192,1024]{1,0:T(8,128)(2,1)S(1)}, u32[]{:S(2)}, u32[]{:S(2)}) collective-permute-start(bf16[192,1024]{1,0:T(8,128)(2,1)S(1)} %get-tuple-element.153), channel_id=1, source_target_pairs={{0,2},{1,3},{2,0},{3,1},{4,6},{5,7},{6,4},{7,5},{8,10},{9,11},{10,... | collective-permute-start | bytes 1179656 | tf_op jit(solution)/shard_map/ppermute | solution.py:348
  92.3 12.8 %collective-permute-start.29 = (bf16[192,1024]{1,0:T(8,128)(2,1)S(1)}, bf16[192,1024]{1,0:T(8,128)(2,1)S(1)}, u32[]{:S(2)}, u32[]{:S(2)}) collective-permute-start(bf16[192,1024]{1,0:T(8,128)(2,1)S(1)} %add.9), channel_id=1, source_target_pairs={{0,4},{1,5},{2,6},{3,7},{4,8},{5,9},{6,10},{7,11},{8,12},{9,13},{1... | collective-permute-start | bytes 1179656 | tf_op jit(solution)/shard_map/ppermute | solution.py:348
  105.2 11.7 %collective-permute-start.32 = (bf16[192,1024]{1,0:T(8,128)(2,1)S(1)}, bf16[192,1024]{1,0:T(8,128)(2,1)S(1)}, u32[]{:S(2)}, u32[]{:S(2)}) collective-permute-start(bf16[192,1024]{1,0:T(8,128)(2,1)S(1)} %add.10), channel_id=1, source_target_pairs={{0,4},{1,5},{2,6},{3,7},{4,8},{5,9},{6,10},{7,11},{8,12},{9,13},{1... | collective-permute-start | bytes 1179656 | tf_op jit(solution)/shard_map/ppermute | solution.py:348
  105.6 11.3 %collective-permute-start.31 = (bf16[192,1024]{1,0:T(8,128)(2,1)S(1)}, bf16[192,1024]{1,0:T(8,128)(2,1)S(1)}, u32[]{:S(2)}, u32[]{:S(2)}) collective-permute-start(bf16[192,1024]{1,0:T(8,128)(2,1)S(1)} %get-tuple-element.172), channel_id=1, source_target_pairs={{0,2},{1,3},{2,0},{3,1},{4,6},{5,7},{6,4},{7,5},{8,10},{9,11},{10,... | collective-permute-start | bytes 1179656 | tf_op jit(solution)/shard_map/ppermute | solution.py:348
  (16 other events, 154.8 us)

commit v5 on v4

--- a/solution.py
+++ b/solution.py
@@ -122,14 +122,19 @@
     for a, (rec, wd) in enumerate(((rec0, wd0), (rec1, wd1))):
         gh = contract_cols(rec[...], wd[...])
         share[a * n * cap : (a + 1) * n * cap, :] = gh
-        share_out[a][...] = gh.astype(bf16)
+        if n == 1:
+            share_out[0][a * cap : (a + 1) * cap, :] = gh.astype(bf16)
+        else:
+            share_out[a][...] = gh.astype(bf16)
 
 
 def dispatch(here, toks, wd0, wd1, cap):
     n = len(toks)
     tok, d = toks[0].shape
     h = wd0.shape[0]
-    outs = [((n * cap, d), bf16), ((n * cap, d), bf16), ((2 * n * cap, h), f32), ((n * cap, h), bf16), ((n * cap, h), bf16), ((8, tok - 8), f32)]
+    outs = [((n * cap, d), bf16), ((n * cap, d), bf16), ((2 * n * cap, h), f32)]
+    outs += [((2 * cap, h), bf16)] if n == 1 else [((n * cap, h), bf16)] * 2
+    outs += [((8, tok - 8), f32)]
     return pl.pallas_call(
         functools.partial(dispatch_kernel, n, cap),
         out_shape=[jax.ShapeDtypeStruct(s, t) for s, t in outs],
@@ -141,10 +146,15 @@
     )(here, *toks, wd0, wd1)
 
 
-def combine_kernel(chunk, cap, here, share, peer0, peer1, pos, *refs):
+def combine_kernel(chunk, cap, here, share, *refs):
     n = len(chunk)
+    if n == 1:
+        peer0, peer1 = refs[0].at[:cap, :], refs[0].at[cap:, :]
+        pos, *refs = refs[1:]
+    else:
+        peer0, peer1, pos, *refs = refs
     saved, (w0, w1, rec1), (gp0, both) = refs[:4], refs[4:7], refs[7:9]
-    backs, (held, sems) = refs[9 : 9 + n], refs[9 + n :]
+    backs, (held, sems) = refs[9:-2], refs[-2:]
     d = rec1.shape[1]
     gp1 = both.at[:, d:]
     both[:, :d] = rec1[...]
@@ -175,20 +185,25 @@
             pick = jnp.where(slot == pos[i : i + 1, :], 1.0, 0.0).astype(bf16)
             part = contract_rows(pick, slots[rel * cap : (rel + 1) * cap])
             sums[rel] = part if sums[rel] is None else sums[rel] + part
-    for rel in range(n):
-        backs[rel][...] = sums[rel].astype(bf16)
-
-
-def combine(here, chunk, share, peers, pos, saved0, saved1, w0, w1, rec1, cap):
+    if len(backs) > n:
+        half = backs[0].shape[1]
+        for k, back in enumerate(backs):
+            back[...] = sums[0][:, k * half : (k + 1) * half].astype(bf16)
+    else:
+        for rel in range(n):
+            backs[rel][...] = sums[rel].astype(bf16)
+
+
+def combine(here, chunk, share, peers, pos, saved0, saved1, w0, w1, rec1, cap, halves=False):
     n = len(chunk)
     h = share.shape[1]
     d = w0.shape[0]
     tok = pos.shape[1]
-    outs = [(n * cap, 2 * h), (n * cap, d + 2 * h)] + [(tok, d)] * n
+    outs = [(n * cap, 2 * h), (n * cap, d + 2 * h)] + ([(tok, d // 2)] * 2 if halves else [(tok, d)] * n)
     return pl.pallas_call(
         functools.partial(combine_kernel, chunk, cap),
         out_shape=[jax.ShapeDtypeStruct(s, bf16) for s in outs],
-        in_specs=[on_scalar] + [on_chip] * 4 + [anywhere] * 4 + [on_chip] * 3,
+        in_specs=[on_scalar] + [on_chip] * (2 + len(peers)) + [anywhere] * 4 + [on_chip] * 3,
         out_specs=[on_chip] * len(outs),
         scratch_shapes=[pltpu.VMEM((4 * n, cap, h), bf16), pltpu.SemaphoreType.DMA((4 * n,))],
         cost_estimate=light,
@@ -215,17 +230,20 @@
     )(left, right)
 
 
-def add_kernel(*refs):
-    total = refs[0][...].astype(f32)
-    for r in refs[1:-1]:
-        total = total + r[...].astype(f32)
-    refs[-1][...] = total.astype(refs[-1].dtype)
-
-
-def add(*values):
-    return pl.pallas_call(
-        add_kernel,
-        out_shape=jax.ShapeDtypeStruct(values[0].shape, values[0].dtype),
+def add_kernel(part, *refs):
+    wide = refs[-1].shape[1]
+    total = None
+    for r in refs[:-1]:
+        v = r[...] if part is None or r.shape[1] == wide else r[:, part * wide : (part + 1) * wide]
+        total = v.astype(f32) if total is None else total + v.astype(f32)
+    refs[-1][...] = total.astype(bf16)
+
+
+def add(values, part=None):
+    rows, wide = values[0].shape
+    return pl.pallas_call(
+        functools.partial(add_kernel, part),
+        out_shape=jax.ShapeDtypeStruct((rows, wide if part is None else wide // 2), bf16),
         in_specs=[on_chip] * len(values),
         out_specs=on_chip,
         cost_estimate=light,
@@ -234,8 +252,71 @@
     )(*values)
 
 
-def weights_kernel(order, cap, sorted_left, starts, here, *refs):
-    count = 1 if sorted_left else 2
+def finish_kernel(a, b, left, right, out):
+    half = left.shape[1]
+    for at, v in ((0, left), (half, right)):
+        total = a[:, at : at + half].astype(f32) + b[:, at : at + half].astype(f32) + v[...].astype(f32)
+        out[:, at : at + half] = total.astype(bf16)
+
+
+def finish(a, b, left, right):
+    return pl.pallas_call(
+        finish_kernel,
+        out_shape=jax.ShapeDtypeStruct(a.shape, bf16),
+        in_specs=[on_chip] * 4,
+        out_specs=on_chip,
+        cost_estimate=light,
+        compiler_params=params(8),
+        name="finish",
+    )(a, b, left, right)
+
+
+def hidden_kernel(gate, up, out):
+    gate_pre = gate[...].astype(f32)
+    out[...] = (gate_pre * jax.nn.sigmoid(gate_pre) * up[...].astype(f32)).astype(bf16)
+
+
+def hidden(gate, up):
+    rows, h = gate.shape
+    tile = rows // 4
+    spec = pl.BlockSpec((tile, h), lambda i: (i, 0))
+    return pl.pallas_call(
+        hidden_kernel,
+        out_shape=jax.ShapeDtypeStruct((rows, h), bf16),
+        grid=(rows // tile,),
+        in_specs=[spec, spec],
+        out_specs=spec,
+        cost_estimate=light,
+        compiler_params=params(8),
+        name="hidden",
+    )(gate, up)
+
+
+def pack_kernel(line, tokens, routes, codes, out):
+    tok = tokens.shape[0]
+    out[:tok, :] = tokens[...]
+    same = lax.broadcasted_iota(jnp.int32, (tok, tok), 0) == lax.broadcasted_iota(jnp.int32, (tok, tok), 1)
+    same = jnp.where(same, 1.0, 0.0).astype(bf16)
+    out[tok:, :] = jnp.zeros((8, out.shape[1]), bf16)
+    for at, v in ((0, routes), (line, codes)):
+        out[tok:, at : at + tok] = contract_rows(v[...].astype(f32).astype(bf16), same).astype(bf16)
+
+
+def pack(tokens, routes, codes, line):
+    tok, d = tokens.shape
+    return pl.pallas_call(
+        functools.partial(pack_kernel, line),
+        out_shape=jax.ShapeDtypeStruct((tok + 8, d), bf16),
+        in_specs=[on_chip] * 3,
+        out_specs=on_chip,
+        cost_estimate=light,
+        compiler_params=params(8),
+        name="pack",
+    )(tokens, routes, codes)
+
+
+def weights_kernel(order, cap, sorted_left, starts, base_tile, here, *refs):
+    count = 1
     by_source, pieces, out = refs[:count], refs[count:-5], refs[-5]
     ls, rs, left_sems, right_sems = refs[-4:]
     i = pl.program_id(0)
@@ -265,13 +346,13 @@
     def left(step):
         slot = lax.rem(step, 2)
         if sorted_left:
-            return copies_of_sorted(by_source[0], step, ls.at[slot], left_sems.at[slot])
-        return copies_of_pieces(step, ls.at[slot], left_sems.at[slot])
+            return copies_of_sorted(by_source[0], base_tile + step, ls.at[slot], left_sems.at[slot])
+        return copies_of_pieces(base_tile + step, ls.at[slot], left_sems.at[slot])
 
     def right():
         if sorted_left:
             return copies_of_pieces(None, rs.at[0], right_sems.at[0])
-        return [c for k in range(2) for c in copies_of_sorted(by_source[k], None, rs.at[k], right_sems.at[k])]
+        return copies_of_sorted(by_source[0], None, rs.at[0], right_sems.at[0])
 
     @pl.when(i == 0)
     def _():
@@ -287,9 +368,6 @@
     def _():
         for c in right():
             c.wait()
-        if not sorted_left:
-            gate_pre = rs[0].astype(f32)
-            rs[0] = (gate_pre * jax.nn.sigmoid(gate_pre) * rs[1].astype(f32)).astype(bf16)
 
     for c in left(i):
         c.wait()
@@ -297,7 +375,7 @@
     out[0] = (contract_rows(ls[lax.rem(i, 2)], rs[0]) * loss_scale).astype(bf16)
 
 
-def weight_sums(here, order, by_source, pieces, starts, sorted_left, into, cap):
+def weight_sums(here, order, by_source, pieces, starts, sorted_left, tiles, into, cap):
     slots, wide = by_source[0].shape
     d = pieces[0].shape[1]
     if sorted_left:
@@ -306,16 +384,16 @@
     at = 0 if sorted_left else 2
     whole_out = jax.ShapeDtypeStruct((1, d, 3 * (wide // 2 if sorted_left else wide)), bf16)
     given = [*by_source, *pieces]
-    kernel = functools.partial(weights_kernel, order, cap, sorted_left, starts)
+    kernel = functools.partial(weights_kernel, order, cap, sorted_left, starts, tiles[0])
     body = kernel if into is None else (lambda here, old, *refs: kernel(here, *refs))
     return pl.pallas_call(
         body,
         out_shape=whole_out,
         grid_spec=pltpu.PrefetchScalarGridSpec(
             num_scalar_prefetch=1,
-            grid=(d // tile,),
+            grid=(tiles[1],),
             in_specs=[anywhere] * (len(given) + (into is not None)),
-            out_specs=pl.BlockSpec((1, tile, wide), lambda i, here: (0, i, at)),
+            out_specs=pl.BlockSpec((1, tile, wide), lambda i, here: (0, tiles[0] + i, at)),
             scratch_shapes=[
                 pltpu.VMEM((2, slots, tile), bf16),
                 pltpu.VMEM((len(by_source), slots, wide), bf16),
@@ -348,14 +426,7 @@
         return lax.ppermute(v, "expert", perm)
 
     line = 256 * pl.cdiv(tok, 256)
-    named = jnp.concatenate(
-        [
-            jnp.pad(routes.T.astype(bf16), ((0, 8 - choices), (0, line - tok)), constant_values=-1),
-            jnp.pad(gate_codes.T.astype(bf16), ((0, 8 - choices), (0, d - line - tok))),
-        ],
-        axis=1,
-    )
-    block = jnp.concatenate([out_grad, named], axis=0)
+    block = pack(out_grad, routes, gate_codes, line)
     here = me.reshape(1).astype(jnp.int32)
 
     def ring(v, hops=1):
@@ -367,66 +438,80 @@
     order, recs, gps = [], [], []
 
     def first(chunk, toks):
-        rec, rec_c, share, share0, share1, pos = dispatch(here, toks, wd, wd_c, cap)
+        rec, rec_c, share, *shares, pos = dispatch(here, toks, wd, wd_c, cap)
         order.extend((k, col, 0) for col, k in chunk)
         recs.append(rec)
-        return (chunk, share, pos, rec_c), share0, share1
+        return (chunk, share, pos, rec_c), *shares
 
     def exchange(v):
         return lax.ppermute(v, "dp", [(0, 1), (1, 0)])
 
-    def second(state, *peers):
+    def second(state, *peers, halves=False):
         chunk, share, pos, rec_c = state
-        gp, both, *sums = combine(here, chunk, share, peers, pos, (sg, su), (sg_c, su_c), w, w_c, rec_c, cap)
+        gp, both, *sums = combine(here, chunk, share, peers, pos, (sg, su), (sg_c, su_c), w, w_c, rec_c, cap, halves)
         gps.append(gp)
         return both, *sums
 
     r1, x0 = ring(block), send(block, to_x)
-    c0, h0, g0 = first([(0, 0)], [block])
+    c0, h0 = first([(0, 0)], [block])
     w = join(w_gate[0], w_up[0])
-    r1, x0, h0, g0, w, sg_c, su_c = together(r1, x0, h0, g0, w, sg_c, su_c)
+    hid = hidden(sg, su)
+    r1, x0, h0, w, hid, sg_c, su_c = together(r1, x0, h0, w, hid, sg_c, su_c)
     r2, x1 = ring(r1), send(r1, to_x)
-    h0, g0, w_c = exchange(h0), exchange(g0), send(w, to_core)
+    h0, w_c = exchange(h0), send(w, to_core)
     c1, h1, g1 = first([(1, 0), (0, 1)], [x0, r1])
     h1 = exchange(h1)
-    both0, t_r0 = second(c0, h0, g0)
+    both0, t_r0 = second(c0, h0)
     r2, x1, h1, g1, t_r0, both0 = together(r2, x1, h1, g1, t_r0, both0)
     r3, x2 = ring(r2), send(r2, to_x)
-    g1, p0 = exchange(g1), send(both0, to_core)
+    g1 = exchange(g1)
     c2, h2, g2 = first([(1, 1), (0, 2)], [x1, r2])
-    h2 = exchange(h2)
+    h2, p0 = exchange(h2), send(both0, to_core)
     both1, t_x0, t_r1 = second(c1, h1, g1)
     r3, x2, p0, h2, g2, t_x0, t_r1, both1 = together(r3, x2, p0, h2, g2, t_x0, t_r1, both1)
-    x3 = send(r3, to_x)
-    g2, p1 = exchange(g2), send(both1, to_core)
+    x3, w1 = send(r3, to_x), ring(t_r1)
+    g2 = exchange(g2)
     c3, h3, g3 = first([(1, 2), (0, 3)], [x2, r3])
-    h3 = exchange(h3)
+    h3, p1 = exchange(h3), send(both1, to_core)
     both2, t_x1, t_r2 = second(c2, h2, g2)
-    x3, p1, h3, g3, t_x1, t_r2, both2 = together(x3, p1, h3, g3, t_x1, t_r2, both2)
-    b1 = send(t_x1, to_x)
-    g3, p2 = exchange(g3), send(both2, to_core)
-    c4, h4, g4 = first([(1, 3)], [x3])
-    h4, g4 = exchange(h4), exchange(g4)
+    x3, w1, p1, h3, g3, t_x1, t_r2, both2 = together(x3, w1, p1, h3, g3, t_x1, t_r2, both2)
+    u1, b0 = ring(t_x1), send(t_x0, to_x)
+    g3 = exchange(g3)
+    c4, h4 = first([(1, 3)], [x3])
+    h4, p2 = exchange(h4), send(both2, to_core)
     both3, t_x2, t_r3 = second(c3, h3, g3)
-    b1, p2, h4, g4, t_x2, t_r3, both3 = together(b1, p2, h4, g4, t_x2, t_r3, both3)
-    b2 = send(t_x2, to_x)
+    u1, b0, p2, h4, t_x2, t_r3, both3 = together(u1, b0, p2, h4, t_x2, t_r3, both3)
+    a0, a1, h4 = together(add([t_x2, u1], 0), add([t_x2, u1], 1), h4)
+    b2 = [send(a0, to_x), send(a1, to_x)]
     p3 = send(both3, to_core)
-    w1 = ring(add(t_r1, b1))
-    both4, t_x3 = second(c4, h4, g4)
-    b3, p4 = send(t_x3, to_x), send(both4, to_core)
-    b2, p3, w1, _ = together(b2, p3, w1, t_x3)
-    w2 = ring(add(t_r2, b2, w1))
+    both4, *t_x3 = second(c4, h4, halves=True)
+    b3 = [send(t, to_x) for t in t_x3]
+    b2[0], p3, both4, _ = together(b2[0], p3, both4, t_x3[0])
+    p4 = send(both4, to_core)
     away = [p0, p1, p2, p3, p4]
     order_all = order + [(k, col, 1) for k, col, _ in order]
-    zeros = [0] * len(recs)
-    part = weight_sums(here, order_all, [sg, su], recs + away, zeros + zeros, False, None, cap)
-    b3, w2, part, t_x0 = together(b3, w2, part, t_x0)
-    w3 = ring(add(t_r3, b3, w2))
-    b0 = send(t_x0, to_x)
-    skip = [d] * len(recs)
-    weight_grads = weight_sums(here, order_all, [saved_inputs[0]], gps + away, zeros + skip, True, part, cap)
-    total = add(t_r0, b0, w3)
-    return (total, weight_grads)
+    zeros, skip = [0] * len(recs), [d] * len(recs)
+
+    def received_part(tiles, into):
+        return weight_sums(here, order_all, [hid], recs + away, zeros + zeros, False, tiles, into, cap)
+
+    def inputs_part(tiles, into):
+        return weight_sums(here, order_all, [saved_inputs[0]], gps + away, zeros + skip, True, tiles, into, cap)
+
+    tiles = d // 256
+    low, high = (0, tiles // 2), (tiles // 2, tiles - tiles // 2)
+    w2 = [ring(add([t_r2, w1, b2[0]], 0))]
+    part = received_part(low, None)
+    b2[1], part = together(b2[1], part)
+    w2.append(ring(add([t_r2, w1, b2[1]], 1)))
+    part = received_part(high, part)
+    b3[0], w2[0], part = together(b3[0], w2[0], part)
+    w3 = [ring(add([t_r3, b3[0], w2[0]], 0))]
+    part = inputs_part(low, part)
+    b3[1], w2[1], part = together(b3[1], w2[1], part)
+    w3.append(ring(add([t_r3, b3[1], w2[1]], 1)))
+    weight_grads = inputs_part(high, part)
+    return (finish(t_r0, b0, *w3), weight_grads)
 
 
 def solution(mesh):

time: 118 us -> 122 us (1.034)
  local copies, waits for them, and re-layouts: 2.36 us -> 9.76 us
  Pallas kernels: 47.3 us -> 52 us
  waiting for transfers between devices: 36.2 us -> 31.5 us
  other arithmetic: 2.49 us -> 0.01 us
  starting transfers between devices: 28.5 us -> 27.2 us
    unnamed x14 -> x26, local copies, waits for them, and re-layouts: 2.36 us -> 9.76 us
    ppermute x23 -> x27, waiting for transfers between devices: 16.3 us -> 13 us  [send(): return lax.ppermute(v, 'expert', perm)]
    pallas_call x2 -> x4, Pallas kernels: 19.6 us -> 22.5 us  [weight_sums(): pl.pallas_call(body, out_shape=whole_out, grid_spec=pltpu.PrefetchScalarG...]
    ppermute x10 -> x8, starting transfers between devices: 10.4 us -> 8.37 us  [exchange(): return lax.ppermute(v, 'dp', [(0, 1), (1, 0)])]
    pallas_call x4 -> x9, Pallas kernels: 1.27 us -> 3.08 us  [the longest x1 0.93 us: pack(): pl.pallas_call(functools.partial(pack_kernel, line), out_shape=jax.ShapeD...]
    concatenate x1 -> x0, other arithmetic: 1.77 us -> none  [body_grid(): block = jnp.concatenate([out_grad, named], axis=0)]
    ppermute x10 -> x8, waiting for transfers between devices: 19.8 us -> 18.5 us  [exchange(): return lax.ppermute(v, 'dp', [(0, 1), (1, 0)])]
    ppermute x23 -> x27, starting transfers between devices: 18.2 us -> 18.9 us  [send(): return lax.ppermute(v, 'expert', perm)]
  transfers between devices with their start and end apart: 33 -> 35, of which waited for: 11 -> 15; matrix products, arithmetic and copies ran while one was open for 2% -> 2% of each run, Pallas kernels for 39% -> 42%
where the time goes in v5:
time: 122 us; the launch traced here: 121 us
  Pallas kernels  52 us (43%)
  waiting for transfers between devices  31.5 us (26%)
  starting transfers between devices  27.2 us (22%)
  local copies, waits for them, and re-layouts  9.76 us (8%)
    pallas_call x4, Pallas kernels, weight_sums(): pl.pallas_call(body, out_shape=whole_out, grid_spec=pltpu.PrefetchScalarG...  22.5 us
    ppermute x27, starting transfers between devices, send(): return lax.ppermute(v, 'expert', perm)  18.9 us
    ppermute x8, waiting for transfers between devices, exchange(): return lax.ppermute(v, 'dp', [(0, 1), (1, 0)])  18.5 us
    pallas_call x5, Pallas kernels, combine(): pl.pallas_call(functools.partial(combine_kernel, chunk, cap), out_shape=[...  14.8 us
    ppermute x27, waiting for transfers between devices, send(): return lax.ppermute(v, 'expert', perm)  13 us
    pallas_call x5, Pallas kernels, dispatch(): pl.pallas_call(functools.partial(dispatch_kernel, n, cap), out_shape=[jax...  11.6 us
    unnamed x26, local copies, waits for them, and re-layouts  9.76 us
    ppermute x8, starting transfers between devices, exchange(): return lax.ppermute(v, 'dp', [(0, 1), (1, 0)])  8.37 us
  transfers between devices with their start and end apart: 35, of which 15 were waited for; matrix products, arithmetic and copies ran while one was open for 2% of the time, Pallas kernels for 42%

profile of v5, /device:TPU:0, one launch (start us, length us, event | category | flops | bytes accessed | tf_op | source)
XLA Modules:
  0.0 121.5 jit_solution(4284134797082634004)
XLA Ops:
  8.3 2.6 %collective-permute-start.1 = (bf16[200,1024]{1,0:T(8,128)(2,1)}, bf16[200,1024]{1,0:T(8,128)(2,1)}, u32[]{:S(2)}, u32[]{:S(2)}) collective-permute-start(bf16[200,1024]{1,0:T(8,128)(2,1)} %pack.1.refs_0_), channel_id=1, source_target_pairs={{0,2},{1,3},{2,0},{3,1},{4,6},{5,7},{6,4},{7,5},{8,10},{9,11},{10,... | collective-permute-start | bytes 1228808 | tf_op jit(solution)/shard_map/ppermute | solution.py:426
  10.8 1.6 %collective-permute-start = (bf16[200,1024]{1,0:T(8,128)(2,1)}, bf16[200,1024]{1,0:T(8,128)(2,1)}, u32[]{:S(2)}, u32[]{:S(2)}) collective-permute-start(bf16[200,1024]{1,0:T(8,128)(2,1)} %pack.1.refs_0_), channel_id=1, source_target_pairs={{0,4},{1,5},{2,6},{3,7},{4,8},{5,9},{6,10},{7,11},{8,12},{9,13},{1... | collective-permute-start | bytes 1228808 | tf_op jit(solution)/shard_map/ppermute | solution.py:426
  17.5 2.3 %dispatch.5 = (bf16[144,1024]{1,0:T(8,128)(2,1)S(1)}, bf16[144,1024]{1,0:T(8,128)(2,1)S(1)}, f32[288,384]{1,0:T(8,128)S(1)}, bf16[288,384]{1,0:T(8,128)(2,1)S(1)}, f32[8,192]{1,0:T(8,128)S(1)}) custom-call(s32[1]{0:T(128)} %bitcast.here, bf16[200,1024]{1,0:T(8,128)(2,1)} %pack.1.refs_0_, bf16[384,1024]{1,0:T(8,128)(2,1)S(1)} %bitcast.22, ...), custom_call_target="tpu_custom_call" | custom-call | flops 1048576 | bytes 16384 | tf_op jit(solution)/shard_map/dispatch/pallas_call | solution.py:138
  21.2 3.4 %collective-permute-done.refs_1_ = bf16[200,1024]{1,0:T(8,128)(2,1)} collective-permute-done((bf16[200,1024]{1,0:T(8,128)(2,1)}, bf16[200,1024]{1,0:T(8,128)(2,1)}, u32[]{:S(2)}, u32[]{:S(2)}) %collective-permute-start) | collective-permute-done | bytes 409632 | tf_op jit(solution)/shard_map/ppermute | solution.py:426
  26.7 2.6 %dispatch.6 = (bf16[288,1024]{1,0:T(8,128)(2,1)S(1)}, bf16[288,1024]{1,0:T(8,128)(2,1)S(1)}, f32[576,384]{1,0:T(8,128)S(1)}, bf16[288,384]{1,0:T(8,128)(2,1)S(1)...) custom-call(s32[1]{0:T(128)} %bitcast.here, bf16[200,1024]{1,0:T(8,128)(2,1)} %collective-permute-done.1.refs_0_, ...), custom_call_target="tpu_custom_call" | custom-call | flops 1048576 | bytes 16384 | tf_op jit(solution)/shard_map/dispatch/pallas_call | solution.py:138
  29.9 3.6 %collective-permute-done.8.refs_0_ = bf16[288,384]{1,0:T(8,128)(2,1)S(1)} collective-permute-done((bf16[288,384]{1,0:T(8,128)(2,1)S(1)}, bf16[288,384]{1,0:T(8,128)(2,1)S(1)}, u32[]{:S(2)}, u32[]{:S(2)}) %collective-permute-start.8) | collective-permute-done | bytes 221216 | tf_op jit(solution)/shard_map/ppermute | solution.py:447
  33.5 2.3 %combine.5 = (bf16[144,768]{1,0:T(8,128)(2,1)S(1)}, bf16[144,1792]{1,0:T(8,128)(2,1)S(1)}, bf16[192,1024]{1,0:T(8,128)(2,1)S(1)}) custom-call(s32[1]{0:T(128)} %bitcast.here, f32[288,384]{1,0:T(8,128)S(1)} %get-tuple-element.104.share, bf16[288,384]{1,0:T(8,128)(2,1)S(1)} %collective-permute-done.8.refs_0_, f32[8,192]{1,0:T(8,128)S(1)} %get-tuple-element.106.refs_1_, ...), custom_call_target="tpu_custom_call" | custom-call | flops 1048576 | bytes 16384 | tf_op jit(solution)/shard_map/combine/pallas_call | solution.py:203
  35.8 1.6 %collective-permute-done.7.refs_0_ = bf16[288,384]{1,0:T(8,128)(2,1)S(1)} collective-permute-done((bf16[288,384]{1,0:T(8,128)(2,1)S(1)}, bf16[288,384]{1,0:T(8,128)(2,1)S(1)}, u32[]{:S(2)}, u32[]{:S(2)}) %collective-permute-start.7) | collective-permute-done | bytes 221216 | tf_op jit(solution)/shard_map/ppermute | solution.py:447
  41.8 2.4 %dispatch.7 = (bf16[288,1024]{1,0:T(8,128)(2,1)S(1)}, bf16[288,1024]{1,0:T(8,128)(2,1)S(1)}, f32[576,384]{1,0:T(8,128)S(1)}, bf16[288,384]{1,0:T(8,128)(2,1)S(1)...) custom-call(s32[1]{0:T(128)} %bitcast.here, bf16[200,1024]{1,0:T(8,128)(2,1)S(1)} %collective-permute-done.6.refs_0_, ...), custom_call_target="tpu_custom_call" | custom-call | flops 1048576 | bytes 16384 | tf_op jit(solution)/shard_map/dispatch/pallas_call | solution.py:138
  44.7 3.8 %collective-permute-done.14.refs_1_ = bf16[288,384]{1,0:T(8,128)(2,1)S(1)} collective-permute-done((bf16[288,384]{1,0:T(8,128)(2,1)S(1)}, bf16[288,384]{1,0:T(8,128)(2,1)S(1)}, u32[]{:S(2)}, u32[]{:S(2)}) %collective-permute-start.14) | collective-permute-done | bytes 221216 | tf_op jit(solution)/shard_map/ppermute | solution.py:447
  48.5 3.4 %combine.6 = (bf16[288,768]{1,0:T(8,128)(2,1)S(1)}, bf16[288,1792]{1,0:T(8,128)(2,1)S(1)}, bf16[192,1024]{1,0:T(8,128)(2,1)S(1)}, bf16[192,1024]{1,0:T(8,128)(2,1)S(1)}) custom-call(s32[1]{0:T(128)} %bitcast.here, f32[576,384]{1,0:T(8,128)S(1)} %get-tuple-element.119.share, bf16[288,384]{1,0:T(8,128)(2,1)S(1)} %collective-permute-done.7.refs_0_, ...), custom_call_target="tpu_custom_call" | custom-call | flops 1048576 | bytes 16384 | tf_op jit(solution)/shard_map/combine/pallas_call | solution.py:203
  55.7 2.4 %dispatch.8 = (bf16[288,1024]{1,0:T(8,128)(2,1)S(1)}, bf16[288,1024]{1,0:T(8,128)(2,1)S(1)}, f32[576,384]{1,0:T(8,128)S(1)}, bf16[288,384]{1,0:T(8,128)(2,1)S(1)...) custom-call(s32[1]{0:T(128)} %bitcast.here, bf16[200,1024]{1,0:T(8,128)(2,1)S(1)} %collective-permute-done.11.refs_0_, ...), custom_call_target="tpu_custom_call" | custom-call | flops 1048576 | bytes 16384 | tf_op jit(solution)/shard_map/dispatch/pallas_call | solution.py:138
  58.7 3.8 %collective-permute-done.19.refs_1_ = bf16[288,384]{1,0:T(8,128)(2,1)S(1)} collective-permute-done((bf16[288,384]{1,0:T(8,128)(2,1)S(1)}, bf16[288,384]{1,0:T(8,128)(2,1)S(1)}, u32[]{:S(2)}, u32[]{:S(2)}) %collective-permute-start.19) | collective-permute-done | bytes 221216 | tf_op jit(solution)/shard_map/ppermute | solution.py:447
  62.5 3.4 %combine.7 = (bf16[288,768]{1,0:T(8,128)(2,1)S(1)}, bf16[288,1792]{1,0:T(8,128)(2,1)S(1)}, bf16[192,1024]{1,0:T(8,128)(2,1)S(1)}, bf16[192,1024]{1,0:T(8,128)(2,1)S(1)}) custom-call(s32[1]{0:T(128)} %bitcast.here, f32[576,384]{1,0:T(8,128)S(1)} %get-tuple-element.133.share, bf16[288,384]{1,0:T(8,128)(2,1)S(1)} %collective-permute-done.13.refs_0_, ...), custom_call_target="tpu_custom_call" | custom-call | flops 1048576 | bytes 16384 | tf_op jit(solution)/shard_map/combine/pallas_call | solution.py:203
  71.5 2.0 %dispatch.9 = (bf16[144,1024]{1,0:T(8,128)(2,1)S(1)}, bf16[144,1024]{1,0:T(8,128)(2,1)S(1)}, f32[288,384]{1,0:T(8,128)S(1)}, bf16[288,384]{1,0:T(8,128)(2,1)S(1)}, f32[8,192]{1,0:T(8,128)S(1)}) custom-call(s32[1]{0:T(128)} %bitcast.here, bf16[200,1024]{1,0:T(8,128)(2,1)S(1)} %collective-permute-done.15.refs_0_, bf16[384,1024]{1,0:T(8,128)(2,1)S(1)} %bitcast.26, ...), custom_call_target="tpu_custom_call" | custom-call | flops 1048576 | bytes 16384 | tf_op jit(solution)/shard_map/dispatch/pallas_call | solution.py:138
  74.0 4.2 %collective-permute-done.24.refs_1_ = bf16[288,384]{1,0:T(8,128)(2,1)S(1)} collective-permute-done((bf16[288,384]{1,0:T(8,128)(2,1)S(1)}, bf16[288,384]{1,0:T(8,128)(2,1)S(1)}, u32[]{:S(2)}, u32[]{:S(2)}) %collective-permute-start.24) | collective-permute-done | bytes 221216 | tf_op jit(solution)/shard_map/ppermute | solution.py:447
  78.2 3.4 %combine.8 = (bf16[288,768]{1,0:T(8,128)(2,1)S(1)}, bf16[288,1792]{1,0:T(8,128)(2,1)S(1)}, bf16[192,1024]{1,0:T(8,128)(2,1)S(1)}, bf16[192,1024]{1,0:T(8,128)(2,1)S(1)}) custom-call(s32[1]{0:T(128)} %bitcast.here, f32[576,384]{1,0:T(8,128)S(1)} %get-tuple-element.146.share, bf16[288,384]{1,0:T(8,128)(2,1)S(1)} %collective-permute-done.18.refs_0_, ...), custom_call_target="tpu_custom_call" | custom-call | flops 1048576 | bytes 16384 | tf_op jit(solution)/shard_map/combine/pallas_call | solution.py:203
  82.6 2.3 %combine.9 = (bf16[144,768]{1,0:T(8,128)(2,1)S(1)}, bf16[144,1792]{1,0:T(8,128)(2,1)S(1)}, bf16[192,512]{1,0:T(8,128)(2,1)S(1)}, bf16[192,512]{1,0:T(8,128)(2,1)S(1)}) custom-call(s32[1]{0:T(128)} %bitcast.here, f32[288,384]{1,0:T(8,128)S(1)} %get-tuple-element.156.share, bf16[288,384]{1,0:T(8,128)(2,1)S(1)} %collective-permute-done.23.refs_0_, ...), custom_call_target="tpu_custom_call" | custom-call | flops 1048576 | bytes 16384 | tf_op jit(solution)/shard_map/combine/pallas_call | solution.py:203
  84.9 4.5 %collective-permute-done.26.refs_2_ = bf16[192,512]{1,0:T(8,128)(2,1)S(1)} collective-permute-done((bf16[192,512]{1,0:T(8,128)(2,1)S(1)}, bf16[192,512]{1,0:T(8,128)(2,1)S(1)}, u32[]{:S(2)}, u32[]{:S(2)}) %collective-permute-start.26) | collective-permute-done | bytes 196640 | tf_op jit(solution)/shard_map/ppermute | solution.py:426
  92.0 1.6 %collective-permute-start.28 = (bf16[192,512]{1,0:T(8,128)(2,1)S(1)}, bf16[192,512]{1,0:T(8,128)(2,1)S(1)}, u32[]{:S(2)}, u32[]{:S(2)}) collective-permute-start(bf16[192,512]{1,0:T(8,128)(2,1)S(1)} %add.8), channel_id=1, source_target_pairs={{0,4},{1,5},{2,6},{3,7},{4,8},{5,9},{6,10},{7,11},{8,12},{9,13},{1... | collective-permute-start | bytes 589832 | tf_op jit(solution)/shard_map/ppermute | solution.py:426
  93.7 5.5 %weights.4.old = bf16[1,1024,1152]{2,1,0:T(8,128)(2,1)} custom-call(s32[1]{0:T(128)} %bitcast.here, bf16[2304,384]{1,0:T(8,128)(2,1)S(1)} %hidden.1.refs_0_, bf16[144,1024]{1,0:T(8,128)(2,1)S(1)} %get-tuple-element.172.refs_1_, bf16[288,1024]{1,0:T(8,128)(2,1)S(1)} %get-tuple-element.173.refs_2_, bf16[288,1024]{1,0:T(8,128)(2,1)S(1)} %get-tuple-element.174.refs_3_, ...), custom_call_target="tpu_custom_call" | custom-call | flops 1048576 | bytes 16384 | tf_op jit(solution)/shard_map/weights/pallas_call | solution.py:389
  100.6 5.5 %weights.5.old = bf16[1,1024,1152]{2,1,0:T(8,128)(2,1)} custom-call(s32[1]{0:T(128)} %bitcast.here, bf16[1,1024,1152]{2,1,0:T(8,128)(2,1)} %weights.4.old, bf16[2304,384]{1,0:T(8,128)(2,1)S(1)} %hidden.1.refs_0_, bf16[144,1024]{1,0:T(8,128)(2,1)S(1)} %get-tuple-element.172.refs_1_, ...), custom_call_target="tpu_custom_call", output_to_operand_aliasing={{}: (1, {})} | custom-call | flops 1048576 | bytes 16384 | tf_op jit(solution)/shard_map/weights/pallas_call | solution.py:389
  107.2 5.8 %weights.6.old = bf16[1,1024,1152]{2,1,0:T(8,128)(2,1)} custom-call(s32[1]{0:T(128)} %bitcast.here, bf16[1,1024,1152]{2,1,0:T(8,128)(2,1)} %weights.5.old, bf16[2304,1024]{1,0:T(8,128)(2,1)S(1)} %bitcast.29, bf16[144,768]{1,0:T(8,128)(2,1)S(1)} %get-tuple-element.188.refs_1_, ...), custom_call_target="tpu_custom_call", output_to_operand_aliasing={{}: (1, {})} | custom-call | flops 1048576 | bytes 16384 | tf_op jit(solution)/shard_map/weights/pallas_call | solution.py:389
  114.3 5.8 %weights.7 = bf16[1,1024,1152]{2,1,0:T(8,128)(2,1)} custom-call(s32[1]{0:T(128)} %bitcast.here, bf16[1,1024,1152]{2,1,0:T(8,128)(2,1)} %weights.6.old, bf16[2304,1024]{1,0:T(8,128)(2,1)S(1)} %bitcast.30, bf16[144,768]{1,0:T(8,128)(2,1)S(1)} %get-tuple-element.188.refs_1_, ...), custom_call_target="tpu_custom_call", output_to_operand_aliasing={{}: (1, {})} | custom-call | flops 1048576 | bytes 16384 | tf_op jit(solution)/shard_map/weights/pallas_call | solution.py:389
  (97 shorter events, 41.1 us)
Async XLA Ops:
  0.6 24.0 %collective-permute-start.3 = (bf16[2304,384]{1,0:T(8,128)(2,1)}, bf16[2304,384]{1,0:T(8,128)(2,1)S(1)}, u32[]{:S(2)}, u32[]{:S(2)}) collective-permute-start(bf16[2304,384]{1,0:T(8,128)(2,1)} %bitcast.7), channel_id=1, source_target_pairs={{0,1},{1,0},{2,3},{3,2},{4,5},{5,4},{6,7},{7,6},{8,9},{9,8},{10,11... | collective-permute-start | bytes 5308424 | tf_op jit(solution)/shard_map/ppermute | solution.py:426
  1.1 23.4 %collective-permute-start.4 = (bf16[2304,384]{1,0:T(8,128)(2,1)}, bf16[2304,384]{1,0:T(8,128)(2,1)S(1)}, u32[]{:S(2)}, u32[]{:S(2)}) collective-permute-start(bf16[2304,384]{1,0:T(8,128)(2,1)} %bitcast.14), channel_id=1, source_target_pairs={{0,1},{1,0},{2,3},{3,2},{4,5},{5,4},{6,7},{7,6},{8,9},{9,8},{10,11... | collective-permute-start | bytes 5308424 | tf_op jit(solution)/shard_map/ppermute | solution.py:426
  1.2 15.7 %collective-permute-start.2 = (bf16[384,1024]{1,0:T(8,128)(2,1)}, bf16[384,1024]{1,0:T(8,128)(2,1)}, u32[]{:S(2)}, u32[]{:S(2)}) collective-permute-start(bf16[384,1024]{1,0:T(8,128)(2,1)} %bitcast.21), channel_id=1, source_target_pairs={{0,1},{1,0},{2,3},{3,2},{4,5},{5,4},{6,7},{7,6},{8,9},{9,8},{10,11... | collective-permute-start | bytes 2359304 | tf_op jit(solution)/shard_map/ppermute | solution.py:426
  8.3 12.9 %collective-permute-start.1 = (bf16[200,1024]{1,0:T(8,128)(2,1)}, bf16[200,1024]{1,0:T(8,128)(2,1)}, u32[]{:S(2)}, u32[]{:S(2)}) collective-permute-start(bf16[200,1024]{1,0:T(8,128)(2,1)} %pack.1.refs_0_), channel_id=1, source_target_pairs={{0,2},{1,3},{2,0},{3,1},{4,6},{5,7},{6,4},{7,5},{8,10},{9,11},{10,... | collective-permute-start | bytes 1228808 | tf_op jit(solution)/shard_map/ppermute | solution.py:426
  10.8 13.7 %collective-permute-start = (bf16[200,1024]{1,0:T(8,128)(2,1)}, bf16[200,1024]{1,0:T(8,128)(2,1)}, u32[]{:S(2)}, u32[]{:S(2)}) collective-permute-start(bf16[200,1024]{1,0:T(8,128)(2,1)} %pack.1.refs_0_), channel_id=1, source_target_pairs={{0,4},{1,5},{2,6},{3,7},{4,8},{5,9},{6,10},{7,11},{8,12},{9,13},{1... | collective-permute-start | bytes 1228808 | tf_op jit(solution)/shard_map/ppermute | solution.py:426
  24.6 8.9 %collective-permute-start.9 = (bf16[1024,768]{1,0:T(8,128)(2,1)S(1)}, bf16[1024,768]{1,0:T(8,128)(2,1)S(1)}, u32[]{:S(2)}, u32[]{:S(2)}) collective-permute-start(bf16[1024,768]{1,0:T(8,128)(2,1)S(1)} %join.1.refs_6_.refs_7_), channel_id=1, source_target_pairs={{0,1},{1,0},{2,3},{3,2},{4,5},{5,4},{6,7},{7,6},{8,9},{9,8},{10,11... | collective-permute-start | bytes 4718600 | tf_op jit(solution)/shard_map/ppermute | solution.py:426
  24.6 12.8 %collective-permute-start.6 = (bf16[200,1024]{1,0:T(8,128)(2,1)}, bf16[200,1024]{1,0:T(8,128)(2,1)S(1)}, u32[]{:S(2)}, u32[]{:S(2)}) collective-permute-start(bf16[200,1024]{1,0:T(8,128)(2,1)} %collective-permute-done.refs_1_), channel_id=1, source_target_pairs={{0,2},{1,3},{2,0},{3,1},{4,6},{5,7},{6,4},{7,5},{8,10},{9,11},{10,... | collective-permute-start | bytes 1228808 | tf_op jit(solution)/shard_map/ppermute | solution.py:426
  25.2 13.5 %collective-permute-start.5 = (bf16[200,1024]{1,0:T(8,128)(2,1)}, bf16[200,1024]{1,0:T(8,128)(2,1)S(1)}, u32[]{:S(2)}, u32[]{:S(2)}) collective-permute-start(bf16[200,1024]{1,0:T(8,128)(2,1)} %collective-permute-done.refs_1_), channel_id=1, source_target_pairs={{0,4},{1,5},{2,6},{3,7},{4,8},{5,9},{6,10},{7,11},{8,12},{9,13},{1... | collective-permute-start | bytes 1228808 | tf_op jit(solution)/shard_map/ppermute | solution.py:426
  38.7 14.9 %collective-permute-start.12 = (bf16[144,1792]{1,0:T(8,128)(2,1)S(1)}, bf16[144,1792]{1,0:T(8,128)(2,1)S(1)}, u32[]{:S(2)}, u32[]{:S(2)}) collective-permute-start(bf16[144,1792]{1,0:T(8,128)(2,1)S(1)} %get-tuple-element.115), channel_id=1, source_target_pairs={{0,1},{1,0},{2,3},{3,2},{4,5},{5,4},{6,7},{7,6},{8,9},{9,8},{10,11... | collective-permute-start | bytes 1548296 | tf_op jit(solution)/shard_map/ppermute | solution.py:426
  38.7 13.8 %collective-permute-start.11 = (bf16[200,1024]{1,0:T(8,128)(2,1)S(1)}, bf16[200,1024]{1,0:T(8,128)(2,1)S(1)}, u32[]{:S(2)}, u32[]{:S(2)}) collective-permute-start(bf16[200,1024]{1,0:T(8,128)(2,1)S(1)} %collective-permute-done.5.refs_1_), channel_id=1, source_target_pairs={{0,2},{1,3},{2,0},{3,1},{4,6},{5,7},{6,4},{7,5},{8,10},{9,11},{10,... | collective-permute-start | bytes 1228808 | tf_op jit(solution)/shard_map/ppermute | solution.py:426
  40.2 13.4 %collective-permute-start.10 = (bf16[200,1024]{1,0:T(8,128)(2,1)S(1)}, bf16[200,1024]{1,0:T(8,128)(2,1)S(1)}, u32[]{:S(2)}, u32[]{:S(2)}) collective-permute-start(bf16[200,1024]{1,0:T(8,128)(2,1)S(1)} %collective-permute-done.5.refs_1_), channel_id=1, source_target_pairs={{0,4},{1,5},{2,6},{3,7},{4,8},{5,9},{6,10},{7,11},{8,12},{9,13},{1... | collective-permute-start | bytes 1228808 | tf_op jit(solution)/shard_map/ppermute | solution.py:426
  53.6 13.6 %collective-permute-start.17 = (bf16[288,1792]{1,0:T(8,128)(2,1)S(1)}, bf16[288,1792]{1,0:T(8,128)(2,1)S(1)}, u32[]{:S(2)}, u32[]{:S(2)}) collective-permute-start(bf16[288,1792]{1,0:T(8,128)(2,1)S(1)} %get-tuple-element.129), channel_id=1, source_target_pairs={{0,1},{1,0},{2,3},{3,2},{4,5},{5,4},{6,7},{7,6},{8,9},{9,8},{10,11... | collective-permute-start | bytes 3096584 | tf_op jit(solution)/shard_map/ppermute | solution.py:426
  53.6 13.6 %collective-permute-start.15 = (bf16[200,1024]{1,0:T(8,128)(2,1)S(1)}, bf16[200,1024]{1,0:T(8,128)(2,1)S(1)}, u32[]{:S(2)}, u32[]{:S(2)}) collective-permute-start(bf16[200,1024]{1,0:T(8,128)(2,1)S(1)} %collective-permute-done.10.refs_1_), channel_id=1, source_target_pairs={{0,2},{1,3},{2,0},{3,1},{4,6},{5,7},{6,4},{7,5},{8,10},{9,11},{10,... | collective-permute-start | bytes 1228808 | tf_op jit(solution)/shard_map/ppermute | solution.py:426
  54.2 13.0 %collective-permute-start.16 = (bf16[192,1024]{1,0:T(8,128)(2,1)S(1)}, bf16[192,1024]{1,0:T(8,128)(2,1)S(1)}, u32[]{:S(2)}, u32[]{:S(2)}) collective-permute-start(bf16[192,1024]{1,0:T(8,128)(2,1)S(1)} %get-tuple-element.128), channel_id=1, source_target_pairs={{0,4},{1,5},{2,6},{3,7},{4,8},{5,9},{6,10},{7,11},{8,12},{9,13},{1... | collective-permute-start | bytes 1179656 | tf_op jit(solution)/shard_map/ppermute | solution.py:426
  67.2 14.7 %collective-permute-start.22 = (bf16[288,1792]{1,0:T(8,128)(2,1)S(1)}, bf16[288,1792]{1,0:T(8,128)(2,1)S(1)}, u32[]{:S(2)}, u32[]{:S(2)}) collective-permute-start(bf16[288,1792]{1,0:T(8,128)(2,1)S(1)} %get-tuple-element.143), channel_id=1, source_target_pairs={{0,1},{1,0},{2,3},{3,2},{4,5},{5,4},{6,7},{7,6},{8,9},{9,8},{10,11... | collective-permute-start | bytes 3096584 | tf_op jit(solution)/shard_map/ppermute | solution.py:426
  67.2 14.4 %collective-permute-start.21 = (bf16[192,1024]{1,0:T(8,128)(2,1)S(1)}, bf16[192,1024]{1,0:T(8,128)(2,1)S(1)}, u32[]{:S(2)}, u32[]{:S(2)}) collective-permute-start(bf16[192,1024]{1,0:T(8,128)(2,1)S(1)} %get-tuple-element.142), channel_id=1, source_target_pairs={{0,2},{1,3},{2,0},{3,1},{4,6},{5,7},{6,4},{7,5},{8,10},{9,11},{10,... | collective-permute-start | bytes 1179656 | tf_op jit(solution)/shard_map/ppermute | solution.py:426
  68.8 13.1 %collective-permute-start.20 = (bf16[192,1024]{1,0:T(8,128)(2,1)S(1)}, bf16[192,1024]{1,0:T(8,128)(2,1)S(1)}, u32[]{:S(2)}, u32[]{:S(2)}) collective-permute-start(bf16[192,1024]{1,0:T(8,128)(2,1)S(1)} %get-tuple-element.141), channel_id=1, source_target_pairs={{0,4},{1,5},{2,6},{3,7},{4,8},{5,9},{6,10},{7,11},{8,12},{9,13},{1... | collective-permute-start | bytes 1179656 | tf_op jit(solution)/shard_map/ppermute | solution.py:426
  73.5 8.4 %collective-permute-start.23 = (bf16[288,384]{1,0:T(8,128)(2,1)S(1)}, bf16[288,384]{1,0:T(8,128)(2,1)S(1)}, u32[]{:S(2)}, u32[]{:S(2)}) collective-permute-start(bf16[288,384]{1,0:T(8,128)(2,1)S(1)} %get-tuple-element.145), channel_id=1, source_target_pairs={{0,16},{16,0},{1,17},{17,1},{2,18},{18,2},{3,19},{19,3},{4,20},{20... | collective-permute-start | bytes 663560 | tf_op jit(solution)/shard_map/ppermute | solution.py:447
  89.4 9.7 %collective-permute-start.29 = (bf16[192,512]{1,0:T(8,128)(2,1)S(1)}, bf16[192,512]{1,0:T(8,128)(2,1)S(1)}, u32[]{:S(2)}, u32[]{:S(2)}) collective-permute-start(bf16[192,512]{1,0:T(8,128)(2,1)S(1)} %add.7), channel_id=1, source_target_pairs={{0,2},{1,3},{2,0},{3,1},{4,6},{5,7},{6,4},{7,5},{8,10},{9,11},{10,... | collective-permute-start | bytes 589832 | tf_op jit(solution)/shard_map/ppermute | solution.py:426
  89.9 16.1 %collective-permute-start.25 = (bf16[192,512]{1,0:T(8,128)(2,1)S(1)}, bf16[192,512]{1,0:T(8,128)(2,1)S(1)}, u32[]{:S(2)}, u32[]{:S(2)}) collective-permute-start(bf16[192,512]{1,0:T(8,128)(2,1)S(1)} %get-tuple-element.163), channel_id=1, source_target_pairs={{0,2},{1,3},{2,0},{3,1},{4,6},{5,7},{6,4},{7,5},{8,10},{9,11},{10,... | collective-permute-start | bytes 589832 | tf_op jit(solution)/shard_map/ppermute | solution.py:426
  91.4 21.5 %collective-permute-start.32 = (bf16[192,512]{1,0:T(8,128)(2,1)S(1)}, bf16[192,512]{1,0:T(8,128)(2,1)S(1)}, u32[]{:S(2)}, u32[]{:S(2)}) collective-permute-start(bf16[192,512]{1,0:T(8,128)(2,1)S(1)} %get-tuple-element.185), channel_id=1, source_target_pairs={{0,2},{1,3},{2,0},{3,1},{4,6},{5,7},{6,4},{7,5},{8,10},{9,11},{10,... | collective-permute-start | bytes 589832 | tf_op jit(solution)/shard_map/ppermute | solution.py:426
  92.0 14.0 %collective-permute-start.28 = (bf16[192,512]{1,0:T(8,128)(2,1)S(1)}, bf16[192,512]{1,0:T(8,128)(2,1)S(1)}, u32[]{:S(2)}, u32[]{:S(2)}) collective-permute-start(bf16[192,512]{1,0:T(8,128)(2,1)S(1)} %add.8), channel_id=1, source_target_pairs={{0,4},{1,5},{2,6},{3,7},{4,8},{5,9},{6,10},{7,11},{8,12},{9,13},{1... | collective-permute-start | bytes 589832 | tf_op jit(solution)/shard_map/ppermute | solution.py:426
  99.3 13.7 %collective-permute-start.33 = (bf16[192,512]{1,0:T(8,128)(2,1)S(1)}, bf16[192,512]{1,0:T(8,128)(2,1)S(1)}, u32[]{:S(2)}, u32[]{:S(2)}) collective-permute-start(bf16[192,512]{1,0:T(8,128)(2,1)S(1)} %add.10), channel_id=1, source_target_pairs={{0,4},{1,5},{2,6},{3,7},{4,8},{5,9},{6,10},{7,11},{8,12},{9,13},{1... | collective-permute-start | bytes 589832 | tf_op jit(solution)/shard_map/ppermute | solution.py:426
  106.2 13.9 %collective-permute-start.31 = (bf16[192,512]{1,0:T(8,128)(2,1)S(1)}, bf16[192,512]{1,0:T(8,128)(2,1)S(1)}, u32[]{:S(2)}, u32[]{:S(2)}) collective-permute-start(bf16[192,512]{1,0:T(8,128)(2,1)S(1)} %add.9), channel_id=1, source_target_pairs={{0,4},{1,5},{2,6},{3,7},{4,8},{5,9},{6,10},{7,11},{8,12},{9,13},{1... | collective-permute-start | bytes 589832 | tf_op jit(solution)/shard_map/ppermute | solution.py:426
  (23 other events, 142.1 us)

commit v6 on v5

--- a/solution.py
+++ b/solution.py
@@ -271,35 +271,64 @@
     )(a, b, left, right)
 
 
+def in_hbm(v):
+    return pltpu.with_memory_space_constraint(v, pltpu.HBM)
+
+
 def hidden_kernel(gate, up, out):
     gate_pre = gate[...].astype(f32)
-    out[...] = (gate_pre * jax.nn.sigmoid(gate_pre) * up[...].astype(f32)).astype(bf16)
+    out[...] = (gate_pre * jax.nn.sigmoid(gate_pre) * up[...].astype(f32)).astype(bf16).T
 
 
 def hidden(gate, up):
     rows, h = gate.shape
-    tile = rows // 4
+    tile = 768
     spec = pl.BlockSpec((tile, h), lambda i: (i, 0))
     return pl.pallas_call(
         hidden_kernel,
-        out_shape=jax.ShapeDtypeStruct((rows, h), bf16),
+        out_shape=jax.ShapeDtypeStruct((h, rows), bf16),
         grid=(rows // tile,),
         in_specs=[spec, spec],
-        out_specs=spec,
-        cost_estimate=light,
-        compiler_params=params(8),
+        out_specs=pl.BlockSpec((h, tile), lambda i: (0, i)),
+        cost_estimate=light,
+        compiler_params=params(12),
         name="hidden",
-    )(gate, up)
-
-
-def pack_kernel(line, tokens, routes, codes, out):
+    )(in_hbm(gate), in_hbm(up))
+
+
+def turn_kernel(v, out):
+    out[...] = v[...].T
+
+
+def turn(v):
+    rows, d = v.shape
+    tile = 256
+    return pl.pallas_call(
+        turn_kernel,
+        out_shape=jax.ShapeDtypeStruct((d, rows), v.dtype),
+        grid=(d // tile,),
+        in_specs=[pl.BlockSpec((rows, tile), lambda i: (0, i))],
+        out_specs=pl.BlockSpec((tile, rows), lambda i: (i, 0)),
+        cost_estimate=light,
+        compiler_params=params(12),
+        name="turn",
+    )(in_hbm(v))
+
+
+def pack_kernel(line, tokens, routes, codes, out, named, sems):
     tok = tokens.shape[0]
-    out[:tok, :] = tokens[...]
-    same = lax.broadcasted_iota(jnp.int32, (tok, tok), 0) == lax.broadcasted_iota(jnp.int32, (tok, tok), 1)
-    same = jnp.where(same, 1.0, 0.0).astype(bf16)
+    copies = [
+        pltpu.make_async_copy(tokens, out.at[:tok, :], sems.at[0]),
+        pltpu.make_async_copy(routes, named.at[0], sems.at[1]),
+        pltpu.make_async_copy(codes, named.at[1], sems.at[2]),
+    ]
+    for c in copies:
+        c.start()
     out[tok:, :] = jnp.zeros((8, out.shape[1]), bf16)
-    for at, v in ((0, routes), (line, codes)):
-        out[tok:, at : at + tok] = contract_rows(v[...].astype(f32).astype(bf16), same).astype(bf16)
+    for k, at in enumerate((0, line)):
+        copies[1 + k].wait()
+        out[tok:, at : at + tok] = named[k].astype(f32).astype(bf16)
+    copies[0].wait()
 
 
 def pack(tokens, routes, codes, line):
@@ -307,105 +336,83 @@
     return pl.pallas_call(
         functools.partial(pack_kernel, line),
         out_shape=jax.ShapeDtypeStruct((tok + 8, d), bf16),
-        in_specs=[on_chip] * 3,
+        in_specs=[anywhere] * 3,
         out_specs=on_chip,
+        scratch_shapes=[pltpu.VMEM((2, *routes.shape), jnp.int32), pltpu.SemaphoreType.DMA((3,))],
         cost_estimate=light,
         compiler_params=params(8),
         name="pack",
-    )(tokens, routes, codes)
-
-
-def weights_kernel(order, cap, sorted_left, starts, base_tile, here, *refs):
-    count = 1
-    by_source, pieces, out = refs[:count], refs[count:-5], refs[-5]
-    ls, rs, left_sems, right_sems = refs[-4:]
+    )(in_hbm(tokens), in_hbm(routes), in_hbm(codes))
+
+
+def weights_kernel(order, cap, starts, left_whole, here, left, *refs):
+    pieces, out, held, sems = refs[:-3], refs[-3], refs[-2], refs[-1]
     i = pl.program_id(0)
-    tile = ls.shape[2]
-    steps = pl.num_programs(0)
-
-    def copies_of_sorted(v, column, to, sems):
+    wide = held.shape[2]
+
+    def copies(step):
+        slot = lax.rem(step, 2) if left_whole else 0
         made = []
-        for p, (step, other, plane) in enumerate(order):
-            src = jnp.bitwise_xor(source(here[0], step, other), plane)
-            rows = pl.ds(pl.multiple_of(src * cap, 16), cap)
-            at = v.at[rows, :] if column is None else v.at[rows, pl.ds(pl.multiple_of(column * tile, 128), tile)]
-            made.append(pltpu.make_async_copy(at, to.at[pl.ds(p * cap, cap), :], sems.at[len(made)]))
+        for r, first in zip(pieces, starts):
+            column = pl.ds(pl.multiple_of(first + step * wide, 128), wide) if left_whole else pl.ds(first, wide)
+            for at in range(0, r.shape[0], cap):
+                k, other, plane = order[len(made)]
+                src = jnp.bitwise_xor(source(here[0], k, other), plane)
+                to = held.at[slot, pl.ds(pl.multiple_of(src * cap, 16), cap), :]
+                made.append(pltpu.make_async_copy(r.at[pl.ds(at, cap), column], to, sems.at[slot, len(made)]))
         return made
-
-    def copies_of_pieces(column, to, sems):
-        made, base = [], 0
-        for r, first in zip(pieces, starts):
-            if column is None:
-                at = r.at[:, pl.ds(first, to.shape[1])]
-            else:
-                at = r.at[:, pl.ds(pl.multiple_of(first + column * tile, 128), tile)]
-            made.append(pltpu.make_async_copy(at, to.at[pl.ds(base, r.shape[0]), :], sems.at[len(made)]))
-            base += r.shape[0]
-        return made
-
-    def left(step):
-        slot = lax.rem(step, 2)
-        if sorted_left:
-            return copies_of_sorted(by_source[0], base_tile + step, ls.at[slot], left_sems.at[slot])
-        return copies_of_pieces(base_tile + step, ls.at[slot], left_sems.at[slot])
-
-    def right():
-        if sorted_left:
-            return copies_of_pieces(None, rs.at[0], right_sems.at[0])
-        return copies_of_sorted(by_source[0], None, rs.at[0], right_sems.at[0])
 
     @pl.when(i == 0)
     def _():
-        for c in right() + left(i):
+        for c in copies(i):
             c.start()
 
-    @pl.when(i + 1 < steps)
-    def _():
-        for c in left(i + 1):
-            c.start()
-
-    @pl.when(i == 0)
-    def _():
-        for c in right():
+    if left_whole:
+        @pl.when(i + 1 < pl.num_programs(0))
+        def _():
+            for c in copies(i + 1):
+                c.start()
+
+        for c in copies(i):
             c.wait()
-
-    for c in left(i):
-        c.wait()
-
-    out[0] = (contract_rows(ls[lax.rem(i, 2)], rs[0]) * loss_scale).astype(bf16)
-
-
-def weight_sums(here, order, by_source, pieces, starts, sorted_left, tiles, into, cap):
-    slots, wide = by_source[0].shape
-    d = pieces[0].shape[1]
-    if sorted_left:
-        d, wide = wide, d
+        part = jnp.dot(left[...], held[lax.rem(i, 2)], preferred_element_type=f32)
+        out[0] = (part * loss_scale).astype(bf16).T
+    else:
+        @pl.when(i == 0)
+        def _():
+            for c in copies(i):
+                c.wait()
+
+        part = jnp.dot(left[...], held[0], preferred_element_type=f32)
+        out[0] = (part * loss_scale).astype(bf16)
+
+
+def weight_sums(here, order, left, pieces, starts, left_whole, into, cap, d):
+    rows, slots = left.shape
     tile = 256
-    at = 0 if sorted_left else 2
-    whole_out = jax.ShapeDtypeStruct((1, d, 3 * (wide // 2 if sorted_left else wide)), bf16)
-    given = [*by_source, *pieces]
-    kernel = functools.partial(weights_kernel, order, cap, sorted_left, starts, tiles[0])
+    h = rows if left_whole else (pieces[0].shape[1] // 2)
+    wide, at = (h, 2) if left_whole else (2 * h, 0)
+    kernel = functools.partial(weights_kernel, order, cap, starts, left_whole)
     body = kernel if into is None else (lambda here, old, *refs: kernel(here, *refs))
+    left_spec = pl.BlockSpec((rows, slots), lambda i, here: (0, 0))
+    if not left_whole:
+        left_spec = pl.BlockSpec((tile, slots), lambda i, here: (i, 0))
+    held = (2, slots, tile) if left_whole else (1, slots, wide)
     return pl.pallas_call(
         body,
-        out_shape=whole_out,
+        out_shape=jax.ShapeDtypeStruct((1, d, 3 * h), bf16),
         grid_spec=pltpu.PrefetchScalarGridSpec(
             num_scalar_prefetch=1,
-            grid=(tiles[1],),
-            in_specs=[anywhere] * (len(given) + (into is not None)),
-            out_specs=pl.BlockSpec((1, tile, wide), lambda i, here: (0, tiles[0] + i, at)),
-            scratch_shapes=[
-                pltpu.VMEM((2, slots, tile), bf16),
-                pltpu.VMEM((len(by_source), slots, wide), bf16),
-                pltpu.SemaphoreType.DMA((2, len(order))),
-                pltpu.SemaphoreType.DMA((len(by_source), len(order))),
-            ],
+            grid=(d // tile,),
+            in_specs=[anywhere] * (into is not None) + [left_spec] + [anywhere] * len(pieces),
+            out_specs=pl.BlockSpec((1, tile, wide), lambda i, here: (0, i, at)),
+            scratch_shapes=[pltpu.VMEM(held, bf16), pltpu.SemaphoreType.DMA((2, len(order)))],
         ),
         input_output_aliases={} if into is None else {1: 0},
         cost_estimate=light,
         compiler_params=params(20),
         name="weights",
-    )(here, *([] if into is None else [into]), *given)
+    )(here, *([] if into is None else [into]), left, *pieces)
 
 
 def together(*values):
@@ -426,7 +433,7 @@
         return lax.ppermute(v, "expert", perm)
 
     line = 256 * pl.cdiv(tok, 256)
-    block = pack(out_grad, routes, gate_codes, line)
+    block = pack(out_grad, routes.T, gate_codes.T, line)
     here = me.reshape(1).astype(jnp.int32)
 
     def ring(v, hops=1):
@@ -455,8 +462,8 @@
     r1, x0 = ring(block), send(block, to_x)
     c0, h0 = first([(0, 0)], [block])
     w = join(w_gate[0], w_up[0])
-    hid = hidden(sg, su)
-    r1, x0, h0, w, hid, sg_c, su_c = together(r1, x0, h0, w, hid, sg_c, su_c)
+    hid, inputs = hidden(sg, su), turn(saved_inputs[0])
+    r1, x0, h0, w, hid, inputs, sg_c, su_c = together(r1, x0, h0, w, hid, inputs, sg_c, su_c)
     r2, x1 = ring(r1), send(r1, to_x)
     h0, w_c = exchange(h0), send(w, to_core)
     c1, h1, g1 = first([(1, 0), (0, 1)], [x0, r1])
@@ -492,25 +499,13 @@
     order_all = order + [(k, col, 1) for k, col, _ in order]
     zeros, skip = [0] * len(recs), [d] * len(recs)
 
-    def received_part(tiles, into):
-        return weight_sums(here, order_all, [hid], recs + away, zeros + zeros, False, tiles, into, cap)
-
-    def inputs_part(tiles, into):
-        return weight_sums(here, order_all, [saved_inputs[0]], gps + away, zeros + skip, True, tiles, into, cap)
-
-    tiles = d // 256
-    low, high = (0, tiles // 2), (tiles // 2, tiles - tiles // 2)
     w2 = [ring(add([t_r2, w1, b2[0]], 0))]
-    part = received_part(low, None)
+    part = weight_sums(here, order_all, hid, recs + away, zeros + zeros, True, None, cap, d)
     b2[1], part = together(b2[1], part)
     w2.append(ring(add([t_r2, w1, b2[1]], 1)))
-    part = received_part(high, part)
-    b3[0], w2[0], part = together(b3[0], w2[0], part)
-    w3 = [ring(add([t_r3, b3[0], w2[0]], 0))]
-    part = inputs_part(low, part)
-    b3[1], w2[1], part = together(b3[1], w2[1], part)
-    w3.append(ring(add([t_r3, b3[1], w2[1]], 1)))
-    weight_grads = inputs_part(high, part)
+    weight_grads = weight_sums(here, order_all, inputs, gps + away, zeros + skip, False, part, cap, d)
+    b3[0], w2[0], weight_grads = together(b3[0], w2[0], weight_grads)
+    w3 = [ring(add([t_r3, b3[0], w2[0]], 0)), ring(add([t_r3, b3[1], w2[1]], 1))]
     return (finish(t_r0, b0, *w3), weight_grads)
 
 

time: 122 us -> 117 us (0.959)
  local copies, waits for them, and re-layouts: 9.76 us -> 0.97 us
  waiting for transfers between devices: 31.5 us -> 37.2 us
  Pallas kernels: 52 us -> 49.5 us
    unnamed x26 -> x10, local copies, waits for them, and re-layouts: 9.76 us -> 0.97 us
    ppermute x27, waiting for transfers between devices: 13 us -> 18.9 us  [send(): return lax.ppermute(v, 'expert', perm)]
    pallas_call x5 -> x4, Pallas kernels: 23.3 us -> 19.9 us  [the longest x2 12.8 us: weight_sums(): pl.pallas_call(body, out_shape=jax.ShapeDtypeStruct((1, d, 3 * h), bf16),...]
  transfers between devices with their start and end apart: 35 -> 35, of which waited for: 15 -> 15; matrix products, arithmetic and copies ran while one was open for 2% -> 0% of each run, Pallas kernels for 42% -> 42%
where the time goes in v6:
time: 117 us; the launch traced here: 116 us
  Pallas kernels  49.5 us (42%)
  waiting for transfers between devices  37.2 us (32%)
  starting transfers between devices  27.5 us (24%)
    ppermute x27, starting transfers between devices, send(): return lax.ppermute(v, 'expert', perm)  19.2 us
    ppermute x27, waiting for transfers between devices, send(): return lax.ppermute(v, 'expert', perm)  18.9 us
    ppermute x8, waiting for transfers between devices, exchange(): return lax.ppermute(v, 'dp', [(0, 1), (1, 0)])  18.3 us
    pallas_call x5, Pallas kernels, combine(): pl.pallas_call(functools.partial(combine_kernel, chunk, cap), out_shape=[...  14.8 us
    pallas_call x2, Pallas kernels, weight_sums(): pl.pallas_call(body, out_shape=jax.ShapeDtypeStruct((1, d, 3 * h), bf16),...  12.8 us
    pallas_call x5, Pallas kernels, dispatch(): pl.pallas_call(functools.partial(dispatch_kernel, n, cap), out_shape=[jax...  11.6 us
    ppermute x8, starting transfers between devices, exchange(): return lax.ppermute(v, 'dp', [(0, 1), (1, 0)])  8.36 us
    pallas_call x1, Pallas kernels, turn(): pl.pallas_call(turn_kernel, out_shape=jax.ShapeDtypeStruct((d, rows), v.d...  3.86 us
  transfers between devices with their start and end apart: 35, of which 15 were waited for; matrix products, arithmetic and copies ran while one was open for 0% of the time, Pallas kernels for 42%

profile of v6, /device:TPU:0, one launch (start us, length us, event | category | flops | bytes accessed | tf_op | source)
XLA Modules:
  0.0 116.1 jit_solution(5668852216580115155)
XLA Ops:
  1.7 1.8 %pack.1.refs_0_ = bf16[200,1024]{1,0:T(8,128)(2,1)} custom-call(bf16[192,1024]{1,0:T(8,128)(2,1)} %tokens.1, s32[8,192]{1,0:T(8,128)} %bitcast.32, s32[8,192]{1,0:T(8,128)} %bitcast.33), custom_call_target="tpu_custom_call" | custom-call | flops 1048576 | bytes 16384 | tf_op jit(solution)/shard_map/pack/pallas_call | solution.py:336
  3.4 2.6 %collective-permute-start.1 = (bf16[200,1024]{1,0:T(8,128)(2,1)}, bf16[200,1024]{1,0:T(8,128)(2,1)}, u32[]{:S(2)}, u32[]{:S(2)}) collective-permute-start(bf16[200,1024]{1,0:T(8,128)(2,1)} %pack.1.refs_0_), channel_id=1, source_target_pairs={{0,2},{1,3},{2,0},{3,1},{4,6},{5,7},{6,4},{7,5},{8,10},{9,11},{10,... | collective-permute-start | bytes 1228808 | tf_op jit(solution)/shard_map/ppermute | solution.py:433
  7.6 3.2 %hidden.1.left = bf16[384,2304]{1,0:T(8,128)(2,1)S(1)} custom-call(bf16[2304,384]{1,0:T(8,128)(2,1)} %bitcast.10, bf16[2304,384]{1,0:T(8,128)(2,1)} %bitcast.17), custom_call_target="tpu_custom_call" | custom-call | flops 1048576 | bytes 16384 | tf_op jit(solution)/shard_map/hidden/pallas_call | solution.py:287
  10.9 3.9 %turn.1.refs_0_ = bf16[1024,2304]{1,0:T(8,128)(2,1)S(1)} custom-call(bf16[2304,1024]{1,0:T(8,128)(2,1)} %bitcast.31), custom_call_target="tpu_custom_call" | custom-call | flops 1048576 | bytes 16384 | tf_op jit(solution)/shard_map/turn/pallas_call | solution.py:306
  15.9 2.3 %dispatch.5 = (bf16[144,1024]{1,0:T(8,128)(2,1)S(1)}, bf16[144,1024]{1,0:T(8,128)(2,1)S(1)}, f32[288,384]{1,0:T(8,128)S(1)}, bf16[288,384]{1,0:T(8,128)(2,1)S(1)}, f32[8,192]{1,0:T(8,128)S(1)}) custom-call(s32[1]{0:T(128)} %bitcast.2.here, bf16[200,1024]{1,0:T(8,128)(2,1)} %pack.1.refs_0_, bf16[384,1024]{1,0:T(8,128)(2,1)S(1)} %bitcast.24, ...), custom_call_target="tpu_custom_call" | custom-call | flops 1048576 | bytes 16384 | tf_op jit(solution)/shard_map/dispatch/pallas_call | solution.py:138
  22.0 2.6 %dispatch.6 = (bf16[288,1024]{1,0:T(8,128)(2,1)S(1)}, bf16[288,1024]{1,0:T(8,128)(2,1)S(1)}, f32[576,384]{1,0:T(8,128)S(1)}, bf16[288,384]{1,0:T(8,128)(2,1)S(1)...) custom-call(s32[1]{0:T(128)} %bitcast.2.here, bf16[200,1024]{1,0:T(8,128)(2,1)} %collective-permute-done.1.refs_0_, ...), custom_call_target="tpu_custom_call" | custom-call | flops 1048576 | bytes 16384 | tf_op jit(solution)/shard_map/dispatch/pallas_call | solution.py:138
  25.2 3.5 %collective-permute-done.8.refs_0_ = bf16[288,384]{1,0:T(8,128)(2,1)S(1)} collective-permute-done((bf16[288,384]{1,0:T(8,128)(2,1)S(1)}, bf16[288,384]{1,0:T(8,128)(2,1)S(1)}, u32[]{:S(2)}, u32[]{:S(2)}) %collective-permute-start.8) | collective-permute-done | bytes 221216 | tf_op jit(solution)/shard_map/ppermute | solution.py:454
  28.7 2.3 %combine.5 = (bf16[144,768]{1,0:T(8,128)(2,1)S(1)}, bf16[144,1792]{1,0:T(8,128)(2,1)S(1)}, bf16[192,1024]{1,0:T(8,128)(2,1)S(1)}) custom-call(s32[1]{0:T(128)} %bitcast.2.here, f32[288,384]{1,0:T(8,128)S(1)} %get-tuple-element.102.share, bf16[288,384]{1,0:T(8,128)(2,1)S(1)} %collective-permute-done.8.refs_0_, f32[8,192]{1,0:T(8,128)S(1)} %get-tuple-element.104.refs_1_, ...), custom_call_target="tpu_custom_call" | custom-call | flops 1048576 | bytes 16384 | tf_op jit(solution)/shard_map/combine/pallas_call | solution.py:203
  31.0 1.7 %collective-permute-done.7.refs_0_ = bf16[288,384]{1,0:T(8,128)(2,1)S(1)} collective-permute-done((bf16[288,384]{1,0:T(8,128)(2,1)S(1)}, bf16[288,384]{1,0:T(8,128)(2,1)S(1)}, u32[]{:S(2)}, u32[]{:S(2)}) %collective-permute-start.7) | collective-permute-done | bytes 221216 | tf_op jit(solution)/shard_map/ppermute | solution.py:454
  37.1 2.4 %dispatch.7 = (bf16[288,1024]{1,0:T(8,128)(2,1)S(1)}, bf16[288,1024]{1,0:T(8,128)(2,1)S(1)}, f32[576,384]{1,0:T(8,128)S(1)}, bf16[288,384]{1,0:T(8,128)(2,1)S(1)...) custom-call(s32[1]{0:T(128)} %bitcast.2.here, bf16[200,1024]{1,0:T(8,128)(2,1)S(1)} %collective-permute-done.6.refs_0_, ...), custom_call_target="tpu_custom_call" | custom-call | flops 1048576 | bytes 16384 | tf_op jit(solution)/shard_map/dispatch/pallas_call | solution.py:138
  40.1 3.8 %collective-permute-done.14.refs_1_ = bf16[288,384]{1,0:T(8,128)(2,1)S(1)} collective-permute-done((bf16[288,384]{1,0:T(8,128)(2,1)S(1)}, bf16[288,384]{1,0:T(8,128)(2,1)S(1)}, u32[]{:S(2)}, u32[]{:S(2)}) %collective-permute-start.14) | collective-permute-done | bytes 221216 | tf_op jit(solution)/shard_map/ppermute | solution.py:454
  43.9 3.4 %combine.6 = (bf16[288,768]{1,0:T(8,128)(2,1)S(1)}, bf16[288,1792]{1,0:T(8,128)(2,1)S(1)}, bf16[192,1024]{1,0:T(8,128)(2,1)S(1)}, bf16[192,1024]{1,0:T(8,128)(2,1)S(1)}) custom-call(s32[1]{0:T(128)} %bitcast.2.here, f32[576,384]{1,0:T(8,128)S(1)} %get-tuple-element.117.share, bf16[288,384]{1,0:T(8,128)(2,1)S(1)} %collective-permute-done.7.refs_0_, ...), custom_call_target="tpu_custom_call" | custom-call | flops 1048576 | bytes 16384 | tf_op jit(solution)/shard_map/combine/pallas_call | solution.py:203
  51.0 2.4 %dispatch.8 = (bf16[288,1024]{1,0:T(8,128)(2,1)S(1)}, bf16[288,1024]{1,0:T(8,128)(2,1)S(1)}, f32[576,384]{1,0:T(8,128)S(1)}, bf16[288,384]{1,0:T(8,128)(2,1)S(1)...) custom-call(s32[1]{0:T(128)} %bitcast.2.here, bf16[200,1024]{1,0:T(8,128)(2,1)S(1)} %collective-permute-done.11.refs_0_, ...), custom_call_target="tpu_custom_call" | custom-call | flops 1048576 | bytes 16384 | tf_op jit(solution)/shard_map/dispatch/pallas_call | solution.py:138
  53.9 3.8 %collective-permute-done.19.refs_1_ = bf16[288,384]{1,0:T(8,128)(2,1)S(1)} collective-permute-done((bf16[288,384]{1,0:T(8,128)(2,1)S(1)}, bf16[288,384]{1,0:T(8,128)(2,1)S(1)}, u32[]{:S(2)}, u32[]{:S(2)}) %collective-permute-start.19) | collective-permute-done | bytes 221216 | tf_op jit(solution)/shard_map/ppermute | solution.py:454
  57.7 3.4 %combine.7 = (bf16[288,768]{1,0:T(8,128)(2,1)S(1)}, bf16[288,1792]{1,0:T(8,128)(2,1)S(1)}, bf16[192,1024]{1,0:T(8,128)(2,1)S(1)}, bf16[192,1024]{1,0:T(8,128)(2,1)S(1)}) custom-call(s32[1]{0:T(128)} %bitcast.2.here, f32[576,384]{1,0:T(8,128)S(1)} %get-tuple-element.131.share, bf16[288,384]{1,0:T(8,128)(2,1)S(1)} %collective-permute-done.13.refs_0_, ...), custom_call_target="tpu_custom_call" | custom-call | flops 1048576 | bytes 16384 | tf_op jit(solution)/shard_map/combine/pallas_call | solution.py:203
  66.7 2.0 %dispatch.9 = (bf16[144,1024]{1,0:T(8,128)(2,1)S(1)}, bf16[144,1024]{1,0:T(8,128)(2,1)S(1)}, f32[288,384]{1,0:T(8,128)S(1)}, bf16[288,384]{1,0:T(8,128)(2,1)S(1)}, f32[8,192]{1,0:T(8,128)S(1)}) custom-call(s32[1]{0:T(128)} %bitcast.2.here, bf16[200,1024]{1,0:T(8,128)(2,1)S(1)} %collective-permute-done.15.refs_0_, bf16[384,1024]{1,0:T(8,128)(2,1)S(1)} %bitcast.28, ...), custom_call_target="tpu_custom_call" | custom-call | flops 1048576 | bytes 16384 | tf_op jit(solution)/shard_map/dispatch/pallas_call | solution.py:138
  69.3 4.2 %collective-permute-done.24.refs_1_ = bf16[288,384]{1,0:T(8,128)(2,1)S(1)} collective-permute-done((bf16[288,384]{1,0:T(8,128)(2,1)S(1)}, bf16[288,384]{1,0:T(8,128)(2,1)S(1)}, u32[]{:S(2)}, u32[]{:S(2)}) %collective-permute-start.24) | collective-permute-done | bytes 221216 | tf_op jit(solution)/shard_map/ppermute | solution.py:454
  73.5 3.4 %combine.8 = (bf16[288,768]{1,0:T(8,128)(2,1)S(1)}, bf16[288,1792]{1,0:T(8,128)(2,1)S(1)}, bf16[192,1024]{1,0:T(8,128)(2,1)S(1)}, bf16[192,1024]{1,0:T(8,128)(2,1)S(1)}) custom-call(s32[1]{0:T(128)} %bitcast.2.here, f32[576,384]{1,0:T(8,128)S(1)} %get-tuple-element.144.share, bf16[288,384]{1,0:T(8,128)(2,1)S(1)} %collective-permute-done.18.refs_0_, ...), custom_call_target="tpu_custom_call" | custom-call | flops 1048576 | bytes 16384 | tf_op jit(solution)/shard_map/combine/pallas_call | solution.py:203
  77.8 2.3 %combine.9 = (bf16[144,768]{1,0:T(8,128)(2,1)S(1)}, bf16[144,1792]{1,0:T(8,128)(2,1)S(1)}, bf16[192,512]{1,0:T(8,128)(2,1)S(1)}, bf16[192,512]{1,0:T(8,128)(2,1)S(1)}) custom-call(s32[1]{0:T(128)} %bitcast.2.here, f32[288,384]{1,0:T(8,128)S(1)} %get-tuple-element.154.share, bf16[288,384]{1,0:T(8,128)(2,1)S(1)} %collective-permute-done.23.refs_0_, ...), custom_call_target="tpu_custom_call" | custom-call | flops 1048576 | bytes 16384 | tf_op jit(solution)/shard_map/combine/pallas_call | solution.py:203
  80.1 4.5 %collective-permute-done.26.refs_2_ = bf16[192,512]{1,0:T(8,128)(2,1)S(1)} collective-permute-done((bf16[192,512]{1,0:T(8,128)(2,1)S(1)}, bf16[192,512]{1,0:T(8,128)(2,1)S(1)}, u32[]{:S(2)}, u32[]{:S(2)}) %collective-permute-start.26) | collective-permute-done | bytes 196640 | tf_op jit(solution)/shard_map/ppermute | solution.py:433
  88.9 4.8 %weights.2.old = bf16[1,1024,1152]{2,1,0:T(8,128)(2,1)} custom-call(s32[1]{0:T(128)} %bitcast.2.here, bf16[384,2304]{1,0:T(8,128)(2,1)S(1)} %hidden.1.left, bf16[144,1024]{1,0:T(8,128)(2,1)S(1)} %get-tuple-element.170.refs_0_, bf16[288,1024]{1,0:T(8,128)(2,1)S(1)} %get-tuple-element.171.refs_1_, bf16[288,1024]{1,0:T(8,128)(2,1)S(1)} %get-tuple-element.172.refs_2_, ...), custom_call_target="tpu_custom_call" | custom-call | flops 1048576 | bytes 16384 | tf_op jit(solution)/shard_map/weights/pallas_call | solution.py:401
  95.2 8.0 %weights.3 = bf16[1,1024,1152]{2,1,0:T(8,128)(2,1)} custom-call(s32[1]{0:T(128)} %bitcast.2.here, bf16[1,1024,1152]{2,1,0:T(8,128)(2,1)} %weights.2.old, bf16[1024,2304]{1,0:T(8,128)(2,1)S(1)} %turn.1.refs_0_, bf16[144,768]{1,0:T(8,128)(2,1)S(1)} %get-tuple-element.182.refs_1_, ...), custom_call_target="tpu_custom_call", output_to_operand_aliasing={{}: (1, {})} | custom-call | flops 1048576 | bytes 16384 | tf_op jit(solution)/shard_map/weights/pallas_call | solution.py:401
  105.5 7.4 %collective-permute-done.31.left = bf16[192,512]{1,0:T(8,128)(2,1)S(1)} collective-permute-done((bf16[192,512]{1,0:T(8,128)(2,1)S(1)}, bf16[192,512]{1,0:T(8,128)(2,1)S(1)}, u32[]{:S(2)}, u32[]{:S(2)}) %collective-permute-start.31) | collective-permute-done | bytes 196640 | tf_op jit(solution)/shard_map/ppermute | solution.py:433
  112.9 2.3 %collective-permute-done.34.right = bf16[192,512]{1,0:T(8,128)(2,1)S(1)} collective-permute-done((bf16[192,512]{1,0:T(8,128)(2,1)S(1)}, bf16[192,512]{1,0:T(8,128)(2,1)S(1)}, u32[]{:S(2)}, u32[]{:S(2)}) %collective-permute-start.34) | collective-permute-done | bytes 196640 | tf_op jit(solution)/shard_map/ppermute | solution.py:433
  (79 shorter events, 33.4 us)
Async XLA Ops:
  0.6 19.2 %collective-permute-start.3 = (bf16[2304,384]{1,0:T(8,128)(2,1)}, bf16[2304,384]{1,0:T(8,128)(2,1)S(1)}, u32[]{:S(2)}, u32[]{:S(2)}) collective-permute-start(bf16[2304,384]{1,0:T(8,128)(2,1)} %bitcast.9), channel_id=1, source_target_pairs={{0,1},{1,0},{2,3},{3,2},{4,5},{5,4},{6,7},{7,6},{8,9},{9,8},{10,11... | collective-permute-start | bytes 5308424 | tf_op jit(solution)/shard_map/ppermute | solution.py:433
  1.1 18.7 %collective-permute-start.4 = (bf16[2304,384]{1,0:T(8,128)(2,1)}, bf16[2304,384]{1,0:T(8,128)(2,1)S(1)}, u32[]{:S(2)}, u32[]{:S(2)}) collective-permute-start(bf16[2304,384]{1,0:T(8,128)(2,1)} %bitcast.16), channel_id=1, source_target_pairs={{0,1},{1,0},{2,3},{3,2},{4,5},{5,4},{6,7},{7,6},{8,9},{9,8},{10,11... | collective-permute-start | bytes 5308424 | tf_op jit(solution)/shard_map/ppermute | solution.py:433
  1.2 13.7 %collective-permute-start.2 = (bf16[384,1024]{1,0:T(8,128)(2,1)}, bf16[384,1024]{1,0:T(8,128)(2,1)}, u32[]{:S(2)}, u32[]{:S(2)}) collective-permute-start(bf16[384,1024]{1,0:T(8,128)(2,1)} %bitcast.23), channel_id=1, source_target_pairs={{0,1},{1,0},{2,3},{3,2},{4,5},{5,4},{6,7},{7,6},{8,9},{9,8},{10,11... | collective-permute-start | bytes 2359304 | tf_op jit(solution)/shard_map/ppermute | solution.py:433
  3.4 14.8 %collective-permute-start.1 = (bf16[200,1024]{1,0:T(8,128)(2,1)}, bf16[200,1024]{1,0:T(8,128)(2,1)}, u32[]{:S(2)}, u32[]{:S(2)}) collective-permute-start(bf16[200,1024]{1,0:T(8,128)(2,1)} %pack.1.refs_0_), channel_id=1, source_target_pairs={{0,2},{1,3},{2,0},{3,1},{4,6},{5,7},{6,4},{7,5},{8,10},{9,11},{10,... | collective-permute-start | bytes 1228808 | tf_op jit(solution)/shard_map/ppermute | solution.py:433
  6.1 13.7 %collective-permute-start = (bf16[200,1024]{1,0:T(8,128)(2,1)}, bf16[200,1024]{1,0:T(8,128)(2,1)}, u32[]{:S(2)}, u32[]{:S(2)}) collective-permute-start(bf16[200,1024]{1,0:T(8,128)(2,1)} %pack.1.refs_0_), channel_id=1, source_target_pairs={{0,4},{1,5},{2,6},{3,7},{4,8},{5,9},{6,10},{7,11},{8,12},{9,13},{1... | collective-permute-start | bytes 1228808 | tf_op jit(solution)/shard_map/ppermute | solution.py:433
  19.8 8.9 %collective-permute-start.9 = (bf16[1024,768]{1,0:T(8,128)(2,1)S(1)}, bf16[1024,768]{1,0:T(8,128)(2,1)S(1)}, u32[]{:S(2)}, u32[]{:S(2)}) collective-permute-start(bf16[1024,768]{1,0:T(8,128)(2,1)S(1)} %join.1.refs_6_.refs_7_), channel_id=1, source_target_pairs={{0,1},{1,0},{2,3},{3,2},{4,5},{5,4},{6,7},{7,6},{8,9},{9,8},{10,11... | collective-permute-start | bytes 4718600 | tf_op jit(solution)/shard_map/ppermute | solution.py:433
  19.8 12.8 %collective-permute-start.6 = (bf16[200,1024]{1,0:T(8,128)(2,1)}, bf16[200,1024]{1,0:T(8,128)(2,1)S(1)}, u32[]{:S(2)}, u32[]{:S(2)}) collective-permute-start(bf16[200,1024]{1,0:T(8,128)(2,1)} %collective-permute-done.refs_1_), channel_id=1, source_target_pairs={{0,2},{1,3},{2,0},{3,1},{4,6},{5,7},{6,4},{7,5},{8,10},{9,11},{10,... | collective-permute-start | bytes 1228808 | tf_op jit(solution)/shard_map/ppermute | solution.py:433
  20.4 13.5 %collective-permute-start.5 = (bf16[200,1024]{1,0:T(8,128)(2,1)}, bf16[200,1024]{1,0:T(8,128)(2,1)S(1)}, u32[]{:S(2)}, u32[]{:S(2)}) collective-permute-start(bf16[200,1024]{1,0:T(8,128)(2,1)} %collective-permute-done.refs_1_), channel_id=1, source_target_pairs={{0,4},{1,5},{2,6},{3,7},{4,8},{5,9},{6,10},{7,11},{8,12},{9,13},{1... | collective-permute-start | bytes 1228808 | tf_op jit(solution)/shard_map/ppermute | solution.py:433
  34.0 14.9 %collective-permute-start.12 = (bf16[144,1792]{1,0:T(8,128)(2,1)S(1)}, bf16[144,1792]{1,0:T(8,128)(2,1)S(1)}, u32[]{:S(2)}, u32[]{:S(2)}) collective-permute-start(bf16[144,1792]{1,0:T(8,128)(2,1)S(1)} %get-tuple-element.113), channel_id=1, source_target_pairs={{0,1},{1,0},{2,3},{3,2},{4,5},{5,4},{6,7},{7,6},{8,9},{9,8},{10,11... | collective-permute-start | bytes 1548296 | tf_op jit(solution)/shard_map/ppermute | solution.py:433
  34.0 13.8 %collective-permute-start.11 = (bf16[200,1024]{1,0:T(8,128)(2,1)S(1)}, bf16[200,1024]{1,0:T(8,128)(2,1)S(1)}, u32[]{:S(2)}, u32[]{:S(2)}) collective-permute-start(bf16[200,1024]{1,0:T(8,128)(2,1)S(1)} %collective-permute-done.5.refs_1_), channel_id=1, source_target_pairs={{0,2},{1,3},{2,0},{3,1},{4,6},{5,7},{6,4},{7,5},{8,10},{9,11},{10,... | collective-permute-start | bytes 1228808 | tf_op jit(solution)/shard_map/ppermute | solution.py:433
  35.5 13.4 %collective-permute-start.10 = (bf16[200,1024]{1,0:T(8,128)(2,1)S(1)}, bf16[200,1024]{1,0:T(8,128)(2,1)S(1)}, u32[]{:S(2)}, u32[]{:S(2)}) collective-permute-start(bf16[200,1024]{1,0:T(8,128)(2,1)S(1)} %collective-permute-done.5.refs_1_), channel_id=1, source_target_pairs={{0,4},{1,5},{2,6},{3,7},{4,8},{5,9},{6,10},{7,11},{8,12},{9,13},{1... | collective-permute-start | bytes 1228808 | tf_op jit(solution)/shard_map/ppermute | solution.py:433
  48.9 13.6 %collective-permute-start.17 = (bf16[288,1792]{1,0:T(8,128)(2,1)S(1)}, bf16[288,1792]{1,0:T(8,128)(2,1)S(1)}, u32[]{:S(2)}, u32[]{:S(2)}) collective-permute-start(bf16[288,1792]{1,0:T(8,128)(2,1)S(1)} %get-tuple-element.127), channel_id=1, source_target_pairs={{0,1},{1,0},{2,3},{3,2},{4,5},{5,4},{6,7},{7,6},{8,9},{9,8},{10,11... | collective-permute-start | bytes 3096584 | tf_op jit(solution)/shard_map/ppermute | solution.py:433
  48.9 13.6 %collective-permute-start.15 = (bf16[200,1024]{1,0:T(8,128)(2,1)S(1)}, bf16[200,1024]{1,0:T(8,128)(2,1)S(1)}, u32[]{:S(2)}, u32[]{:S(2)}) collective-permute-start(bf16[200,1024]{1,0:T(8,128)(2,1)S(1)} %collective-permute-done.10.refs_1_), channel_id=1, source_target_pairs={{0,2},{1,3},{2,0},{3,1},{4,6},{5,7},{6,4},{7,5},{8,10},{9,11},{10,... | collective-permute-start | bytes 1228808 | tf_op jit(solution)/shard_map/ppermute | solution.py:433
  49.4 13.0 %collective-permute-start.16 = (bf16[192,1024]{1,0:T(8,128)(2,1)S(1)}, bf16[192,1024]{1,0:T(8,128)(2,1)S(1)}, u32[]{:S(2)}, u32[]{:S(2)}) collective-permute-start(bf16[192,1024]{1,0:T(8,128)(2,1)S(1)} %get-tuple-element.126), channel_id=1, source_target_pairs={{0,4},{1,5},{2,6},{3,7},{4,8},{5,9},{6,10},{7,11},{8,12},{9,13},{1... | collective-permute-start | bytes 1179656 | tf_op jit(solution)/shard_map/ppermute | solution.py:433
  62.5 14.7 %collective-permute-start.22 = (bf16[288,1792]{1,0:T(8,128)(2,1)S(1)}, bf16[288,1792]{1,0:T(8,128)(2,1)S(1)}, u32[]{:S(2)}, u32[]{:S(2)}) collective-permute-start(bf16[288,1792]{1,0:T(8,128)(2,1)S(1)} %get-tuple-element.141), channel_id=1, source_target_pairs={{0,1},{1,0},{2,3},{3,2},{4,5},{5,4},{6,7},{7,6},{8,9},{9,8},{10,11... | collective-permute-start | bytes 3096584 | tf_op jit(solution)/shard_map/ppermute | solution.py:433
  62.5 14.4 %collective-permute-start.21 = (bf16[192,1024]{1,0:T(8,128)(2,1)S(1)}, bf16[192,1024]{1,0:T(8,128)(2,1)S(1)}, u32[]{:S(2)}, u32[]{:S(2)}) collective-permute-start(bf16[192,1024]{1,0:T(8,128)(2,1)S(1)} %get-tuple-element.140), channel_id=1, source_target_pairs={{0,2},{1,3},{2,0},{3,1},{4,6},{5,7},{6,4},{7,5},{8,10},{9,11},{10,... | collective-permute-start | bytes 1179656 | tf_op jit(solution)/shard_map/ppermute | solution.py:433
  64.0 13.1 %collective-permute-start.20 = (bf16[192,1024]{1,0:T(8,128)(2,1)S(1)}, bf16[192,1024]{1,0:T(8,128)(2,1)S(1)}, u32[]{:S(2)}, u32[]{:S(2)}) collective-permute-start(bf16[192,1024]{1,0:T(8,128)(2,1)S(1)} %get-tuple-element.139), channel_id=1, source_target_pairs={{0,4},{1,5},{2,6},{3,7},{4,8},{5,9},{6,10},{7,11},{8,12},{9,13},{1... | collective-permute-start | bytes 1179656 | tf_op jit(solution)/shard_map/ppermute | solution.py:433
  84.6 9.1 %collective-permute-start.29 = (bf16[192,512]{1,0:T(8,128)(2,1)S(1)}, bf16[192,512]{1,0:T(8,128)(2,1)S(1)}, u32[]{:S(2)}, u32[]{:S(2)}) collective-permute-start(bf16[192,512]{1,0:T(8,128)(2,1)S(1)} %add.7), channel_id=1, source_target_pairs={{0,2},{1,3},{2,0},{3,1},{4,6},{5,7},{6,4},{7,5},{8,10},{9,11},{10,... | collective-permute-start | bytes 589832 | tf_op jit(solution)/shard_map/ppermute | solution.py:433
  85.2 18.0 %collective-permute-start.25 = (bf16[192,512]{1,0:T(8,128)(2,1)S(1)}, bf16[192,512]{1,0:T(8,128)(2,1)S(1)}, u32[]{:S(2)}, u32[]{:S(2)}) collective-permute-start(bf16[192,512]{1,0:T(8,128)(2,1)S(1)} %get-tuple-element.161), channel_id=1, source_target_pairs={{0,2},{1,3},{2,0},{3,1},{4,6},{5,7},{6,4},{7,5},{8,10},{9,11},{10,... | collective-permute-start | bytes 589832 | tf_op jit(solution)/shard_map/ppermute | solution.py:433
  86.7 17.6 %collective-permute-start.32 = (bf16[192,512]{1,0:T(8,128)(2,1)S(1)}, bf16[192,512]{1,0:T(8,128)(2,1)S(1)}, u32[]{:S(2)}, u32[]{:S(2)}) collective-permute-start(bf16[192,512]{1,0:T(8,128)(2,1)S(1)} %get-tuple-element.189), channel_id=1, source_target_pairs={{0,2},{1,3},{2,0},{3,1},{4,6},{5,7},{6,4},{7,5},{8,10},{9,11},{10,... | collective-permute-start | bytes 589832 | tf_op jit(solution)/shard_map/ppermute | solution.py:433
  87.3 15.9 %collective-permute-start.28 = (bf16[192,512]{1,0:T(8,128)(2,1)S(1)}, bf16[192,512]{1,0:T(8,128)(2,1)S(1)}, u32[]{:S(2)}, u32[]{:S(2)}) collective-permute-start(bf16[192,512]{1,0:T(8,128)(2,1)S(1)} %add.8), channel_id=1, source_target_pairs={{0,4},{1,5},{2,6},{3,7},{4,8},{5,9},{6,10},{7,11},{8,12},{9,13},{1... | collective-permute-start | bytes 589832 | tf_op jit(solution)/shard_map/ppermute | solution.py:433
  93.8 10.4 %collective-permute-start.33 = (bf16[192,512]{1,0:T(8,128)(2,1)S(1)}, bf16[192,512]{1,0:T(8,128)(2,1)S(1)}, u32[]{:S(2)}, u32[]{:S(2)}) collective-permute-start(bf16[192,512]{1,0:T(8,128)(2,1)S(1)} %add.10), channel_id=1, source_target_pairs={{0,4},{1,5},{2,6},{3,7},{4,8},{5,9},{6,10},{7,11},{8,12},{9,13},{1... | collective-permute-start | bytes 589832 | tf_op jit(solution)/shard_map/ppermute | solution.py:433
  103.2 9.7 %collective-permute-start.31 = (bf16[192,512]{1,0:T(8,128)(2,1)S(1)}, bf16[192,512]{1,0:T(8,128)(2,1)S(1)}, u32[]{:S(2)}, u32[]{:S(2)}) collective-permute-start(bf16[192,512]{1,0:T(8,128)(2,1)S(1)} %add.9), channel_id=1, source_target_pairs={{0,4},{1,5},{2,6},{3,7},{4,8},{5,9},{6,10},{7,11},{8,12},{9,13},{1... | collective-permute-start | bytes 589832 | tf_op jit(solution)/shard_map/ppermute | solution.py:433
  104.3 10.9 %collective-permute-start.34 = (bf16[192,512]{1,0:T(8,128)(2,1)S(1)}, bf16[192,512]{1,0:T(8,128)(2,1)S(1)}, u32[]{:S(2)}, u32[]{:S(2)}) collective-permute-start(bf16[192,512]{1,0:T(8,128)(2,1)S(1)} %add.11), channel_id=1, source_target_pairs={{0,4},{1,5},{2,6},{3,7},{4,8},{5,9},{6,10},{7,11},{8,12},{9,13},{1... | collective-permute-start | bytes 589832 | tf_op jit(solution)/shard_map/ppermute | solution.py:433
  (16 other events, 119.7 us)

commit v7 on v6

--- a/solution.py
+++ b/solution.py
@@ -153,11 +153,8 @@
         pos, *refs = refs[1:]
     else:
         peer0, peer1, pos, *refs = refs
-    saved, (w0, w1, rec1), (gp0, both) = refs[:4], refs[4:7], refs[7:9]
-    backs, (held, sems) = refs[9:-2], refs[-2:]
-    d = rec1.shape[1]
-    gp1 = both.at[:, d:]
-    both[:, :d] = rec1[...]
+    saved, (w0, w1), (gp0, gp1) = refs[:4], refs[4:6], refs[6:8]
+    backs, (held, sems) = refs[8:-2], refs[-2:]
     h = share.shape[1]
     copies = []
     for a in range(2):
@@ -194,22 +191,22 @@
             backs[rel][...] = sums[rel].astype(bf16)
 
 
-def combine(here, chunk, share, peers, pos, saved0, saved1, w0, w1, rec1, cap, halves=False):
+def combine(here, chunk, share, peers, pos, saved0, saved1, w0, w1, cap, halves=False):
     n = len(chunk)
     h = share.shape[1]
     d = w0.shape[0]
     tok = pos.shape[1]
-    outs = [(n * cap, 2 * h), (n * cap, d + 2 * h)] + ([(tok, d // 2)] * 2 if halves else [(tok, d)] * n)
+    outs = [(n * cap, 2 * h)] * 2 + ([(tok, d // 2)] * 2 if halves else [(tok, d)] * n)
     return pl.pallas_call(
         functools.partial(combine_kernel, chunk, cap),
         out_shape=[jax.ShapeDtypeStruct(s, bf16) for s in outs],
-        in_specs=[on_scalar] + [on_chip] * (2 + len(peers)) + [anywhere] * 4 + [on_chip] * 3,
+        in_specs=[on_scalar] + [on_chip] * (2 + len(peers)) + [anywhere] * 4 + [on_chip] * 2,
         out_specs=[on_chip] * len(outs),
         scratch_shapes=[pltpu.VMEM((4 * n, cap, h), bf16), pltpu.SemaphoreType.DMA((4 * n,))],
         cost_estimate=light,
         compiler_params=params(20),
         name="combine",
-    )(here, share, *peers, pos, *saved0, *saved1, w0, w1, rec1)
+    )(here, share, *peers, pos, *saved0, *saved1, w0, w1)
 
 
 def join_kernel(left, right, out):
@@ -275,44 +272,63 @@
     return pltpu.with_memory_space_constraint(v, pltpu.HBM)
 
 
-def hidden_kernel(gate, up, out):
-    gate_pre = gate[...].astype(f32)
-    out[...] = (gate_pre * jax.nn.sigmoid(gate_pre) * up[...].astype(f32)).astype(bf16).T
-
-
-def hidden(gate, up):
+def hidden_kernel(cap, here, gate, up, out, held, sems):
+    copies = []
+    for k, v in enumerate((gate, up)):
+        for q in range(held.shape[1] // cap):
+            rows = pl.ds(pl.multiple_of((2 * q + lax.rem(here[0], 2)) * cap, 16), cap)
+            to = held.at[k, pl.ds(q * cap, cap), :]
+            copies.append(pltpu.make_async_copy(v.at[rows, :], to, sems.at[len(copies)]))
+    for c in copies:
+        c.start()
+    for c in copies:
+        c.wait()
+    gate_pre = held[0].astype(f32)
+    out[...] = (gate_pre * jax.nn.sigmoid(gate_pre) * held[1].astype(f32)).astype(bf16).T
+
+
+def hidden(here, gate, up, cap):
     rows, h = gate.shape
-    tile = 768
-    spec = pl.BlockSpec((tile, h), lambda i: (i, 0))
-    return pl.pallas_call(
-        hidden_kernel,
+    rows = rows // 2
+    return pl.pallas_call(
+        functools.partial(hidden_kernel, cap),
         out_shape=jax.ShapeDtypeStruct((h, rows), bf16),
-        grid=(rows // tile,),
-        in_specs=[spec, spec],
-        out_specs=pl.BlockSpec((h, tile), lambda i: (0, i)),
-        cost_estimate=light,
-        compiler_params=params(12),
+        in_specs=[on_scalar, anywhere, anywhere],
+        out_specs=on_chip,
+        scratch_shapes=[pltpu.VMEM((2, rows, h), bf16), pltpu.SemaphoreType.DMA((2 * rows // cap,))],
+        cost_estimate=light,
+        compiler_params=params(16),
         name="hidden",
-    )(in_hbm(gate), in_hbm(up))
-
-
-def turn_kernel(v, out):
-    out[...] = v[...].T
-
-
-def turn(v):
-    rows, d = v.shape
+    )(here, gate, up)
+
+
+def turn_kernel(cap, here, v, own, other, held):
+    for k, out in enumerate((own, other)):
+        plane = lax.rem(here[0] + k, 2)
+        for q in range(held.shape[0] // cap):
+            held[q * cap : (q + 1) * cap, :] = v[pl.ds(pl.multiple_of((2 * q + plane) * cap, 16), cap), :]
+        out[...] = held[...].T
+
+
+def turn(here, v, cap):
+    slots, d = v.shape
+    rows = slots // 2
     tile = 256
-    return pl.pallas_call(
-        turn_kernel,
-        out_shape=jax.ShapeDtypeStruct((d, rows), v.dtype),
-        grid=(d // tile,),
-        in_specs=[pl.BlockSpec((rows, tile), lambda i: (0, i))],
-        out_specs=pl.BlockSpec((tile, rows), lambda i: (i, 0)),
+    out = pl.BlockSpec((tile, rows), lambda i, here: (i, 0))
+    return pl.pallas_call(
+        functools.partial(turn_kernel, cap),
+        out_shape=[jax.ShapeDtypeStruct((d, rows), v.dtype)] * 2,
+        grid_spec=pltpu.PrefetchScalarGridSpec(
+            num_scalar_prefetch=1,
+            grid=(d // tile,),
+            in_specs=[pl.BlockSpec((slots, tile), lambda i, here: (0, i))],
+            out_specs=[out, out],
+            scratch_shapes=[pltpu.VMEM((rows, tile), v.dtype)],
+        ),
         cost_estimate=light,
         compiler_params=params(12),
         name="turn",
-    )(in_hbm(v))
+    )(here, in_hbm(v))
 
 
 def pack_kernel(line, tokens, routes, codes, out, named, sems):
@@ -345,74 +361,87 @@
     )(in_hbm(tokens), in_hbm(routes), in_hbm(codes))
 
 
-def weights_kernel(order, cap, starts, left_whole, here, left, *refs):
-    pieces, out, held, sems = refs[:-3], refs[-3], refs[-2], refs[-1]
+def weights_kernel(order, cap, count, here, inputs, hid, *refs):
+    recs, gps, refs = refs[:count], refs[count : 2 * count], refs[2 * count :]
+    summed, (out, rs, gs, rec_sems, gp_sems) = refs[:-5], refs[-5:]
     i = pl.program_id(0)
-    wide = held.shape[2]
-
-    def copies(step):
-        slot = lax.rem(step, 2) if left_whole else 0
+    tile = rs.shape[2]
+
+    def copies(pieces, column, to, sems):
         made = []
-        for r, first in zip(pieces, starts):
-            column = pl.ds(pl.multiple_of(first + step * wide, 128), wide) if left_whole else pl.ds(first, wide)
+        for r in pieces:
             for at in range(0, r.shape[0], cap):
-                k, other, plane = order[len(made)]
-                src = jnp.bitwise_xor(source(here[0], k, other), plane)
-                to = held.at[slot, pl.ds(pl.multiple_of(src * cap, 16), cap), :]
-                made.append(pltpu.make_async_copy(r.at[pl.ds(at, cap), column], to, sems.at[slot, len(made)]))
+                src = source(here[0], *order[len(made)])
+                rows = pl.ds(pl.multiple_of((src // 2) * cap, 16), cap)
+                made.append(pltpu.make_async_copy(r.at[pl.ds(at, cap), column], to.at[rows, :], sems.at[len(made)]))
         return made
+
+    def received(step):
+        slot = lax.rem(step, 2)
+        return copies(recs, pl.ds(pl.multiple_of(step * tile, 128), tile), rs.at[slot], rec_sems.at[slot])
+
+    fixed = copies(gps, pl.ds(0, gs.shape[1]), gs, gp_sems)
 
     @pl.when(i == 0)
     def _():
-        for c in copies(i):
+        for c in fixed + received(i):
             c.start()
 
-    if left_whole:
-        @pl.when(i + 1 < pl.num_programs(0))
-        def _():
-            for c in copies(i + 1):
-                c.start()
-
-        for c in copies(i):
+    @pl.when(i + 1 < pl.num_programs(0))
+    def _():
+        for c in received(i + 1):
+            c.start()
+
+    @pl.when(i == 0)
+    def _():
+        for c in fixed:
             c.wait()
-        part = jnp.dot(left[...], held[lax.rem(i, 2)], preferred_element_type=f32)
-        out[0] = (part * loss_scale).astype(bf16).T
+
+    wide = gs.shape[1]
+    left = jnp.dot(inputs[...], gs[...], preferred_element_type=f32)
+    for c in received(i):
+        c.wait()
+    right = jnp.dot(hid[...], rs[lax.rem(i, 2)], preferred_element_type=f32)
+    if summed:
+        other = summed[0]
+        out[0, :, :wide] = ((left + other[:, :wide].astype(f32)) * loss_scale).astype(bf16)
+        out[0, :, wide:] = ((right.T + other[:, wide:].astype(f32)) * loss_scale).astype(bf16)
     else:
-        @pl.when(i == 0)
-        def _():
-            for c in copies(i):
-                c.wait()
-
-        part = jnp.dot(left[...], held[0], preferred_element_type=f32)
-        out[0] = (part * loss_scale).astype(bf16)
-
-
-def weight_sums(here, order, left, pieces, starts, left_whole, into, cap, d):
-    rows, slots = left.shape
-    tile = 256
-    h = rows if left_whole else (pieces[0].shape[1] // 2)
-    wide, at = (h, 2) if left_whole else (2 * h, 0)
-    kernel = functools.partial(weights_kernel, order, cap, starts, left_whole)
-    body = kernel if into is None else (lambda here, old, *refs: kernel(here, *refs))
-    left_spec = pl.BlockSpec((rows, slots), lambda i, here: (0, 0))
-    if not left_whole:
-        left_spec = pl.BlockSpec((tile, slots), lambda i, here: (i, 0))
-    held = (2, slots, tile) if left_whole else (1, slots, wide)
-    return pl.pallas_call(
-        body,
-        out_shape=jax.ShapeDtypeStruct((1, d, 3 * h), bf16),
+        out[:, :wide] = left.astype(bf16)
+        out[:, wide:] = right.astype(bf16).T
+
+
+def weight_sums(here, order, inputs, hid, recs, gps, cap, summed=None):
+    d, slots = inputs.shape
+    h = hid.shape[0]
+    tile = 512
+    block = pl.BlockSpec((tile, 3 * h), lambda i, here: (i, 0))
+    given = [] if summed is None else [summed]
+    last = summed is not None
+    return pl.pallas_call(
+        functools.partial(weights_kernel, order, cap, len(recs)),
+        out_shape=jax.ShapeDtypeStruct((1, d, 3 * h) if last else (d, 3 * h), bf16),
         grid_spec=pltpu.PrefetchScalarGridSpec(
             num_scalar_prefetch=1,
             grid=(d // tile,),
-            in_specs=[anywhere] * (into is not None) + [left_spec] + [anywhere] * len(pieces),
-            out_specs=pl.BlockSpec((1, tile, wide), lambda i, here: (0, i, at)),
-            scratch_shapes=[pltpu.VMEM(held, bf16), pltpu.SemaphoreType.DMA((2, len(order)))],
+            in_specs=[
+                pl.BlockSpec((tile, slots), lambda i, here: (i, 0)),
+                pl.BlockSpec((h, slots), lambda i, here: (0, 0)),
+            ]
+            + [anywhere] * (2 * len(recs))
+            + [block] * len(given),
+            out_specs=pl.BlockSpec((1, tile, 3 * h), lambda i, here: (0, i, 0)) if last else block,
+            scratch_shapes=[
+                pltpu.VMEM((2, slots, tile), bf16),
+                pltpu.VMEM((slots, 2 * h), bf16),
+                pltpu.SemaphoreType.DMA((2, len(order))),
+                pltpu.SemaphoreType.DMA((len(order),)),
+            ],
         ),
-        input_output_aliases={} if into is None else {1: 0},
-        cost_estimate=light,
-        compiler_params=params(20),
+        cost_estimate=light,
+        compiler_params=params(28),
         name="weights",
-    )(here, *([] if into is None else [into]), left, *pieces)
+    )(here, inputs, hid, *recs, *gps, *given)
 
 
 def together(*values):
@@ -442,70 +471,67 @@
     wd, sg, su = w_down[0], saved_gate[0], saved_up[0]
     wd_c, sg_c, su_c = [send(v, to_core) for v in (wd, sg, su)]
 
-    order, recs, gps = [], [], []
+    order, recs, recs_c, gps, gps_c = [], [], [], [], []
 
     def first(chunk, toks):
         rec, rec_c, share, *shares, pos = dispatch(here, toks, wd, wd_c, cap)
-        order.extend((k, col, 0) for col, k in chunk)
+        order.extend((k, col) for col, k in chunk)
         recs.append(rec)
-        return (chunk, share, pos, rec_c), *shares
+        recs_c.append(rec_c)
+        return (chunk, share, pos), *shares
 
     def exchange(v):
         return lax.ppermute(v, "dp", [(0, 1), (1, 0)])
 
     def second(state, *peers, halves=False):
-        chunk, share, pos, rec_c = state
-        gp, both, *sums = combine(here, chunk, share, peers, pos, (sg, su), (sg_c, su_c), w, w_c, rec_c, cap, halves)
+        chunk, share, pos = state
+        gp, gp_c, *sums = combine(here, chunk, share, peers, pos, (sg, su), (sg_c, su_c), w, w_c, cap, halves)
         gps.append(gp)
-        return both, *sums
+        gps_c.append(gp_c)
+        return sums
 
     r1, x0 = ring(block), send(block, to_x)
     c0, h0 = first([(0, 0)], [block])
     w = join(w_gate[0], w_up[0])
-    hid, inputs = hidden(sg, su), turn(saved_inputs[0])
-    r1, x0, h0, w, hid, inputs, sg_c, su_c = together(r1, x0, h0, w, hid, inputs, sg_c, su_c)
+    inputs, inputs_away = turn(here, saved_inputs[0], cap)
+    r1, x0, h0, w, inputs, inputs_away, sg_c, su_c = together(r1, x0, h0, w, inputs, inputs_away, sg_c, su_c)
     r2, x1 = ring(r1), send(r1, to_x)
     h0, w_c = exchange(h0), send(w, to_core)
     c1, h1, g1 = first([(1, 0), (0, 1)], [x0, r1])
     h1 = exchange(h1)
-    both0, t_r0 = second(c0, h0)
-    r2, x1, h1, g1, t_r0, both0 = together(r2, x1, h1, g1, t_r0, both0)
+    (t_r0,) = second(c0, h0)
+    r2, x1, h1, g1, t_r0 = together(r2, x1, h1, g1, t_r0)
     r3, x2 = ring(r2), send(r2, to_x)
-    g1 = exchange(g1)
+    g1, inputs_c = exchange(g1), send(inputs_away, to_core)
     c2, h2, g2 = first([(1, 1), (0, 2)], [x1, r2])
-    h2, p0 = exchange(h2), send(both0, to_core)
-    both1, t_x0, t_r1 = second(c1, h1, g1)
-    r3, x2, p0, h2, g2, t_x0, t_r1, both1 = together(r3, x2, p0, h2, g2, t_x0, t_r1, both1)
+    h2 = exchange(h2)
+    t_x0, t_r1 = second(c1, h1, g1)
+    hid = hidden(here, sg, su, cap)
+    r3, x2, h2, g2, t_x0, t_r1, inputs_c, hid = together(r3, x2, h2, g2, t_x0, t_r1, inputs_c, hid)
     x3, w1 = send(r3, to_x), ring(t_r1)
     g2 = exchange(g2)
     c3, h3, g3 = first([(1, 2), (0, 3)], [x2, r3])
-    h3, p1 = exchange(h3), send(both1, to_core)
-    both2, t_x1, t_r2 = second(c2, h2, g2)
-    x3, w1, p1, h3, g3, t_x1, t_r2, both2 = together(x3, w1, p1, h3, g3, t_x1, t_r2, both2)
+    h3 = exchange(h3)
+    t_x1, t_r2 = second(c2, h2, g2)
+    hid_c = hidden(here, sg_c, su_c, cap)
+    x3, w1, h3, g3, t_x0, t_x1, t_r2, hid_c = together(x3, w1, h3, g3, t_x0, t_x1, t_r2, hid_c)
     u1, b0 = ring(t_x1), send(t_x0, to_x)
     g3 = exchange(g3)
     c4, h4 = first([(1, 3)], [x3])
-    h4, p2 = exchange(h4), send(both2, to_core)
-    both3, t_x2, t_r3 = second(c3, h3, g3)
-    u1, b0, p2, h4, t_x2, t_r3, both3 = together(u1, b0, p2, h4, t_x2, t_r3, both3)
+    h4 = exchange(h4)
+    t_x2, t_r3 = second(c3, h3, g3)
+    u1, b0, h4, t_x2, t_r3 = together(u1, b0, h4, t_x2, t_r3)
     a0, a1, h4 = together(add([t_x2, u1], 0), add([t_x2, u1], 1), h4)
     b2 = [send(a0, to_x), send(a1, to_x)]
-    p3 = send(both3, to_core)
-    both4, *t_x3 = second(c4, h4, halves=True)
+    t_x3 = second(c4, h4, halves=True)
     b3 = [send(t, to_x) for t in t_x3]
-    b2[0], p3, both4, _ = together(b2[0], p3, both4, t_x3[0])
-    p4 = send(both4, to_core)
-    away = [p0, p1, p2, p3, p4]
-    order_all = order + [(k, col, 1) for k, col, _ in order]
-    zeros, skip = [0] * len(recs), [d] * len(recs)
-
-    w2 = [ring(add([t_r2, w1, b2[0]], 0))]
-    part = weight_sums(here, order_all, hid, recs + away, zeros + zeros, True, None, cap, d)
-    b2[1], part = together(b2[1], part)
-    w2.append(ring(add([t_r2, w1, b2[1]], 1)))
-    weight_grads = weight_sums(here, order_all, inputs, gps + away, zeros + skip, False, part, cap, d)
-    b3[0], w2[0], weight_grads = together(b3[0], w2[0], weight_grads)
-    w3 = [ring(add([t_r3, b3[0], w2[0]], 0)), ring(add([t_r3, b3[1], w2[1]], 1))]
+    away = weight_sums(here, order, inputs_c, hid_c, recs_c, gps_c, cap)
+    b2[0], away = together(b2[0], away)
+    summed = send(away, to_core)
+    w2 = [ring(add([t_r2, w1, b2[k]], k)) for k in range(2)]
+    w3 = [ring(add([t_r3, b3[k], w2[k]], k)) for k in range(2)]
+    weight_grads = weight_sums(here, order, inputs, hid, recs, gps, cap, summed)
+    w3[1], weight_grads = together(w3[1], weight_grads)
     return (finish(t_r0, b0, *w3), weight_grads)
 
 

time: 117 us -> 117 us (level)
  waiting for transfers between devices: 37.2 us -> 24.7 us
  Pallas kernels: 49.5 us -> 56.3 us
  starting transfers between devices: 27.5 us -> 32.7 us
  local copies, waits for them, and re-layouts: 0.97 us -> 2.28 us
    ppermute x8, waiting for transfers between devices: 18.3 us -> 8.23 us  [exchange(): return lax.ppermute(v, 'dp', [(0, 1), (1, 0)])]
    pallas_call x4 -> x5, Pallas kernels: 19.9 us -> 26.9 us  [the longest x2 17.3 us: weight_sums(): pl.pallas_call(functools.partial(weights_kernel, order, cap, len(recs)),...]
    ppermute x27 -> x24, starting transfers between devices: 19.2 us -> 23.3 us  [send(): return lax.ppermute(v, 'expert', perm)]
    ppermute x27 -> x24, waiting for transfers between devices: 18.9 us -> 16.5 us  [send(): return lax.ppermute(v, 'expert', perm)]
    unnamed x10, local copies, waits for them, and re-layouts: 0.97 us -> 2.28 us
  transfers between devices with their start and end apart: 35 -> 32, of which waited for: 15 -> 10; matrix products, arithmetic and copies ran while one was open for 0% -> 0% of each run, Pallas kernels for 42% -> 47%
where the time goes in v7:
time: 117 us
  Pallas kernels  56.3 us (48%)
  starting transfers between devices  32.7 us (28%)
  waiting for transfers between devices  24.7 us (21%)
  local copies, waits for them, and re-layouts  2.28 us (2%)
    ppermute x24, starting transfers between devices, send(): return lax.ppermute(v, 'expert', perm)  23.3 us
    pallas_call x2, Pallas kernels, weight_sums(): pl.pallas_call(functools.partial(weights_kernel, order, cap, len(recs)),...  17.3 us
    ppermute x24, waiting for transfers between devices, send(): return lax.ppermute(v, 'expert', perm)  16.5 us
    pallas_call x5, Pallas kernels, combine(): pl.pallas_call(functools.partial(combine_kernel, chunk, cap), out_shape=[...  14.6 us
    pallas_call x5, Pallas kernels, dispatch(): pl.pallas_call(functools.partial(dispatch_kernel, n, cap), out_shape=[jax...  11.6 us
    ppermute x8, starting transfers between devices, exchange(): return lax.ppermute(v, 'dp', [(0, 1), (1, 0)])  9.31 us
    ppermute x8, waiting for transfers between devices, exchange(): return lax.ppermute(v, 'dp', [(0, 1), (1, 0)])  8.23 us
    pallas_call x2, Pallas kernels, hidden(): pl.pallas_call(functools.partial(hidden_kernel, cap), out_shape=jax.Shape...  5.77 us
  transfers between devices with their start and end apart: 32, of which 10 were waited for; matrix products, arithmetic and copies ran while one was open for 0% of the time, Pallas kernels for 47%

profile of v7, /device:TPU:0, one launch (start us, length us, event | category | flops | bytes accessed | tf_op | source)
XLA Modules:
  0.0 116.9 jit_solution(15792716126416532505)
XLA Ops:
  3.4 2.6 %collective-permute-start.1 = (bf16[200,1024]{1,0:T(8,128)(2,1)}, bf16[200,1024]{1,0:T(8,128)(2,1)}, u32[]{:S(2)}, u32[]{:S(2)}) collective-permute-start(bf16[200,1024]{1,0:T(8,128)(2,1)} %pack.1.refs_0_), channel_id=1, source_target_pairs={{0,2},{1,3},{2,0},{3,1},{4,6},{5,7},{6,4},{7,5},{8,10},{9,11},{10,... | collective-permute-start | bytes 1228808 | tf_op jit(solution)/shard_map/ppermute | solution.py:462
  10.1 3.8 %turn.1 = (bf16[1024,1152]{1,0:T(8,128)(2,1)S(1)}, bf16[1024,1152]{1,0:T(8,128)(2,1)S(1)}) custom-call(s32[1]{0:T(128)} %bitcast.2.here, bf16[2304,1024]{1,0:T(8,128)(2,1)} %bitcast.31), custom_call_target="tpu_custom_call" | custom-call | flops 1048576 | bytes 16384 | tf_op jit(solution)/shard_map/turn/pallas_call | solution.py:318
  13.9 2.3 %dispatch.5 = (bf16[144,1024]{1,0:T(8,128)(2,1)S(1)}, bf16[144,1024]{1,0:T(8,128)(2,1)S(1)}, f32[288,384]{1,0:T(8,128)S(1)}, bf16[288,384]{1,0:T(8,128)(2,1)S(1)}, f32[8,192]{1,0:T(8,128)S(1)}) custom-call(s32[1]{0:T(128)} %bitcast.2.here, bf16[200,1024]{1,0:T(8,128)(2,1)} %pack.1.refs_0_, bf16[384,1024]{1,0:T(8,128)(2,1)S(1)} %bitcast.24, ...), custom_call_target="tpu_custom_call" | custom-call | flops 1048576 | bytes 16384 | tf_op jit(solution)/shard_map/dispatch/pallas_call | solution.py:138
  16.4 3.4 %collective-permute-done.refs_1_ = bf16[200,1024]{1,0:T(8,128)(2,1)} collective-permute-done((bf16[200,1024]{1,0:T(8,128)(2,1)}, bf16[200,1024]{1,0:T(8,128)(2,1)}, u32[]{:S(2)}, u32[]{:S(2)}) %collective-permute-start) | collective-permute-done | bytes 409632 | tf_op jit(solution)/shard_map/ppermute | solution.py:462
  22.4 2.6 %dispatch.6 = (bf16[288,1024]{1,0:T(8,128)(2,1)S(1)}, bf16[288,1024]{1,0:T(8,128)(2,1)S(1)}, f32[576,384]{1,0:T(8,128)S(1)}, bf16[288,384]{1,0:T(8,128)(2,1)S(1)...) custom-call(s32[1]{0:T(128)} %bitcast.2.here, bf16[200,1024]{1,0:T(8,128)(2,1)} %collective-permute-done.1.refs_0_, ...), custom_call_target="tpu_custom_call" | custom-call | flops 1048576 | bytes 16384 | tf_op jit(solution)/shard_map/dispatch/pallas_call | solution.py:138
  25.0 2.7 %collective-permute-done.8.refs_0_ = bf16[288,384]{1,0:T(8,128)(2,1)S(1)} collective-permute-done((bf16[288,384]{1,0:T(8,128)(2,1)S(1)}, bf16[288,384]{1,0:T(8,128)(2,1)S(1)}, u32[]{:S(2)}, u32[]{:S(2)}) %collective-permute-start.8) | collective-permute-done | bytes 221216 | tf_op jit(solution)/shard_map/ppermute | solution.py:484
  29.3 2.3 %combine.5 = (bf16[144,768]{1,0:T(8,128)(2,1)S(1)}, bf16[144,768]{1,0:T(8,128)(2,1)S(1)}, bf16[192,1024]{1,0:T(8,128)(2,1)S(1)}) custom-call(s32[1]{0:T(128)} %bitcast.2.here, f32[288,384]{1,0:T(8,128)S(1)} %get-tuple-element.99.share, bf16[288,384]{1,0:T(8,128)(2,1)S(1)} %collective-permute-done.8.refs_0_, f32[8,192]{1,0:T(8,128)S(1)} %get-tuple-element.101.refs_1_, ...), custom_call_target="tpu_custom_call" | custom-call | flops 1048576 | bytes 16384 | tf_op jit(solution)/shard_map/combine/pallas_call | solution.py:200
  31.6 2.7 %collective-permute-done.7.refs_0_ = bf16[288,384]{1,0:T(8,128)(2,1)S(1)} collective-permute-done((bf16[288,384]{1,0:T(8,128)(2,1)S(1)}, bf16[288,384]{1,0:T(8,128)(2,1)S(1)}, u32[]{:S(2)}, u32[]{:S(2)}) %collective-permute-start.7) | collective-permute-done | bytes 221216 | tf_op jit(solution)/shard_map/ppermute | solution.py:484
  37.3 2.4 %dispatch.7 = (bf16[288,1024]{1,0:T(8,128)(2,1)S(1)}, bf16[288,1024]{1,0:T(8,128)(2,1)S(1)}, f32[576,384]{1,0:T(8,128)S(1)}, bf16[288,384]{1,0:T(8,128)(2,1)S(1)...) custom-call(s32[1]{0:T(128)} %bitcast.2.here, bf16[200,1024]{1,0:T(8,128)(2,1)S(1)} %collective-permute-done.6.refs_0_, ...), custom_call_target="tpu_custom_call" | custom-call | flops 1048576 | bytes 16384 | tf_op jit(solution)/shard_map/dispatch/pallas_call | solution.py:138
  41.2 2.9 %hidden.2.hid = bf16[384,1152]{1,0:T(8,128)(2,1)S(1)} custom-call(s32[1]{0:T(128)} %bitcast.2.here, bf16[2304,384]{1,0:T(8,128)(2,1)S(1)} %bitcast.11, bf16[2304,384]{1,0:T(8,128)(2,1)S(1)} %bitcast.18), custom_call_target="tpu_custom_call" | custom-call | flops 1048576 | bytes 16384 | tf_op jit(solution)/shard_map/hidden/pallas_call | solution.py:293
  45.1 3.3 %combine.6 = (bf16[288,768]{1,0:T(8,128)(2,1)S(1)}, bf16[288,768]{1,0:T(8,128)(2,1)S(1)}, bf16[192,1024]{1,0:T(8,128)(2,1)S(1)}, bf16[192,1024]{1,0:T(8,128)(2,1)S(1)}) custom-call(s32[1]{0:T(128)} %bitcast.2.here, f32[576,384]{1,0:T(8,128)S(1)} %get-tuple-element.111.share, bf16[288,384]{1,0:T(8,128)(2,1)S(1)} %collective-permute-done.7.refs_0_, ...), custom_call_target="tpu_custom_call" | custom-call | flops 1048576 | bytes 16384 | tf_op jit(solution)/shard_map/combine/pallas_call | solution.py:200
  50.3 2.4 %dispatch.8 = (bf16[288,1024]{1,0:T(8,128)(2,1)S(1)}, bf16[288,1024]{1,0:T(8,128)(2,1)S(1)}, f32[576,384]{1,0:T(8,128)S(1)}, bf16[288,384]{1,0:T(8,128)(2,1)S(1)...) custom-call(s32[1]{0:T(128)} %bitcast.2.here, bf16[200,1024]{1,0:T(8,128)(2,1)S(1)} %collective-permute-done.11.refs_0_, ...), custom_call_target="tpu_custom_call" | custom-call | flops 1048576 | bytes 16384 | tf_op jit(solution)/shard_map/dispatch/pallas_call | solution.py:138
  53.5 2.9 %hidden.3.hid = bf16[384,1152]{1,0:T(8,128)(2,1)S(1)} custom-call(s32[1]{0:T(128)} %bitcast.2.here, bf16[2304,384]{1,0:T(8,128)(2,1)S(1)} %collective-permute-done.3.refs_4_.refs_5_.gate, bf16[2304,384]{1,0:T(8,128)(2,1)S(1)} %collective-permute-done.4.refs_5_.refs_6_.up), custom_call_target="tpu_custom_call" | custom-call | flops 1048576 | bytes 16384 | tf_op jit(solution)/shard_map/hidden/pallas_call | solution.py:293
  56.4 3.4 %combine.7 = (bf16[288,768]{1,0:T(8,128)(2,1)S(1)}, bf16[288,768]{1,0:T(8,128)(2,1)S(1)}, bf16[192,1024]{1,0:T(8,128)(2,1)S(1)}, bf16[192,1024]{1,0:T(8,128)(2,1)S(1)}) custom-call(s32[1]{0:T(128)} %bitcast.2.here, f32[576,384]{1,0:T(8,128)S(1)} %get-tuple-element.124.share, bf16[288,384]{1,0:T(8,128)(2,1)S(1)} %collective-permute-done.12.refs_0_, ...), custom_call_target="tpu_custom_call" | custom-call | flops 1048576 | bytes 16384 | tf_op jit(solution)/shard_map/combine/pallas_call | solution.py:200
  63.8 2.0 %dispatch.9 = (bf16[144,1024]{1,0:T(8,128)(2,1)S(1)}, bf16[144,1024]{1,0:T(8,128)(2,1)S(1)}, f32[288,384]{1,0:T(8,128)S(1)}, bf16[288,384]{1,0:T(8,128)(2,1)S(1)}, f32[8,192]{1,0:T(8,128)S(1)}) custom-call(s32[1]{0:T(128)} %bitcast.2.here, bf16[200,1024]{1,0:T(8,128)(2,1)S(1)} %collective-permute-done.15.refs_0_, bf16[384,1024]{1,0:T(8,128)(2,1)S(1)} %bitcast.28, ...), custom_call_target="tpu_custom_call" | custom-call | flops 1048576 | bytes 16384 | tf_op jit(solution)/shard_map/dispatch/pallas_call | solution.py:138
  68.7 3.3 %combine.8 = (bf16[288,768]{1,0:T(8,128)(2,1)S(1)}, bf16[288,768]{1,0:T(8,128)(2,1)S(1)}, bf16[192,1024]{1,0:T(8,128)(2,1)S(1)}, bf16[192,1024]{1,0:T(8,128)(2,1)S(1)}) custom-call(s32[1]{0:T(128)} %bitcast.2.here, f32[576,384]{1,0:T(8,128)S(1)} %get-tuple-element.134.share, bf16[288,384]{1,0:T(8,128)(2,1)S(1)} %collective-permute-done.17.refs_0_, ...), custom_call_target="tpu_custom_call" | custom-call | flops 1048576 | bytes 16384 | tf_op jit(solution)/shard_map/combine/pallas_call | solution.py:200
  73.1 2.3 %combine.9 = (bf16[144,768]{1,0:T(8,128)(2,1)S(1)}, bf16[144,768]{1,0:T(8,128)(2,1)S(1)}, bf16[192,512]{1,0:T(8,128)(2,1)S(1)}, bf16[192,512]{1,0:T(8,128)(2,1)S(1)}) custom-call(s32[1]{0:T(128)} %bitcast.2.here, f32[288,384]{1,0:T(8,128)S(1)} %get-tuple-element.142.share, bf16[288,384]{1,0:T(8,128)(2,1)S(1)} %collective-permute-done.21.refs_0_, ...), custom_call_target="tpu_custom_call" | custom-call | flops 1048576 | bytes 16384 | tf_op jit(solution)/shard_map/combine/pallas_call | solution.py:200
  75.4 9.3 %weights.2 = bf16[1024,1152]{1,0:T(8,128)(2,1)S(1)} custom-call(s32[1]{0:T(128)} %bitcast.2.here, bf16[1024,1152]{1,0:T(8,128)(2,1)S(1)} %collective-permute-done.14.inputs, bf16[384,1152]{1,0:T(8,128)(2,1)S(1)} %hidden.3.hid, bf16[144,1024]{1,0:T(8,128)(2,1)S(1)} %get-tuple-element.154.refs_0_, bf16[288,1024]{1,0:T(8,128)(2,1)S(1)} %get-tuple-element.155.refs_1_, ...), custom_call_target="tpu_custom_call" | custom-call | flops 1048576 | bytes 16384 | tf_op jit(solution)/shard_map/weights/pallas_call | solution.py:421
  86.8 5.7 %collective-permute-done.28.refs_2_ = bf16[192,512]{1,0:T(8,128)(2,1)S(1)} collective-permute-done((bf16[192,512]{1,0:T(8,128)(2,1)S(1)}, bf16[192,512]{1,0:T(8,128)(2,1)S(1)}, u32[]{:S(2)}, u32[]{:S(2)}) %collective-permute-start.28) | collective-permute-done | bytes 196640 | tf_op jit(solution)/shard_map/ppermute | solution.py:462
  92.6 3.1 %collective-permute-start.29 = (bf16[192,512]{1,0:T(8,128)(2,1)S(1)}, bf16[192,512]{1,0:T(8,128)(2,1)S(1)}, u32[]{:S(2)}, u32[]{:S(2)}) collective-permute-start(bf16[192,512]{1,0:T(8,128)(2,1)S(1)} %add.10), channel_id=1, source_target_pairs={{0,4},{1,5},{2,6},{3,7},{4,8},{5,9},{6,10},{7,11},{8,12},{9,13},{1... | collective-permute-start | bytes 589832 | tf_op jit(solution)/shard_map/ppermute | solution.py:462
  97.6 3.5 %collective-permute-done.29.refs_2_ = bf16[192,512]{1,0:T(8,128)(2,1)S(1)} collective-permute-done((bf16[192,512]{1,0:T(8,128)(2,1)S(1)}, bf16[192,512]{1,0:T(8,128)(2,1)S(1)}, u32[]{:S(2)}, u32[]{:S(2)}) %collective-permute-start.29) | collective-permute-done | bytes 196640 | tf_op jit(solution)/shard_map/ppermute | solution.py:462
  101.2 2.5 %collective-permute-start.30 = (bf16[192,512]{1,0:T(8,128)(2,1)S(1)}, bf16[192,512]{1,0:T(8,128)(2,1)S(1)}, u32[]{:S(2)}, u32[]{:S(2)}) collective-permute-start(bf16[192,512]{1,0:T(8,128)(2,1)S(1)} %add.11), channel_id=1, source_target_pairs={{0,4},{1,5},{2,6},{3,7},{4,8},{5,9},{6,10},{7,11},{8,12},{9,13},{1... | collective-permute-start | bytes 589832 | tf_op jit(solution)/shard_map/ppermute | solution.py:462
  103.7 2.7 %collective-permute-done.25.refs_2_ = bf16[192,512]{1,0:T(8,128)(2,1)S(1)} collective-permute-done((bf16[192,512]{1,0:T(8,128)(2,1)S(1)}, bf16[192,512]{1,0:T(8,128)(2,1)S(1)}, u32[]{:S(2)}, u32[]{:S(2)}) %collective-permute-start.25) | collective-permute-done | bytes 196640 | tf_op jit(solution)/shard_map/ppermute | solution.py:462
  107.9 8.0 %weights.3 = bf16[1,1024,1152]{2,1,0:T(8,128)(2,1)} custom-call(s32[1]{0:T(128)} %bitcast.2.here, bf16[1024,1152]{1,0:T(8,128)(2,1)S(1)} %get-tuple-element.167.inputs, bf16[384,1152]{1,0:T(8,128)(2,1)S(1)} %hidden.2.hid, bf16[144,1024]{1,0:T(8,128)(2,1)S(1)} %get-tuple-element.169.refs_0_, bf16[288,1024]{1,0:T(8,128)(2,1)S(1)} %get-tuple-element.170.refs_1_, ...), custom_call_target="tpu_custom_call" | custom-call | flops 1048576 | bytes 16384 | tf_op jit(solution)/shard_map/weights/pallas_call | solution.py:421
  (74 shorter events, 33.9 us)
Async XLA Ops:
  0.6 19.2 %collective-permute-start.3 = (bf16[2304,384]{1,0:T(8,128)(2,1)}, bf16[2304,384]{1,0:T(8,128)(2,1)S(1)}, u32[]{:S(2)}, u32[]{:S(2)}) collective-permute-start(bf16[2304,384]{1,0:T(8,128)(2,1)} %bitcast.9), channel_id=1, source_target_pairs={{0,1},{1,0},{2,3},{3,2},{4,5},{5,4},{6,7},{7,6},{8,9},{9,8},{10,11... | collective-permute-start | bytes 5308424 | tf_op jit(solution)/shard_map/ppermute | solution.py:462
  1.1 18.7 %collective-permute-start.4 = (bf16[2304,384]{1,0:T(8,128)(2,1)}, bf16[2304,384]{1,0:T(8,128)(2,1)S(1)}, u32[]{:S(2)}, u32[]{:S(2)}) collective-permute-start(bf16[2304,384]{1,0:T(8,128)(2,1)} %bitcast.16), channel_id=1, source_target_pairs={{0,1},{1,0},{2,3},{3,2},{4,5},{5,4},{6,7},{7,6},{8,9},{9,8},{10,11... | collective-permute-start | bytes 5308424 | tf_op jit(solution)/shard_map/ppermute | solution.py:462
  1.2 12.7 %collective-permute-start.2 = (bf16[384,1024]{1,0:T(8,128)(2,1)}, bf16[384,1024]{1,0:T(8,128)(2,1)}, u32[]{:S(2)}, u32[]{:S(2)}) collective-permute-start(bf16[384,1024]{1,0:T(8,128)(2,1)} %bitcast.23), channel_id=1, source_target_pairs={{0,1},{1,0},{2,3},{3,2},{4,5},{5,4},{6,7},{7,6},{8,9},{9,8},{10,11... | collective-permute-start | bytes 2359304 | tf_op jit(solution)/shard_map/ppermute | solution.py:462
  3.4 13.0 %collective-permute-start.1 = (bf16[200,1024]{1,0:T(8,128)(2,1)}, bf16[200,1024]{1,0:T(8,128)(2,1)}, u32[]{:S(2)}, u32[]{:S(2)}) collective-permute-start(bf16[200,1024]{1,0:T(8,128)(2,1)} %pack.1.refs_0_), channel_id=1, source_target_pairs={{0,2},{1,3},{2,0},{3,1},{4,6},{5,7},{6,4},{7,5},{8,10},{9,11},{10,... | collective-permute-start | bytes 1228808 | tf_op jit(solution)/shard_map/ppermute | solution.py:462
  6.1 13.7 %collective-permute-start = (bf16[200,1024]{1,0:T(8,128)(2,1)}, bf16[200,1024]{1,0:T(8,128)(2,1)}, u32[]{:S(2)}, u32[]{:S(2)}) collective-permute-start(bf16[200,1024]{1,0:T(8,128)(2,1)} %pack.1.refs_0_), channel_id=1, source_target_pairs={{0,4},{1,5},{2,6},{3,7},{4,8},{5,9},{6,10},{7,11},{8,12},{9,13},{1... | collective-permute-start | bytes 1228808 | tf_op jit(solution)/shard_map/ppermute | solution.py:462
  19.8 28.6 %collective-permute-start.14 = (bf16[1024,1152]{1,0:T(8,128)(2,1)S(1)}, bf16[1024,1152]{1,0:T(8,128)(2,1)S(1)}, u32[]{:S(2)}, u32[]{:S(2)}) collective-permute-start(bf16[1024,1152]{1,0:T(8,128)(2,1)S(1)} %get-tuple-element.117), channel_id=1, source_target_pairs={{0,1},{1,0},{2,3},{3,2},{4,5},{5,4},{6,7},{7,6},{8,9},{9,8},{10,11... | collective-permute-start | bytes 7077896 | tf_op jit(solution)/shard_map/ppermute | solution.py:462
  19.8 9.4 %collective-permute-start.9 = (bf16[1024,768]{1,0:T(8,128)(2,1)S(1)}, bf16[1024,768]{1,0:T(8,128)(2,1)S(1)}, u32[]{:S(2)}, u32[]{:S(2)}) collective-permute-start(bf16[1024,768]{1,0:T(8,128)(2,1)S(1)} %join.1.refs_6_.refs_7_), channel_id=1, source_target_pairs={{0,1},{1,0},{2,3},{3,2},{4,5},{5,4},{6,7},{7,6},{8,9},{9,8},{10,11... | collective-permute-start | bytes 4718600 | tf_op jit(solution)/shard_map/ppermute | solution.py:462
  21.9 12.5 %collective-permute-start.6 = (bf16[200,1024]{1,0:T(8,128)(2,1)}, bf16[200,1024]{1,0:T(8,128)(2,1)S(1)}, u32[]{:S(2)}, u32[]{:S(2)}) collective-permute-start(bf16[200,1024]{1,0:T(8,128)(2,1)} %collective-permute-done.refs_1_), channel_id=1, source_target_pairs={{0,2},{1,3},{2,0},{3,1},{4,6},{5,7},{6,4},{7,5},{8,10},{9,11},{10,... | collective-permute-start | bytes 1228808 | tf_op jit(solution)/shard_map/ppermute | solution.py:462
  22.4 12.9 %collective-permute-start.5 = (bf16[200,1024]{1,0:T(8,128)(2,1)}, bf16[200,1024]{1,0:T(8,128)(2,1)S(1)}, u32[]{:S(2)}, u32[]{:S(2)}) collective-permute-start(bf16[200,1024]{1,0:T(8,128)(2,1)} %collective-permute-done.refs_1_), channel_id=1, source_target_pairs={{0,4},{1,5},{2,6},{3,7},{4,8},{5,9},{6,10},{7,11},{8,12},{9,13},{1... | collective-permute-start | bytes 1228808 | tf_op jit(solution)/shard_map/ppermute | solution.py:462
  35.3 13.1 %collective-permute-start.11 = (bf16[200,1024]{1,0:T(8,128)(2,1)S(1)}, bf16[200,1024]{1,0:T(8,128)(2,1)S(1)}, u32[]{:S(2)}, u32[]{:S(2)}) collective-permute-start(bf16[200,1024]{1,0:T(8,128)(2,1)S(1)} %collective-permute-done.5.refs_1_), channel_id=1, source_target_pairs={{0,2},{1,3},{2,0},{3,1},{4,6},{5,7},{6,4},{7,5},{8,10},{9,11},{10,... | collective-permute-start | bytes 1228808 | tf_op jit(solution)/shard_map/ppermute | solution.py:462
  36.8 11.7 %collective-permute-start.10 = (bf16[200,1024]{1,0:T(8,128)(2,1)S(1)}, bf16[200,1024]{1,0:T(8,128)(2,1)S(1)}, u32[]{:S(2)}, u32[]{:S(2)}) collective-permute-start(bf16[200,1024]{1,0:T(8,128)(2,1)S(1)} %collective-permute-done.5.refs_1_), channel_id=1, source_target_pairs={{0,4},{1,5},{2,6},{3,7},{4,8},{5,9},{6,10},{7,11},{8,12},{9,13},{1... | collective-permute-start | bytes 1228808 | tf_op jit(solution)/shard_map/ppermute | solution.py:462
  36.8 8.3 %collective-permute-start.13 = (bf16[288,384]{1,0:T(8,128)(2,1)S(1)}, bf16[288,384]{1,0:T(8,128)(2,1)S(1)}, u32[]{:S(2)}, u32[]{:S(2)}) collective-permute-start(bf16[288,384]{1,0:T(8,128)(2,1)S(1)} %get-tuple-element.113), channel_id=1, source_target_pairs={{0,16},{16,0},{1,17},{17,1},{2,18},{18,2},{3,19},{19,3},{4,20},{20... | collective-permute-start | bytes 663560 | tf_op jit(solution)/shard_map/ppermute | solution.py:484
  39.6 8.8 %collective-permute-start.12 = (bf16[288,384]{1,0:T(8,128)(2,1)S(1)}, bf16[288,384]{1,0:T(8,128)(2,1)S(1)}, u32[]{:S(2)}, u32[]{:S(2)}) collective-permute-start(bf16[288,384]{1,0:T(8,128)(2,1)S(1)} %get-tuple-element.109), channel_id=1, source_target_pairs={{0,16},{16,0},{1,17},{17,1},{2,18},{18,2},{3,19},{19,3},{4,20},{20... | collective-permute-start | bytes 663560 | tf_op jit(solution)/shard_map/ppermute | solution.py:484
  48.4 11.3 %collective-permute-start.15 = (bf16[200,1024]{1,0:T(8,128)(2,1)S(1)}, bf16[200,1024]{1,0:T(8,128)(2,1)S(1)}, u32[]{:S(2)}, u32[]{:S(2)}) collective-permute-start(bf16[200,1024]{1,0:T(8,128)(2,1)S(1)} %collective-permute-done.10.refs_1_), channel_id=1, source_target_pairs={{0,2},{1,3},{2,0},{3,1},{4,6},{5,7},{6,4},{7,5},{8,10},{9,11},{10,... | collective-permute-start | bytes 1228808 | tf_op jit(solution)/shard_map/ppermute | solution.py:462
  49.0 10.7 %collective-permute-start.16 = (bf16[192,1024]{1,0:T(8,128)(2,1)S(1)}, bf16[192,1024]{1,0:T(8,128)(2,1)S(1)}, u32[]{:S(2)}, u32[]{:S(2)}) collective-permute-start(bf16[192,1024]{1,0:T(8,128)(2,1)S(1)} %get-tuple-element.119), channel_id=1, source_target_pairs={{0,4},{1,5},{2,6},{3,7},{4,8},{5,9},{6,10},{7,11},{8,12},{9,13},{1... | collective-permute-start | bytes 1179656 | tf_op jit(solution)/shard_map/ppermute | solution.py:462
  59.8 12.3 %collective-permute-start.19 = (bf16[192,1024]{1,0:T(8,128)(2,1)S(1)}, bf16[192,1024]{1,0:T(8,128)(2,1)S(1)}, u32[]{:S(2)}, u32[]{:S(2)}) collective-permute-start(bf16[192,1024]{1,0:T(8,128)(2,1)S(1)} %get-tuple-element.130), channel_id=1, source_target_pairs={{0,4},{1,5},{2,6},{3,7},{4,8},{5,9},{6,10},{7,11},{8,12},{9,13},{1... | collective-permute-start | bytes 1179656 | tf_op jit(solution)/shard_map/ppermute | solution.py:462
  61.5 10.5 %collective-permute-start.20 = (bf16[192,1024]{1,0:T(8,128)(2,1)S(1)}, bf16[192,1024]{1,0:T(8,128)(2,1)S(1)}, u32[]{:S(2)}, u32[]{:S(2)}) collective-permute-start(bf16[192,1024]{1,0:T(8,128)(2,1)S(1)} %get-tuple-element.131), channel_id=1, source_target_pairs={{0,2},{1,3},{2,0},{3,1},{4,6},{5,7},{6,4},{7,5},{8,10},{9,11},{10,... | collective-permute-start | bytes 1179656 | tf_op jit(solution)/shard_map/ppermute | solution.py:462
  72.2 12.5 %collective-permute-start.24 = (bf16[192,512]{1,0:T(8,128)(2,1)S(1)}, bf16[192,512]{1,0:T(8,128)(2,1)S(1)}, u32[]{:S(2)}, u32[]{:S(2)}) collective-permute-start(bf16[192,512]{1,0:T(8,128)(2,1)S(1)} %add.6), channel_id=1, source_target_pairs={{0,2},{1,3},{2,0},{3,1},{4,6},{5,7},{6,4},{7,5},{8,10},{9,11},{10,... | collective-permute-start | bytes 589832 | tf_op jit(solution)/shard_map/ppermute | solution.py:462
  84.7 23.3 %collective-permute-start.31 = (bf16[1024,1152]{1,0:T(8,128)(2,1)S(1)}, bf16[1024,1152]{1,0:T(8,128)(2,1)S(1)}, u32[]{:S(2)}, u32[]{:S(2)}) collective-permute-start(bf16[1024,1152]{1,0:T(8,128)(2,1)S(1)} %weights.2), channel_id=1, source_target_pairs={{0,1},{1,0},{2,3},{3,2},{4,5},{5,4},{6,7},{7,6},{8,9},{9,8},{10,11... | collective-permute-start | bytes 7077896 | tf_op jit(solution)/shard_map/ppermute | solution.py:462
  86.0 11.7 %collective-permute-start.27 = (bf16[192,512]{1,0:T(8,128)(2,1)S(1)}, bf16[192,512]{1,0:T(8,128)(2,1)S(1)}, u32[]{:S(2)}, u32[]{:S(2)}) collective-permute-start(bf16[192,512]{1,0:T(8,128)(2,1)S(1)} %get-tuple-element.165), channel_id=1, source_target_pairs={{0,2},{1,3},{2,0},{3,1},{4,6},{5,7},{6,4},{7,5},{8,10},{9,11},{10,... | collective-permute-start | bytes 589832 | tf_op jit(solution)/shard_map/ppermute | solution.py:462
  92.6 8.5 %collective-permute-start.29 = (bf16[192,512]{1,0:T(8,128)(2,1)S(1)}, bf16[192,512]{1,0:T(8,128)(2,1)S(1)}, u32[]{:S(2)}, u32[]{:S(2)}) collective-permute-start(bf16[192,512]{1,0:T(8,128)(2,1)S(1)} %add.10), channel_id=1, source_target_pairs={{0,4},{1,5},{2,6},{3,7},{4,8},{5,9},{6,10},{7,11},{8,12},{9,13},{1... | collective-permute-start | bytes 589832 | tf_op jit(solution)/shard_map/ppermute | solution.py:462
  97.3 9.1 %collective-permute-start.25 = (bf16[192,512]{1,0:T(8,128)(2,1)S(1)}, bf16[192,512]{1,0:T(8,128)(2,1)S(1)}, u32[]{:S(2)}, u32[]{:S(2)}) collective-permute-start(bf16[192,512]{1,0:T(8,128)(2,1)S(1)} %add.8), channel_id=1, source_target_pairs={{0,4},{1,5},{2,6},{3,7},{4,8},{5,9},{6,10},{7,11},{8,12},{9,13},{1... | collective-permute-start | bytes 589832 | tf_op jit(solution)/shard_map/ppermute | solution.py:462
  101.2 14.8 %collective-permute-start.30 = (bf16[192,512]{1,0:T(8,128)(2,1)S(1)}, bf16[192,512]{1,0:T(8,128)(2,1)S(1)}, u32[]{:S(2)}, u32[]{:S(2)}) collective-permute-start(bf16[192,512]{1,0:T(8,128)(2,1)S(1)} %add.11), channel_id=1, source_target_pairs={{0,4},{1,5},{2,6},{3,7},{4,8},{5,9},{6,10},{7,11},{8,12},{9,13},{1... | collective-permute-start | bytes 589832 | tf_op jit(solution)/shard_map/ppermute | solution.py:462
  106.5 9.5 %collective-permute-start.26 = (bf16[192,512]{1,0:T(8,128)(2,1)S(1)}, bf16[192,512]{1,0:T(8,128)(2,1)S(1)}, u32[]{:S(2)}, u32[]{:S(2)}) collective-permute-start(bf16[192,512]{1,0:T(8,128)(2,1)S(1)} %add.9), channel_id=1, source_target_pairs={{0,4},{1,5},{2,6},{3,7},{4,8},{5,9},{6,10},{7,11},{8,12},{9,13},{1... | collective-permute-start | bytes 589832 | tf_op jit(solution)/shard_map/ppermute | solution.py:462
  (13 other events, 93.2 us)

commit v8 on v7

--- a/solution.py
+++ b/solution.py
@@ -91,9 +91,14 @@
     return pltpu.CompilerParams(vmem_limit_bytes=mib << 20)
 
 
-def dispatch_kernel(n, cap, here, *refs):
+def plane_rows(here, other, step, cap):
+    return pl.ds(pl.multiple_of((source(here, step, other) // 2) * cap, 16), cap)
+
+
+def dispatch_kernel(chunk, cap, begun, here, *refs):
+    n = len(chunk)
     toks, (wd0, wd1) = refs[:n], refs[n : n + 2]
-    rec0, rec1, share, *share_out, pos_out = refs[n + 2 :]
+    buf0, buf1, share, *share_out, pos_out, rec, sems = refs[n + 2 + 2 * begun :]
     tok = toks[0].shape[0] - 8
     line = 256 * pl.cdiv(tok, 256)
     before = lax.broadcasted_iota(jnp.int32, (tok, tok), 0) < lax.broadcasted_iota(jnp.int32, (tok, tok), 1)
@@ -111,50 +116,59 @@
     pos = jnp.dot(mask.astype(bf16), before, preferred_element_type=f32)
     pos = jnp.where(mask > 0.0, pos, -1.0)
     pos_out[...] = pos
+    copies = []
     for rel, t in enumerate(toks):
         w = [
             jnp.where(slot == pos[i : i + 1, :], gates[i] * gate_unit, 0.0).astype(bf16)
             for i in (rel, n + rel)
         ]
         rows = jnp.dot(jnp.concatenate(w, axis=0), t[:tok, :], preferred_element_type=f32).astype(bf16)
-        rec0[rel * cap : (rel + 1) * cap, :] = rows[:cap]
-        rec1[rel * cap : (rel + 1) * cap, :] = rows[cap:]
-    for a, (rec, wd) in enumerate(((rec0, wd0), (rec1, wd1))):
-        gh = contract_cols(rec[...], wd[...])
+        at = pl.ds(rel * cap, cap)
+        for a, buf in enumerate((buf0, buf1)):
+            rec[a, at, :] = rows[a * cap : (a + 1) * cap]
+            to = plane_rows(here[0], *chunk[rel], cap)
+            copies.append(pltpu.make_async_copy(rec.at[a, at, :], buf.at[to, :], sems.at[len(copies)]))
+            copies[-1].start()
+    for a, wd in enumerate((wd0, wd1)):
+        gh = contract_cols(rec[a], wd[...])
         share[a * n * cap : (a + 1) * n * cap, :] = gh
         if n == 1:
             share_out[0][a * cap : (a + 1) * cap, :] = gh.astype(bf16)
         else:
             share_out[a][...] = gh.astype(bf16)
-
-
-def dispatch(here, toks, wd0, wd1, cap):
+    for c in copies:
+        c.wait()
+
+
+def dispatch(here, chunk, toks, wd0, wd1, cap, rows, old):
     n = len(toks)
     tok, d = toks[0].shape
     h = wd0.shape[0]
-    outs = [((n * cap, d), bf16), ((n * cap, d), bf16), ((2 * n * cap, h), f32)]
+    outs = [((rows, d), bf16)] * 2 + [((2 * n * cap, h), f32)]
     outs += [((2 * cap, h), bf16)] if n == 1 else [((n * cap, h), bf16)] * 2
     outs += [((8, tok - 8), f32)]
     return pl.pallas_call(
-        functools.partial(dispatch_kernel, n, cap),
+        functools.partial(dispatch_kernel, chunk, cap, len(old) // 2),
         out_shape=[jax.ShapeDtypeStruct(s, t) for s, t in outs],
-        in_specs=[on_scalar] + [on_chip] * (n + 2),
-        out_specs=[on_chip] * len(outs),
+        in_specs=[on_scalar] + [on_chip] * (n + 2) + [anywhere] * len(old),
+        out_specs=[anywhere] * 2 + [on_chip] * (len(outs) - 2),
+        scratch_shapes=[pltpu.VMEM((2, n * cap, d), bf16), pltpu.SemaphoreType.DMA((2 * n,))],
+        input_output_aliases={n + 3 + k: k for k in range(len(old))},
         cost_estimate=light,
         compiler_params=params(16),
         name="dispatch",
-    )(here, *toks, wd0, wd1)
-
-
-def combine_kernel(chunk, cap, here, share, *refs):
+    )(here, *toks, wd0, wd1, *old)
+
+
+def combine_kernel(chunk, cap, begun, last, here, share, *refs):
     n = len(chunk)
     if n == 1:
         peer0, peer1 = refs[0].at[:cap, :], refs[0].at[cap:, :]
         pos, *refs = refs[1:]
     else:
         peer0, peer1, pos, *refs = refs
-    saved, (w0, w1), (gp0, gp1) = refs[:4], refs[4:6], refs[6:8]
-    backs, (held, sems) = refs[8:-2], refs[-2:]
+    saved, ws, refs = refs[:4], refs[4:6], refs[6 + begun * (1 if last else 2) :]
+    buffers, backs, (held, gps, sems, out_sems) = refs[:2], refs[2:-4], refs[-4:]
     h = share.shape[1]
     copies = []
     for a in range(2):
@@ -166,8 +180,9 @@
     for c in copies:
         c.start()
     slot = lax.broadcasted_iota(jnp.int32, (cap, pos.shape[1]), 0).astype(f32)
-    sums = [None] * n
-    for a, (gp, w, peer) in enumerate(((gp0, w0, peer0), (gp1, w1, peer1))):
+    sums, leaving = [None] * n, []
+    for a, (w, peer) in enumerate(zip(ws, (peer0, peer1))):
+        gp = gps.at[a]
         for rel in range(n):
             i = a * n + rel
             copies[2 * i].wait()
@@ -176,6 +191,12 @@
             gg, gu = activation_grads(gh, held[2 * i].astype(f32), held[2 * i + 1].astype(f32))
             gp[rel * cap : (rel + 1) * cap, :h] = gg
             gp[rel * cap : (rel + 1) * cap, h:] = gu
+            if a == 0 or not last:
+                to = buffers[a].at[plane_rows(here[0], *chunk[rel], cap), :]
+                leaving.append(pltpu.make_async_copy(gp.at[rel * cap : (rel + 1) * cap, :], to, out_sems.at[i]))
+                leaving[-1].start()
+        if a == 1 and last:
+            buffers[1][...] = gp[...]
         slots = contract_cols(gp[...], w[...]).astype(bf16)
         for rel in range(n):
             i = a * n + rel
@@ -189,24 +210,34 @@
     else:
         for rel in range(n):
             backs[rel][...] = sums[rel].astype(bf16)
-
-
-def combine(here, chunk, share, peers, pos, saved0, saved1, w0, w1, cap, halves=False):
+    for c in leaving:
+        c.wait()
+
+
+def combine(here, chunk, share, peers, pos, saved0, saved1, w0, w1, cap, rows, old, last=False):
     n = len(chunk)
     h = share.shape[1]
     d = w0.shape[0]
     tok = pos.shape[1]
-    outs = [(n * cap, 2 * h)] * 2 + ([(tok, d // 2)] * 2 if halves else [(tok, d)] * n)
-    return pl.pallas_call(
-        functools.partial(combine_kernel, chunk, cap),
+    old = old[:1] if last else old
+    outs = [(rows, 2 * h), (n * cap if last else rows, 2 * h)] + ([(tok, d // 2)] * 2 if last else [(tok, d)] * n)
+    first_old = 2 + len(peers) + 1 + 4 + 2
+    return pl.pallas_call(
+        functools.partial(combine_kernel, chunk, cap, 1 if old else 0, last),
         out_shape=[jax.ShapeDtypeStruct(s, bf16) for s in outs],
-        in_specs=[on_scalar] + [on_chip] * (2 + len(peers)) + [anywhere] * 4 + [on_chip] * 2,
-        out_specs=[on_chip] * len(outs),
-        scratch_shapes=[pltpu.VMEM((4 * n, cap, h), bf16), pltpu.SemaphoreType.DMA((4 * n,))],
+        in_specs=[on_scalar] + [on_chip] * (2 + len(peers)) + [anywhere] * 4 + [on_chip] * 2 + [anywhere] * len(old),
+        out_specs=[anywhere, on_chip if last else anywhere] + [on_chip] * (len(outs) - 2),
+        scratch_shapes=[
+            pltpu.VMEM((4 * n, cap, h), bf16),
+            pltpu.VMEM((2, n * cap, 2 * h), bf16),
+            pltpu.SemaphoreType.DMA((4 * n,)),
+            pltpu.SemaphoreType.DMA((2 * n,)),
+        ],
+        input_output_aliases={first_old + k: k for k in range(len(old))},
         cost_estimate=light,
         compiler_params=params(20),
         name="combine",
-    )(here, share, *peers, pos, *saved0, *saved1, w0, w1)
+    )(here, share, *peers, pos, *saved0, *saved1, w0, w1, *old)
 
 
 def join_kernel(left, right, out):
@@ -273,57 +304,61 @@
 
 
 def hidden_kernel(cap, here, gate, up, out, held, sems):
+    rows = held.shape[2]
     copies = []
-    for k, v in enumerate((gate, up)):
-        for q in range(held.shape[1] // cap):
-            rows = pl.ds(pl.multiple_of((2 * q + lax.rem(here[0], 2)) * cap, 16), cap)
-            to = held.at[k, pl.ds(q * cap, cap), :]
-            copies.append(pltpu.make_async_copy(v.at[rows, :], to, sems.at[len(copies)]))
+    for k in range(2):
+        plane = lax.rem(here[0] + k, 2)
+        for i, v in enumerate((gate, up)):
+            for q in range(rows // cap):
+                at = pl.ds(pl.multiple_of((2 * q + plane) * cap, 16), cap)
+                to = held.at[k, i, pl.ds(q * cap, cap), :]
+                copies.append(pltpu.make_async_copy(v.at[at, :], to, sems.at[len(copies)]))
     for c in copies:
         c.start()
-    for c in copies:
-        c.wait()
-    gate_pre = held[0].astype(f32)
-    out[...] = (gate_pre * jax.nn.sigmoid(gate_pre) * held[1].astype(f32)).astype(bf16).T
+    for k in range(2):
+        for c in copies[k * len(copies) // 2 : (k + 1) * len(copies) // 2]:
+            c.wait()
+        gate_pre = held[k, 0].astype(f32)
+        out[:, k * rows : (k + 1) * rows] = (
+            (gate_pre * jax.nn.sigmoid(gate_pre) * held[k, 1].astype(f32)).astype(bf16).T
+        )
 
 
 def hidden(here, gate, up, cap):
-    rows, h = gate.shape
-    rows = rows // 2
+    slots, h = gate.shape
     return pl.pallas_call(
         functools.partial(hidden_kernel, cap),
-        out_shape=jax.ShapeDtypeStruct((h, rows), bf16),
+        out_shape=jax.ShapeDtypeStruct((h, slots), bf16),
         in_specs=[on_scalar, anywhere, anywhere],
         out_specs=on_chip,
-        scratch_shapes=[pltpu.VMEM((2, rows, h), bf16), pltpu.SemaphoreType.DMA((2 * rows // cap,))],
-        cost_estimate=light,
-        compiler_params=params(16),
+        scratch_shapes=[pltpu.VMEM((2, 2, slots // 2, h), bf16), pltpu.SemaphoreType.DMA((2 * slots // cap,))],
+        cost_estimate=light,
+        compiler_params=params(24),
         name="hidden",
     )(here, gate, up)
 
 
-def turn_kernel(cap, here, v, own, other, held):
-    for k, out in enumerate((own, other)):
+def turn_kernel(cap, here, v, out, held):
+    rows = held.shape[0]
+    for k in range(2):
         plane = lax.rem(here[0] + k, 2)
-        for q in range(held.shape[0] // cap):
+        for q in range(rows // cap):
             held[q * cap : (q + 1) * cap, :] = v[pl.ds(pl.multiple_of((2 * q + plane) * cap, 16), cap), :]
-        out[...] = held[...].T
+        out[:, k * rows : (k + 1) * rows] = held[...].T
 
 
 def turn(here, v, cap):
     slots, d = v.shape
-    rows = slots // 2
     tile = 256
-    out = pl.BlockSpec((tile, rows), lambda i, here: (i, 0))
     return pl.pallas_call(
         functools.partial(turn_kernel, cap),
-        out_shape=[jax.ShapeDtypeStruct((d, rows), v.dtype)] * 2,
+        out_shape=jax.ShapeDtypeStruct((d, slots), v.dtype),
         grid_spec=pltpu.PrefetchScalarGridSpec(
             num_scalar_prefetch=1,
             grid=(d // tile,),
             in_specs=[pl.BlockSpec((slots, tile), lambda i, here: (0, i))],
-            out_specs=[out, out],
-            scratch_shapes=[pltpu.VMEM((rows, tile), v.dtype)],
+            out_specs=pl.BlockSpec((tile, slots), lambda i, here: (i, 0)),
+            scratch_shapes=[pltpu.VMEM((slots // 2, tile), v.dtype)],
         ),
         cost_estimate=light,
         compiler_params=params(12),
@@ -361,87 +396,65 @@
     )(in_hbm(tokens), in_hbm(routes), in_hbm(codes))
 
 
-def weights_kernel(order, cap, count, here, inputs, hid, *refs):
-    recs, gps, refs = refs[:count], refs[count : 2 * count], refs[2 * count :]
-    summed, (out, rs, gs, rec_sems, gp_sems) = refs[:-5], refs[-5:]
-    i = pl.program_id(0)
-    tile = rs.shape[2]
-
-    def copies(pieces, column, to, sems):
-        made = []
-        for r in pieces:
-            for at in range(0, r.shape[0], cap):
-                src = source(here[0], *order[len(made)])
-                rows = pl.ds(pl.multiple_of((src // 2) * cap, 16), cap)
-                made.append(pltpu.make_async_copy(r.at[pl.ds(at, cap), column], to.at[rows, :], sems.at[len(made)]))
-        return made
-
-    def received(step):
-        slot = lax.rem(step, 2)
-        return copies(recs, pl.ds(pl.multiple_of(step * tile, 128), tile), rs.at[slot], rec_sems.at[slot])
-
-    fixed = copies(gps, pl.ds(0, gs.shape[1]), gs, gp_sems)
-
-    @pl.when(i == 0)
+def received_kernel(hid, own, other, out):
+    rows = own.shape[0]
+    part = jnp.dot(hid[:, :rows], own[...], preferred_element_type=f32)
+    part = part + jnp.dot(hid[:, rows:], other[...], preferred_element_type=f32)
+    out[0] = (part * loss_scale).astype(bf16).T
+
+
+def received_part(hid, own, other):
+    h, slots = hid.shape
+    rows, d = own.shape
+    tile = 256
+    return pl.pallas_call(
+        received_kernel,
+        out_shape=jax.ShapeDtypeStruct((1, d, 3 * h), bf16),
+        grid=(d // tile,),
+        in_specs=[pl.BlockSpec((h, slots), lambda i: (0, 0))] + [pl.BlockSpec((rows, tile), lambda i: (0, i))] * 2,
+        out_specs=pl.BlockSpec((1, tile, h), lambda i: (0, i, 2)),
+        cost_estimate=light,
+        compiler_params=params(20),
+        name="received_part",
+    )(hid, own, other)
+
+
+def inputs_kernel(cap, last, here, old, inputs, own, other, late, out, held):
+    rows = own.shape[0]
+
+    @pl.when(pl.program_id(0) == 0)
     def _():
-        for c in fixed + received(i):
-            c.start()
-
-    @pl.when(i + 1 < pl.num_programs(0))
-    def _():
-        for c in received(i + 1):
-            c.start()
-
-    @pl.when(i == 0)
-    def _():
-        for c in fixed:
-            c.wait()
-
-    wide = gs.shape[1]
-    left = jnp.dot(inputs[...], gs[...], preferred_element_type=f32)
-    for c in received(i):
-        c.wait()
-    right = jnp.dot(hid[...], rs[lax.rem(i, 2)], preferred_element_type=f32)
-    if summed:
-        other = summed[0]
-        out[0, :, :wide] = ((left + other[:, :wide].astype(f32)) * loss_scale).astype(bf16)
-        out[0, :, wide:] = ((right.T + other[:, wide:].astype(f32)) * loss_scale).astype(bf16)
-    else:
-        out[:, :wide] = left.astype(bf16)
-        out[:, wide:] = right.astype(bf16).T
-
-
-def weight_sums(here, order, inputs, hid, recs, gps, cap, summed=None):
+        held[...] = other[...]
+        held[plane_rows(here[0], *last, cap), :] = late[...]
+
+    part = jnp.dot(inputs[:, :rows], own[...], preferred_element_type=f32)
+    part = part + jnp.dot(inputs[:, rows:], held[...], preferred_element_type=f32)
+    out[0] = (part * loss_scale).astype(bf16)
+
+
+def inputs_part(here, last, old, inputs, own, other, late, cap):
     d, slots = inputs.shape
-    h = hid.shape[0]
-    tile = 512
-    block = pl.BlockSpec((tile, 3 * h), lambda i, here: (i, 0))
-    given = [] if summed is None else [summed]
-    last = summed is not None
-    return pl.pallas_call(
-        functools.partial(weights_kernel, order, cap, len(recs)),
-        out_shape=jax.ShapeDtypeStruct((1, d, 3 * h) if last else (d, 3 * h), bf16),
+    rows, wide = own.shape
+    tile = 256
+
+    def fixed(v):
+        return pl.BlockSpec(v.shape, lambda i, here: (0, 0))
+
+    return pl.pallas_call(
+        functools.partial(inputs_kernel, cap, last),
+        out_shape=jax.ShapeDtypeStruct(old.shape, bf16),
         grid_spec=pltpu.PrefetchScalarGridSpec(
             num_scalar_prefetch=1,
             grid=(d // tile,),
-            in_specs=[
-                pl.BlockSpec((tile, slots), lambda i, here: (i, 0)),
-                pl.BlockSpec((h, slots), lambda i, here: (0, 0)),
-            ]
-            + [anywhere] * (2 * len(recs))
-            + [block] * len(given),
-            out_specs=pl.BlockSpec((1, tile, 3 * h), lambda i, here: (0, i, 0)) if last else block,
-            scratch_shapes=[
-                pltpu.VMEM((2, slots, tile), bf16),
-                pltpu.VMEM((slots, 2 * h), bf16),
-                pltpu.SemaphoreType.DMA((2, len(order))),
-                pltpu.SemaphoreType.DMA((len(order),)),
-            ],
+            in_specs=[anywhere, pl.BlockSpec((tile, slots), lambda i, here: (i, 0)), fixed(own), fixed(other), fixed(late)],
+            out_specs=pl.BlockSpec((1, tile, wide), lambda i, here: (0, i, 0)),
+            scratch_shapes=[pltpu.VMEM((rows, wide), bf16)],
         ),
-        cost_estimate=light,
-        compiler_params=params(28),
-        name="weights",
-    )(here, inputs, hid, *recs, *gps, *given)
+        input_output_aliases={1: 0},
+        cost_estimate=light,
+        compiler_params=params(24),
+        name="inputs_part",
+    )(here, old, inputs, own, other, late)
 
 
 def together(*values):
@@ -471,66 +484,67 @@
     wd, sg, su = w_down[0], saved_gate[0], saved_up[0]
     wd_c, sg_c, su_c = [send(v, to_core) for v in (wd, sg, su)]
 
-    order, recs, recs_c, gps, gps_c = [], [], [], [], []
+    half = slots // 2
+    recs, gps = [], []
 
     def first(chunk, toks):
-        rec, rec_c, share, *shares, pos = dispatch(here, toks, wd, wd_c, cap)
-        order.extend((k, col) for col, k in chunk)
-        recs.append(rec)
-        recs_c.append(rec_c)
+        recs[:], (share, *shares, pos) = (lambda a, b, *rest: ([a, b], rest))(
+            *dispatch(here, chunk, toks, wd, wd_c, cap, half, recs)
+        )
         return (chunk, share, pos), *shares
 
     def exchange(v):
         return lax.ppermute(v, "dp", [(0, 1), (1, 0)])
 
-    def second(state, *peers, halves=False):
+    def second(state, *peers, last=False):
         chunk, share, pos = state
-        gp, gp_c, *sums = combine(here, chunk, share, peers, pos, (sg, su), (sg_c, su_c), w, w_c, cap, halves)
-        gps.append(gp)
-        gps_c.append(gp_c)
+        gps[:], sums = (lambda a, b, *rest: ([a, b], rest))(
+            *combine(here, chunk, share, peers, pos, (sg, su), (sg_c, su_c), w, w_c, cap, half, gps, last)
+        )
         return sums
 
     r1, x0 = ring(block), send(block, to_x)
     c0, h0 = first([(0, 0)], [block])
     w = join(w_gate[0], w_up[0])
-    inputs, inputs_away = turn(here, saved_inputs[0], cap)
-    r1, x0, h0, w, inputs, inputs_away, sg_c, su_c = together(r1, x0, h0, w, inputs, inputs_away, sg_c, su_c)
+    inputs = turn(here, saved_inputs[0], cap)
+    r1, x0, h0, w, inputs, sg_c, su_c = together(r1, x0, h0, w, inputs, sg_c, su_c)
     r2, x1 = ring(r1), send(r1, to_x)
     h0, w_c = exchange(h0), send(w, to_core)
     c1, h1, g1 = first([(1, 0), (0, 1)], [x0, r1])
     h1 = exchange(h1)
     (t_r0,) = second(c0, h0)
-    r2, x1, h1, g1, t_r0 = together(r2, x1, h1, g1, t_r0)
+    hid = hidden(here, sg, su, cap)
+    r2, x1, h1, g1, t_r0, hid = together(r2, x1, h1, g1, t_r0, hid)
     r3, x2 = ring(r2), send(r2, to_x)
-    g1, inputs_c = exchange(g1), send(inputs_away, to_core)
+    g1 = exchange(g1)
     c2, h2, g2 = first([(1, 1), (0, 2)], [x1, r2])
     h2 = exchange(h2)
     t_x0, t_r1 = second(c1, h1, g1)
-    hid = hidden(here, sg, su, cap)
-    r3, x2, h2, g2, t_x0, t_r1, inputs_c, hid = together(r3, x2, h2, g2, t_x0, t_r1, inputs_c, hid)
+    r3, x2, h2, g2, t_x0, t_r1 = together(r3, x2, h2, g2, t_x0, t_r1)
     x3, w1 = send(r3, to_x), ring(t_r1)
     g2 = exchange(g2)
     c3, h3, g3 = first([(1, 2), (0, 3)], [x2, r3])
     h3 = exchange(h3)
     t_x1, t_r2 = second(c2, h2, g2)
-    hid_c = hidden(here, sg_c, su_c, cap)
-    x3, w1, h3, g3, t_x0, t_x1, t_r2, hid_c = together(x3, w1, h3, g3, t_x0, t_x1, t_r2, hid_c)
+    x3, w1, h3, g3, t_x0, t_x1, t_r2 = together(x3, w1, h3, g3, t_x0, t_x1, t_r2)
     u1, b0 = ring(t_x1), send(t_x0, to_x)
     g3 = exchange(g3)
     c4, h4 = first([(1, 3)], [x3])
     h4 = exchange(h4)
     t_x2, t_r3 = second(c3, h3, g3)
-    u1, b0, h4, t_x2, t_r3 = together(u1, b0, h4, t_x2, t_r3)
+    u1, b0, h4, t_x2, t_r3, rec_away, gp_away = together(u1, b0, h4, t_x2, t_r3, recs[1], gps[1])
+    rec_c, gp_c = send(rec_away, to_core), send(gp_away, to_core)
     a0, a1, h4 = together(add([t_x2, u1], 0), add([t_x2, u1], 1), h4)
     b2 = [send(a0, to_x), send(a1, to_x)]
-    t_x3 = second(c4, h4, halves=True)
+    t_x3 = second(c4, h4, last=True)
     b3 = [send(t, to_x) for t in t_x3]
-    away = weight_sums(here, order, inputs_c, hid_c, recs_c, gps_c, cap)
-    b2[0], away = together(b2[0], away)
-    summed = send(away, to_core)
-    w2 = [ring(add([t_r2, w1, b2[k]], k)) for k in range(2)]
+    late = send(gps[1], to_core)
+    w2 = [ring(add([t_r2, w1, b2[0]], 0))]
+    part = received_part(hid, recs[0], rec_c)
+    b2[1], part = together(b2[1], part)
+    w2.append(ring(add([t_r2, w1, b2[1]], 1)))
     w3 = [ring(add([t_r3, b3[k], w2[k]], k)) for k in range(2)]
-    weight_grads = weight_sums(here, order, inputs, hid, recs, gps, cap, summed)
+    weight_grads = inputs_part(here, (1, 3), part, inputs, gps[0], gp_c, late, cap)
     w3[1], weight_grads = together(w3[1], weight_grads)
     return (finish(t_r0, b0, *w3), weight_grads)
 

time: 117 us -> 111 us (0.949)
  waiting for transfers between devices: 24.7 us -> 21 us
  starting transfers between devices: 32.7 us -> 30.9 us
  local copies, waits for them, and re-layouts: 2.28 us -> 0.97 us
    ppermute x8, waiting for transfers between devices: 8.23 us -> 5.55 us  [exchange(): return lax.ppermute(v, 'dp', [(0, 1), (1, 0)])]
    ppermute x24 -> x25, starting transfers between devices: 23.3 us -> 22 us  [send(): return lax.ppermute(v, 'expert', perm)]
    unnamed x10, local copies, waits for them, and re-layouts: 2.28 us -> 0.97 us
    ppermute x24 -> x25, waiting for transfers between devices: 16.5 us -> 15.5 us  [send(): return lax.ppermute(v, 'expert', perm)]
    pallas_call x2 -> x1, Pallas kernels: 5.77 us -> 5.84 us  [hidden(): pl.pallas_call(functools.partial(hidden_kernel, cap), out_shape=jax.Shape...]
  transfers between devices with their start and end apart: 32 -> 33, of which waited for: 10 -> 8; matrix products, arithmetic and copies ran while one was open for 0% -> 0% of each run, Pallas kernels for 47% -> 51%
where the time goes in v8:
time: 111 us
  Pallas kernels  57 us (51%)
  starting transfers between devices  30.9 us (28%)
  waiting for transfers between devices  21 us (19%)
    ppermute x25, starting transfers between devices, send(): return lax.ppermute(v, 'expert', perm)  22 us
    pallas_call x5, Pallas kernels, combine(): pl.pallas_call(functools.partial(combine_kernel, chunk, cap, 1 if old els...  19.7 us
    ppermute x25, waiting for transfers between devices, send(): return lax.ppermute(v, 'expert', perm)  15.5 us
    pallas_call x5, Pallas kernels, dispatch(): pl.pallas_call(functools.partial(dispatch_kernel, chunk, cap, len(old) //...  14.3 us
    ppermute x8, starting transfers between devices, exchange(): return lax.ppermute(v, 'dp', [(0, 1), (1, 0)])  8.84 us
    pallas_call x1, Pallas kernels, hidden(): pl.pallas_call(functools.partial(hidden_kernel, cap), out_shape=jax.Shape...  5.84 us
    pallas_call x1, Pallas kernels, inputs_part(): pl.pallas_call(functools.partial(inputs_kernel, cap, last), out_shape=jax...  5.69 us
    ppermute x8, waiting for transfers between devices, exchange(): return lax.ppermute(v, 'dp', [(0, 1), (1, 0)])  5.55 us
  transfers between devices with their start and end apart: 33, of which 8 were waited for; matrix products, arithmetic and copies ran while one was open for 0% of the time, Pallas kernels for 51%

profile of v8, /device:TPU:0, one launch (start us, length us, event | category | flops | bytes accessed | tf_op | source)
XLA Modules:
  0.0 110.8 jit_solution(2095254103321044779)
XLA Ops:
  1.7 1.8 %pack.1.refs_0_ = bf16[200,1024]{1,0:T(8,128)(2,1)} custom-call(bf16[192,1024]{1,0:T(8,128)(2,1)} %tokens.1, s32[8,192]{1,0:T(8,128)} %bitcast.32, s32[8,192]{1,0:T(8,128)} %bitcast.33), custom_call_target="tpu_custom_call" | custom-call | flops 1048576 | bytes 16384 | tf_op jit(solution)/shard_map/pack/pallas_call | solution.py:387
  3.4 2.7 %collective-permute-start = (bf16[200,1024]{1,0:T(8,128)(2,1)}, bf16[200,1024]{1,0:T(8,128)(2,1)}, u32[]{:S(2)}, u32[]{:S(2)}) collective-permute-start(bf16[200,1024]{1,0:T(8,128)(2,1)} %pack.1.refs_0_), channel_id=1, source_target_pairs={{0,4},{1,5},{2,6},{3,7},{4,8},{5,9},{6,10},{7,11},{8,12},{9,13},{1... | collective-permute-start | bytes 1228808 | tf_op jit(solution)/shard_map/ppermute | solution.py:475
  7.6 3.9 %turn.1.inputs = bf16[1024,2304]{1,0:T(8,128)(2,1)S(1)} custom-call(s32[1]{0:T(128)} %bitcast.2.here, bf16[2304,1024]{1,0:T(8,128)(2,1)} %bitcast.31), custom_call_target="tpu_custom_call" | custom-call | flops 1048576 | bytes 16384 | tf_op jit(solution)/shard_map/turn/pallas_call | solution.py:353
  12.6 2.5 %dispatch.5 = (bf16[1152,1024]{1,0:T(8,128)(2,1)S(1)}, bf16[1152,1024]{1,0:T(8,128)(2,1)S(1)}, f32[288,384]{1,0:T(8,128)S(1)}, bf16[288,384]{1,0:T(8,128)(2,1)S(1)}, f32[8,192]{1,0:T(8,128)S(1)}) custom-call(s32[1]{0:T(128)} %bitcast.2.here, bf16[200,1024]{1,0:T(8,128)(2,1)} %pack.1.refs_0_, bf16[384,1024]{1,0:T(8,128)(2,1)S(1)} %bitcast.24, ...), custom_call_target="tpu_custom_call" | custom-call | flops 1048576 | bytes 16384 | tf_op jit(solution)/shard_map/dispatch/pallas_call | solution.py:150
  15.1 3.4 %collective-permute-done.refs_1_ = bf16[200,1024]{1,0:T(8,128)(2,1)} collective-permute-done((bf16[200,1024]{1,0:T(8,128)(2,1)}, bf16[200,1024]{1,0:T(8,128)(2,1)}, u32[]{:S(2)}, u32[]{:S(2)}) %collective-permute-start) | collective-permute-done | bytes 409632 | tf_op jit(solution)/shard_map/ppermute | solution.py:475
  22.7 3.4 %dispatch.6 = (bf16[1152,1024]{1,0:T(8,128)(2,1)S(1)}, bf16[1152,1024]{1,0:T(8,128)(2,1)S(1)}, f32[576,384]{1,0:T(8,128)S(1)}, bf16[288,384]{1,0:T(8,128)(2,1)S(...) custom-call(s32[1]{0:T(128)} %bitcast.2.here, ...), custom_call_target="tpu_custom_call", output_to_operand_aliasing={{0}: (5, {}), {1}: (6, {})} | custom-call | flops 1048576 | bytes 16384 | tf_op jit(solution)/shard_map/dispatch/pallas_call | solution.py:150
  26.7 5.8 %hidden.1.hid = bf16[384,2304]{1,0:T(8,128)(2,1)S(1)} custom-call(s32[1]{0:T(128)} %bitcast.2.here, bf16[2304,384]{1,0:T(8,128)(2,1)S(1)} %bitcast.10, bf16[2304,384]{1,0:T(8,128)(2,1)S(1)} %bitcast.17), custom_call_target="tpu_custom_call" | custom-call | flops 1048576 | bytes 16384 | tf_op jit(solution)/shard_map/hidden/pallas_call | solution.py:329
  32.5 3.1 %combine.5 = (bf16[1152,768]{1,0:T(8,128)(2,1)S(1)}, bf16[1152,768]{1,0:T(8,128)(2,1)S(1)}, bf16[192,1024]{1,0:T(8,128)(2,1)S(1)}) custom-call(s32[1]{0:T(128)} %bitcast.2.here, f32[288,384]{1,0:T(8,128)S(1)} %get-tuple-element.96.share, bf16[288,384]{1,0:T(8,128)(2,1)S(1)} %collective-permute-done.8.refs_0_, f32[8,192]{1,0:T(8,128)S(1)} %get-tuple-element.98.refs_1_, ...), custom_call_target="tpu_custom_call" | custom-call | flops 1048576 | bytes 16384 | tf_op jit(solution)/shard_map/combine/pallas_call | solution.py:225
  39.3 3.0 %dispatch.7 = (bf16[1152,1024]{1,0:T(8,128)(2,1)S(1)}, bf16[1152,1024]{1,0:T(8,128)(2,1)S(1)}, f32[576,384]{1,0:T(8,128)S(1)}, bf16[288,384]{1,0:T(8,128)(2,1)S(...) custom-call(s32[1]{0:T(128)} %bitcast.2.here, ...), custom_call_target="tpu_custom_call", output_to_operand_aliasing={{0}: (5, {}), {1}: (6, {})} | custom-call | flops 1048576 | bytes 16384 | tf_op jit(solution)/shard_map/dispatch/pallas_call | solution.py:150
  44.4 4.7 %combine.6 = (bf16[1152,768]{1,0:T(8,128)(2,1)S(1)}, bf16[1152,768]{1,0:T(8,128)(2,1)S(1)}, bf16[192,1024]{1,0:T(8,128)(2,1)S(1)}, bf16[192,1024]{1,0:T(8,128)(2,1)S(1)}) custom-call(s32[1]{0:T(128)} %bitcast.2.here, f32[576,384]{1,0:T(8,128)S(1)} %get-tuple-element.110.share, ...), custom_call_target="tpu_custom_call", output_to_operand_aliasing={{0}: (11, {}), {1}: (12, {})} | custom-call | flops 1048576 | bytes 16384 | tf_op jit(solution)/shard_map/combine/pallas_call | solution.py:225
  51.0 2.5 %collective-permute-start.17 = (bf16[288,384]{1,0:T(8,128)(2,1)S(1)}, bf16[288,384]{1,0:T(8,128)(2,1)S(1)}, u32[]{:S(2)}, u32[]{:S(2)}) collective-permute-start(bf16[288,384]{1,0:T(8,128)(2,1)S(1)} %get-tuple-element.128), channel_id=1, source_target_pairs={{0,16},{16,0},{1,17},{17,1},{2,18},{18,2},{3,19},{19,3},{4,20},{20... | collective-permute-start | bytes 663560 | tf_op jit(solution)/shard_map/ppermute | solution.py:497
  53.5 3.0 %dispatch.8 = (bf16[1152,1024]{1,0:T(8,128)(2,1)S(1)}, bf16[1152,1024]{1,0:T(8,128)(2,1)S(1)}, f32[576,384]{1,0:T(8,128)S(1)}, bf16[288,384]{1,0:T(8,128)(2,1)S(...) custom-call(s32[1]{0:T(128)} %bitcast.2.here, ...), custom_call_target="tpu_custom_call", output_to_operand_aliasing={{0}: (5, {}), {1}: (6, {})} | custom-call | flops 1048576 | bytes 16384 | tf_op jit(solution)/shard_map/dispatch/pallas_call | solution.py:150
  56.6 2.6 %collective-permute-done.17.refs_1_ = bf16[288,384]{1,0:T(8,128)(2,1)S(1)} collective-permute-done((bf16[288,384]{1,0:T(8,128)(2,1)S(1)}, bf16[288,384]{1,0:T(8,128)(2,1)S(1)}, u32[]{:S(2)}, u32[]{:S(2)}) %collective-permute-start.17) | collective-permute-done | bytes 221216 | tf_op jit(solution)/shard_map/ppermute | solution.py:497
  59.2 4.7 %combine.7 = (bf16[1152,768]{1,0:T(8,128)(2,1)S(1)}, bf16[1152,768]{1,0:T(8,128)(2,1)S(1)}, bf16[192,1024]{1,0:T(8,128)(2,1)S(1)}, bf16[192,1024]{1,0:T(8,128)(2,1)S(1)}) custom-call(s32[1]{0:T(128)} %bitcast.2.here, f32[576,384]{1,0:T(8,128)S(1)} %get-tuple-element.126.share, ...), custom_call_target="tpu_custom_call", output_to_operand_aliasing={{0}: (11, {}), {1}: (12, {})} | custom-call | flops 1048576 | bytes 16384 | tf_op jit(solution)/shard_map/combine/pallas_call | solution.py:225
  63.9 2.1 %collective-permute-start.18 = (bf16[192,1024]{1,0:T(8,128)(2,1)S(1)}, bf16[192,1024]{1,0:T(8,128)(2,1)S(1)}, u32[]{:S(2)}, u32[]{:S(2)}) collective-permute-start(bf16[192,1024]{1,0:T(8,128)(2,1)S(1)} %get-tuple-element.134), channel_id=1, source_target_pairs={{0,4},{1,5},{2,6},{3,7},{4,8},{5,9},{6,10},{7,11},{8,12},{9,13},{1... | collective-permute-start | bytes 1179656 | tf_op jit(solution)/shard_map/ppermute | solution.py:475
  68.0 2.3 %dispatch.9 = (bf16[1152,1024]{1,0:T(8,128)(2,1)S(1)}, bf16[1152,1024]{1,0:T(8,128)(2,1)S(1)}, f32[288,384]{1,0:T(8,128)S(1)}, bf16[288,384]{1,0:T(8,128)(2,1)S(1)}, f32[8,192]{1,0:T(8,128)S(1)}) custom-call(s32[1]{0:T(128)} %bitcast.2.here, bf16[200,1024]{1,0:T(8,128)(2,1)S(1)} %collective-permute-done.14.refs_0_, ...), custom_call_target="tpu_custom_call", output_to_operand_aliasing={{0}: (4, {}), {1}: (5, {})} | custom-call | flops 1048576 | bytes 16384 | tf_op jit(solution)/shard_map/dispatch/pallas_call | solution.py:150
  72.5 4.7 %combine.8 = (bf16[1152,768]{1,0:T(8,128)(2,1)S(1)}, bf16[1152,768]{1,0:T(8,128)(2,1)S(1)}, bf16[192,1024]{1,0:T(8,128)(2,1)S(1)}, bf16[192,1024]{1,0:T(8,128)(2,1)S(1)}) custom-call(s32[1]{0:T(128)} %bitcast.2.here, f32[576,384]{1,0:T(8,128)S(1)} %get-tuple-element.140.share, ...), custom_call_target="tpu_custom_call", output_to_operand_aliasing={{0}: (11, {}), {1}: (12, {})} | custom-call | flops 1048576 | bytes 16384 | tf_op jit(solution)/shard_map/combine/pallas_call | solution.py:225
  79.9 2.7 %combine.9 = (bf16[1152,768]{1,0:T(8,128)(2,1)S(1)}, bf16[144,768]{1,0:T(8,128)(2,1)S(1)}, bf16[192,512]{1,0:T(8,128)(2,1)S(1)}, bf16[192,512]{1,0:T(8,128)(2,1)S(1)}) custom-call(s32[1]{0:T(128)} %bitcast.2.here, f32[288,384]{1,0:T(8,128)S(1)} %get-tuple-element.152.share, ...), custom_call_target="tpu_custom_call", output_to_operand_aliasing={{0}: (10, {})} | custom-call | flops 1048576 | bytes 16384 | tf_op jit(solution)/shard_map/combine/pallas_call | solution.py:225
  84.2 4.4 %received_part.1.old = bf16[1,1024,1152]{2,1,0:T(8,128)(2,1)} custom-call(bf16[384,2304]{1,0:T(8,128)(2,1)S(1)} %hidden.1.hid, bf16[1152,1024]{1,0:T(8,128)(2,1)S(1)} %get-tuple-element.166.own, bf16[1152,1024]{1,0:T(8,128)(2,1)S(1)} %collective-permute-done.28.other), custom_call_target="tpu_custom_call" | custom-call | flops 1048576 | bytes 16384 | tf_op jit(solution)/shard_map/received_part/pallas_call | solution.py:410
  91.9 2.2 %collective-permute-done.26.refs_1_ = bf16[192,512]{1,0:T(8,128)(2,1)S(1)} collective-permute-done((bf16[192,512]{1,0:T(8,128)(2,1)S(1)}, bf16[192,512]{1,0:T(8,128)(2,1)S(1)}, u32[]{:S(2)}, u32[]{:S(2)}) %collective-permute-start.26) | collective-permute-done | bytes 196640 | tf_op jit(solution)/shard_map/ppermute | solution.py:475
  94.1 4.2 %collective-permute-done.29.refs_2_ = bf16[192,512]{1,0:T(8,128)(2,1)S(1)} collective-permute-done((bf16[192,512]{1,0:T(8,128)(2,1)S(1)}, bf16[192,512]{1,0:T(8,128)(2,1)S(1)}, u32[]{:S(2)}, u32[]{:S(2)}) %collective-permute-start.29) | collective-permute-done | bytes 196640 | tf_op jit(solution)/shard_map/ppermute | solution.py:475
  98.5 3.6 %collective-permute-done.24.refs_2_ = bf16[192,512]{1,0:T(8,128)(2,1)S(1)} collective-permute-done((bf16[192,512]{1,0:T(8,128)(2,1)S(1)}, bf16[192,512]{1,0:T(8,128)(2,1)S(1)}, u32[]{:S(2)}, u32[]{:S(2)}) %collective-permute-start.24) | collective-permute-done | bytes 196640 | tf_op jit(solution)/shard_map/ppermute | solution.py:475
  102.2 5.7 %inputs_part.1 = bf16[1,1024,1152]{2,1,0:T(8,128)(2,1)} custom-call(s32[1]{0:T(128)} %bitcast.2.here, bf16[1,1024,1152]{2,1,0:T(8,128)(2,1)} %received_part.1.old, bf16[1024,2304]{1,0:T(8,128)(2,1)S(1)} %turn.1.inputs, bf16[1152,768]{1,0:T(8,128)(2,1)S(1)} %get-tuple-element.171.own, ...), custom_call_target="tpu_custom_call", output_to_operand_aliasing={{}: (1, {})} | custom-call | flops 1048576 | bytes 16384 | tf_op jit(solution)/shard_map/inputs_part/pallas_call | solution.py:443
  107.9 2.0 %collective-permute-done.25.left = bf16[192,512]{1,0:T(8,128)(2,1)S(1)} collective-permute-done((bf16[192,512]{1,0:T(8,128)(2,1)S(1)}, bf16[192,512]{1,0:T(8,128)(2,1)S(1)}, u32[]{:S(2)}, u32[]{:S(2)}) %collective-permute-start.25) | collective-permute-done | bytes 196640 | tf_op jit(solution)/shard_map/ppermute | solution.py:475
  (75 shorter events, 28.9 us)
Async XLA Ops:
  0.6 17.9 %collective-permute-start.3 = (bf16[2304,384]{1,0:T(8,128)(2,1)}, bf16[2304,384]{1,0:T(8,128)(2,1)S(1)}, u32[]{:S(2)}, u32[]{:S(2)}) collective-permute-start(bf16[2304,384]{1,0:T(8,128)(2,1)} %bitcast.9), channel_id=1, source_target_pairs={{0,1},{1,0},{2,3},{3,2},{4,5},{5,4},{6,7},{7,6},{8,9},{9,8},{10,11... | collective-permute-start | bytes 5308424 | tf_op jit(solution)/shard_map/ppermute | solution.py:475
  1.1 17.4 %collective-permute-start.4 = (bf16[2304,384]{1,0:T(8,128)(2,1)}, bf16[2304,384]{1,0:T(8,128)(2,1)S(1)}, u32[]{:S(2)}, u32[]{:S(2)}) collective-permute-start(bf16[2304,384]{1,0:T(8,128)(2,1)} %bitcast.16), channel_id=1, source_target_pairs={{0,1},{1,0},{2,3},{3,2},{4,5},{5,4},{6,7},{7,6},{8,9},{9,8},{10,11... | collective-permute-start | bytes 5308424 | tf_op jit(solution)/shard_map/ppermute | solution.py:475
  1.2 10.5 %collective-permute-start.2 = (bf16[384,1024]{1,0:T(8,128)(2,1)}, bf16[384,1024]{1,0:T(8,128)(2,1)}, u32[]{:S(2)}, u32[]{:S(2)}) collective-permute-start(bf16[384,1024]{1,0:T(8,128)(2,1)} %bitcast.23), channel_id=1, source_target_pairs={{0,1},{1,0},{2,3},{3,2},{4,5},{5,4},{6,7},{7,6},{8,9},{9,8},{10,11... | collective-permute-start | bytes 2359304 | tf_op jit(solution)/shard_map/ppermute | solution.py:475
  3.4 15.1 %collective-permute-start = (bf16[200,1024]{1,0:T(8,128)(2,1)}, bf16[200,1024]{1,0:T(8,128)(2,1)}, u32[]{:S(2)}, u32[]{:S(2)}) collective-permute-start(bf16[200,1024]{1,0:T(8,128)(2,1)} %pack.1.refs_0_), channel_id=1, source_target_pairs={{0,4},{1,5},{2,6},{3,7},{4,8},{5,9},{6,10},{7,11},{8,12},{9,13},{1... | collective-permute-start | bytes 1228808 | tf_op jit(solution)/shard_map/ppermute | solution.py:475
  6.1 12.4 %collective-permute-start.1 = (bf16[200,1024]{1,0:T(8,128)(2,1)}, bf16[200,1024]{1,0:T(8,128)(2,1)}, u32[]{:S(2)}, u32[]{:S(2)}) collective-permute-start(bf16[200,1024]{1,0:T(8,128)(2,1)} %pack.1.refs_0_), channel_id=1, source_target_pairs={{0,2},{1,3},{2,0},{3,1},{4,6},{5,7},{6,4},{7,5},{8,10},{9,11},{10,... | collective-permute-start | bytes 1228808 | tf_op jit(solution)/shard_map/ppermute | solution.py:475
  18.6 14.0 %collective-permute-start.9 = (bf16[1024,768]{1,0:T(8,128)(2,1)S(1)}, bf16[1024,768]{1,0:T(8,128)(2,1)S(1)}, u32[]{:S(2)}, u32[]{:S(2)}) collective-permute-start(bf16[1024,768]{1,0:T(8,128)(2,1)S(1)} %join.1.refs_6_.refs_7_), channel_id=1, source_target_pairs={{0,1},{1,0},{2,3},{3,2},{4,5},{5,4},{6,7},{7,6},{8,9},{9,8},{10,11... | collective-permute-start | bytes 4718600 | tf_op jit(solution)/shard_map/ppermute | solution.py:475
  18.6 17.0 %collective-permute-start.5 = (bf16[200,1024]{1,0:T(8,128)(2,1)}, bf16[200,1024]{1,0:T(8,128)(2,1)S(1)}, u32[]{:S(2)}, u32[]{:S(2)}) collective-permute-start(bf16[200,1024]{1,0:T(8,128)(2,1)} %collective-permute-done.refs_1_), channel_id=1, source_target_pairs={{0,4},{1,5},{2,6},{3,7},{4,8},{5,9},{6,10},{7,11},{8,12},{9,13},{1... | collective-permute-start | bytes 1228808 | tf_op jit(solution)/shard_map/ppermute | solution.py:475
  19.6 16.0 %collective-permute-start.6 = (bf16[200,1024]{1,0:T(8,128)(2,1)}, bf16[200,1024]{1,0:T(8,128)(2,1)S(1)}, u32[]{:S(2)}, u32[]{:S(2)}) collective-permute-start(bf16[200,1024]{1,0:T(8,128)(2,1)} %collective-permute-done.refs_1_), channel_id=1, source_target_pairs={{0,2},{1,3},{2,0},{3,1},{4,6},{5,7},{6,4},{7,5},{8,10},{9,11},{10,... | collective-permute-start | bytes 1228808 | tf_op jit(solution)/shard_map/ppermute | solution.py:475
  21.1 11.4 %collective-permute-start.8 = (bf16[288,384]{1,0:T(8,128)(2,1)S(1)}, bf16[288,384]{1,0:T(8,128)(2,1)S(1)}, u32[]{:S(2)}, u32[]{:S(2)}) collective-permute-start(bf16[288,384]{1,0:T(8,128)(2,1)S(1)} %get-tuple-element.97), channel_id=1, source_target_pairs={{0,16},{16,0},{1,17},{17,1},{2,18},{18,2},{3,19},{19,3},{4,20},{20... | collective-permute-start | bytes 663560 | tf_op jit(solution)/shard_map/ppermute | solution.py:497
  26.1 9.5 %collective-permute-start.7 = (bf16[288,384]{1,0:T(8,128)(2,1)S(1)}, bf16[288,384]{1,0:T(8,128)(2,1)S(1)}, u32[]{:S(2)}, u32[]{:S(2)}) collective-permute-start(bf16[288,384]{1,0:T(8,128)(2,1)S(1)} %get-tuple-element.94), channel_id=1, source_target_pairs={{0,16},{16,0},{1,17},{17,1},{2,18},{18,2},{3,19},{19,3},{4,20},{20... | collective-permute-start | bytes 663560 | tf_op jit(solution)/shard_map/ppermute | solution.py:497
  35.6 13.4 %collective-permute-start.10 = (bf16[200,1024]{1,0:T(8,128)(2,1)S(1)}, bf16[200,1024]{1,0:T(8,128)(2,1)S(1)}, u32[]{:S(2)}, u32[]{:S(2)}) collective-permute-start(bf16[200,1024]{1,0:T(8,128)(2,1)S(1)} %collective-permute-done.5.refs_1_), channel_id=1, source_target_pairs={{0,4},{1,5},{2,6},{3,7},{4,8},{5,9},{6,10},{7,11},{8,12},{9,13},{1... | collective-permute-start | bytes 1228808 | tf_op jit(solution)/shard_map/ppermute | solution.py:475
  37.3 11.8 %collective-permute-start.11 = (bf16[200,1024]{1,0:T(8,128)(2,1)S(1)}, bf16[200,1024]{1,0:T(8,128)(2,1)S(1)}, u32[]{:S(2)}, u32[]{:S(2)}) collective-permute-start(bf16[200,1024]{1,0:T(8,128)(2,1)S(1)} %collective-permute-done.5.refs_1_), channel_id=1, source_target_pairs={{0,2},{1,3},{2,0},{3,1},{4,6},{5,7},{6,4},{7,5},{8,10},{9,11},{10,... | collective-permute-start | bytes 1228808 | tf_op jit(solution)/shard_map/ppermute | solution.py:475
  49.0 14.9 %collective-permute-start.14 = (bf16[200,1024]{1,0:T(8,128)(2,1)S(1)}, bf16[200,1024]{1,0:T(8,128)(2,1)S(1)}, u32[]{:S(2)}, u32[]{:S(2)}) collective-permute-start(bf16[200,1024]{1,0:T(8,128)(2,1)S(1)} %collective-permute-done.10.refs_1_), channel_id=1, source_target_pairs={{0,2},{1,3},{2,0},{3,1},{4,6},{5,7},{6,4},{7,5},{8,10},{9,11},{10,... | collective-permute-start | bytes 1228808 | tf_op jit(solution)/shard_map/ppermute | solution.py:475
  50.6 13.3 %collective-permute-start.15 = (bf16[192,1024]{1,0:T(8,128)(2,1)S(1)}, bf16[192,1024]{1,0:T(8,128)(2,1)S(1)}, u32[]{:S(2)}, u32[]{:S(2)}) collective-permute-start(bf16[192,1024]{1,0:T(8,128)(2,1)S(1)} %get-tuple-element.119), channel_id=1, source_target_pairs={{0,4},{1,5},{2,6},{3,7},{4,8},{5,9},{6,10},{7,11},{8,12},{9,13},{1... | collective-permute-start | bytes 1179656 | tf_op jit(solution)/shard_map/ppermute | solution.py:475
  63.9 13.2 %collective-permute-start.18 = (bf16[192,1024]{1,0:T(8,128)(2,1)S(1)}, bf16[192,1024]{1,0:T(8,128)(2,1)S(1)}, u32[]{:S(2)}, u32[]{:S(2)}) collective-permute-start(bf16[192,1024]{1,0:T(8,128)(2,1)S(1)} %get-tuple-element.134), channel_id=1, source_target_pairs={{0,4},{1,5},{2,6},{3,7},{4,8},{5,9},{6,10},{7,11},{8,12},{9,13},{1... | collective-permute-start | bytes 1179656 | tf_op jit(solution)/shard_map/ppermute | solution.py:475
  66.0 11.1 %collective-permute-start.19 = (bf16[192,1024]{1,0:T(8,128)(2,1)S(1)}, bf16[192,1024]{1,0:T(8,128)(2,1)S(1)}, u32[]{:S(2)}, u32[]{:S(2)}) collective-permute-start(bf16[192,1024]{1,0:T(8,128)(2,1)S(1)} %get-tuple-element.135), channel_id=1, source_target_pairs={{0,2},{1,3},{2,0},{3,1},{4,6},{5,7},{6,4},{7,5},{8,10},{9,11},{10,... | collective-permute-start | bytes 1179656 | tf_op jit(solution)/shard_map/ppermute | solution.py:475
  77.2 25.0 %collective-permute-start.31 = (bf16[1152,768]{1,0:T(8,128)(2,1)S(1)}, bf16[1152,768]{1,0:T(8,128)(2,1)S(1)}, u32[]{:S(2)}, u32[]{:S(2)}) collective-permute-start(bf16[1152,768]{1,0:T(8,128)(2,1)S(1)} %get-tuple-element.172), channel_id=1, source_target_pairs={{0,1},{1,0},{2,3},{3,2},{4,5},{5,4},{6,7},{7,6},{8,9},{9,8},{10,11... | collective-permute-start | bytes 5308424 | tf_op jit(solution)/shard_map/ppermute | solution.py:475
  77.8 10.7 %collective-permute-start.27 = (bf16[192,512]{1,0:T(8,128)(2,1)S(1)}, bf16[192,512]{1,0:T(8,128)(2,1)S(1)}, u32[]{:S(2)}, u32[]{:S(2)}) collective-permute-start(bf16[192,512]{1,0:T(8,128)(2,1)S(1)} %add.7), channel_id=1, source_target_pairs={{0,2},{1,3},{2,0},{3,1},{4,6},{5,7},{6,4},{7,5},{8,10},{9,11},{10,... | collective-permute-start | bytes 589832 | tf_op jit(solution)/shard_map/ppermute | solution.py:475
  79.4 10.8 %collective-permute-start.23 = (bf16[192,512]{1,0:T(8,128)(2,1)S(1)}, bf16[192,512]{1,0:T(8,128)(2,1)S(1)}, u32[]{:S(2)}, u32[]{:S(2)}) collective-permute-start(bf16[192,512]{1,0:T(8,128)(2,1)S(1)} %add.6), channel_id=1, source_target_pairs={{0,2},{1,3},{2,0},{3,1},{4,6},{5,7},{6,4},{7,5},{8,10},{9,11},{10,... | collective-permute-start | bytes 589832 | tf_op jit(solution)/shard_map/ppermute | solution.py:475
  82.6 11.5 %collective-permute-start.26 = (bf16[192,512]{1,0:T(8,128)(2,1)S(1)}, bf16[192,512]{1,0:T(8,128)(2,1)S(1)}, u32[]{:S(2)}, u32[]{:S(2)}) collective-permute-start(bf16[192,512]{1,0:T(8,128)(2,1)S(1)} %get-tuple-element.163), channel_id=1, source_target_pairs={{0,2},{1,3},{2,0},{3,1},{4,6},{5,7},{6,4},{7,5},{8,10},{9,11},{10,... | collective-permute-start | bytes 589832 | tf_op jit(solution)/shard_map/ppermute | solution.py:475
  88.6 9.7 %collective-permute-start.29 = (bf16[192,512]{1,0:T(8,128)(2,1)S(1)}, bf16[192,512]{1,0:T(8,128)(2,1)S(1)}, u32[]{:S(2)}, u32[]{:S(2)}) collective-permute-start(bf16[192,512]{1,0:T(8,128)(2,1)S(1)} %add.10), channel_id=1, source_target_pairs={{0,4},{1,5},{2,6},{3,7},{4,8},{5,9},{6,10},{7,11},{8,12},{9,13},{1... | collective-permute-start | bytes 589832 | tf_op jit(solution)/shard_map/ppermute | solution.py:475
  89.6 8.9 %collective-permute-start.22 = (bf16[192,512]{1,0:T(8,128)(2,1)S(1)}, bf16[192,512]{1,0:T(8,128)(2,1)S(1)}, u32[]{:S(2)}, u32[]{:S(2)}) collective-permute-start(bf16[192,512]{1,0:T(8,128)(2,1)S(1)} %get-tuple-element.159), channel_id=1, source_target_pairs={{0,2},{1,3},{2,0},{3,1},{4,6},{5,7},{6,4},{7,5},{8,10},{9,11},{10,... | collective-permute-start | bytes 589832 | tf_op jit(solution)/shard_map/ppermute | solution.py:475
  90.3 11.8 %collective-permute-start.24 = (bf16[192,512]{1,0:T(8,128)(2,1)S(1)}, bf16[192,512]{1,0:T(8,128)(2,1)S(1)}, u32[]{:S(2)}, u32[]{:S(2)}) collective-permute-start(bf16[192,512]{1,0:T(8,128)(2,1)S(1)} %add.8), channel_id=1, source_target_pairs={{0,4},{1,5},{2,6},{3,7},{4,8},{5,9},{6,10},{7,11},{8,12},{9,13},{1... | collective-permute-start | bytes 589832 | tf_op jit(solution)/shard_map/ppermute | solution.py:475
  98.4 9.5 %collective-permute-start.30 = (bf16[192,512]{1,0:T(8,128)(2,1)S(1)}, bf16[192,512]{1,0:T(8,128)(2,1)S(1)}, u32[]{:S(2)}, u32[]{:S(2)}) collective-permute-start(bf16[192,512]{1,0:T(8,128)(2,1)S(1)} %add.11), channel_id=1, source_target_pairs={{0,4},{1,5},{2,6},{3,7},{4,8},{5,9},{6,10},{7,11},{8,12},{9,13},{1... | collective-permute-start | bytes 589832 | tf_op jit(solution)/shard_map/ppermute | solution.py:475
  (14 other events, 81.4 us)

commit v9 on v8

--- a/solution.py
+++ b/solution.py
@@ -28,6 +28,17 @@
     grad_gate_pre = (grad_hidden * up_pre * dsilu).astype(bf16)
     grad_up_pre = (grad_hidden * silu).astype(bf16)
     return (grad_gate_pre, grad_up_pre)
+
+
+def sigmoid_of(x):
+    return 0.5 * jnp.tanh(0.5 * x) + 0.5
+
+
+def kernel_grads(grad_hidden, gate_pre, up_pre):
+    sigmoid = sigmoid_of(gate_pre)
+    silu = gate_pre * sigmoid
+    dsilu = sigmoid + silu * (1.0 - sigmoid)
+    return ((grad_hidden * up_pre * dsilu).astype(bf16), (grad_hidden * silu).astype(bf16))
 
 
 def body_any(out_grad, routes, gate_codes, w_gate, w_up, w_down, saved_inputs, saved_gate, saved_up):
@@ -128,7 +139,8 @@
             rec[a, at, :] = rows[a * cap : (a + 1) * cap]
             to = plane_rows(here[0], *chunk[rel], cap)
             copies.append(pltpu.make_async_copy(rec.at[a, at, :], buf.at[to, :], sems.at[len(copies)]))
-            copies[-1].start()
+    for c in copies:
+        c.start()
     for a, wd in enumerate((wd0, wd1)):
         gh = contract_cols(rec[a], wd[...])
         share[a * n * cap : (a + 1) * n * cap, :] = gh
@@ -167,7 +179,7 @@
         pos, *refs = refs[1:]
     else:
         peer0, peer1, pos, *refs = refs
-    saved, ws, refs = refs[:4], refs[4:6], refs[6 + begun * (1 if last else 2) :]
+    saved, ws, refs = refs[:4], refs[4:6], refs[6 + begun :]
     buffers, backs, (held, gps, sems, out_sems) = refs[:2], refs[2:-4], refs[-4:]
     h = share.shape[1]
     copies = []
@@ -180,24 +192,27 @@
     for c in copies:
         c.start()
     slot = lax.broadcasted_iota(jnp.int32, (cap, pos.shape[1]), 0).astype(f32)
-    sums, leaving = [None] * n, []
-    for a, (w, peer) in enumerate(zip(ws, (peer0, peer1))):
-        gp = gps.at[a]
+    leaving = []
+    for c in copies:
+        c.wait()
+    for a, peer in enumerate((peer0, peer1)):
         for rel in range(n):
             i = a * n + rel
-            copies[2 * i].wait()
-            copies[2 * i + 1].wait()
-            gh = share[i * cap : (i + 1) * cap, :] + peer[rel * cap : (rel + 1) * cap, :].astype(f32)
-            gg, gu = activation_grads(gh, held[2 * i].astype(f32), held[2 * i + 1].astype(f32))
-            gp[rel * cap : (rel + 1) * cap, :h] = gg
-            gp[rel * cap : (rel + 1) * cap, h:] = gu
+            at = slice(rel * cap, (rel + 1) * cap)
+            gh = share[i * cap : (i + 1) * cap, :] + peer[at, :].astype(f32)
+            gg, gu = kernel_grads(gh, held[2 * i].astype(f32), held[2 * i + 1].astype(f32))
+            gps[a, at, :h] = gg
+            gps[a, at, h:] = gu
             if a == 0 or not last:
                 to = buffers[a].at[plane_rows(here[0], *chunk[rel], cap), :]
-                leaving.append(pltpu.make_async_copy(gp.at[rel * cap : (rel + 1) * cap, :], to, out_sems.at[i]))
-                leaving[-1].start()
-        if a == 1 and last:
-            buffers[1][...] = gp[...]
-        slots = contract_cols(gp[...], w[...]).astype(bf16)
+                leaving.append(pltpu.make_async_copy(gps.at[a, at, :], to, out_sems.at[i]))
+    for c in leaving:
+        c.start()
+    if last:
+        buffers[1][...] = gps[1]
+    sums = [None] * n
+    for a, w in enumerate(ws):
+        slots = contract_cols(gps[a], w[...]).astype(bf16)
         for rel in range(n):
             i = a * n + rel
             pick = jnp.where(slot == pos[i : i + 1, :], 1.0, 0.0).astype(bf16)
@@ -223,7 +238,7 @@
     outs = [(rows, 2 * h), (n * cap if last else rows, 2 * h)] + ([(tok, d // 2)] * 2 if last else [(tok, d)] * n)
     first_old = 2 + len(peers) + 1 + 4 + 2
     return pl.pallas_call(
-        functools.partial(combine_kernel, chunk, cap, 1 if old else 0, last),
+        functools.partial(combine_kernel, chunk, cap, len(old), last),
         out_shape=[jax.ShapeDtypeStruct(s, bf16) for s in outs],
         in_specs=[on_scalar] + [on_chip] * (2 + len(peers)) + [anywhere] * 4 + [on_chip] * 2 + [anywhere] * len(old),
         out_specs=[anywhere, on_chip if last else anywhere] + [on_chip] * (len(outs) - 2),
@@ -303,39 +318,34 @@
     return pltpu.with_memory_space_constraint(v, pltpu.HBM)
 
 
-def hidden_kernel(cap, here, gate, up, out, held, sems):
-    rows = held.shape[2]
+def hidden_kernel(cap, k, here, gate, up, out, held, sems):
+    plane = lax.rem(here[0] + k, 2)
     copies = []
-    for k in range(2):
-        plane = lax.rem(here[0] + k, 2)
-        for i, v in enumerate((gate, up)):
-            for q in range(rows // cap):
-                at = pl.ds(pl.multiple_of((2 * q + plane) * cap, 16), cap)
-                to = held.at[k, i, pl.ds(q * cap, cap), :]
-                copies.append(pltpu.make_async_copy(v.at[at, :], to, sems.at[len(copies)]))
+    for i, v in enumerate((gate, up)):
+        for q in range(held.shape[1] // cap):
+            at = pl.ds(pl.multiple_of((2 * q + plane) * cap, 16), cap)
+            to = held.at[i, pl.ds(q * cap, cap), :]
+            copies.append(pltpu.make_async_copy(v.at[at, :], to, sems.at[len(copies)]))
     for c in copies:
         c.start()
-    for k in range(2):
-        for c in copies[k * len(copies) // 2 : (k + 1) * len(copies) // 2]:
-            c.wait()
-        gate_pre = held[k, 0].astype(f32)
-        out[:, k * rows : (k + 1) * rows] = (
-            (gate_pre * jax.nn.sigmoid(gate_pre) * held[k, 1].astype(f32)).astype(bf16).T
-        )
-
-
-def hidden(here, gate, up, cap):
+    for c in copies:
+        c.wait()
+    gate_pre = held[0].astype(f32)
+    out[...] = (gate_pre * sigmoid_of(gate_pre) * held[1].astype(f32)).astype(bf16).T
+
+
+def hidden(here, gate, up, cap, k):
     slots, h = gate.shape
     return pl.pallas_call(
-        functools.partial(hidden_kernel, cap),
-        out_shape=jax.ShapeDtypeStruct((h, slots), bf16),
+        functools.partial(hidden_kernel, cap, k),
+        out_shape=jax.ShapeDtypeStruct((h, slots // 2), bf16),
         in_specs=[on_scalar, anywhere, anywhere],
         out_specs=on_chip,
-        scratch_shapes=[pltpu.VMEM((2, 2, slots // 2, h), bf16), pltpu.SemaphoreType.DMA((2 * slots // cap,))],
-        cost_estimate=light,
-        compiler_params=params(24),
+        scratch_shapes=[pltpu.VMEM((2, slots // 2, h), bf16), pltpu.SemaphoreType.DMA((slots // cap,))],
+        cost_estimate=light,
+        compiler_params=params(16),
         name="hidden",
-    )(here, gate, up)
+    )(here, in_hbm(gate), in_hbm(up))
 
 
 def turn_kernel(cap, here, v, out, held):
@@ -396,27 +406,26 @@
     )(in_hbm(tokens), in_hbm(routes), in_hbm(codes))
 
 
-def received_kernel(hid, own, other, out):
-    rows = own.shape[0]
-    part = jnp.dot(hid[:, :rows], own[...], preferred_element_type=f32)
-    part = part + jnp.dot(hid[:, rows:], other[...], preferred_element_type=f32)
+def received_kernel(hid, hid_c, own, other, out):
+    part = jnp.dot(hid[...], own[...], preferred_element_type=f32)
+    part = part + jnp.dot(hid_c[...], other[...], preferred_element_type=f32)
     out[0] = (part * loss_scale).astype(bf16).T
 
 
-def received_part(hid, own, other):
-    h, slots = hid.shape
+def received_part(hid, hid_c, own, other):
+    h = hid.shape[0]
     rows, d = own.shape
     tile = 256
     return pl.pallas_call(
         received_kernel,
         out_shape=jax.ShapeDtypeStruct((1, d, 3 * h), bf16),
         grid=(d // tile,),
-        in_specs=[pl.BlockSpec((h, slots), lambda i: (0, 0))] + [pl.BlockSpec((rows, tile), lambda i: (0, i))] * 2,
+        in_specs=[pl.BlockSpec((h, rows), lambda i: (0, 0))] * 2 + [pl.BlockSpec((rows, tile), lambda i: (0, i))] * 2,
         out_specs=pl.BlockSpec((1, tile, h), lambda i: (0, i, 2)),
         cost_estimate=light,
         compiler_params=params(20),
         name="received_part",
-    )(hid, own, other)
+    )(hid, hid_c, own, other)
 
 
 def inputs_kernel(cap, last, here, old, inputs, own, other, late, out, held):
@@ -507,14 +516,14 @@
     c0, h0 = first([(0, 0)], [block])
     w = join(w_gate[0], w_up[0])
     inputs = turn(here, saved_inputs[0], cap)
-    r1, x0, h0, w, inputs, sg_c, su_c = together(r1, x0, h0, w, inputs, sg_c, su_c)
+    hid = hidden(here, sg, su, cap, 0)
+    r1, x0, h0, w, inputs, hid, sg_c, su_c = together(r1, x0, h0, w, inputs, hid, sg_c, su_c)
     r2, x1 = ring(r1), send(r1, to_x)
     h0, w_c = exchange(h0), send(w, to_core)
     c1, h1, g1 = first([(1, 0), (0, 1)], [x0, r1])
     h1 = exchange(h1)
     (t_r0,) = second(c0, h0)
-    hid = hidden(here, sg, su, cap)
-    r2, x1, h1, g1, t_r0, hid = together(r2, x1, h1, g1, t_r0, hid)
+    r2, x1, h1, g1, t_r0 = together(r2, x1, h1, g1, t_r0)
     r3, x2 = ring(r2), send(r2, to_x)
     g1 = exchange(g1)
     c2, h2, g2 = first([(1, 1), (0, 2)], [x1, r2])
@@ -532,17 +541,18 @@
     c4, h4 = first([(1, 3)], [x3])
     h4 = exchange(h4)
     t_x2, t_r3 = second(c3, h3, g3)
-    u1, b0, h4, t_x2, t_r3, rec_away, gp_away = together(u1, b0, h4, t_x2, t_r3, recs[1], gps[1])
+    hid_c = hidden(here, sg, su, cap, 1)
+    u1, b0, h4, t_x2, t_r3, hid_c, rec_away, gp_away = together(u1, b0, h4, t_x2, t_r3, hid_c, recs[1], gps[1])
     rec_c, gp_c = send(rec_away, to_core), send(gp_away, to_core)
     a0, a1, h4 = together(add([t_x2, u1], 0), add([t_x2, u1], 1), h4)
     b2 = [send(a0, to_x), send(a1, to_x)]
-    t_x3 = second(c4, h4, last=True)
-    b3 = [send(t, to_x) for t in t_x3]
+    left, right = second(c4, h4, last=True)
+    left, rec_c = together(left, rec_c)
+    b3 = [send(left, to_x), send(right, to_x)]
     late = send(gps[1], to_core)
-    w2 = [ring(add([t_r2, w1, b2[0]], 0))]
-    part = received_part(hid, recs[0], rec_c)
-    b2[1], part = together(b2[1], part)
-    w2.append(ring(add([t_r2, w1, b2[1]], 1)))
+    w2 = [ring(add([t_r2, w1, b2[k]], k)) for k in range(2)]
+    part = received_part(hid, hid_c, recs[0], rec_c)
+    w2[0], part = together(w2[0], part)
     w3 = [ring(add([t_r3, b3[k], w2[k]], k)) for k in range(2)]
     weight_grads = inputs_part(here, (1, 3), part, inputs, gps[0], gp_c, late, cap)
     w3[1], weight_grads = together(w3[1], weight_grads)

time: 111 us -> 109 us (0.982)
  starting transfers between devices: 30.9 us -> 34.8 us
  waiting for transfers between devices: 21 us -> 17.4 us
  Pallas kernels: 57 us -> 54.2 us
    ppermute x25, waiting for transfers between devices: 15.5 us -> 8.85 us  [send(): return lax.ppermute(v, 'expert', perm)]
    ppermute x25, starting transfers between devices: 22 us -> 26 us  [send(): return lax.ppermute(v, 'expert', perm)]
    ppermute x8, waiting for transfers between devices: 5.55 us -> 8.55 us  [exchange(): return lax.ppermute(v, 'dp', [(0, 1), (1, 0)])]
    pallas_call x6 -> x7, Pallas kernels: 25.6 us -> 23.4 us  [the longest x5 19 us: combine(): pl.pallas_call(functools.partial(combine_kernel, chunk, cap, len(old), la...]
  transfers between devices with their start and end apart: 33 -> 33, of which waited for: 8 -> 9; matrix products, arithmetic and copies ran while one was open for 0% -> 0% of each run, Pallas kernels for 51% -> 49%
where the time goes in v9:
time: 109 us; the launch traced here: 108 us
  Pallas kernels  54.2 us (50%)
  starting transfers between devices  34.8 us (32%)
  waiting for transfers between devices  17.4 us (16%)
    ppermute x25, starting transfers between devices, send(): return lax.ppermute(v, 'expert', perm)  26 us
    pallas_call x5, Pallas kernels, combine(): pl.pallas_call(functools.partial(combine_kernel, chunk, cap, len(old), la...  19 us
    pallas_call x5, Pallas kernels, dispatch(): pl.pallas_call(functools.partial(dispatch_kernel, chunk, cap, len(old) //...  13.7 us
    ppermute x25, waiting for transfers between devices, send(): return lax.ppermute(v, 'expert', perm)  8.85 us
    ppermute x8, starting transfers between devices, exchange(): return lax.ppermute(v, 'dp', [(0, 1), (1, 0)])  8.83 us
    ppermute x8, waiting for transfers between devices, exchange(): return lax.ppermute(v, 'dp', [(0, 1), (1, 0)])  8.55 us
    pallas_call x1, Pallas kernels, inputs_part(): pl.pallas_call(functools.partial(inputs_kernel, cap, last), out_shape=jax...  5.66 us
    pallas_call x2, Pallas kernels, hidden(): pl.pallas_call(functools.partial(hidden_kernel, cap, k), out_shape=jax.Sh...  4.44 us
  transfers between devices with their start and end apart: 33, of which 9 were waited for; matrix products, arithmetic and copies ran while one was open for 0% of the time, Pallas kernels for 49%

profile of v9, /device:TPU:0, one launch (start us, length us, event | category | flops | bytes accessed | tf_op | source)
XLA Modules:
  0.0 108.4 jit_solution(11848735644124639680)
XLA Ops:
  3.4 2.7 %collective-permute-start = (bf16[200,1024]{1,0:T(8,128)(2,1)}, bf16[200,1024]{1,0:T(8,128)(2,1)}, u32[]{:S(2)}, u32[]{:S(2)}) collective-permute-start(bf16[200,1024]{1,0:T(8,128)(2,1)} %pack.1.refs_0_), channel_id=1, source_target_pairs={{0,4},{1,5},{2,6},{3,7},{4,8},{5,9},{6,10},{7,11},{8,12},{9,13},{1... | collective-permute-start | bytes 1228808 | tf_op jit(solution)/shard_map/ppermute | solution.py:484
  7.6 2.2 %hidden.2.hid = bf16[384,1152]{1,0:T(8,128)(2,1)S(1)} custom-call(s32[1]{0:T(128)} %bitcast.2.here, bf16[2304,384]{1,0:T(8,128)(2,1)} %bitcast.10, bf16[2304,384]{1,0:T(8,128)(2,1)} %bitcast.18), custom_call_target="tpu_custom_call" | custom-call | flops 1048576 | bytes 16384 | tf_op jit(solution)/shard_map/hidden/pallas_call | solution.py:339
  9.9 3.9 %turn.1.inputs = bf16[1024,2304]{1,0:T(8,128)(2,1)S(1)} custom-call(s32[1]{0:T(128)} %bitcast.2.here, bf16[2304,1024]{1,0:T(8,128)(2,1)} %bitcast.33), custom_call_target="tpu_custom_call" | custom-call | flops 1048576 | bytes 16384 | tf_op jit(solution)/shard_map/turn/pallas_call | solution.py:363
  14.9 2.5 %dispatch.5 = (bf16[1152,1024]{1,0:T(8,128)(2,1)S(1)}, bf16[1152,1024]{1,0:T(8,128)(2,1)S(1)}, f32[288,384]{1,0:T(8,128)S(1)}, bf16[288,384]{1,0:T(8,128)(2,1)S(1)}, f32[8,192]{1,0:T(8,128)S(1)}) custom-call(s32[1]{0:T(128)} %bitcast.2.here, bf16[200,1024]{1,0:T(8,128)(2,1)} %pack.1.refs_0_, bf16[384,1024]{1,0:T(8,128)(2,1)S(1)} %bitcast.26, ...), custom_call_target="tpu_custom_call" | custom-call | flops 1048576 | bytes 16384 | tf_op jit(solution)/shard_map/dispatch/pallas_call | solution.py:162
  22.7 3.2 %dispatch.6 = (bf16[1152,1024]{1,0:T(8,128)(2,1)S(1)}, bf16[1152,1024]{1,0:T(8,128)(2,1)S(1)}, f32[576,384]{1,0:T(8,128)S(1)}, bf16[288,384]{1,0:T(8,128)(2,1)S(...) custom-call(s32[1]{0:T(128)} %bitcast.2.here, ...), custom_call_target="tpu_custom_call", output_to_operand_aliasing={{0}: (5, {}), {1}: (6, {})} | custom-call | flops 1048576 | bytes 16384 | tf_op jit(solution)/shard_map/dispatch/pallas_call | solution.py:162
  26.5 2.0 %collective-permute-done.8.refs_0_ = bf16[288,384]{1,0:T(8,128)(2,1)S(1)} collective-permute-done((bf16[288,384]{1,0:T(8,128)(2,1)S(1)}, bf16[288,384]{1,0:T(8,128)(2,1)S(1)}, u32[]{:S(2)}, u32[]{:S(2)}) %collective-permute-start.8) | collective-permute-done | bytes 221216 | tf_op jit(solution)/shard_map/ppermute | solution.py:506
  28.5 2.9 %combine.5 = (bf16[1152,768]{1,0:T(8,128)(2,1)S(1)}, bf16[1152,768]{1,0:T(8,128)(2,1)S(1)}, bf16[192,1024]{1,0:T(8,128)(2,1)S(1)}) custom-call(s32[1]{0:T(128)} %bitcast.2.here, f32[288,384]{1,0:T(8,128)S(1)} %get-tuple-element.99.share, bf16[288,384]{1,0:T(8,128)(2,1)S(1)} %collective-permute-done.8.refs_0_, f32[8,192]{1,0:T(8,128)S(1)} %get-tuple-element.101.refs_1_, ...), custom_call_target="tpu_custom_call" | custom-call | flops 1048576 | bytes 16384 | tf_op jit(solution)/shard_map/combine/pallas_call | solution.py:240
  36.7 2.8 %dispatch.7 = (bf16[1152,1024]{1,0:T(8,128)(2,1)S(1)}, bf16[1152,1024]{1,0:T(8,128)(2,1)S(1)}, f32[576,384]{1,0:T(8,128)S(1)}, bf16[288,384]{1,0:T(8,128)(2,1)S(...) custom-call(s32[1]{0:T(128)} %bitcast.2.here, ...), custom_call_target="tpu_custom_call", output_to_operand_aliasing={{0}: (5, {}), {1}: (6, {})} | custom-call | flops 1048576 | bytes 16384 | tf_op jit(solution)/shard_map/dispatch/pallas_call | solution.py:162
  40.1 2.0 %collective-permute-done.13.refs_1_ = bf16[288,384]{1,0:T(8,128)(2,1)S(1)} collective-permute-done((bf16[288,384]{1,0:T(8,128)(2,1)S(1)}, bf16[288,384]{1,0:T(8,128)(2,1)S(1)}, u32[]{:S(2)}, u32[]{:S(2)}) %collective-permute-start.13) | collective-permute-done | bytes 221216 | tf_op jit(solution)/shard_map/ppermute | solution.py:506
  42.1 4.5 %combine.6 = (bf16[1152,768]{1,0:T(8,128)(2,1)S(1)}, bf16[1152,768]{1,0:T(8,128)(2,1)S(1)}, bf16[192,1024]{1,0:T(8,128)(2,1)S(1)}, bf16[192,1024]{1,0:T(8,128)(2,1)S(1)}) custom-call(s32[1]{0:T(128)} %bitcast.2.here, f32[576,384]{1,0:T(8,128)S(1)} %get-tuple-element.113.share, ...), custom_call_target="tpu_custom_call", output_to_operand_aliasing={{0}: (11, {}), {1}: (12, {})} | custom-call | flops 1048576 | bytes 16384 | tf_op jit(solution)/shard_map/combine/pallas_call | solution.py:240
  48.6 2.5 %collective-permute-start.17 = (bf16[288,384]{1,0:T(8,128)(2,1)S(1)}, bf16[288,384]{1,0:T(8,128)(2,1)S(1)}, u32[]{:S(2)}, u32[]{:S(2)}) collective-permute-start(bf16[288,384]{1,0:T(8,128)(2,1)S(1)} %get-tuple-element.131), channel_id=1, source_target_pairs={{0,16},{16,0},{1,17},{17,1},{2,18},{18,2},{3,19},{19,3},{4,20},{20... | collective-permute-start | bytes 663560 | tf_op jit(solution)/shard_map/ppermute | solution.py:506
  51.0 2.8 %dispatch.8 = (bf16[1152,1024]{1,0:T(8,128)(2,1)S(1)}, bf16[1152,1024]{1,0:T(8,128)(2,1)S(1)}, f32[576,384]{1,0:T(8,128)S(1)}, bf16[288,384]{1,0:T(8,128)(2,1)S(...) custom-call(s32[1]{0:T(128)} %bitcast.2.here, ...), custom_call_target="tpu_custom_call", output_to_operand_aliasing={{0}: (5, {}), {1}: (6, {})} | custom-call | flops 1048576 | bytes 16384 | tf_op jit(solution)/shard_map/dispatch/pallas_call | solution.py:162
  54.0 2.9 %collective-permute-done.17.refs_1_ = bf16[288,384]{1,0:T(8,128)(2,1)S(1)} collective-permute-done((bf16[288,384]{1,0:T(8,128)(2,1)S(1)}, bf16[288,384]{1,0:T(8,128)(2,1)S(1)}, u32[]{:S(2)}, u32[]{:S(2)}) %collective-permute-start.17) | collective-permute-done | bytes 221216 | tf_op jit(solution)/shard_map/ppermute | solution.py:506
  56.9 4.5 %combine.7 = (bf16[1152,768]{1,0:T(8,128)(2,1)S(1)}, bf16[1152,768]{1,0:T(8,128)(2,1)S(1)}, bf16[192,1024]{1,0:T(8,128)(2,1)S(1)}, bf16[192,1024]{1,0:T(8,128)(2,1)S(1)}) custom-call(s32[1]{0:T(128)} %bitcast.2.here, f32[576,384]{1,0:T(8,128)S(1)} %get-tuple-element.129.share, ...), custom_call_target="tpu_custom_call", output_to_operand_aliasing={{0}: (11, {}), {1}: (12, {})} | custom-call | flops 1048576 | bytes 16384 | tf_op jit(solution)/shard_map/combine/pallas_call | solution.py:240
  61.4 2.3 %collective-permute-start.18 = (bf16[192,1024]{1,0:T(8,128)(2,1)S(1)}, bf16[192,1024]{1,0:T(8,128)(2,1)S(1)}, u32[]{:S(2)}, u32[]{:S(2)}) collective-permute-start(bf16[192,1024]{1,0:T(8,128)(2,1)S(1)} %get-tuple-element.137), channel_id=1, source_target_pairs={{0,4},{1,5},{2,6},{3,7},{4,8},{5,9},{6,10},{7,11},{8,12},{9,13},{1... | collective-permute-start | bytes 1179656 | tf_op jit(solution)/shard_map/ppermute | solution.py:484
  64.5 2.3 %dispatch.9 = (bf16[1152,1024]{1,0:T(8,128)(2,1)S(1)}, bf16[1152,1024]{1,0:T(8,128)(2,1)S(1)}, f32[288,384]{1,0:T(8,128)S(1)}, bf16[288,384]{1,0:T(8,128)(2,1)S(1)}, f32[8,192]{1,0:T(8,128)S(1)}) custom-call(s32[1]{0:T(128)} %bitcast.2.here, bf16[200,1024]{1,0:T(8,128)(2,1)S(1)} %collective-permute-done.14.refs_0_, ...), custom_call_target="tpu_custom_call", output_to_operand_aliasing={{0}: (4, {}), {1}: (5, {})} | custom-call | flops 1048576 | bytes 16384 | tf_op jit(solution)/shard_map/dispatch/pallas_call | solution.py:162
  68.6 2.2 %hidden.3.hid_c = bf16[384,1152]{1,0:T(8,128)(2,1)S(1)} custom-call(s32[1]{0:T(128)} %bitcast.2.here, bf16[2304,384]{1,0:T(8,128)(2,1)} %bitcast.11, bf16[2304,384]{1,0:T(8,128)(2,1)} %bitcast.19), custom_call_target="tpu_custom_call" | custom-call | flops 1048576 | bytes 16384 | tf_op jit(solution)/shard_map/hidden/pallas_call | solution.py:339
  70.9 4.5 %combine.8 = (bf16[1152,768]{1,0:T(8,128)(2,1)S(1)}, bf16[1152,768]{1,0:T(8,128)(2,1)S(1)}, bf16[192,1024]{1,0:T(8,128)(2,1)S(1)}, bf16[192,1024]{1,0:T(8,128)(2,1)S(1)}) custom-call(s32[1]{0:T(128)} %bitcast.2.here, f32[576,384]{1,0:T(8,128)S(1)} %get-tuple-element.143.share, ...), custom_call_target="tpu_custom_call", output_to_operand_aliasing={{0}: (11, {}), {1}: (12, {})} | custom-call | flops 1048576 | bytes 16384 | tf_op jit(solution)/shard_map/combine/pallas_call | solution.py:240
  78.2 2.6 %combine.9 = (bf16[1152,768]{1,0:T(8,128)(2,1)S(1)}, bf16[144,768]{1,0:T(8,128)(2,1)S(1)}, bf16[192,512]{1,0:T(8,128)(2,1)S(1)}, bf16[192,512]{1,0:T(8,128)(2,1)S(1)}) custom-call(s32[1]{0:T(128)} %bitcast.2.here, f32[288,384]{1,0:T(8,128)S(1)} %get-tuple-element.155.share, ...), custom_call_target="tpu_custom_call", output_to_operand_aliasing={{0}: (10, {})} | custom-call | flops 1048576 | bytes 16384 | tf_op jit(solution)/shard_map/combine/pallas_call | solution.py:240
  85.7 2.4 %collective-permute-done.24.refs_2_ = bf16[192,512]{1,0:T(8,128)(2,1)S(1)} collective-permute-done((bf16[192,512]{1,0:T(8,128)(2,1)S(1)}, bf16[192,512]{1,0:T(8,128)(2,1)S(1)}, u32[]{:S(2)}, u32[]{:S(2)}) %collective-permute-start.24) | collective-permute-done | bytes 196640 | tf_op jit(solution)/shard_map/ppermute | solution.py:484
  92.4 1.8 %collective-permute-start.30 = (bf16[192,512]{1,0:T(8,128)(2,1)S(1)}, bf16[192,512]{1,0:T(8,128)(2,1)S(1)}, u32[]{:S(2)}, u32[]{:S(2)}) collective-permute-start(bf16[192,512]{1,0:T(8,128)(2,1)S(1)} %add.11), channel_id=1, source_target_pairs={{0,4},{1,5},{2,6},{3,7},{4,8},{5,9},{6,10},{7,11},{8,12},{9,13},{1... | collective-permute-start | bytes 589832 | tf_op jit(solution)/shard_map/ppermute | solution.py:484
  94.1 4.4 %received_part.1.old = bf16[1,1024,1152]{2,1,0:T(8,128)(2,1)} custom-call(bf16[384,1152]{1,0:T(8,128)(2,1)S(1)} %hidden.2.hid, bf16[384,1152]{1,0:T(8,128)(2,1)S(1)} %hidden.3.hid_c, bf16[1152,1024]{1,0:T(8,128)(2,1)S(1)} %get-tuple-element.170.own, bf16[1152,1024]{1,0:T(8,128)(2,1)S(1)} %collective-permute-done.22.other), custom_call_target="tpu_custom_call" | custom-call | flops 1048576 | bytes 16384 | tf_op jit(solution)/shard_map/received_part/pallas_call | solution.py:419
  99.5 5.7 %inputs_part.1 = bf16[1,1024,1152]{2,1,0:T(8,128)(2,1)} custom-call(s32[1]{0:T(128)} %bitcast.2.here, bf16[1,1024,1152]{2,1,0:T(8,128)(2,1)} %received_part.1.old, bf16[1024,2304]{1,0:T(8,128)(2,1)S(1)} %turn.1.inputs, bf16[1152,768]{1,0:T(8,128)(2,1)S(1)} %get-tuple-element.177.own, ...), custom_call_target="tpu_custom_call", output_to_operand_aliasing={{}: (1, {})} | custom-call | flops 1048576 | bytes 16384 | tf_op jit(solution)/shard_map/inputs_part/pallas_call | solution.py:452
  105.2 2.3 %collective-permute-done.26.left = bf16[192,512]{1,0:T(8,128)(2,1)S(1)} collective-permute-done((bf16[192,512]{1,0:T(8,128)(2,1)S(1)}, bf16[192,512]{1,0:T(8,128)(2,1)S(1)}, u32[]{:S(2)}, u32[]{:S(2)}) %collective-permute-start.26) | collective-permute-done | bytes 196640 | tf_op jit(solution)/shard_map/ppermute | solution.py:484
  (80 shorter events, 35.6 us)
Async XLA Ops:
  0.6 17.9 %collective-permute-start.3 = (bf16[2304,384]{1,0:T(8,128)(2,1)}, bf16[2304,384]{1,0:T(8,128)(2,1)S(1)}, u32[]{:S(2)}, u32[]{:S(2)}) collective-permute-start(bf16[2304,384]{1,0:T(8,128)(2,1)} %bitcast.9), channel_id=1, source_target_pairs={{0,1},{1,0},{2,3},{3,2},{4,5},{5,4},{6,7},{7,6},{8,9},{9,8},{10,11... | collective-permute-start | bytes 5308424 | tf_op jit(solution)/shard_map/ppermute | solution.py:484
  1.1 17.4 %collective-permute-start.4 = (bf16[2304,384]{1,0:T(8,128)(2,1)}, bf16[2304,384]{1,0:T(8,128)(2,1)S(1)}, u32[]{:S(2)}, u32[]{:S(2)}) collective-permute-start(bf16[2304,384]{1,0:T(8,128)(2,1)} %bitcast.17), channel_id=1, source_target_pairs={{0,1},{1,0},{2,3},{3,2},{4,5},{5,4},{6,7},{7,6},{8,9},{9,8},{10,11... | collective-permute-start | bytes 5308424 | tf_op jit(solution)/shard_map/ppermute | solution.py:484
  1.2 12.7 %collective-permute-start.2 = (bf16[384,1024]{1,0:T(8,128)(2,1)}, bf16[384,1024]{1,0:T(8,128)(2,1)}, u32[]{:S(2)}, u32[]{:S(2)}) collective-permute-start(bf16[384,1024]{1,0:T(8,128)(2,1)} %bitcast.25), channel_id=1, source_target_pairs={{0,1},{1,0},{2,3},{3,2},{4,5},{5,4},{6,7},{7,6},{8,9},{9,8},{10,11... | collective-permute-start | bytes 2359304 | tf_op jit(solution)/shard_map/ppermute | solution.py:484
  3.4 15.1 %collective-permute-start = (bf16[200,1024]{1,0:T(8,128)(2,1)}, bf16[200,1024]{1,0:T(8,128)(2,1)}, u32[]{:S(2)}, u32[]{:S(2)}) collective-permute-start(bf16[200,1024]{1,0:T(8,128)(2,1)} %pack.1.refs_0_), channel_id=1, source_target_pairs={{0,4},{1,5},{2,6},{3,7},{4,8},{5,9},{6,10},{7,11},{8,12},{9,13},{1... | collective-permute-start | bytes 1228808 | tf_op jit(solution)/shard_map/ppermute | solution.py:484
  6.1 12.4 %collective-permute-start.1 = (bf16[200,1024]{1,0:T(8,128)(2,1)}, bf16[200,1024]{1,0:T(8,128)(2,1)}, u32[]{:S(2)}, u32[]{:S(2)}) collective-permute-start(bf16[200,1024]{1,0:T(8,128)(2,1)} %pack.1.refs_0_), channel_id=1, source_target_pairs={{0,2},{1,3},{2,0},{3,1},{4,6},{5,7},{6,4},{7,5},{8,10},{9,11},{10,... | collective-permute-start | bytes 1228808 | tf_op jit(solution)/shard_map/ppermute | solution.py:484
  18.6 9.9 %collective-permute-start.9 = (bf16[1024,768]{1,0:T(8,128)(2,1)S(1)}, bf16[1024,768]{1,0:T(8,128)(2,1)S(1)}, u32[]{:S(2)}, u32[]{:S(2)}) collective-permute-start(bf16[1024,768]{1,0:T(8,128)(2,1)S(1)} %join.1.refs_6_.refs_7_), channel_id=1, source_target_pairs={{0,1},{1,0},{2,3},{3,2},{4,5},{5,4},{6,7},{7,6},{8,9},{9,8},{10,11... | collective-permute-start | bytes 4718600 | tf_op jit(solution)/shard_map/ppermute | solution.py:484
  18.6 14.5 %collective-permute-start.5 = (bf16[200,1024]{1,0:T(8,128)(2,1)}, bf16[200,1024]{1,0:T(8,128)(2,1)S(1)}, u32[]{:S(2)}, u32[]{:S(2)}) collective-permute-start(bf16[200,1024]{1,0:T(8,128)(2,1)} %collective-permute-done.refs_1_), channel_id=1, source_target_pairs={{0,4},{1,5},{2,6},{3,7},{4,8},{5,9},{6,10},{7,11},{8,12},{9,13},{1... | collective-permute-start | bytes 1228808 | tf_op jit(solution)/shard_map/ppermute | solution.py:484
  19.6 13.5 %collective-permute-start.6 = (bf16[200,1024]{1,0:T(8,128)(2,1)}, bf16[200,1024]{1,0:T(8,128)(2,1)S(1)}, u32[]{:S(2)}, u32[]{:S(2)}) collective-permute-start(bf16[200,1024]{1,0:T(8,128)(2,1)} %collective-permute-done.refs_1_), channel_id=1, source_target_pairs={{0,2},{1,3},{2,0},{3,1},{4,6},{5,7},{6,4},{7,5},{8,10},{9,11},{10,... | collective-permute-start | bytes 1228808 | tf_op jit(solution)/shard_map/ppermute | solution.py:484
  33.1 13.5 %collective-permute-start.10 = (bf16[200,1024]{1,0:T(8,128)(2,1)S(1)}, bf16[200,1024]{1,0:T(8,128)(2,1)S(1)}, u32[]{:S(2)}, u32[]{:S(2)}) collective-permute-start(bf16[200,1024]{1,0:T(8,128)(2,1)S(1)} %collective-permute-done.5.refs_1_), channel_id=1, source_target_pairs={{0,4},{1,5},{2,6},{3,7},{4,8},{5,9},{6,10},{7,11},{8,12},{9,13},{1... | collective-permute-start | bytes 1228808 | tf_op jit(solution)/shard_map/ppermute | solution.py:484
  34.7 11.9 %collective-permute-start.11 = (bf16[200,1024]{1,0:T(8,128)(2,1)S(1)}, bf16[200,1024]{1,0:T(8,128)(2,1)S(1)}, u32[]{:S(2)}, u32[]{:S(2)}) collective-permute-start(bf16[200,1024]{1,0:T(8,128)(2,1)S(1)} %collective-permute-done.5.refs_1_), channel_id=1, source_target_pairs={{0,2},{1,3},{2,0},{3,1},{4,6},{5,7},{6,4},{7,5},{8,10},{9,11},{10,... | collective-permute-start | bytes 1228808 | tf_op jit(solution)/shard_map/ppermute | solution.py:484
  46.6 14.7 %collective-permute-start.14 = (bf16[200,1024]{1,0:T(8,128)(2,1)S(1)}, bf16[200,1024]{1,0:T(8,128)(2,1)S(1)}, u32[]{:S(2)}, u32[]{:S(2)}) collective-permute-start(bf16[200,1024]{1,0:T(8,128)(2,1)S(1)} %collective-permute-done.10.refs_1_), channel_id=1, source_target_pairs={{0,2},{1,3},{2,0},{3,1},{4,6},{5,7},{6,4},{7,5},{8,10},{9,11},{10,... | collective-permute-start | bytes 1228808 | tf_op jit(solution)/shard_map/ppermute | solution.py:484
  48.2 13.2 %collective-permute-start.15 = (bf16[192,1024]{1,0:T(8,128)(2,1)S(1)}, bf16[192,1024]{1,0:T(8,128)(2,1)S(1)}, u32[]{:S(2)}, u32[]{:S(2)}) collective-permute-start(bf16[192,1024]{1,0:T(8,128)(2,1)S(1)} %get-tuple-element.122), channel_id=1, source_target_pairs={{0,4},{1,5},{2,6},{3,7},{4,8},{5,9},{6,10},{7,11},{8,12},{9,13},{1... | collective-permute-start | bytes 1179656 | tf_op jit(solution)/shard_map/ppermute | solution.py:484
  48.6 8.3 %collective-permute-start.17 = (bf16[288,384]{1,0:T(8,128)(2,1)S(1)}, bf16[288,384]{1,0:T(8,128)(2,1)S(1)}, u32[]{:S(2)}, u32[]{:S(2)}) collective-permute-start(bf16[288,384]{1,0:T(8,128)(2,1)S(1)} %get-tuple-element.131), channel_id=1, source_target_pairs={{0,16},{16,0},{1,17},{17,1},{2,18},{18,2},{3,19},{19,3},{4,20},{20... | collective-permute-start | bytes 663560 | tf_op jit(solution)/shard_map/ppermute | solution.py:506
  61.4 14.0 %collective-permute-start.18 = (bf16[192,1024]{1,0:T(8,128)(2,1)S(1)}, bf16[192,1024]{1,0:T(8,128)(2,1)S(1)}, u32[]{:S(2)}, u32[]{:S(2)}) collective-permute-start(bf16[192,1024]{1,0:T(8,128)(2,1)S(1)} %get-tuple-element.137), channel_id=1, source_target_pairs={{0,4},{1,5},{2,6},{3,7},{4,8},{5,9},{6,10},{7,11},{8,12},{9,13},{1... | collective-permute-start | bytes 1179656 | tf_op jit(solution)/shard_map/ppermute | solution.py:484
  63.6 11.8 %collective-permute-start.19 = (bf16[192,1024]{1,0:T(8,128)(2,1)S(1)}, bf16[192,1024]{1,0:T(8,128)(2,1)S(1)}, u32[]{:S(2)}, u32[]{:S(2)}) collective-permute-start(bf16[192,1024]{1,0:T(8,128)(2,1)S(1)} %get-tuple-element.138), channel_id=1, source_target_pairs={{0,2},{1,3},{2,0},{3,1},{4,6},{5,7},{6,4},{7,5},{8,10},{9,11},{10,... | collective-permute-start | bytes 1179656 | tf_op jit(solution)/shard_map/ppermute | solution.py:484
  66.9 8.5 %collective-permute-start.20 = (bf16[288,384]{1,0:T(8,128)(2,1)S(1)}, bf16[288,384]{1,0:T(8,128)(2,1)S(1)}, u32[]{:S(2)}, u32[]{:S(2)}) collective-permute-start(bf16[288,384]{1,0:T(8,128)(2,1)S(1)} %get-tuple-element.142), channel_id=1, source_target_pairs={{0,16},{16,0},{1,17},{17,1},{2,18},{18,2},{3,19},{19,3},{4,20},{20... | collective-permute-start | bytes 663560 | tf_op jit(solution)/shard_map/ppermute | solution.py:506
  75.4 14.5 %collective-permute-start.22 = (bf16[1152,1024]{1,0:T(8,128)(2,1)S(1)}, bf16[1152,1024]{1,0:T(8,128)(2,1)S(1)}, u32[]{:S(2)}, u32[]{:S(2)}) collective-permute-start(bf16[1152,1024]{1,0:T(8,128)(2,1)S(1)} %get-tuple-element.163), channel_id=1, source_target_pairs={{0,1},{1,0},{2,3},{3,2},{4,5},{5,4},{6,7},{7,6},{8,9},{9,8},{10,11... | collective-permute-start | bytes 7077896 | tf_op jit(solution)/shard_map/ppermute | solution.py:484
  75.5 24.0 %collective-permute-start.31 = (bf16[1152,768]{1,0:T(8,128)(2,1)S(1)}, bf16[1152,768]{1,0:T(8,128)(2,1)S(1)}, u32[]{:S(2)}, u32[]{:S(2)}) collective-permute-start(bf16[1152,768]{1,0:T(8,128)(2,1)S(1)} %get-tuple-element.178), channel_id=1, source_target_pairs={{0,1},{1,0},{2,3},{3,2},{4,5},{5,4},{6,7},{7,6},{8,9},{9,8},{10,11... | collective-permute-start | bytes 5308424 | tf_op jit(solution)/shard_map/ppermute | solution.py:484
  77.6 10.5 %collective-permute-start.24 = (bf16[192,512]{1,0:T(8,128)(2,1)S(1)}, bf16[192,512]{1,0:T(8,128)(2,1)S(1)}, u32[]{:S(2)}, u32[]{:S(2)}) collective-permute-start(bf16[192,512]{1,0:T(8,128)(2,1)S(1)} %add.6), channel_id=1, source_target_pairs={{0,2},{1,3},{2,0},{3,1},{4,6},{5,7},{6,4},{7,5},{8,10},{9,11},{10,... | collective-permute-start | bytes 589832 | tf_op jit(solution)/shard_map/ppermute | solution.py:484
  80.8 11.5 %collective-permute-start.27 = (bf16[192,512]{1,0:T(8,128)(2,1)S(1)}, bf16[192,512]{1,0:T(8,128)(2,1)S(1)}, u32[]{:S(2)}, u32[]{:S(2)}) collective-permute-start(bf16[192,512]{1,0:T(8,128)(2,1)S(1)} %get-tuple-element.173), channel_id=1, source_target_pairs={{0,2},{1,3},{2,0},{3,1},{4,6},{5,7},{6,4},{7,5},{8,10},{9,11},{10,... | collective-permute-start | bytes 589832 | tf_op jit(solution)/shard_map/ppermute | solution.py:484
  88.2 10.3 %collective-permute-start.25 = (bf16[192,512]{1,0:T(8,128)(2,1)S(1)}, bf16[192,512]{1,0:T(8,128)(2,1)S(1)}, u32[]{:S(2)}, u32[]{:S(2)}) collective-permute-start(bf16[192,512]{1,0:T(8,128)(2,1)S(1)} %add.8), channel_id=1, source_target_pairs={{0,4},{1,5},{2,6},{3,7},{4,8},{5,9},{6,10},{7,11},{8,12},{9,13},{1... | collective-permute-start | bytes 589832 | tf_op jit(solution)/shard_map/ppermute | solution.py:484
  89.9 8.6 %collective-permute-start.23 = (bf16[192,512]{1,0:T(8,128)(2,1)S(1)}, bf16[192,512]{1,0:T(8,128)(2,1)S(1)}, u32[]{:S(2)}, u32[]{:S(2)}) collective-permute-start(bf16[192,512]{1,0:T(8,128)(2,1)S(1)} %get-tuple-element.164), channel_id=1, source_target_pairs={{0,2},{1,3},{2,0},{3,1},{4,6},{5,7},{6,4},{7,5},{8,10},{9,11},{10,... | collective-permute-start | bytes 589832 | tf_op jit(solution)/shard_map/ppermute | solution.py:484
  92.4 12.8 %collective-permute-start.30 = (bf16[192,512]{1,0:T(8,128)(2,1)S(1)}, bf16[192,512]{1,0:T(8,128)(2,1)S(1)}, u32[]{:S(2)}, u32[]{:S(2)}) collective-permute-start(bf16[192,512]{1,0:T(8,128)(2,1)S(1)} %add.11), channel_id=1, source_target_pairs={{0,4},{1,5},{2,6},{3,7},{4,8},{5,9},{6,10},{7,11},{8,12},{9,13},{1... | collective-permute-start | bytes 589832 | tf_op jit(solution)/shard_map/ppermute | solution.py:484
  98.6 8.9 %collective-permute-start.26 = (bf16[192,512]{1,0:T(8,128)(2,1)S(1)}, bf16[192,512]{1,0:T(8,128)(2,1)S(1)}, u32[]{:S(2)}, u32[]{:S(2)}) collective-permute-start(bf16[192,512]{1,0:T(8,128)(2,1)S(1)} %add.9), channel_id=1, source_target_pairs={{0,4},{1,5},{2,6},{3,7},{4,8},{5,9},{6,10},{7,11},{8,12},{9,13},{1... | collective-permute-start | bytes 589832 | tf_op jit(solution)/shard_map/ppermute | solution.py:484
  (16 other events, 94.6 us)

commit v10 on v9

--- a/solution.py
+++ b/solution.py
@@ -180,27 +180,18 @@
     else:
         peer0, peer1, pos, *refs = refs
     saved, ws, refs = refs[:4], refs[4:6], refs[6 + begun :]
-    buffers, backs, (held, gps, sems, out_sems) = refs[:2], refs[2:-4], refs[-4:]
+    buffers, backs, (gps, out_sems) = refs[:2], refs[2:-2], refs[-2:]
     h = share.shape[1]
-    copies = []
-    for a in range(2):
-        for other, step in chunk:
-            rows = pl.ds(pl.multiple_of(source(here[0], step, other) * cap, 16), cap)
-            for v in saved[2 * a : 2 * a + 2]:
-                i = len(copies)
-                copies.append(pltpu.make_async_copy(v.at[rows, :], held.at[i], sems.at[i]))
-    for c in copies:
-        c.start()
     slot = lax.broadcasted_iota(jnp.int32, (cap, pos.shape[1]), 0).astype(f32)
     leaving = []
-    for c in copies:
-        c.wait()
     for a, peer in enumerate((peer0, peer1)):
         for rel in range(n):
             i = a * n + rel
             at = slice(rel * cap, (rel + 1) * cap)
             gh = share[i * cap : (i + 1) * cap, :] + peer[at, :].astype(f32)
-            gg, gu = kernel_grads(gh, held[2 * i].astype(f32), held[2 * i + 1].astype(f32))
+            other, step = chunk[rel]
+            own = pl.ds(pl.multiple_of(source(here[0], step, other) * cap, 16), cap)
+            gg, gu = kernel_grads(gh, saved[2 * a][own, :].astype(f32), saved[2 * a + 1][own, :].astype(f32))
             gps[a, at, :h] = gg
             gps[a, at, h:] = gu
             if a == 0 or not last:
@@ -240,12 +231,10 @@
     return pl.pallas_call(
         functools.partial(combine_kernel, chunk, cap, len(old), last),
         out_shape=[jax.ShapeDtypeStruct(s, bf16) for s in outs],
-        in_specs=[on_scalar] + [on_chip] * (2 + len(peers)) + [anywhere] * 4 + [on_chip] * 2 + [anywhere] * len(old),
+        in_specs=[on_scalar] + [on_chip] * (2 + len(peers) + 6) + [anywhere] * len(old),
         out_specs=[anywhere, on_chip if last else anywhere] + [on_chip] * (len(outs) - 2),
         scratch_shapes=[
-            pltpu.VMEM((4 * n, cap, h), bf16),
             pltpu.VMEM((2, n * cap, 2 * h), bf16),
-            pltpu.SemaphoreType.DMA((4 * n,)),
             pltpu.SemaphoreType.DMA((2 * n,)),
         ],
         input_output_aliases={first_old + k: k for k in range(len(old))},
@@ -293,6 +282,25 @@
         compiler_params=params(8),
         name="add",
     )(*values)
+
+
+def add_halves_kernel(a, b, left, right):
+    total = (a[...].astype(f32) + b[...].astype(f32)).astype(bf16)
+    left[...] = total[:, : left.shape[1]]
+    right[...] = total[:, left.shape[1] :]
+
+
+def add_halves(a, b):
+    rows, wide = a.shape
+    return pl.pallas_call(
+        add_halves_kernel,
+        out_shape=[jax.ShapeDtypeStruct((rows, wide // 2), bf16)] * 2,
+        in_specs=[on_chip] * 2,
+        out_specs=[on_chip] * 2,
+        cost_estimate=light,
+        compiler_params=params(8),
+        name="add_halves",
+    )(a, b)
 
 
 def finish_kernel(a, b, left, right, out):
@@ -523,7 +531,8 @@
     c1, h1, g1 = first([(1, 0), (0, 1)], [x0, r1])
     h1 = exchange(h1)
     (t_r0,) = second(c0, h0)
-    r2, x1, h1, g1, t_r0 = together(r2, x1, h1, g1, t_r0)
+    hid_c = hidden(here, sg, su, cap, 1)
+    r2, x1, h1, g1, t_r0, hid_c = together(r2, x1, h1, g1, t_r0, hid_c)
     r3, x2 = ring(r2), send(r2, to_x)
     g1 = exchange(g1)
     c2, h2, g2 = first([(1, 1), (0, 2)], [x1, r2])
@@ -541,10 +550,9 @@
     c4, h4 = first([(1, 3)], [x3])
     h4 = exchange(h4)
     t_x2, t_r3 = second(c3, h3, g3)
-    hid_c = hidden(here, sg, su, cap, 1)
-    u1, b0, h4, t_x2, t_r3, hid_c, rec_away, gp_away = together(u1, b0, h4, t_x2, t_r3, hid_c, recs[1], gps[1])
+    u1, b0, h4, t_x2, t_r3, rec_away, gp_away = together(u1, b0, h4, t_x2, t_r3, recs[1], gps[1])
     rec_c, gp_c = send(rec_away, to_core), send(gp_away, to_core)
-    a0, a1, h4 = together(add([t_x2, u1], 0), add([t_x2, u1], 1), h4)
+    a0, a1, h4 = together(*add_halves(t_x2, u1), h4)
     b2 = [send(a0, to_x), send(a1, to_x)]
     left, right = second(c4, h4, last=True)
     left, rec_c = together(left, rec_c)

time: 109 us -> 106 us (0.972)
  Pallas kernels: 54.2 us -> 49.5 us
  starting transfers between devices: 34.8 us -> 36.7 us
    pallas_call x5, Pallas kernels: 19 us -> 14.2 us  [combine(): pl.pallas_call(functools.partial(combine_kernel, chunk, cap, len(old), la...]
    ppermute x25, starting transfers between devices: 26 us -> 28.2 us  [send(): return lax.ppermute(v, 'expert', perm)]
  transfers between devices with their start and end apart: 33 -> 33, of which waited for: 9 -> 13; matrix products, arithmetic and copies ran while one was open for 0% -> 0% of each run, Pallas kernels for 49% -> 46%
where the time goes in v10:
time: 106 us
  Pallas kernels  49.5 us (47%)
  starting transfers between devices  36.7 us (35%)
  waiting for transfers between devices  17.5 us (17%)
    ppermute x25, starting transfers between devices, send(): return lax.ppermute(v, 'expert', perm)  28.2 us
    pallas_call x5, Pallas kernels, combine(): pl.pallas_call(functools.partial(combine_kernel, chunk, cap, len(old), la...  14.2 us
    pallas_call x5, Pallas kernels, dispatch(): pl.pallas_call(functools.partial(dispatch_kernel, chunk, cap, len(old) //...  13.5 us
    ppermute x8, waiting for transfers between devices, exchange(): return lax.ppermute(v, 'dp', [(0, 1), (1, 0)])  9.57 us
    ppermute x8, starting transfers between devices, exchange(): return lax.ppermute(v, 'dp', [(0, 1), (1, 0)])  8.41 us
    ppermute x25, waiting for transfers between devices, send(): return lax.ppermute(v, 'expert', perm)  7.96 us
    pallas_call x1, Pallas kernels, inputs_part(): pl.pallas_call(functools.partial(inputs_kernel, cap, last), out_shape=jax...  5.66 us
    pallas_call x2, Pallas kernels, hidden(): pl.pallas_call(functools.partial(hidden_kernel, cap, k), out_shape=jax.Sh...  4.73 us
  transfers between devices with their start and end apart: 33, of which 13 were waited for; matrix products, arithmetic and copies ran while one was open for 0% of the time, Pallas kernels for 46%

profile of v10, /device:TPU:0, one launch (start us, length us, event | category | flops | bytes accessed | tf_op | source)
XLA Modules:
  0.0 105.6 jit_solution(4704931633485114504)
XLA Ops:
  3.4 2.7 %collective-permute-start = (bf16[200,1024]{1,0:T(8,128)(2,1)}, bf16[200,1024]{1,0:T(8,128)(2,1)}, u32[]{:S(2)}, u32[]{:S(2)}) collective-permute-start(bf16[200,1024]{1,0:T(8,128)(2,1)} %pack.1.refs_0_), channel_id=1, source_target_pairs={{0,4},{1,5},{2,6},{3,7},{4,8},{5,9},{6,10},{7,11},{8,12},{9,13},{1... | collective-permute-start | bytes 1228808 | tf_op jit(solution)/shard_map/ppermute | solution.py:492
  7.6 2.2 %hidden.2.hid = bf16[384,1152]{1,0:T(8,128)(2,1)S(1)} custom-call(s32[1]{0:T(128)} %bitcast.2.here, bf16[2304,384]{1,0:T(8,128)(2,1)} %bitcast.10, bf16[2304,384]{1,0:T(8,128)(2,1)} %bitcast.18), custom_call_target="tpu_custom_call" | custom-call | flops 1048576 | bytes 16384 | tf_op jit(solution)/shard_map/hidden/pallas_call | solution.py:347
  9.9 3.9 %turn.1.inputs = bf16[1024,2304]{1,0:T(8,128)(2,1)S(1)} custom-call(s32[1]{0:T(128)} %bitcast.2.here, bf16[2304,1024]{1,0:T(8,128)(2,1)} %bitcast.33), custom_call_target="tpu_custom_call" | custom-call | flops 1048576 | bytes 16384 | tf_op jit(solution)/shard_map/turn/pallas_call | solution.py:371
  14.9 2.5 %dispatch.5 = (bf16[1152,1024]{1,0:T(8,128)(2,1)S(1)}, bf16[1152,1024]{1,0:T(8,128)(2,1)S(1)}, f32[288,384]{1,0:T(8,128)S(1)}, bf16[288,384]{1,0:T(8,128)(2,1)S(1)}, f32[8,192]{1,0:T(8,128)S(1)}) custom-call(s32[1]{0:T(128)} %bitcast.2.here, bf16[200,1024]{1,0:T(8,128)(2,1)} %pack.1.refs_0_, bf16[384,1024]{1,0:T(8,128)(2,1)S(1)} %bitcast.26, ...), custom_call_target="tpu_custom_call" | custom-call | flops 1048576 | bytes 16384 | tf_op jit(solution)/shard_map/dispatch/pallas_call | solution.py:162
  22.7 3.1 %dispatch.6 = (bf16[1152,1024]{1,0:T(8,128)(2,1)S(1)}, bf16[1152,1024]{1,0:T(8,128)(2,1)S(1)}, f32[576,384]{1,0:T(8,128)S(1)}, bf16[288,384]{1,0:T(8,128)(2,1)S(...) custom-call(s32[1]{0:T(128)} %bitcast.2.here, ...), custom_call_target="tpu_custom_call", output_to_operand_aliasing={{0}: (5, {}), {1}: (6, {})} | custom-call | flops 1048576 | bytes 16384 | tf_op jit(solution)/shard_map/dispatch/pallas_call | solution.py:162
  26.3 2.5 %hidden.3.hid_c = bf16[384,1152]{1,0:T(8,128)(2,1)S(1)} custom-call(s32[1]{0:T(128)} %bitcast.2.here, bf16[2304,384]{1,0:T(8,128)(2,1)} %bitcast.11, bf16[2304,384]{1,0:T(8,128)(2,1)} %bitcast.19), custom_call_target="tpu_custom_call" | custom-call | flops 1048576 | bytes 16384 | tf_op jit(solution)/shard_map/hidden/pallas_call | solution.py:347
  28.9 2.3 %combine.5 = (bf16[1152,768]{1,0:T(8,128)(2,1)S(1)}, bf16[1152,768]{1,0:T(8,128)(2,1)S(1)}, bf16[192,1024]{1,0:T(8,128)(2,1)S(1)}) custom-call(s32[1]{0:T(128)} %bitcast.2.here, f32[288,384]{1,0:T(8,128)S(1)} %get-tuple-element.101.share, bf16[288,384]{1,0:T(8,128)(2,1)S(1)} %collective-permute-done.8.refs_0_, f32[8,192]{1,0:T(8,128)S(1)} %get-tuple-element.103.refs_1_, ...), custom_call_target="tpu_custom_call" | custom-call | flops 1048576 | bytes 16384 | tf_op jit(solution)/shard_map/combine/pallas_call | solution.py:231
  36.7 2.8 %dispatch.7 = (bf16[1152,1024]{1,0:T(8,128)(2,1)S(1)}, bf16[1152,1024]{1,0:T(8,128)(2,1)S(1)}, f32[576,384]{1,0:T(8,128)S(1)}, bf16[288,384]{1,0:T(8,128)(2,1)S(...) custom-call(s32[1]{0:T(128)} %bitcast.2.here, ...), custom_call_target="tpu_custom_call", output_to_operand_aliasing={{0}: (5, {}), {1}: (6, {})} | custom-call | flops 1048576 | bytes 16384 | tf_op jit(solution)/shard_map/dispatch/pallas_call | solution.py:162
  42.0 3.3 %combine.6 = (bf16[1152,768]{1,0:T(8,128)(2,1)S(1)}, bf16[1152,768]{1,0:T(8,128)(2,1)S(1)}, bf16[192,1024]{1,0:T(8,128)(2,1)S(1)}, bf16[192,1024]{1,0:T(8,128)(2,1)S(1)}) custom-call(s32[1]{0:T(128)} %bitcast.2.here, f32[576,384]{1,0:T(8,128)S(1)} %get-tuple-element.115.share, ...), custom_call_target="tpu_custom_call", output_to_operand_aliasing={{0}: (11, {}), {1}: (12, {})} | custom-call | flops 1048576 | bytes 16384 | tf_op jit(solution)/shard_map/combine/pallas_call | solution.py:231
  49.7 2.8 %dispatch.8 = (bf16[1152,1024]{1,0:T(8,128)(2,1)S(1)}, bf16[1152,1024]{1,0:T(8,128)(2,1)S(1)}, f32[576,384]{1,0:T(8,128)S(1)}, bf16[288,384]{1,0:T(8,128)(2,1)S(...) custom-call(s32[1]{0:T(128)} %bitcast.2.here, ...), custom_call_target="tpu_custom_call", output_to_operand_aliasing={{0}: (5, {}), {1}: (6, {})} | custom-call | flops 1048576 | bytes 16384 | tf_op jit(solution)/shard_map/dispatch/pallas_call | solution.py:162
  52.7 2.4 %collective-permute-done.17.refs_1_ = bf16[288,384]{1,0:T(8,128)(2,1)S(1)} collective-permute-done((bf16[288,384]{1,0:T(8,128)(2,1)S(1)}, bf16[288,384]{1,0:T(8,128)(2,1)S(1)}, u32[]{:S(2)}, u32[]{:S(2)}) %collective-permute-start.17) | collective-permute-done | bytes 221216 | tf_op jit(solution)/shard_map/ppermute | solution.py:514
  55.1 3.3 %combine.7 = (bf16[1152,768]{1,0:T(8,128)(2,1)S(1)}, bf16[1152,768]{1,0:T(8,128)(2,1)S(1)}, bf16[192,1024]{1,0:T(8,128)(2,1)S(1)}, bf16[192,1024]{1,0:T(8,128)(2,1)S(1)}) custom-call(s32[1]{0:T(128)} %bitcast.2.here, f32[576,384]{1,0:T(8,128)S(1)} %get-tuple-element.131.share, ...), custom_call_target="tpu_custom_call", output_to_operand_aliasing={{0}: (11, {}), {1}: (12, {})} | custom-call | flops 1048576 | bytes 16384 | tf_op jit(solution)/shard_map/combine/pallas_call | solution.py:231
  58.6 2.1 %collective-permute-start.18 = (bf16[192,1024]{1,0:T(8,128)(2,1)S(1)}, bf16[192,1024]{1,0:T(8,128)(2,1)S(1)}, u32[]{:S(2)}, u32[]{:S(2)}) collective-permute-start(bf16[192,1024]{1,0:T(8,128)(2,1)S(1)} %get-tuple-element.139), channel_id=1, source_target_pairs={{0,4},{1,5},{2,6},{3,7},{4,8},{5,9},{6,10},{7,11},{8,12},{9,13},{1... | collective-permute-start | bytes 1179656 | tf_op jit(solution)/shard_map/ppermute | solution.py:492
  61.2 2.1 %collective-permute-start.21 = (bf16[288,384]{1,0:T(8,128)(2,1)S(1)}, bf16[288,384]{1,0:T(8,128)(2,1)S(1)}, u32[]{:S(2)}, u32[]{:S(2)}) collective-permute-start(bf16[288,384]{1,0:T(8,128)(2,1)S(1)} %get-tuple-element.147), channel_id=1, source_target_pairs={{0,16},{16,0},{1,17},{17,1},{2,18},{18,2},{3,19},{19,3},{4,20},{20... | collective-permute-start | bytes 663560 | tf_op jit(solution)/shard_map/ppermute | solution.py:514
  63.2 2.3 %dispatch.9 = (bf16[1152,1024]{1,0:T(8,128)(2,1)S(1)}, bf16[1152,1024]{1,0:T(8,128)(2,1)S(1)}, f32[288,384]{1,0:T(8,128)S(1)}, bf16[288,384]{1,0:T(8,128)(2,1)S(1)}, f32[8,192]{1,0:T(8,128)S(1)}) custom-call(s32[1]{0:T(128)} %bitcast.2.here, bf16[200,1024]{1,0:T(8,128)(2,1)S(1)} %collective-permute-done.14.refs_0_, ...), custom_call_target="tpu_custom_call", output_to_operand_aliasing={{0}: (4, {}), {1}: (5, {})} | custom-call | flops 1048576 | bytes 16384 | tf_op jit(solution)/shard_map/dispatch/pallas_call | solution.py:162
  65.6 2.5 %collective-permute-done.21.refs_1_ = bf16[288,384]{1,0:T(8,128)(2,1)S(1)} collective-permute-done((bf16[288,384]{1,0:T(8,128)(2,1)S(1)}, bf16[288,384]{1,0:T(8,128)(2,1)S(1)}, u32[]{:S(2)}, u32[]{:S(2)}) %collective-permute-start.21) | collective-permute-done | bytes 221216 | tf_op jit(solution)/shard_map/ppermute | solution.py:514
  68.1 3.3 %combine.8 = (bf16[1152,768]{1,0:T(8,128)(2,1)S(1)}, bf16[1152,768]{1,0:T(8,128)(2,1)S(1)}, bf16[192,1024]{1,0:T(8,128)(2,1)S(1)}, bf16[192,1024]{1,0:T(8,128)(2,1)S(1)}) custom-call(s32[1]{0:T(128)} %bitcast.2.here, f32[576,384]{1,0:T(8,128)S(1)} %get-tuple-element.145.share, ...), custom_call_target="tpu_custom_call", output_to_operand_aliasing={{0}: (11, {}), {1}: (12, {})} | custom-call | flops 1048576 | bytes 16384 | tf_op jit(solution)/shard_map/combine/pallas_call | solution.py:231
  77.9 2.1 %collective-permute-done.28.refs_2_ = bf16[192,512]{1,0:T(8,128)(2,1)S(1)} collective-permute-done((bf16[192,512]{1,0:T(8,128)(2,1)S(1)}, bf16[192,512]{1,0:T(8,128)(2,1)S(1)}, u32[]{:S(2)}, u32[]{:S(2)}) %collective-permute-start.28) | collective-permute-done | bytes 196640 | tf_op jit(solution)/shard_map/ppermute | solution.py:492
  80.1 2.9 %collective-permute-start.29 = (bf16[192,512]{1,0:T(8,128)(2,1)S(1)}, bf16[192,512]{1,0:T(8,128)(2,1)S(1)}, u32[]{:S(2)}, u32[]{:S(2)}) collective-permute-start(bf16[192,512]{1,0:T(8,128)(2,1)S(1)} %add.6), channel_id=1, source_target_pairs={{0,4},{1,5},{2,6},{3,7},{4,8},{5,9},{6,10},{7,11},{8,12},{9,13},{1... | collective-permute-start | bytes 589832 | tf_op jit(solution)/shard_map/ppermute | solution.py:492
  84.3 2.9 %collective-permute-start.25 = (bf16[192,512]{1,0:T(8,128)(2,1)S(1)}, bf16[192,512]{1,0:T(8,128)(2,1)S(1)}, u32[]{:S(2)}, u32[]{:S(2)}) collective-permute-start(bf16[192,512]{1,0:T(8,128)(2,1)S(1)} %add.4), channel_id=1, source_target_pairs={{0,4},{1,5},{2,6},{3,7},{4,8},{5,9},{6,10},{7,11},{8,12},{9,13},{1... | collective-permute-start | bytes 589832 | tf_op jit(solution)/shard_map/ppermute | solution.py:492
  88.1 3.3 %collective-permute-start.30 = (bf16[192,512]{1,0:T(8,128)(2,1)S(1)}, bf16[192,512]{1,0:T(8,128)(2,1)S(1)}, u32[]{:S(2)}, u32[]{:S(2)}) collective-permute-start(bf16[192,512]{1,0:T(8,128)(2,1)S(1)} %add.7), channel_id=1, source_target_pairs={{0,4},{1,5},{2,6},{3,7},{4,8},{5,9},{6,10},{7,11},{8,12},{9,13},{1... | collective-permute-start | bytes 589832 | tf_op jit(solution)/shard_map/ppermute | solution.py:492
  91.4 4.4 %received_part.1.old = bf16[1,1024,1152]{2,1,0:T(8,128)(2,1)} custom-call(bf16[384,1152]{1,0:T(8,128)(2,1)S(1)} %hidden.2.hid, bf16[384,1152]{1,0:T(8,128)(2,1)S(1)} %hidden.3.hid_c, bf16[1152,1024]{1,0:T(8,128)(2,1)S(1)} %get-tuple-element.174.own, bf16[1152,1024]{1,0:T(8,128)(2,1)S(1)} %collective-permute-done.22.other), custom_call_target="tpu_custom_call" | custom-call | flops 1048576 | bytes 16384 | tf_op jit(solution)/shard_map/received_part/pallas_call | solution.py:427
  96.2 5.7 %inputs_part.1 = bf16[1,1024,1152]{2,1,0:T(8,128)(2,1)} custom-call(s32[1]{0:T(128)} %bitcast.2.here, bf16[1,1024,1152]{2,1,0:T(8,128)(2,1)} %received_part.1.old, bf16[1024,2304]{1,0:T(8,128)(2,1)S(1)} %turn.1.inputs, bf16[1152,768]{1,0:T(8,128)(2,1)S(1)} %get-tuple-element.181.own, ...), custom_call_target="tpu_custom_call", output_to_operand_aliasing={{}: (1, {})} | custom-call | flops 1048576 | bytes 16384 | tf_op jit(solution)/shard_map/inputs_part/pallas_call | solution.py:460
  101.9 2.8 %collective-permute-done.26.left = bf16[192,512]{1,0:T(8,128)(2,1)S(1)} collective-permute-done((bf16[192,512]{1,0:T(8,128)(2,1)S(1)}, bf16[192,512]{1,0:T(8,128)(2,1)S(1)}, u32[]{:S(2)}, u32[]{:S(2)}) %collective-permute-start.26) | collective-permute-done | bytes 196640 | tf_op jit(solution)/shard_map/ppermute | solution.py:492
  (75 shorter events, 34.7 us)
Async XLA Ops:
  0.6 17.9 %collective-permute-start.3 = (bf16[2304,384]{1,0:T(8,128)(2,1)}, bf16[2304,384]{1,0:T(8,128)(2,1)S(1)}, u32[]{:S(2)}, u32[]{:S(2)}) collective-permute-start(bf16[2304,384]{1,0:T(8,128)(2,1)} %bitcast.9), channel_id=1, source_target_pairs={{0,1},{1,0},{2,3},{3,2},{4,5},{5,4},{6,7},{7,6},{8,9},{9,8},{10,11... | collective-permute-start | bytes 5308424 | tf_op jit(solution)/shard_map/ppermute | solution.py:492
  1.1 17.4 %collective-permute-start.4 = (bf16[2304,384]{1,0:T(8,128)(2,1)}, bf16[2304,384]{1,0:T(8,128)(2,1)S(1)}, u32[]{:S(2)}, u32[]{:S(2)}) collective-permute-start(bf16[2304,384]{1,0:T(8,128)(2,1)} %bitcast.17), channel_id=1, source_target_pairs={{0,1},{1,0},{2,3},{3,2},{4,5},{5,4},{6,7},{7,6},{8,9},{9,8},{10,11... | collective-permute-start | bytes 5308424 | tf_op jit(solution)/shard_map/ppermute | solution.py:492
  1.2 12.7 %collective-permute-start.2 = (bf16[384,1024]{1,0:T(8,128)(2,1)}, bf16[384,1024]{1,0:T(8,128)(2,1)}, u32[]{:S(2)}, u32[]{:S(2)}) collective-permute-start(bf16[384,1024]{1,0:T(8,128)(2,1)} %bitcast.25), channel_id=1, source_target_pairs={{0,1},{1,0},{2,3},{3,2},{4,5},{5,4},{6,7},{7,6},{8,9},{9,8},{10,11... | collective-permute-start | bytes 2359304 | tf_op jit(solution)/shard_map/ppermute | solution.py:492
  3.4 15.1 %collective-permute-start = (bf16[200,1024]{1,0:T(8,128)(2,1)}, bf16[200,1024]{1,0:T(8,128)(2,1)}, u32[]{:S(2)}, u32[]{:S(2)}) collective-permute-start(bf16[200,1024]{1,0:T(8,128)(2,1)} %pack.1.refs_0_), channel_id=1, source_target_pairs={{0,4},{1,5},{2,6},{3,7},{4,8},{5,9},{6,10},{7,11},{8,12},{9,13},{1... | collective-permute-start | bytes 1228808 | tf_op jit(solution)/shard_map/ppermute | solution.py:492
  6.1 12.4 %collective-permute-start.1 = (bf16[200,1024]{1,0:T(8,128)(2,1)}, bf16[200,1024]{1,0:T(8,128)(2,1)}, u32[]{:S(2)}, u32[]{:S(2)}) collective-permute-start(bf16[200,1024]{1,0:T(8,128)(2,1)} %pack.1.refs_0_), channel_id=1, source_target_pairs={{0,2},{1,3},{2,0},{3,1},{4,6},{5,7},{6,4},{7,5},{8,10},{9,11},{10,... | collective-permute-start | bytes 1228808 | tf_op jit(solution)/shard_map/ppermute | solution.py:492
  18.6 10.3 %collective-permute-start.9 = (bf16[1024,768]{1,0:T(8,128)(2,1)S(1)}, bf16[1024,768]{1,0:T(8,128)(2,1)S(1)}, u32[]{:S(2)}, u32[]{:S(2)}) collective-permute-start(bf16[1024,768]{1,0:T(8,128)(2,1)S(1)} %join.1.refs_6_.refs_7_), channel_id=1, source_target_pairs={{0,1},{1,0},{2,3},{3,2},{4,5},{5,4},{6,7},{7,6},{8,9},{9,8},{10,11... | collective-permute-start | bytes 4718600 | tf_op jit(solution)/shard_map/ppermute | solution.py:492
  18.6 14.5 %collective-permute-start.5 = (bf16[200,1024]{1,0:T(8,128)(2,1)}, bf16[200,1024]{1,0:T(8,128)(2,1)S(1)}, u32[]{:S(2)}, u32[]{:S(2)}) collective-permute-start(bf16[200,1024]{1,0:T(8,128)(2,1)} %collective-permute-done.refs_1_), channel_id=1, source_target_pairs={{0,4},{1,5},{2,6},{3,7},{4,8},{5,9},{6,10},{7,11},{8,12},{9,13},{1... | collective-permute-start | bytes 1228808 | tf_op jit(solution)/shard_map/ppermute | solution.py:492
  19.6 13.5 %collective-permute-start.6 = (bf16[200,1024]{1,0:T(8,128)(2,1)}, bf16[200,1024]{1,0:T(8,128)(2,1)S(1)}, u32[]{:S(2)}, u32[]{:S(2)}) collective-permute-start(bf16[200,1024]{1,0:T(8,128)(2,1)} %collective-permute-done.refs_1_), channel_id=1, source_target_pairs={{0,2},{1,3},{2,0},{3,1},{4,6},{5,7},{6,4},{7,5},{8,10},{9,11},{10,... | collective-permute-start | bytes 1228808 | tf_op jit(solution)/shard_map/ppermute | solution.py:492
  33.1 12.8 %collective-permute-start.10 = (bf16[200,1024]{1,0:T(8,128)(2,1)S(1)}, bf16[200,1024]{1,0:T(8,128)(2,1)S(1)}, u32[]{:S(2)}, u32[]{:S(2)}) collective-permute-start(bf16[200,1024]{1,0:T(8,128)(2,1)S(1)} %collective-permute-done.5.refs_1_), channel_id=1, source_target_pairs={{0,4},{1,5},{2,6},{3,7},{4,8},{5,9},{6,10},{7,11},{8,12},{9,13},{1... | collective-permute-start | bytes 1228808 | tf_op jit(solution)/shard_map/ppermute | solution.py:492
  34.7 11.2 %collective-permute-start.11 = (bf16[200,1024]{1,0:T(8,128)(2,1)S(1)}, bf16[200,1024]{1,0:T(8,128)(2,1)S(1)}, u32[]{:S(2)}, u32[]{:S(2)}) collective-permute-start(bf16[200,1024]{1,0:T(8,128)(2,1)S(1)} %collective-permute-done.5.refs_1_), channel_id=1, source_target_pairs={{0,2},{1,3},{2,0},{3,1},{4,6},{5,7},{6,4},{7,5},{8,10},{9,11},{10,... | collective-permute-start | bytes 1228808 | tf_op jit(solution)/shard_map/ppermute | solution.py:492
  45.9 12.7 %collective-permute-start.14 = (bf16[200,1024]{1,0:T(8,128)(2,1)S(1)}, bf16[200,1024]{1,0:T(8,128)(2,1)S(1)}, u32[]{:S(2)}, u32[]{:S(2)}) collective-permute-start(bf16[200,1024]{1,0:T(8,128)(2,1)S(1)} %collective-permute-done.10.refs_1_), channel_id=1, source_target_pairs={{0,2},{1,3},{2,0},{3,1},{4,6},{5,7},{6,4},{7,5},{8,10},{9,11},{10,... | collective-permute-start | bytes 1228808 | tf_op jit(solution)/shard_map/ppermute | solution.py:492
  47.4 11.2 %collective-permute-start.15 = (bf16[192,1024]{1,0:T(8,128)(2,1)S(1)}, bf16[192,1024]{1,0:T(8,128)(2,1)S(1)}, u32[]{:S(2)}, u32[]{:S(2)}) collective-permute-start(bf16[192,1024]{1,0:T(8,128)(2,1)S(1)} %get-tuple-element.124), channel_id=1, source_target_pairs={{0,4},{1,5},{2,6},{3,7},{4,8},{5,9},{6,10},{7,11},{8,12},{9,13},{1... | collective-permute-start | bytes 1179656 | tf_op jit(solution)/shard_map/ppermute | solution.py:492
  58.6 13.0 %collective-permute-start.18 = (bf16[192,1024]{1,0:T(8,128)(2,1)S(1)}, bf16[192,1024]{1,0:T(8,128)(2,1)S(1)}, u32[]{:S(2)}, u32[]{:S(2)}) collective-permute-start(bf16[192,1024]{1,0:T(8,128)(2,1)S(1)} %get-tuple-element.139), channel_id=1, source_target_pairs={{0,4},{1,5},{2,6},{3,7},{4,8},{5,9},{6,10},{7,11},{8,12},{9,13},{1... | collective-permute-start | bytes 1179656 | tf_op jit(solution)/shard_map/ppermute | solution.py:492
  60.6 10.9 %collective-permute-start.19 = (bf16[192,1024]{1,0:T(8,128)(2,1)S(1)}, bf16[192,1024]{1,0:T(8,128)(2,1)S(1)}, u32[]{:S(2)}, u32[]{:S(2)}) collective-permute-start(bf16[192,1024]{1,0:T(8,128)(2,1)S(1)} %get-tuple-element.140), channel_id=1, source_target_pairs={{0,2},{1,3},{2,0},{3,1},{4,6},{5,7},{6,4},{7,5},{8,10},{9,11},{10,... | collective-permute-start | bytes 1179656 | tf_op jit(solution)/shard_map/ppermute | solution.py:492
  71.6 15.6 %collective-permute-start.22 = (bf16[1152,1024]{1,0:T(8,128)(2,1)S(1)}, bf16[1152,1024]{1,0:T(8,128)(2,1)S(1)}, u32[]{:S(2)}, u32[]{:S(2)}) collective-permute-start(bf16[1152,1024]{1,0:T(8,128)(2,1)S(1)} %get-tuple-element.167), channel_id=1, source_target_pairs={{0,1},{1,0},{2,3},{3,2},{4,5},{5,4},{6,7},{7,6},{8,9},{9,8},{10,11... | collective-permute-start | bytes 7077896 | tf_op jit(solution)/shard_map/ppermute | solution.py:492
  71.6 24.6 %collective-permute-start.31 = (bf16[1152,768]{1,0:T(8,128)(2,1)S(1)}, bf16[1152,768]{1,0:T(8,128)(2,1)S(1)}, u32[]{:S(2)}, u32[]{:S(2)}) collective-permute-start(bf16[1152,768]{1,0:T(8,128)(2,1)S(1)} %get-tuple-element.182), channel_id=1, source_target_pairs={{0,1},{1,0},{2,3},{3,2},{4,5},{5,4},{6,7},{7,6},{8,9},{9,8},{10,11... | collective-permute-start | bytes 5308424 | tf_op jit(solution)/shard_map/ppermute | solution.py:492
  73.7 10.5 %collective-permute-start.24 = (bf16[192,512]{1,0:T(8,128)(2,1)S(1)}, bf16[192,512]{1,0:T(8,128)(2,1)S(1)}, u32[]{:S(2)}, u32[]{:S(2)}) collective-permute-start(bf16[192,512]{1,0:T(8,128)(2,1)S(1)} %get-tuple-element.171), channel_id=1, source_target_pairs={{0,2},{1,3},{2,0},{3,1},{4,6},{5,7},{6,4},{7,5},{8,10},{9,11},{10,... | collective-permute-start | bytes 589832 | tf_op jit(solution)/shard_map/ppermute | solution.py:492
  76.3 11.2 %collective-permute-start.27 = (bf16[192,512]{1,0:T(8,128)(2,1)S(1)}, bf16[192,512]{1,0:T(8,128)(2,1)S(1)}, u32[]{:S(2)}, u32[]{:S(2)}) collective-permute-start(bf16[192,512]{1,0:T(8,128)(2,1)S(1)} %get-tuple-element.177), channel_id=1, source_target_pairs={{0,2},{1,3},{2,0},{3,1},{4,6},{5,7},{6,4},{7,5},{8,10},{9,11},{10,... | collective-permute-start | bytes 589832 | tf_op jit(solution)/shard_map/ppermute | solution.py:492
  80.1 7.9 %collective-permute-start.29 = (bf16[192,512]{1,0:T(8,128)(2,1)S(1)}, bf16[192,512]{1,0:T(8,128)(2,1)S(1)}, u32[]{:S(2)}, u32[]{:S(2)}) collective-permute-start(bf16[192,512]{1,0:T(8,128)(2,1)S(1)} %add.6), channel_id=1, source_target_pairs={{0,4},{1,5},{2,6},{3,7},{4,8},{5,9},{6,10},{7,11},{8,12},{9,13},{1... | collective-permute-start | bytes 589832 | tf_op jit(solution)/shard_map/ppermute | solution.py:492
  84.3 11.4 %collective-permute-start.25 = (bf16[192,512]{1,0:T(8,128)(2,1)S(1)}, bf16[192,512]{1,0:T(8,128)(2,1)S(1)}, u32[]{:S(2)}, u32[]{:S(2)}) collective-permute-start(bf16[192,512]{1,0:T(8,128)(2,1)S(1)} %add.4), channel_id=1, source_target_pairs={{0,4},{1,5},{2,6},{3,7},{4,8},{5,9},{6,10},{7,11},{8,12},{9,13},{1... | collective-permute-start | bytes 589832 | tf_op jit(solution)/shard_map/ppermute | solution.py:492
  87.1 8.6 %collective-permute-start.23 = (bf16[192,512]{1,0:T(8,128)(2,1)S(1)}, bf16[192,512]{1,0:T(8,128)(2,1)S(1)}, u32[]{:S(2)}, u32[]{:S(2)}) collective-permute-start(bf16[192,512]{1,0:T(8,128)(2,1)S(1)} %get-tuple-element.168), channel_id=1, source_target_pairs={{0,2},{1,3},{2,0},{3,1},{4,6},{5,7},{6,4},{7,5},{8,10},{9,11},{10,... | collective-permute-start | bytes 589832 | tf_op jit(solution)/shard_map/ppermute | solution.py:492
  87.5 8.7 %collective-permute-start.32 = (bf16[144,768]{1,0:T(8,128)(2,1)S(1)}, bf16[144,768]{1,0:T(8,128)(2,1)S(1)}, u32[]{:S(2)}, u32[]{:S(2)}) collective-permute-start(bf16[144,768]{1,0:T(8,128)(2,1)S(1)} %get-tuple-element.183), channel_id=1, source_target_pairs={{0,1},{1,0},{2,3},{3,2},{4,5},{5,4},{6,7},{7,6},{8,9},{9,8},{10,11... | collective-permute-start | bytes 663560 | tf_op jit(solution)/shard_map/ppermute | solution.py:492
  88.1 13.8 %collective-permute-start.30 = (bf16[192,512]{1,0:T(8,128)(2,1)S(1)}, bf16[192,512]{1,0:T(8,128)(2,1)S(1)}, u32[]{:S(2)}, u32[]{:S(2)}) collective-permute-start(bf16[192,512]{1,0:T(8,128)(2,1)S(1)} %add.7), channel_id=1, source_target_pairs={{0,4},{1,5},{2,6},{3,7},{4,8},{5,9},{6,10},{7,11},{8,12},{9,13},{1... | collective-permute-start | bytes 589832 | tf_op jit(solution)/shard_map/ppermute | solution.py:492
  95.8 8.9 %collective-permute-start.26 = (bf16[192,512]{1,0:T(8,128)(2,1)S(1)}, bf16[192,512]{1,0:T(8,128)(2,1)S(1)}, u32[]{:S(2)}, u32[]{:S(2)}) collective-permute-start(bf16[192,512]{1,0:T(8,128)(2,1)S(1)} %add.5), channel_id=1, source_target_pairs={{0,4},{1,5},{2,6},{3,7},{4,8},{5,9},{6,10},{7,11},{8,12},{9,13},{1... | collective-permute-start | bytes 589832 | tf_op jit(solution)/shard_map/ppermute | solution.py:492
  (14 other events, 77.6 us)

commit v11 on v10

--- a/solution.py
+++ b/solution.py
@@ -414,26 +414,49 @@
     )(in_hbm(tokens), in_hbm(routes), in_hbm(codes))
 
 
-def received_kernel(hid, hid_c, own, other, out):
-    part = jnp.dot(hid[...], own[...], preferred_element_type=f32)
-    part = part + jnp.dot(hid_c[...], other[...], preferred_element_type=f32)
-    out[0] = (part * loss_scale).astype(bf16).T
-
-
-def received_part(hid, hid_c, own, other):
+def received_own_kernel(hid, own, out):
+    out[...] = jnp.dot(hid[...], own[...], preferred_element_type=f32)
+
+
+def received_other_kernel(part, hid, other, out):
+    total = part[...] + jnp.dot(hid[...], other[...], preferred_element_type=f32)
+    out[0] = (total * loss_scale).astype(bf16).T
+
+
+def received_own(hid, own):
     h = hid.shape[0]
     rows, d = own.shape
     tile = 256
     return pl.pallas_call(
-        received_kernel,
+        received_own_kernel,
+        out_shape=jax.ShapeDtypeStruct((h, d), f32),
+        grid=(d // tile,),
+        in_specs=[pl.BlockSpec((h, rows), lambda i: (0, 0)), pl.BlockSpec((rows, tile), lambda i: (0, i))],
+        out_specs=pl.BlockSpec((h, tile), lambda i: (0, i)),
+        cost_estimate=light,
+        compiler_params=params(16),
+        name="received_own",
+    )(hid, own)
+
+
+def received_other(part, hid, other):
+    h, d = part.shape
+    rows = other.shape[0]
+    tile = 256
+    return pl.pallas_call(
+        received_other_kernel,
         out_shape=jax.ShapeDtypeStruct((1, d, 3 * h), bf16),
         grid=(d // tile,),
-        in_specs=[pl.BlockSpec((h, rows), lambda i: (0, 0))] * 2 + [pl.BlockSpec((rows, tile), lambda i: (0, i))] * 2,
+        in_specs=[
+            pl.BlockSpec((h, tile), lambda i: (0, i)),
+            pl.BlockSpec((h, rows), lambda i: (0, 0)),
+            pl.BlockSpec((rows, tile), lambda i: (0, i)),
+        ],
         out_specs=pl.BlockSpec((1, tile, h), lambda i: (0, i, 2)),
         cost_estimate=light,
-        compiler_params=params(20),
-        name="received_part",
-    )(hid, hid_c, own, other)
+        compiler_params=params(16),
+        name="received_other",
+    )(part, hid, other)
 
 
 def inputs_kernel(cap, last, here, old, inputs, own, other, late, out, held):
@@ -555,11 +578,12 @@
     a0, a1, h4 = together(*add_halves(t_x2, u1), h4)
     b2 = [send(a0, to_x), send(a1, to_x)]
     left, right = second(c4, h4, last=True)
-    left, rec_c = together(left, rec_c)
     b3 = [send(left, to_x), send(right, to_x)]
     late = send(gps[1], to_core)
+    part = received_own(hid, recs[0])
+    b2[1], part, rec_c = together(b2[1], part, rec_c)
     w2 = [ring(add([t_r2, w1, b2[k]], k)) for k in range(2)]
-    part = received_part(hid, hid_c, recs[0], rec_c)
+    part = received_other(part, hid_c, rec_c)
     w2[0], part = together(w2[0], part)
     w3 = [ring(add([t_r3, b3[k], w2[k]], k)) for k in range(2)]
     weight_grads = inputs_part(here, (1, 3), part, inputs, gps[0], gp_c, late, cap)

time: 106 us -> 108 us (1.019)
  waiting for transfers between devices: 17.5 us -> 23.7 us
  starting transfers between devices: 36.7 us -> 31.2 us
    ppermute x25, waiting for transfers between devices: 7.96 us -> 14.1 us  [send(): return lax.ppermute(v, 'expert', perm)]
    ppermute x25, starting transfers between devices: 28.2 us -> 22.8 us  [send(): return lax.ppermute(v, 'expert', perm)]
    pallas_call x1 -> x2, Pallas kernels: 4.36 us -> 5.28 us  [the longest x1 3.15 us: received_other(): pl.pallas_call(received_other_kernel, out_shape=jax.ShapeDtypeStruct((1,...]
  transfers between devices with their start and end apart: 33 -> 33, of which waited for: 13 -> 14; matrix products, arithmetic and copies ran while one was open for 0% -> 0% of each run, Pallas kernels for 46% -> 46%
where the time goes in v11:
time: 108 us; the launch traced here: 107 us
  Pallas kernels  50.4 us (47%)
  starting transfers between devices  31.2 us (29%)
  waiting for transfers between devices  23.7 us (22%)
    ppermute x25, starting transfers between devices, send(): return lax.ppermute(v, 'expert', perm)  22.8 us
    pallas_call x5, Pallas kernels, combine(): pl.pallas_call(functools.partial(combine_kernel, chunk, cap, len(old), la...  14.2 us
    ppermute x25, waiting for transfers between devices, send(): return lax.ppermute(v, 'expert', perm)  14.1 us
    pallas_call x5, Pallas kernels, dispatch(): pl.pallas_call(functools.partial(dispatch_kernel, chunk, cap, len(old) //...  13.5 us
    ppermute x8, waiting for transfers between devices, exchange(): return lax.ppermute(v, 'dp', [(0, 1), (1, 0)])  9.56 us
    ppermute x8, starting transfers between devices, exchange(): return lax.ppermute(v, 'dp', [(0, 1), (1, 0)])  8.41 us
    pallas_call x1, Pallas kernels, inputs_part(): pl.pallas_call(functools.partial(inputs_kernel, cap, last), out_shape=jax...  5.66 us
    pallas_call x2, Pallas kernels, hidden(): pl.pallas_call(functools.partial(hidden_kernel, cap, k), out_shape=jax.Sh...  4.73 us
  transfers between devices with their start and end apart: 33, of which 14 were waited for; matrix products, arithmetic and copies ran while one was open for 0% of the time, Pallas kernels for 46%

profile of v11, /device:TPU:0, one launch (start us, length us, event | category | flops | bytes accessed | tf_op | source)
XLA Modules:
  0.0 107.2 jit_solution(4371251972905567331)
XLA Ops:
  3.4 2.7 %collective-permute-start = (bf16[200,1024]{1,0:T(8,128)(2,1)}, bf16[200,1024]{1,0:T(8,128)(2,1)}, u32[]{:S(2)}, u32[]{:S(2)}) collective-permute-start(bf16[200,1024]{1,0:T(8,128)(2,1)} %pack.1.refs_0_), channel_id=1, source_target_pairs={{0,4},{1,5},{2,6},{3,7},{4,8},{5,9},{6,10},{7,11},{8,12},{9,13},{1... | collective-permute-start | bytes 1228808 | tf_op jit(solution)/shard_map/ppermute | solution.py:515
  7.6 2.2 %hidden.2.hid = bf16[384,1152]{1,0:T(8,128)(2,1)S(1)} custom-call(s32[1]{0:T(128)} %bitcast.2.here, bf16[2304,384]{1,0:T(8,128)(2,1)} %bitcast.10, bf16[2304,384]{1,0:T(8,128)(2,1)} %bitcast.18), custom_call_target="tpu_custom_call" | custom-call | flops 1048576 | bytes 16384 | tf_op jit(solution)/shard_map/hidden/pallas_call | solution.py:347
  9.9 3.9 %turn.1.inputs = bf16[1024,2304]{1,0:T(8,128)(2,1)S(1)} custom-call(s32[1]{0:T(128)} %bitcast.2.here, bf16[2304,1024]{1,0:T(8,128)(2,1)} %bitcast.33), custom_call_target="tpu_custom_call" | custom-call | flops 1048576 | bytes 16384 | tf_op jit(solution)/shard_map/turn/pallas_call | solution.py:371
  14.9 2.5 %dispatch.5 = (bf16[1152,1024]{1,0:T(8,128)(2,1)S(1)}, bf16[1152,1024]{1,0:T(8,128)(2,1)S(1)}, f32[288,384]{1,0:T(8,128)S(1)}, bf16[288,384]{1,0:T(8,128)(2,1)S(1)}, f32[8,192]{1,0:T(8,128)S(1)}) custom-call(s32[1]{0:T(128)} %bitcast.2.here, bf16[200,1024]{1,0:T(8,128)(2,1)} %pack.1.refs_0_, bf16[384,1024]{1,0:T(8,128)(2,1)S(1)} %bitcast.26, ...), custom_call_target="tpu_custom_call" | custom-call | flops 1048576 | bytes 16384 | tf_op jit(solution)/shard_map/dispatch/pallas_call | solution.py:162
  22.7 3.1 %dispatch.6 = (bf16[1152,1024]{1,0:T(8,128)(2,1)S(1)}, bf16[1152,1024]{1,0:T(8,128)(2,1)S(1)}, f32[576,384]{1,0:T(8,128)S(1)}, bf16[288,384]{1,0:T(8,128)(2,1)S(...) custom-call(s32[1]{0:T(128)} %bitcast.2.here, ...), custom_call_target="tpu_custom_call", output_to_operand_aliasing={{0}: (5, {}), {1}: (6, {})} | custom-call | flops 1048576 | bytes 16384 | tf_op jit(solution)/shard_map/dispatch/pallas_call | solution.py:162
  26.3 2.5 %hidden.3.hid = bf16[384,1152]{1,0:T(8,128)(2,1)S(1)} custom-call(s32[1]{0:T(128)} %bitcast.2.here, bf16[2304,384]{1,0:T(8,128)(2,1)} %bitcast.11, bf16[2304,384]{1,0:T(8,128)(2,1)} %bitcast.19), custom_call_target="tpu_custom_call" | custom-call | flops 1048576 | bytes 16384 | tf_op jit(solution)/shard_map/hidden/pallas_call | solution.py:347
  28.9 2.3 %combine.5 = (bf16[1152,768]{1,0:T(8,128)(2,1)S(1)}, bf16[1152,768]{1,0:T(8,128)(2,1)S(1)}, bf16[192,1024]{1,0:T(8,128)(2,1)S(1)}) custom-call(s32[1]{0:T(128)} %bitcast.2.here, f32[288,384]{1,0:T(8,128)S(1)} %get-tuple-element.102.share, bf16[288,384]{1,0:T(8,128)(2,1)S(1)} %collective-permute-done.8.refs_0_, f32[8,192]{1,0:T(8,128)S(1)} %get-tuple-element.104.refs_1_, ...), custom_call_target="tpu_custom_call" | custom-call | flops 1048576 | bytes 16384 | tf_op jit(solution)/shard_map/combine/pallas_call | solution.py:231
  36.7 2.8 %dispatch.7 = (bf16[1152,1024]{1,0:T(8,128)(2,1)S(1)}, bf16[1152,1024]{1,0:T(8,128)(2,1)S(1)}, f32[576,384]{1,0:T(8,128)S(1)}, bf16[288,384]{1,0:T(8,128)(2,1)S(...) custom-call(s32[1]{0:T(128)} %bitcast.2.here, ...), custom_call_target="tpu_custom_call", output_to_operand_aliasing={{0}: (5, {}), {1}: (6, {})} | custom-call | flops 1048576 | bytes 16384 | tf_op jit(solution)/shard_map/dispatch/pallas_call | solution.py:162
  42.0 3.3 %combine.6 = (bf16[1152,768]{1,0:T(8,128)(2,1)S(1)}, bf16[1152,768]{1,0:T(8,128)(2,1)S(1)}, bf16[192,1024]{1,0:T(8,128)(2,1)S(1)}, bf16[192,1024]{1,0:T(8,128)(2,1)S(1)}) custom-call(s32[1]{0:T(128)} %bitcast.2.here, f32[576,384]{1,0:T(8,128)S(1)} %get-tuple-element.116.share, ...), custom_call_target="tpu_custom_call", output_to_operand_aliasing={{0}: (11, {}), {1}: (12, {})} | custom-call | flops 1048576 | bytes 16384 | tf_op jit(solution)/shard_map/combine/pallas_call | solution.py:231
  49.7 2.8 %dispatch.8 = (bf16[1152,1024]{1,0:T(8,128)(2,1)S(1)}, bf16[1152,1024]{1,0:T(8,128)(2,1)S(1)}, f32[576,384]{1,0:T(8,128)S(1)}, bf16[288,384]{1,0:T(8,128)(2,1)S(...) custom-call(s32[1]{0:T(128)} %bitcast.2.here, ...), custom_call_target="tpu_custom_call", output_to_operand_aliasing={{0}: (5, {}), {1}: (6, {})} | custom-call | flops 1048576 | bytes 16384 | tf_op jit(solution)/shard_map/dispatch/pallas_call | solution.py:162
  52.7 2.4 %collective-permute-done.17.refs_1_ = bf16[288,384]{1,0:T(8,128)(2,1)S(1)} collective-permute-done((bf16[288,384]{1,0:T(8,128)(2,1)S(1)}, bf16[288,384]{1,0:T(8,128)(2,1)S(1)}, u32[]{:S(2)}, u32[]{:S(2)}) %collective-permute-start.17) | collective-permute-done | bytes 221216 | tf_op jit(solution)/shard_map/ppermute | solution.py:537
  55.1 3.3 %combine.7 = (bf16[1152,768]{1,0:T(8,128)(2,1)S(1)}, bf16[1152,768]{1,0:T(8,128)(2,1)S(1)}, bf16[192,1024]{1,0:T(8,128)(2,1)S(1)}, bf16[192,1024]{1,0:T(8,128)(2,1)S(1)}) custom-call(s32[1]{0:T(128)} %bitcast.2.here, f32[576,384]{1,0:T(8,128)S(1)} %get-tuple-element.132.share, ...), custom_call_target="tpu_custom_call", output_to_operand_aliasing={{0}: (11, {}), {1}: (12, {})} | custom-call | flops 1048576 | bytes 16384 | tf_op jit(solution)/shard_map/combine/pallas_call | solution.py:231
  58.6 2.1 %collective-permute-start.18 = (bf16[192,1024]{1,0:T(8,128)(2,1)S(1)}, bf16[192,1024]{1,0:T(8,128)(2,1)S(1)}, u32[]{:S(2)}, u32[]{:S(2)}) collective-permute-start(bf16[192,1024]{1,0:T(8,128)(2,1)S(1)} %get-tuple-element.140), channel_id=1, source_target_pairs={{0,4},{1,5},{2,6},{3,7},{4,8},{5,9},{6,10},{7,11},{8,12},{9,13},{1... | collective-permute-start | bytes 1179656 | tf_op jit(solution)/shard_map/ppermute | solution.py:515
  61.2 2.1 %collective-permute-start.21 = (bf16[288,384]{1,0:T(8,128)(2,1)S(1)}, bf16[288,384]{1,0:T(8,128)(2,1)S(1)}, u32[]{:S(2)}, u32[]{:S(2)}) collective-permute-start(bf16[288,384]{1,0:T(8,128)(2,1)S(1)} %get-tuple-element.148), channel_id=1, source_target_pairs={{0,16},{16,0},{1,17},{17,1},{2,18},{18,2},{3,19},{19,3},{4,20},{20... | collective-permute-start | bytes 663560 | tf_op jit(solution)/shard_map/ppermute | solution.py:537
  63.2 2.3 %dispatch.9 = (bf16[1152,1024]{1,0:T(8,128)(2,1)S(1)}, bf16[1152,1024]{1,0:T(8,128)(2,1)S(1)}, f32[288,384]{1,0:T(8,128)S(1)}, bf16[288,384]{1,0:T(8,128)(2,1)S(1)}, f32[8,192]{1,0:T(8,128)S(1)}) custom-call(s32[1]{0:T(128)} %bitcast.2.here, bf16[200,1024]{1,0:T(8,128)(2,1)S(1)} %collective-permute-done.14.refs_0_, ...), custom_call_target="tpu_custom_call", output_to_operand_aliasing={{0}: (4, {}), {1}: (5, {})} | custom-call | flops 1048576 | bytes 16384 | tf_op jit(solution)/shard_map/dispatch/pallas_call | solution.py:162
  65.6 2.5 %collective-permute-done.21.refs_1_ = bf16[288,384]{1,0:T(8,128)(2,1)S(1)} collective-permute-done((bf16[288,384]{1,0:T(8,128)(2,1)S(1)}, bf16[288,384]{1,0:T(8,128)(2,1)S(1)}, u32[]{:S(2)}, u32[]{:S(2)}) %collective-permute-start.21) | collective-permute-done | bytes 221216 | tf_op jit(solution)/shard_map/ppermute | solution.py:537
  68.1 3.3 %combine.8 = (bf16[1152,768]{1,0:T(8,128)(2,1)S(1)}, bf16[1152,768]{1,0:T(8,128)(2,1)S(1)}, bf16[192,1024]{1,0:T(8,128)(2,1)S(1)}, bf16[192,1024]{1,0:T(8,128)(2,1)S(1)}) custom-call(s32[1]{0:T(128)} %bitcast.2.here, f32[576,384]{1,0:T(8,128)S(1)} %get-tuple-element.146.share, ...), custom_call_target="tpu_custom_call", output_to_operand_aliasing={{0}: (11, {}), {1}: (12, {})} | custom-call | flops 1048576 | bytes 16384 | tf_op jit(solution)/shard_map/combine/pallas_call | solution.py:231
  74.3 5.7 %collective-permute-done.23.refs_2_ = bf16[192,512]{1,0:T(8,128)(2,1)S(1)} collective-permute-done((bf16[192,512]{1,0:T(8,128)(2,1)S(1)}, bf16[192,512]{1,0:T(8,128)(2,1)S(1)}, u32[]{:S(2)}, u32[]{:S(2)}) %collective-permute-start.23) | collective-permute-done | bytes 196640 | tf_op jit(solution)/shard_map/ppermute | solution.py:515
  80.1 2.9 %collective-permute-start.24 = (bf16[192,512]{1,0:T(8,128)(2,1)S(1)}, bf16[192,512]{1,0:T(8,128)(2,1)S(1)}, u32[]{:S(2)}, u32[]{:S(2)}) collective-permute-start(bf16[192,512]{1,0:T(8,128)(2,1)S(1)} %add.4), channel_id=1, source_target_pairs={{0,4},{1,5},{2,6},{3,7},{4,8},{5,9},{6,10},{7,11},{8,12},{9,13},{1... | collective-permute-start | bytes 589832 | tf_op jit(solution)/shard_map/ppermute | solution.py:515
  82.9 2.1 %received_own.1.part = f32[384,1024]{1,0:T(8,128)S(1)} custom-call(bf16[384,1152]{1,0:T(8,128)(2,1)S(1)} %hidden.2.hid, bf16[1152,1024]{1,0:T(8,128)(2,1)S(1)} %get-tuple-element.173.own), custom_call_target="tpu_custom_call" | custom-call | flops 1048576 | bytes 16384 | tf_op jit(solution)/shard_map/received_own/pallas_call | solution.py:430
  85.1 2.0 %combine.9 = (bf16[1152,768]{1,0:T(8,128)(2,1)S(1)}, bf16[144,768]{1,0:T(8,128)(2,1)S(1)}, bf16[192,512]{1,0:T(8,128)(2,1)S(1)}, bf16[192,512]{1,0:T(8,128)(2,1)S(1)}) custom-call(s32[1]{0:T(128)} %bitcast.2.here, f32[288,384]{1,0:T(8,128)S(1)} %get-tuple-element.158.share, ...), custom_call_target="tpu_custom_call", output_to_operand_aliasing={{0}: (10, {})} | custom-call | flops 1048576 | bytes 16384 | tf_op jit(solution)/shard_map/combine/pallas_call | solution.py:231
  89.7 3.2 %received_other.1.old = bf16[1,1024,1152]{2,1,0:T(8,128)(2,1)} custom-call(f32[384,1024]{1,0:T(8,128)S(1)} %received_own.1.part, bf16[384,1152]{1,0:T(8,128)(2,1)S(1)} %hidden.3.hid, bf16[1152,1024]{1,0:T(8,128)(2,1)S(1)} %collective-permute-done.26.other), custom_call_target="tpu_custom_call" | custom-call | flops 1048576 | bytes 16384 | tf_op jit(solution)/shard_map/received_other/pallas_call | solution.py:446
  96.8 5.7 %inputs_part.1 = bf16[1,1024,1152]{2,1,0:T(8,128)(2,1)} custom-call(s32[1]{0:T(128)} %bitcast.2.here, bf16[1,1024,1152]{2,1,0:T(8,128)(2,1)} %received_other.1.old, bf16[1024,2304]{1,0:T(8,128)(2,1)S(1)} %turn.1.inputs, bf16[1152,768]{1,0:T(8,128)(2,1)S(1)} %get-tuple-element.183.own, ...), custom_call_target="tpu_custom_call", output_to_operand_aliasing={{}: (1, {})} | custom-call | flops 1048576 | bytes 16384 | tf_op jit(solution)/shard_map/inputs_part/pallas_call | solution.py:483
  104.2 2.1 %collective-permute-done.27.left = bf16[192,512]{1,0:T(8,128)(2,1)S(1)} collective-permute-done((bf16[192,512]{1,0:T(8,128)(2,1)S(1)}, bf16[192,512]{1,0:T(8,128)(2,1)S(1)}, u32[]{:S(2)}, u32[]{:S(2)}) %collective-permute-start.27) | collective-permute-done | bytes 196640 | tf_op jit(solution)/shard_map/ppermute | solution.py:515
  (76 shorter events, 36.6 us)
Async XLA Ops:
  0.6 17.9 %collective-permute-start.3 = (bf16[2304,384]{1,0:T(8,128)(2,1)}, bf16[2304,384]{1,0:T(8,128)(2,1)S(1)}, u32[]{:S(2)}, u32[]{:S(2)}) collective-permute-start(bf16[2304,384]{1,0:T(8,128)(2,1)} %bitcast.9), channel_id=1, source_target_pairs={{0,1},{1,0},{2,3},{3,2},{4,5},{5,4},{6,7},{7,6},{8,9},{9,8},{10,11... | collective-permute-start | bytes 5308424 | tf_op jit(solution)/shard_map/ppermute | solution.py:515
  1.1 17.4 %collective-permute-start.4 = (bf16[2304,384]{1,0:T(8,128)(2,1)}, bf16[2304,384]{1,0:T(8,128)(2,1)S(1)}, u32[]{:S(2)}, u32[]{:S(2)}) collective-permute-start(bf16[2304,384]{1,0:T(8,128)(2,1)} %bitcast.17), channel_id=1, source_target_pairs={{0,1},{1,0},{2,3},{3,2},{4,5},{5,4},{6,7},{7,6},{8,9},{9,8},{10,11... | collective-permute-start | bytes 5308424 | tf_op jit(solution)/shard_map/ppermute | solution.py:515
  1.2 12.7 %collective-permute-start.2 = (bf16[384,1024]{1,0:T(8,128)(2,1)}, bf16[384,1024]{1,0:T(8,128)(2,1)}, u32[]{:S(2)}, u32[]{:S(2)}) collective-permute-start(bf16[384,1024]{1,0:T(8,128)(2,1)} %bitcast.25), channel_id=1, source_target_pairs={{0,1},{1,0},{2,3},{3,2},{4,5},{5,4},{6,7},{7,6},{8,9},{9,8},{10,11... | collective-permute-start | bytes 2359304 | tf_op jit(solution)/shard_map/ppermute | solution.py:515
  3.4 15.1 %collective-permute-start = (bf16[200,1024]{1,0:T(8,128)(2,1)}, bf16[200,1024]{1,0:T(8,128)(2,1)}, u32[]{:S(2)}, u32[]{:S(2)}) collective-permute-start(bf16[200,1024]{1,0:T(8,128)(2,1)} %pack.1.refs_0_), channel_id=1, source_target_pairs={{0,4},{1,5},{2,6},{3,7},{4,8},{5,9},{6,10},{7,11},{8,12},{9,13},{1... | collective-permute-start | bytes 1228808 | tf_op jit(solution)/shard_map/ppermute | solution.py:515
  6.1 12.4 %collective-permute-start.1 = (bf16[200,1024]{1,0:T(8,128)(2,1)}, bf16[200,1024]{1,0:T(8,128)(2,1)}, u32[]{:S(2)}, u32[]{:S(2)}) collective-permute-start(bf16[200,1024]{1,0:T(8,128)(2,1)} %pack.1.refs_0_), channel_id=1, source_target_pairs={{0,2},{1,3},{2,0},{3,1},{4,6},{5,7},{6,4},{7,5},{8,10},{9,11},{10,... | collective-permute-start | bytes 1228808 | tf_op jit(solution)/shard_map/ppermute | solution.py:515
  18.6 10.3 %collective-permute-start.9 = (bf16[1024,768]{1,0:T(8,128)(2,1)S(1)}, bf16[1024,768]{1,0:T(8,128)(2,1)S(1)}, u32[]{:S(2)}, u32[]{:S(2)}) collective-permute-start(bf16[1024,768]{1,0:T(8,128)(2,1)S(1)} %join.1.refs_6_.refs_7_), channel_id=1, source_target_pairs={{0,1},{1,0},{2,3},{3,2},{4,5},{5,4},{6,7},{7,6},{8,9},{9,8},{10,11... | collective-permute-start | bytes 4718600 | tf_op jit(solution)/shard_map/ppermute | solution.py:515
  18.6 14.5 %collective-permute-start.5 = (bf16[200,1024]{1,0:T(8,128)(2,1)}, bf16[200,1024]{1,0:T(8,128)(2,1)S(1)}, u32[]{:S(2)}, u32[]{:S(2)}) collective-permute-start(bf16[200,1024]{1,0:T(8,128)(2,1)} %collective-permute-done.refs_1_), channel_id=1, source_target_pairs={{0,4},{1,5},{2,6},{3,7},{4,8},{5,9},{6,10},{7,11},{8,12},{9,13},{1... | collective-permute-start | bytes 1228808 | tf_op jit(solution)/shard_map/ppermute | solution.py:515
  19.6 13.5 %collective-permute-start.6 = (bf16[200,1024]{1,0:T(8,128)(2,1)}, bf16[200,1024]{1,0:T(8,128)(2,1)S(1)}, u32[]{:S(2)}, u32[]{:S(2)}) collective-permute-start(bf16[200,1024]{1,0:T(8,128)(2,1)} %collective-permute-done.refs_1_), channel_id=1, source_target_pairs={{0,2},{1,3},{2,0},{3,1},{4,6},{5,7},{6,4},{7,5},{8,10},{9,11},{10,... | collective-permute-start | bytes 1228808 | tf_op jit(solution)/shard_map/ppermute | solution.py:515
  21.1 7.7 %collective-permute-start.8 = (bf16[288,384]{1,0:T(8,128)(2,1)S(1)}, bf16[288,384]{1,0:T(8,128)(2,1)S(1)}, u32[]{:S(2)}, u32[]{:S(2)}) collective-permute-start(bf16[288,384]{1,0:T(8,128)(2,1)S(1)} %get-tuple-element.103), channel_id=1, source_target_pairs={{0,16},{16,0},{1,17},{17,1},{2,18},{18,2},{3,19},{19,3},{4,20},{20... | collective-permute-start | bytes 663560 | tf_op jit(solution)/shard_map/ppermute | solution.py:537
  33.1 12.8 %collective-permute-start.10 = (bf16[200,1024]{1,0:T(8,128)(2,1)S(1)}, bf16[200,1024]{1,0:T(8,128)(2,1)S(1)}, u32[]{:S(2)}, u32[]{:S(2)}) collective-permute-start(bf16[200,1024]{1,0:T(8,128)(2,1)S(1)} %collective-permute-done.5.refs_1_), channel_id=1, source_target_pairs={{0,4},{1,5},{2,6},{3,7},{4,8},{5,9},{6,10},{7,11},{8,12},{9,13},{1... | collective-permute-start | bytes 1228808 | tf_op jit(solution)/shard_map/ppermute | solution.py:515
  34.7 11.2 %collective-permute-start.11 = (bf16[200,1024]{1,0:T(8,128)(2,1)S(1)}, bf16[200,1024]{1,0:T(8,128)(2,1)S(1)}, u32[]{:S(2)}, u32[]{:S(2)}) collective-permute-start(bf16[200,1024]{1,0:T(8,128)(2,1)S(1)} %collective-permute-done.5.refs_1_), channel_id=1, source_target_pairs={{0,2},{1,3},{2,0},{3,1},{4,6},{5,7},{6,4},{7,5},{8,10},{9,11},{10,... | collective-permute-start | bytes 1228808 | tf_op jit(solution)/shard_map/ppermute | solution.py:515
  45.9 12.7 %collective-permute-start.14 = (bf16[200,1024]{1,0:T(8,128)(2,1)S(1)}, bf16[200,1024]{1,0:T(8,128)(2,1)S(1)}, u32[]{:S(2)}, u32[]{:S(2)}) collective-permute-start(bf16[200,1024]{1,0:T(8,128)(2,1)S(1)} %collective-permute-done.10.refs_1_), channel_id=1, source_target_pairs={{0,2},{1,3},{2,0},{3,1},{4,6},{5,7},{6,4},{7,5},{8,10},{9,11},{10,... | collective-permute-start | bytes 1228808 | tf_op jit(solution)/shard_map/ppermute | solution.py:515
  47.4 11.2 %collective-permute-start.15 = (bf16[192,1024]{1,0:T(8,128)(2,1)S(1)}, bf16[192,1024]{1,0:T(8,128)(2,1)S(1)}, u32[]{:S(2)}, u32[]{:S(2)}) collective-permute-start(bf16[192,1024]{1,0:T(8,128)(2,1)S(1)} %get-tuple-element.125), channel_id=1, source_target_pairs={{0,4},{1,5},{2,6},{3,7},{4,8},{5,9},{6,10},{7,11},{8,12},{9,13},{1... | collective-permute-start | bytes 1179656 | tf_op jit(solution)/shard_map/ppermute | solution.py:515
  58.6 13.0 %collective-permute-start.18 = (bf16[192,1024]{1,0:T(8,128)(2,1)S(1)}, bf16[192,1024]{1,0:T(8,128)(2,1)S(1)}, u32[]{:S(2)}, u32[]{:S(2)}) collective-permute-start(bf16[192,1024]{1,0:T(8,128)(2,1)S(1)} %get-tuple-element.140), channel_id=1, source_target_pairs={{0,4},{1,5},{2,6},{3,7},{4,8},{5,9},{6,10},{7,11},{8,12},{9,13},{1... | collective-permute-start | bytes 1179656 | tf_op jit(solution)/shard_map/ppermute | solution.py:515
  60.6 10.9 %collective-permute-start.19 = (bf16[192,1024]{1,0:T(8,128)(2,1)S(1)}, bf16[192,1024]{1,0:T(8,128)(2,1)S(1)}, u32[]{:S(2)}, u32[]{:S(2)}) collective-permute-start(bf16[192,1024]{1,0:T(8,128)(2,1)S(1)} %get-tuple-element.141), channel_id=1, source_target_pairs={{0,2},{1,3},{2,0},{3,1},{4,6},{5,7},{6,4},{7,5},{8,10},{9,11},{10,... | collective-permute-start | bytes 1179656 | tf_op jit(solution)/shard_map/ppermute | solution.py:515
  71.6 16.0 %collective-permute-start.26 = (bf16[1152,1024]{1,0:T(8,128)(2,1)S(1)}, bf16[1152,1024]{1,0:T(8,128)(2,1)S(1)}, u32[]{:S(2)}, u32[]{:S(2)}) collective-permute-start(bf16[1152,1024]{1,0:T(8,128)(2,1)S(1)} %get-tuple-element.174), channel_id=1, source_target_pairs={{0,1},{1,0},{2,3},{3,2},{4,5},{5,4},{6,7},{7,6},{8,9},{9,8},{10,11... | collective-permute-start | bytes 7077896 | tf_op jit(solution)/shard_map/ppermute | solution.py:515
  71.6 25.2 %collective-permute-start.31 = (bf16[1152,768]{1,0:T(8,128)(2,1)S(1)}, bf16[1152,768]{1,0:T(8,128)(2,1)S(1)}, u32[]{:S(2)}, u32[]{:S(2)}) collective-permute-start(bf16[1152,768]{1,0:T(8,128)(2,1)S(1)} %get-tuple-element.184), channel_id=1, source_target_pairs={{0,1},{1,0},{2,3},{3,2},{4,5},{5,4},{6,7},{7,6},{8,9},{9,8},{10,11... | collective-permute-start | bytes 5308424 | tf_op jit(solution)/shard_map/ppermute | solution.py:515
  72.2 7.8 %collective-permute-start.23 = (bf16[192,512]{1,0:T(8,128)(2,1)S(1)}, bf16[192,512]{1,0:T(8,128)(2,1)S(1)}, u32[]{:S(2)}, u32[]{:S(2)}) collective-permute-start(bf16[192,512]{1,0:T(8,128)(2,1)S(1)} %get-tuple-element.170), channel_id=1, source_target_pairs={{0,2},{1,3},{2,0},{3,1},{4,6},{5,7},{6,4},{7,5},{8,10},{9,11},{10,... | collective-permute-start | bytes 589832 | tf_op jit(solution)/shard_map/ppermute | solution.py:515
  73.7 13.8 %collective-permute-start.25 = (bf16[192,512]{1,0:T(8,128)(2,1)S(1)}, bf16[192,512]{1,0:T(8,128)(2,1)S(1)}, u32[]{:S(2)}, u32[]{:S(2)}) collective-permute-start(bf16[192,512]{1,0:T(8,128)(2,1)S(1)} %get-tuple-element.171), channel_id=1, source_target_pairs={{0,2},{1,3},{2,0},{3,1},{4,6},{5,7},{6,4},{7,5},{8,10},{9,11},{10,... | collective-permute-start | bytes 589832 | tf_op jit(solution)/shard_map/ppermute | solution.py:515
  80.1 9.6 %collective-permute-start.24 = (bf16[192,512]{1,0:T(8,128)(2,1)S(1)}, bf16[192,512]{1,0:T(8,128)(2,1)S(1)}, u32[]{:S(2)}, u32[]{:S(2)}) collective-permute-start(bf16[192,512]{1,0:T(8,128)(2,1)S(1)} %add.4), channel_id=1, source_target_pairs={{0,4},{1,5},{2,6},{3,7},{4,8},{5,9},{6,10},{7,11},{8,12},{9,13},{1... | collective-permute-start | bytes 589832 | tf_op jit(solution)/shard_map/ppermute | solution.py:515
  87.6 7.5 %collective-permute-start.29 = (bf16[192,512]{1,0:T(8,128)(2,1)S(1)}, bf16[192,512]{1,0:T(8,128)(2,1)S(1)}, u32[]{:S(2)}, u32[]{:S(2)}) collective-permute-start(bf16[192,512]{1,0:T(8,128)(2,1)S(1)} %add.6), channel_id=1, source_target_pairs={{0,4},{1,5},{2,6},{3,7},{4,8},{5,9},{6,10},{7,11},{8,12},{9,13},{1... | collective-permute-start | bytes 589832 | tf_op jit(solution)/shard_map/ppermute | solution.py:515
  88.8 7.5 %collective-permute-start.22 = (bf16[192,512]{1,0:T(8,128)(2,1)S(1)}, bf16[192,512]{1,0:T(8,128)(2,1)S(1)}, u32[]{:S(2)}, u32[]{:S(2)}) collective-permute-start(bf16[192,512]{1,0:T(8,128)(2,1)S(1)} %get-tuple-element.167), channel_id=1, source_target_pairs={{0,2},{1,3},{2,0},{3,1},{4,6},{5,7},{6,4},{7,5},{8,10},{9,11},{10,... | collective-permute-start | bytes 589832 | tf_op jit(solution)/shard_map/ppermute | solution.py:515
  95.2 9.0 %collective-permute-start.30 = (bf16[192,512]{1,0:T(8,128)(2,1)S(1)}, bf16[192,512]{1,0:T(8,128)(2,1)S(1)}, u32[]{:S(2)}, u32[]{:S(2)}) collective-permute-start(bf16[192,512]{1,0:T(8,128)(2,1)S(1)} %add.7), channel_id=1, source_target_pairs={{0,4},{1,5},{2,6},{3,7},{4,8},{5,9},{6,10},{7,11},{8,12},{9,13},{1... | collective-permute-start | bytes 589832 | tf_op jit(solution)/shard_map/ppermute | solution.py:515
  96.4 10.0 %collective-permute-start.27 = (bf16[192,512]{1,0:T(8,128)(2,1)S(1)}, bf16[192,512]{1,0:T(8,128)(2,1)S(1)}, u32[]{:S(2)}, u32[]{:S(2)}) collective-permute-start(bf16[192,512]{1,0:T(8,128)(2,1)S(1)} %add.5), channel_id=1, source_target_pairs={{0,4},{1,5},{2,6},{3,7},{4,8},{5,9},{6,10},{7,11},{8,12},{9,13},{1... | collective-permute-start | bytes 589832 | tf_op jit(solution)/shard_map/ppermute | solution.py:515
  (14 other events, 76.1 us)

commit v12 on v11

--- a/solution.py
+++ b/solution.py
@@ -581,7 +581,7 @@
     b3 = [send(left, to_x), send(right, to_x)]
     late = send(gps[1], to_core)
     part = received_own(hid, recs[0])
-    b2[1], part, rec_c = together(b2[1], part, rec_c)
+    b2[0], _, part, rec_c = together(b2[0], left, part, rec_c)
     w2 = [ring(add([t_r2, w1, b2[k]], k)) for k in range(2)]
     part = received_other(part, hid_c, rec_c)
     w2[0], part = together(w2[0], part)

time: 108 us -> 105 us (0.972)
  waiting for transfers between devices: 23.7 us -> 15.8 us
  starting transfers between devices: 31.2 us -> 36.2 us
    ppermute x25, waiting for transfers between devices: 14.1 us -> 6.26 us  [send(): return lax.ppermute(v, 'expert', perm)]
    ppermute x25, starting transfers between devices: 22.8 us -> 27.8 us  [send(): return lax.ppermute(v, 'expert', perm)]
  transfers between devices with their start and end apart: 33 -> 33, of which waited for: 14 -> 11; matrix products, arithmetic and copies ran while one was open for 0% -> 0% of each run, Pallas kernels for 46% -> 47%
where the time goes in v12:
time: 105 us; the launch traced here: 104 us
  Pallas kernels  50.4 us (48%)
  starting transfers between devices  36.2 us (34%)
  waiting for transfers between devices  15.8 us (15%)
    ppermute x25, starting transfers between devices, send(): return lax.ppermute(v, 'expert', perm)  27.8 us
    pallas_call x5, Pallas kernels, combine(): pl.pallas_call(functools.partial(combine_kernel, chunk, cap, len(old), la...  14.2 us
    pallas_call x5, Pallas kernels, dispatch(): pl.pallas_call(functools.partial(dispatch_kernel, chunk, cap, len(old) //...  13.5 us
    ppermute x8, waiting for transfers between devices, exchange(): return lax.ppermute(v, 'dp', [(0, 1), (1, 0)])  9.57 us
    ppermute x8, starting transfers between devices, exchange(): return lax.ppermute(v, 'dp', [(0, 1), (1, 0)])  8.41 us
    ppermute x25, waiting for transfers between devices, send(): return lax.ppermute(v, 'expert', perm)  6.26 us
    pallas_call x1, Pallas kernels, inputs_part(): pl.pallas_call(functools.partial(inputs_kernel, cap, last), out_shape=jax...  5.66 us
    pallas_call x2, Pallas kernels, hidden(): pl.pallas_call(functools.partial(hidden_kernel, cap, k), out_shape=jax.Sh...  4.73 us
  transfers between devices with their start and end apart: 33, of which 11 were waited for; matrix products, arithmetic and copies ran while one was open for 0% of the time, Pallas kernels for 47%

profile of v12, /device:TPU:0, one launch (start us, length us, event | category | flops | bytes accessed | tf_op | source)
XLA Modules:
  0.0 104.4 jit_solution(6908493412076816762)
XLA Ops:
  3.4 2.7 %collective-permute-start = (bf16[200,1024]{1,0:T(8,128)(2,1)}, bf16[200,1024]{1,0:T(8,128)(2,1)}, u32[]{:S(2)}, u32[]{:S(2)}) collective-permute-start(bf16[200,1024]{1,0:T(8,128)(2,1)} %pack.1.refs_0_), channel_id=1, source_target_pairs={{0,4},{1,5},{2,6},{3,7},{4,8},{5,9},{6,10},{7,11},{8,12},{9,13},{1... | collective-permute-start | bytes 1228808 | tf_op jit(solution)/shard_map/ppermute | solution.py:515
  7.6 2.2 %hidden.2.hid = bf16[384,1152]{1,0:T(8,128)(2,1)S(1)} custom-call(s32[1]{0:T(128)} %bitcast.2.here, bf16[2304,384]{1,0:T(8,128)(2,1)} %bitcast.10, bf16[2304,384]{1,0:T(8,128)(2,1)} %bitcast.18), custom_call_target="tpu_custom_call" | custom-call | flops 1048576 | bytes 16384 | tf_op jit(solution)/shard_map/hidden/pallas_call | solution.py:347
  9.9 3.9 %turn.1.inputs = bf16[1024,2304]{1,0:T(8,128)(2,1)S(1)} custom-call(s32[1]{0:T(128)} %bitcast.2.here, bf16[2304,1024]{1,0:T(8,128)(2,1)} %bitcast.33), custom_call_target="tpu_custom_call" | custom-call | flops 1048576 | bytes 16384 | tf_op jit(solution)/shard_map/turn/pallas_call | solution.py:371
  14.9 2.5 %dispatch.5 = (bf16[1152,1024]{1,0:T(8,128)(2,1)S(1)}, bf16[1152,1024]{1,0:T(8,128)(2,1)S(1)}, f32[288,384]{1,0:T(8,128)S(1)}, bf16[288,384]{1,0:T(8,128)(2,1)S(1)}, f32[8,192]{1,0:T(8,128)S(1)}) custom-call(s32[1]{0:T(128)} %bitcast.2.here, bf16[200,1024]{1,0:T(8,128)(2,1)} %pack.1.refs_0_, bf16[384,1024]{1,0:T(8,128)(2,1)S(1)} %bitcast.26, ...), custom_call_target="tpu_custom_call" | custom-call | flops 1048576 | bytes 16384 | tf_op jit(solution)/shard_map/dispatch/pallas_call | solution.py:162
  22.7 3.1 %dispatch.6 = (bf16[1152,1024]{1,0:T(8,128)(2,1)S(1)}, bf16[1152,1024]{1,0:T(8,128)(2,1)S(1)}, f32[576,384]{1,0:T(8,128)S(1)}, bf16[288,384]{1,0:T(8,128)(2,1)S(...) custom-call(s32[1]{0:T(128)} %bitcast.2.here, ...), custom_call_target="tpu_custom_call", output_to_operand_aliasing={{0}: (5, {}), {1}: (6, {})} | custom-call | flops 1048576 | bytes 16384 | tf_op jit(solution)/shard_map/dispatch/pallas_call | solution.py:162
  26.3 2.5 %hidden.3.hid = bf16[384,1152]{1,0:T(8,128)(2,1)S(1)} custom-call(s32[1]{0:T(128)} %bitcast.2.here, bf16[2304,384]{1,0:T(8,128)(2,1)} %bitcast.11, bf16[2304,384]{1,0:T(8,128)(2,1)} %bitcast.19), custom_call_target="tpu_custom_call" | custom-call | flops 1048576 | bytes 16384 | tf_op jit(solution)/shard_map/hidden/pallas_call | solution.py:347
  28.9 2.3 %combine.5 = (bf16[1152,768]{1,0:T(8,128)(2,1)S(1)}, bf16[1152,768]{1,0:T(8,128)(2,1)S(1)}, bf16[192,1024]{1,0:T(8,128)(2,1)S(1)}) custom-call(s32[1]{0:T(128)} %bitcast.2.here, f32[288,384]{1,0:T(8,128)S(1)} %get-tuple-element.102.share, bf16[288,384]{1,0:T(8,128)(2,1)S(1)} %collective-permute-done.8.refs_0_, f32[8,192]{1,0:T(8,128)S(1)} %get-tuple-element.104.refs_1_, ...), custom_call_target="tpu_custom_call" | custom-call | flops 1048576 | bytes 16384 | tf_op jit(solution)/shard_map/combine/pallas_call | solution.py:231
  36.7 2.8 %dispatch.7 = (bf16[1152,1024]{1,0:T(8,128)(2,1)S(1)}, bf16[1152,1024]{1,0:T(8,128)(2,1)S(1)}, f32[576,384]{1,0:T(8,128)S(1)}, bf16[288,384]{1,0:T(8,128)(2,1)S(...) custom-call(s32[1]{0:T(128)} %bitcast.2.here, ...), custom_call_target="tpu_custom_call", output_to_operand_aliasing={{0}: (5, {}), {1}: (6, {})} | custom-call | flops 1048576 | bytes 16384 | tf_op jit(solution)/shard_map/dispatch/pallas_call | solution.py:162
  42.0 3.3 %combine.6 = (bf16[1152,768]{1,0:T(8,128)(2,1)S(1)}, bf16[1152,768]{1,0:T(8,128)(2,1)S(1)}, bf16[192,1024]{1,0:T(8,128)(2,1)S(1)}, bf16[192,1024]{1,0:T(8,128)(2,1)S(1)}) custom-call(s32[1]{0:T(128)} %bitcast.2.here, f32[576,384]{1,0:T(8,128)S(1)} %get-tuple-element.116.share, ...), custom_call_target="tpu_custom_call", output_to_operand_aliasing={{0}: (11, {}), {1}: (12, {})} | custom-call | flops 1048576 | bytes 16384 | tf_op jit(solution)/shard_map/combine/pallas_call | solution.py:231
  49.7 2.8 %dispatch.8 = (bf16[1152,1024]{1,0:T(8,128)(2,1)S(1)}, bf16[1152,1024]{1,0:T(8,128)(2,1)S(1)}, f32[576,384]{1,0:T(8,128)S(1)}, bf16[288,384]{1,0:T(8,128)(2,1)S(...) custom-call(s32[1]{0:T(128)} %bitcast.2.here, ...), custom_call_target="tpu_custom_call", output_to_operand_aliasing={{0}: (5, {}), {1}: (6, {})} | custom-call | flops 1048576 | bytes 16384 | tf_op jit(solution)/shard_map/dispatch/pallas_call | solution.py:162
  52.7 2.4 %collective-permute-done.17.refs_1_ = bf16[288,384]{1,0:T(8,128)(2,1)S(1)} collective-permute-done((bf16[288,384]{1,0:T(8,128)(2,1)S(1)}, bf16[288,384]{1,0:T(8,128)(2,1)S(1)}, u32[]{:S(2)}, u32[]{:S(2)}) %collective-permute-start.17) | collective-permute-done | bytes 221216 | tf_op jit(solution)/shard_map/ppermute | solution.py:537
  55.1 3.3 %combine.7 = (bf16[1152,768]{1,0:T(8,128)(2,1)S(1)}, bf16[1152,768]{1,0:T(8,128)(2,1)S(1)}, bf16[192,1024]{1,0:T(8,128)(2,1)S(1)}, bf16[192,1024]{1,0:T(8,128)(2,1)S(1)}) custom-call(s32[1]{0:T(128)} %bitcast.2.here, f32[576,384]{1,0:T(8,128)S(1)} %get-tuple-element.132.share, ...), custom_call_target="tpu_custom_call", output_to_operand_aliasing={{0}: (11, {}), {1}: (12, {})} | custom-call | flops 1048576 | bytes 16384 | tf_op jit(solution)/shard_map/combine/pallas_call | solution.py:231
  58.6 2.1 %collective-permute-start.18 = (bf16[192,1024]{1,0:T(8,128)(2,1)S(1)}, bf16[192,1024]{1,0:T(8,128)(2,1)S(1)}, u32[]{:S(2)}, u32[]{:S(2)}) collective-permute-start(bf16[192,1024]{1,0:T(8,128)(2,1)S(1)} %get-tuple-element.140), channel_id=1, source_target_pairs={{0,4},{1,5},{2,6},{3,7},{4,8},{5,9},{6,10},{7,11},{8,12},{9,13},{1... | collective-permute-start | bytes 1179656 | tf_op jit(solution)/shard_map/ppermute | solution.py:515
  61.2 2.1 %collective-permute-start.21 = (bf16[288,384]{1,0:T(8,128)(2,1)S(1)}, bf16[288,384]{1,0:T(8,128)(2,1)S(1)}, u32[]{:S(2)}, u32[]{:S(2)}) collective-permute-start(bf16[288,384]{1,0:T(8,128)(2,1)S(1)} %get-tuple-element.148), channel_id=1, source_target_pairs={{0,16},{16,0},{1,17},{17,1},{2,18},{18,2},{3,19},{19,3},{4,20},{20... | collective-permute-start | bytes 663560 | tf_op jit(solution)/shard_map/ppermute | solution.py:537
  63.2 2.3 %dispatch.9 = (bf16[1152,1024]{1,0:T(8,128)(2,1)S(1)}, bf16[1152,1024]{1,0:T(8,128)(2,1)S(1)}, f32[288,384]{1,0:T(8,128)S(1)}, bf16[288,384]{1,0:T(8,128)(2,1)S(1)}, f32[8,192]{1,0:T(8,128)S(1)}) custom-call(s32[1]{0:T(128)} %bitcast.2.here, bf16[200,1024]{1,0:T(8,128)(2,1)S(1)} %collective-permute-done.14.refs_0_, ...), custom_call_target="tpu_custom_call", output_to_operand_aliasing={{0}: (4, {}), {1}: (5, {})} | custom-call | flops 1048576 | bytes 16384 | tf_op jit(solution)/shard_map/dispatch/pallas_call | solution.py:162
  65.6 2.5 %collective-permute-done.21.refs_1_ = bf16[288,384]{1,0:T(8,128)(2,1)S(1)} collective-permute-done((bf16[288,384]{1,0:T(8,128)(2,1)S(1)}, bf16[288,384]{1,0:T(8,128)(2,1)S(1)}, u32[]{:S(2)}, u32[]{:S(2)}) %collective-permute-start.21) | collective-permute-done | bytes 221216 | tf_op jit(solution)/shard_map/ppermute | solution.py:537
  68.1 3.3 %combine.8 = (bf16[1152,768]{1,0:T(8,128)(2,1)S(1)}, bf16[1152,768]{1,0:T(8,128)(2,1)S(1)}, bf16[192,1024]{1,0:T(8,128)(2,1)S(1)}, bf16[192,1024]{1,0:T(8,128)(2,1)S(1)}) custom-call(s32[1]{0:T(128)} %bitcast.2.here, f32[576,384]{1,0:T(8,128)S(1)} %get-tuple-element.146.share, ...), custom_call_target="tpu_custom_call", output_to_operand_aliasing={{0}: (11, {}), {1}: (12, {})} | custom-call | flops 1048576 | bytes 16384 | tf_op jit(solution)/shard_map/combine/pallas_call | solution.py:231
  77.9 2.1 %collective-permute-done.28.refs_2_ = bf16[192,512]{1,0:T(8,128)(2,1)S(1)} collective-permute-done((bf16[192,512]{1,0:T(8,128)(2,1)S(1)}, bf16[192,512]{1,0:T(8,128)(2,1)S(1)}, u32[]{:S(2)}, u32[]{:S(2)}) %collective-permute-start.28) | collective-permute-done | bytes 196640 | tf_op jit(solution)/shard_map/ppermute | solution.py:515
  80.1 2.9 %collective-permute-start.29 = (bf16[192,512]{1,0:T(8,128)(2,1)S(1)}, bf16[192,512]{1,0:T(8,128)(2,1)S(1)}, u32[]{:S(2)}, u32[]{:S(2)}) collective-permute-start(bf16[192,512]{1,0:T(8,128)(2,1)S(1)} %add.6), channel_id=1, source_target_pairs={{0,4},{1,5},{2,6},{3,7},{4,8},{5,9},{6,10},{7,11},{8,12},{9,13},{1... | collective-permute-start | bytes 589832 | tf_op jit(solution)/shard_map/ppermute | solution.py:515
  82.9 2.1 %received_own.1.part = f32[384,1024]{1,0:T(8,128)S(1)} custom-call(bf16[384,1152]{1,0:T(8,128)(2,1)S(1)} %hidden.2.hid, bf16[1152,1024]{1,0:T(8,128)(2,1)S(1)} %get-tuple-element.172.own), custom_call_target="tpu_custom_call" | custom-call | flops 1048576 | bytes 16384 | tf_op jit(solution)/shard_map/received_own/pallas_call | solution.py:430
  87.7 3.7 %collective-permute-start.30 = (bf16[192,512]{1,0:T(8,128)(2,1)S(1)}, bf16[192,512]{1,0:T(8,128)(2,1)S(1)}, u32[]{:S(2)}, u32[]{:S(2)}) collective-permute-start(bf16[192,512]{1,0:T(8,128)(2,1)S(1)} %add.7), channel_id=1, source_target_pairs={{0,4},{1,5},{2,6},{3,7},{4,8},{5,9},{6,10},{7,11},{8,12},{9,13},{1... | collective-permute-start | bytes 589832 | tf_op jit(solution)/shard_map/ppermute | solution.py:515
  91.4 3.1 %received_other.1.old = bf16[1,1024,1152]{2,1,0:T(8,128)(2,1)} custom-call(f32[384,1024]{1,0:T(8,128)S(1)} %received_own.1.part, bf16[384,1152]{1,0:T(8,128)(2,1)S(1)} %hidden.3.hid, bf16[1152,1024]{1,0:T(8,128)(2,1)S(1)} %collective-permute-done.24.other), custom_call_target="tpu_custom_call" | custom-call | flops 1048576 | bytes 16384 | tf_op jit(solution)/shard_map/received_other/pallas_call | solution.py:446
  95.0 5.7 %inputs_part.1 = bf16[1,1024,1152]{2,1,0:T(8,128)(2,1)} custom-call(s32[1]{0:T(128)} %bitcast.2.here, bf16[1,1024,1152]{2,1,0:T(8,128)(2,1)} %received_other.1.old, bf16[1024,2304]{1,0:T(8,128)(2,1)S(1)} %turn.1.inputs, bf16[1152,768]{1,0:T(8,128)(2,1)S(1)} %get-tuple-element.183.own, ...), custom_call_target="tpu_custom_call", output_to_operand_aliasing={{}: (1, {})} | custom-call | flops 1048576 | bytes 16384 | tf_op jit(solution)/shard_map/inputs_part/pallas_call | solution.py:483
  100.7 2.8 %collective-permute-done.26.left = bf16[192,512]{1,0:T(8,128)(2,1)S(1)} collective-permute-done((bf16[192,512]{1,0:T(8,128)(2,1)S(1)}, bf16[192,512]{1,0:T(8,128)(2,1)S(1)}, u32[]{:S(2)}, u32[]{:S(2)}) %collective-permute-start.26) | collective-permute-done | bytes 196640 | tf_op jit(solution)/shard_map/ppermute | solution.py:515
  (76 shorter events, 35.0 us)
Async XLA Ops:
  0.6 17.9 %collective-permute-start.3 = (bf16[2304,384]{1,0:T(8,128)(2,1)}, bf16[2304,384]{1,0:T(8,128)(2,1)S(1)}, u32[]{:S(2)}, u32[]{:S(2)}) collective-permute-start(bf16[2304,384]{1,0:T(8,128)(2,1)} %bitcast.9), channel_id=1, source_target_pairs={{0,1},{1,0},{2,3},{3,2},{4,5},{5,4},{6,7},{7,6},{8,9},{9,8},{10,11... | collective-permute-start | bytes 5308424 | tf_op jit(solution)/shard_map/ppermute | solution.py:515
  1.1 17.4 %collective-permute-start.4 = (bf16[2304,384]{1,0:T(8,128)(2,1)}, bf16[2304,384]{1,0:T(8,128)(2,1)S(1)}, u32[]{:S(2)}, u32[]{:S(2)}) collective-permute-start(bf16[2304,384]{1,0:T(8,128)(2,1)} %bitcast.17), channel_id=1, source_target_pairs={{0,1},{1,0},{2,3},{3,2},{4,5},{5,4},{6,7},{7,6},{8,9},{9,8},{10,11... | collective-permute-start | bytes 5308424 | tf_op jit(solution)/shard_map/ppermute | solution.py:515
  1.2 12.7 %collective-permute-start.2 = (bf16[384,1024]{1,0:T(8,128)(2,1)}, bf16[384,1024]{1,0:T(8,128)(2,1)}, u32[]{:S(2)}, u32[]{:S(2)}) collective-permute-start(bf16[384,1024]{1,0:T(8,128)(2,1)} %bitcast.25), channel_id=1, source_target_pairs={{0,1},{1,0},{2,3},{3,2},{4,5},{5,4},{6,7},{7,6},{8,9},{9,8},{10,11... | collective-permute-start | bytes 2359304 | tf_op jit(solution)/shard_map/ppermute | solution.py:515
  3.4 15.1 %collective-permute-start = (bf16[200,1024]{1,0:T(8,128)(2,1)}, bf16[200,1024]{1,0:T(8,128)(2,1)}, u32[]{:S(2)}, u32[]{:S(2)}) collective-permute-start(bf16[200,1024]{1,0:T(8,128)(2,1)} %pack.1.refs_0_), channel_id=1, source_target_pairs={{0,4},{1,5},{2,6},{3,7},{4,8},{5,9},{6,10},{7,11},{8,12},{9,13},{1... | collective-permute-start | bytes 1228808 | tf_op jit(solution)/shard_map/ppermute | solution.py:515
  6.1 12.4 %collective-permute-start.1 = (bf16[200,1024]{1,0:T(8,128)(2,1)}, bf16[200,1024]{1,0:T(8,128)(2,1)}, u32[]{:S(2)}, u32[]{:S(2)}) collective-permute-start(bf16[200,1024]{1,0:T(8,128)(2,1)} %pack.1.refs_0_), channel_id=1, source_target_pairs={{0,2},{1,3},{2,0},{3,1},{4,6},{5,7},{6,4},{7,5},{8,10},{9,11},{10,... | collective-permute-start | bytes 1228808 | tf_op jit(solution)/shard_map/ppermute | solution.py:515
  18.6 10.3 %collective-permute-start.9 = (bf16[1024,768]{1,0:T(8,128)(2,1)S(1)}, bf16[1024,768]{1,0:T(8,128)(2,1)S(1)}, u32[]{:S(2)}, u32[]{:S(2)}) collective-permute-start(bf16[1024,768]{1,0:T(8,128)(2,1)S(1)} %join.1.refs_6_.refs_7_), channel_id=1, source_target_pairs={{0,1},{1,0},{2,3},{3,2},{4,5},{5,4},{6,7},{7,6},{8,9},{9,8},{10,11... | collective-permute-start | bytes 4718600 | tf_op jit(solution)/shard_map/ppermute | solution.py:515
  18.6 14.5 %collective-permute-start.5 = (bf16[200,1024]{1,0:T(8,128)(2,1)}, bf16[200,1024]{1,0:T(8,128)(2,1)S(1)}, u32[]{:S(2)}, u32[]{:S(2)}) collective-permute-start(bf16[200,1024]{1,0:T(8,128)(2,1)} %collective-permute-done.refs_1_), channel_id=1, source_target_pairs={{0,4},{1,5},{2,6},{3,7},{4,8},{5,9},{6,10},{7,11},{8,12},{9,13},{1... | collective-permute-start | bytes 1228808 | tf_op jit(solution)/shard_map/ppermute | solution.py:515
  19.6 13.5 %collective-permute-start.6 = (bf16[200,1024]{1,0:T(8,128)(2,1)}, bf16[200,1024]{1,0:T(8,128)(2,1)S(1)}, u32[]{:S(2)}, u32[]{:S(2)}) collective-permute-start(bf16[200,1024]{1,0:T(8,128)(2,1)} %collective-permute-done.refs_1_), channel_id=1, source_target_pairs={{0,2},{1,3},{2,0},{3,1},{4,6},{5,7},{6,4},{7,5},{8,10},{9,11},{10,... | collective-permute-start | bytes 1228808 | tf_op jit(solution)/shard_map/ppermute | solution.py:515
  21.1 7.7 %collective-permute-start.8 = (bf16[288,384]{1,0:T(8,128)(2,1)S(1)}, bf16[288,384]{1,0:T(8,128)(2,1)S(1)}, u32[]{:S(2)}, u32[]{:S(2)}) collective-permute-start(bf16[288,384]{1,0:T(8,128)(2,1)S(1)} %get-tuple-element.103), channel_id=1, source_target_pairs={{0,16},{16,0},{1,17},{17,1},{2,18},{18,2},{3,19},{19,3},{4,20},{20... | collective-permute-start | bytes 663560 | tf_op jit(solution)/shard_map/ppermute | solution.py:537
  33.1 12.8 %collective-permute-start.10 = (bf16[200,1024]{1,0:T(8,128)(2,1)S(1)}, bf16[200,1024]{1,0:T(8,128)(2,1)S(1)}, u32[]{:S(2)}, u32[]{:S(2)}) collective-permute-start(bf16[200,1024]{1,0:T(8,128)(2,1)S(1)} %collective-permute-done.5.refs_1_), channel_id=1, source_target_pairs={{0,4},{1,5},{2,6},{3,7},{4,8},{5,9},{6,10},{7,11},{8,12},{9,13},{1... | collective-permute-start | bytes 1228808 | tf_op jit(solution)/shard_map/ppermute | solution.py:515
  34.7 11.2 %collective-permute-start.11 = (bf16[200,1024]{1,0:T(8,128)(2,1)S(1)}, bf16[200,1024]{1,0:T(8,128)(2,1)S(1)}, u32[]{:S(2)}, u32[]{:S(2)}) collective-permute-start(bf16[200,1024]{1,0:T(8,128)(2,1)S(1)} %collective-permute-done.5.refs_1_), channel_id=1, source_target_pairs={{0,2},{1,3},{2,0},{3,1},{4,6},{5,7},{6,4},{7,5},{8,10},{9,11},{10,... | collective-permute-start | bytes 1228808 | tf_op jit(solution)/shard_map/ppermute | solution.py:515
  45.9 12.7 %collective-permute-start.14 = (bf16[200,1024]{1,0:T(8,128)(2,1)S(1)}, bf16[200,1024]{1,0:T(8,128)(2,1)S(1)}, u32[]{:S(2)}, u32[]{:S(2)}) collective-permute-start(bf16[200,1024]{1,0:T(8,128)(2,1)S(1)} %collective-permute-done.10.refs_1_), channel_id=1, source_target_pairs={{0,2},{1,3},{2,0},{3,1},{4,6},{5,7},{6,4},{7,5},{8,10},{9,11},{10,... | collective-permute-start | bytes 1228808 | tf_op jit(solution)/shard_map/ppermute | solution.py:515
  47.4 11.2 %collective-permute-start.15 = (bf16[192,1024]{1,0:T(8,128)(2,1)S(1)}, bf16[192,1024]{1,0:T(8,128)(2,1)S(1)}, u32[]{:S(2)}, u32[]{:S(2)}) collective-permute-start(bf16[192,1024]{1,0:T(8,128)(2,1)S(1)} %get-tuple-element.125), channel_id=1, source_target_pairs={{0,4},{1,5},{2,6},{3,7},{4,8},{5,9},{6,10},{7,11},{8,12},{9,13},{1... | collective-permute-start | bytes 1179656 | tf_op jit(solution)/shard_map/ppermute | solution.py:515
  58.6 13.0 %collective-permute-start.18 = (bf16[192,1024]{1,0:T(8,128)(2,1)S(1)}, bf16[192,1024]{1,0:T(8,128)(2,1)S(1)}, u32[]{:S(2)}, u32[]{:S(2)}) collective-permute-start(bf16[192,1024]{1,0:T(8,128)(2,1)S(1)} %get-tuple-element.140), channel_id=1, source_target_pairs={{0,4},{1,5},{2,6},{3,7},{4,8},{5,9},{6,10},{7,11},{8,12},{9,13},{1... | collective-permute-start | bytes 1179656 | tf_op jit(solution)/shard_map/ppermute | solution.py:515
  60.6 10.9 %collective-permute-start.19 = (bf16[192,1024]{1,0:T(8,128)(2,1)S(1)}, bf16[192,1024]{1,0:T(8,128)(2,1)S(1)}, u32[]{:S(2)}, u32[]{:S(2)}) collective-permute-start(bf16[192,1024]{1,0:T(8,128)(2,1)S(1)} %get-tuple-element.141), channel_id=1, source_target_pairs={{0,2},{1,3},{2,0},{3,1},{4,6},{5,7},{6,4},{7,5},{8,10},{9,11},{10,... | collective-permute-start | bytes 1179656 | tf_op jit(solution)/shard_map/ppermute | solution.py:515
  71.6 13.5 %collective-permute-start.24 = (bf16[1152,1024]{1,0:T(8,128)(2,1)S(1)}, bf16[1152,1024]{1,0:T(8,128)(2,1)S(1)}, u32[]{:S(2)}, u32[]{:S(2)}) collective-permute-start(bf16[1152,1024]{1,0:T(8,128)(2,1)S(1)} %get-tuple-element.173), channel_id=1, source_target_pairs={{0,1},{1,0},{2,3},{3,2},{4,5},{5,4},{6,7},{7,6},{8,9},{9,8},{10,11... | collective-permute-start | bytes 7077896 | tf_op jit(solution)/shard_map/ppermute | solution.py:515
  71.6 23.4 %collective-permute-start.31 = (bf16[1152,768]{1,0:T(8,128)(2,1)S(1)}, bf16[1152,768]{1,0:T(8,128)(2,1)S(1)}, u32[]{:S(2)}, u32[]{:S(2)}) collective-permute-start(bf16[1152,768]{1,0:T(8,128)(2,1)S(1)} %get-tuple-element.184), channel_id=1, source_target_pairs={{0,1},{1,0},{2,3},{3,2},{4,5},{5,4},{6,7},{7,6},{8,9},{9,8},{10,11... | collective-permute-start | bytes 5308424 | tf_op jit(solution)/shard_map/ppermute | solution.py:515
  72.2 7.8 %collective-permute-start.28 = (bf16[192,512]{1,0:T(8,128)(2,1)S(1)}, bf16[192,512]{1,0:T(8,128)(2,1)S(1)}, u32[]{:S(2)}, u32[]{:S(2)}) collective-permute-start(bf16[192,512]{1,0:T(8,128)(2,1)S(1)} %get-tuple-element.180), channel_id=1, source_target_pairs={{0,2},{1,3},{2,0},{3,1},{4,6},{5,7},{6,4},{7,5},{8,10},{9,11},{10,... | collective-permute-start | bytes 589832 | tf_op jit(solution)/shard_map/ppermute | solution.py:515
  73.7 11.3 %collective-permute-start.23 = (bf16[192,512]{1,0:T(8,128)(2,1)S(1)}, bf16[192,512]{1,0:T(8,128)(2,1)S(1)}, u32[]{:S(2)}, u32[]{:S(2)}) collective-permute-start(bf16[192,512]{1,0:T(8,128)(2,1)S(1)} %get-tuple-element.170), channel_id=1, source_target_pairs={{0,2},{1,3},{2,0},{3,1},{4,6},{5,7},{6,4},{7,5},{8,10},{9,11},{10,... | collective-permute-start | bytes 589832 | tf_op jit(solution)/shard_map/ppermute | solution.py:515
  76.3 11.2 %collective-permute-start.27 = (bf16[192,512]{1,0:T(8,128)(2,1)S(1)}, bf16[192,512]{1,0:T(8,128)(2,1)S(1)}, u32[]{:S(2)}, u32[]{:S(2)}) collective-permute-start(bf16[192,512]{1,0:T(8,128)(2,1)S(1)} %get-tuple-element.179), channel_id=1, source_target_pairs={{0,2},{1,3},{2,0},{3,1},{4,6},{5,7},{6,4},{7,5},{8,10},{9,11},{10,... | collective-permute-start | bytes 589832 | tf_op jit(solution)/shard_map/ppermute | solution.py:515
  80.1 7.5 %collective-permute-start.29 = (bf16[192,512]{1,0:T(8,128)(2,1)S(1)}, bf16[192,512]{1,0:T(8,128)(2,1)S(1)}, u32[]{:S(2)}, u32[]{:S(2)}) collective-permute-start(bf16[192,512]{1,0:T(8,128)(2,1)S(1)} %add.6), channel_id=1, source_target_pairs={{0,4},{1,5},{2,6},{3,7},{4,8},{5,9},{6,10},{7,11},{8,12},{9,13},{1... | collective-permute-start | bytes 589832 | tf_op jit(solution)/shard_map/ppermute | solution.py:515
  85.2 9.3 %collective-permute-start.25 = (bf16[192,512]{1,0:T(8,128)(2,1)S(1)}, bf16[192,512]{1,0:T(8,128)(2,1)S(1)}, u32[]{:S(2)}, u32[]{:S(2)}) collective-permute-start(bf16[192,512]{1,0:T(8,128)(2,1)S(1)} %add.4), channel_id=1, source_target_pairs={{0,4},{1,5},{2,6},{3,7},{4,8},{5,9},{6,10},{7,11},{8,12},{9,13},{1... | collective-permute-start | bytes 589832 | tf_op jit(solution)/shard_map/ppermute | solution.py:515
  87.7 13.0 %collective-permute-start.30 = (bf16[192,512]{1,0:T(8,128)(2,1)S(1)}, bf16[192,512]{1,0:T(8,128)(2,1)S(1)}, u32[]{:S(2)}, u32[]{:S(2)}) collective-permute-start(bf16[192,512]{1,0:T(8,128)(2,1)S(1)} %add.7), channel_id=1, source_target_pairs={{0,4},{1,5},{2,6},{3,7},{4,8},{5,9},{6,10},{7,11},{8,12},{9,13},{1... | collective-permute-start | bytes 589832 | tf_op jit(solution)/shard_map/ppermute | solution.py:515
  94.6 8.9 %collective-permute-start.26 = (bf16[192,512]{1,0:T(8,128)(2,1)S(1)}, bf16[192,512]{1,0:T(8,128)(2,1)S(1)}, u32[]{:S(2)}, u32[]{:S(2)}) collective-permute-start(bf16[192,512]{1,0:T(8,128)(2,1)S(1)} %add.5), channel_id=1, source_target_pairs={{0,4},{1,5},{2,6},{3,7},{4,8},{5,9},{6,10},{7,11},{8,12},{9,13},{1... | collective-permute-start | bytes 589832 | tf_op jit(solution)/shard_map/ppermute | solution.py:515
  (14 other events, 76.8 us)

commit v13 on v12

--- a/solution.py
+++ b/solution.py
@@ -418,81 +418,80 @@
     out[...] = jnp.dot(hid[...], own[...], preferred_element_type=f32)
 
 
-def received_other_kernel(part, hid, other, out):
-    total = part[...] + jnp.dot(hid[...], other[...], preferred_element_type=f32)
-    out[0] = (total * loss_scale).astype(bf16).T
-
-
 def received_own(hid, own):
-    h = hid.shape[0]
-    rows, d = own.shape
-    tile = 256
     return pl.pallas_call(
         received_own_kernel,
-        out_shape=jax.ShapeDtypeStruct((h, d), f32),
-        grid=(d // tile,),
-        in_specs=[pl.BlockSpec((h, rows), lambda i: (0, 0)), pl.BlockSpec((rows, tile), lambda i: (0, i))],
-        out_specs=pl.BlockSpec((h, tile), lambda i: (0, i)),
+        out_shape=jax.ShapeDtypeStruct((hid.shape[0], own.shape[1]), f32),
+        in_specs=[on_chip] * 2,
+        out_specs=on_chip,
         cost_estimate=light,
         compiler_params=params(16),
         name="received_own",
     )(hid, own)
 
 
+def received_other_kernel(part, hid, other, out, tiles, sems):
+    count, tile, h = tiles.shape
+    copies = []
+    for i in range(count):
+        at = slice(i * tile, (i + 1) * tile)
+        total = part[:, at] + jnp.dot(hid[...], other[:, at], preferred_element_type=f32)
+        tiles[i] = (total * loss_scale).astype(bf16).T
+        copies.append(pltpu.make_async_copy(tiles.at[i], out.at[0, at, pl.ds(2 * h, h)], sems.at[i]))
+        copies[-1].start()
+    for c in copies:
+        c.wait()
+
+
 def received_other(part, hid, other):
     h, d = part.shape
-    rows = other.shape[0]
     tile = 256
     return pl.pallas_call(
         received_other_kernel,
         out_shape=jax.ShapeDtypeStruct((1, d, 3 * h), bf16),
-        grid=(d // tile,),
-        in_specs=[
-            pl.BlockSpec((h, tile), lambda i: (0, i)),
-            pl.BlockSpec((h, rows), lambda i: (0, 0)),
-            pl.BlockSpec((rows, tile), lambda i: (0, i)),
-        ],
-        out_specs=pl.BlockSpec((1, tile, h), lambda i: (0, i, 2)),
+        in_specs=[on_chip] * 3,
+        out_specs=anywhere,
+        scratch_shapes=[pltpu.VMEM((d // tile, tile, h), bf16), pltpu.SemaphoreType.DMA((d // tile,))],
         cost_estimate=light,
         compiler_params=params(16),
         name="received_other",
     )(part, hid, other)
 
 
-def inputs_kernel(cap, last, here, old, inputs, own, other, late, out, held):
-    rows = own.shape[0]
-
-    @pl.when(pl.program_id(0) == 0)
-    def _():
-        held[...] = other[...]
-        held[plane_rows(here[0], *last, cap), :] = late[...]
-
-    part = jnp.dot(inputs[:, :rows], own[...], preferred_element_type=f32)
-    part = part + jnp.dot(inputs[:, rows:], held[...], preferred_element_type=f32)
-    out[0] = (part * loss_scale).astype(bf16)
+def inputs_kernel(cap, last, here, old, inputs, own, other, late, out, held, tiles, sems):
+    rows, wide = own.shape
+    count, tile, _ = tiles.shape
+    held[...] = other[...]
+    held[plane_rows(here[0], *last, cap), :] = late[...]
+    copies = []
+    for i in range(count):
+        at = slice(i * tile, (i + 1) * tile)
+        part = jnp.dot(inputs[at, :rows], own[...], preferred_element_type=f32)
+        part = part + jnp.dot(inputs[at, rows:], held[...], preferred_element_type=f32)
+        tiles[i] = (part * loss_scale).astype(bf16)
+        copies.append(pltpu.make_async_copy(tiles.at[i], out.at[0, at, pl.ds(0, wide)], sems.at[i]))
+        copies[-1].start()
+    for c in copies:
+        c.wait()
 
 
 def inputs_part(here, last, old, inputs, own, other, late, cap):
-    d, slots = inputs.shape
+    d = inputs.shape[0]
     rows, wide = own.shape
     tile = 256
-
-    def fixed(v):
-        return pl.BlockSpec(v.shape, lambda i, here: (0, 0))
-
     return pl.pallas_call(
         functools.partial(inputs_kernel, cap, last),
         out_shape=jax.ShapeDtypeStruct(old.shape, bf16),
-        grid_spec=pltpu.PrefetchScalarGridSpec(
-            num_scalar_prefetch=1,
-            grid=(d // tile,),
-            in_specs=[anywhere, pl.BlockSpec((tile, slots), lambda i, here: (i, 0)), fixed(own), fixed(other), fixed(late)],
-            out_specs=pl.BlockSpec((1, tile, wide), lambda i, here: (0, i, 0)),
-            scratch_shapes=[pltpu.VMEM((rows, wide), bf16)],
-        ),
+        in_specs=[on_scalar, anywhere] + [on_chip] * 4,
+        out_specs=anywhere,
+        scratch_shapes=[
+            pltpu.VMEM((rows, wide), bf16),
+            pltpu.VMEM((d // tile, tile, wide), bf16),
+            pltpu.SemaphoreType.DMA((d // tile,)),
+        ],
         input_output_aliases={1: 0},
         cost_estimate=light,
-        compiler_params=params(24),
+        compiler_params=params(20),
         name="inputs_part",
     )(here, old, inputs, own, other, late)
 

time: 105 us -> 104 us (level)
  Pallas kernels: 50.4 us -> 47.9 us
  starting transfers between devices: 36.2 us -> 37.7 us
    ppermute x25, starting transfers between devices: 27.8 us -> 29.3 us  [send(): return lax.ppermute(v, 'expert', perm)]
    pallas_call x1, Pallas kernels: 3.15 us -> 2.03 us  [received_other(): pl.pallas_call(received_other_kernel, out_shape=jax.ShapeDtypeStruct((1,...]
  transfers between devices with their start and end apart: 33 -> 33, of which waited for: 11 -> 13; matrix products, arithmetic and copies ran while one was open for 0% -> 0% of each run, Pallas kernels for 47% -> 45%
where the time goes in v13:
time: 104 us; the launch traced here: 103 us
  Pallas kernels  47.9 us (46%)
  starting transfers between devices  37.7 us (36%)
  waiting for transfers between devices  16 us (15%)
    ppermute x25, starting transfers between devices, send(): return lax.ppermute(v, 'expert', perm)  29.3 us
    pallas_call x5, Pallas kernels, combine(): pl.pallas_call(functools.partial(combine_kernel, chunk, cap, len(old), la...  14.2 us
    pallas_call x5, Pallas kernels, dispatch(): pl.pallas_call(functools.partial(dispatch_kernel, chunk, cap, len(old) //...  13.5 us
    ppermute x8, waiting for transfers between devices, exchange(): return lax.ppermute(v, 'dp', [(0, 1), (1, 0)])  9.56 us
    ppermute x8, starting transfers between devices, exchange(): return lax.ppermute(v, 'dp', [(0, 1), (1, 0)])  8.4 us
    ppermute x25, waiting for transfers between devices, send(): return lax.ppermute(v, 'expert', perm)  6.45 us
    pallas_call x1, Pallas kernels, inputs_part(): pl.pallas_call(functools.partial(inputs_kernel, cap, last), out_shape=jax...  5.19 us
    pallas_call x2, Pallas kernels, hidden(): pl.pallas_call(functools.partial(hidden_kernel, cap, k), out_shape=jax.Sh...  4.73 us
  transfers between devices with their start and end apart: 33, of which 13 were waited for; matrix products, arithmetic and copies ran while one was open for 0% of the time, Pallas kernels for 45%

profile of v13, /device:TPU:0, one launch (start us, length us, event | category | flops | bytes accessed | tf_op | source)
XLA Modules:
  0.0 103.5 jit_solution(4888097926863640079)
XLA Ops:
  3.4 2.7 %collective-permute-start = (bf16[200,1024]{1,0:T(8,128)(2,1)}, bf16[200,1024]{1,0:T(8,128)(2,1)}, u32[]{:S(2)}, u32[]{:S(2)}) collective-permute-start(bf16[200,1024]{1,0:T(8,128)(2,1)} %pack.1.refs_0_), channel_id=1, source_target_pairs={{0,4},{1,5},{2,6},{3,7},{4,8},{5,9},{6,10},{7,11},{8,12},{9,13},{1... | collective-permute-start | bytes 1228808 | tf_op jit(solution)/shard_map/ppermute | solution.py:514
  7.6 2.2 %hidden.2.hid = bf16[384,1152]{1,0:T(8,128)(2,1)S(1)} custom-call(s32[1]{0:T(128)} %bitcast.2.here, bf16[2304,384]{1,0:T(8,128)(2,1)} %bitcast.10, bf16[2304,384]{1,0:T(8,128)(2,1)} %bitcast.18), custom_call_target="tpu_custom_call" | custom-call | flops 1048576 | bytes 16384 | tf_op jit(solution)/shard_map/hidden/pallas_call | solution.py:347
  9.9 3.9 %turn.1.inputs = bf16[1024,2304]{1,0:T(8,128)(2,1)S(1)} custom-call(s32[1]{0:T(128)} %bitcast.2.here, bf16[2304,1024]{1,0:T(8,128)(2,1)} %bitcast.33), custom_call_target="tpu_custom_call" | custom-call | flops 1048576 | bytes 16384 | tf_op jit(solution)/shard_map/turn/pallas_call | solution.py:371
  14.9 2.5 %dispatch.5 = (bf16[1152,1024]{1,0:T(8,128)(2,1)S(1)}, bf16[1152,1024]{1,0:T(8,128)(2,1)S(1)}, f32[288,384]{1,0:T(8,128)S(1)}, bf16[288,384]{1,0:T(8,128)(2,1)S(1)}, f32[8,192]{1,0:T(8,128)S(1)}) custom-call(s32[1]{0:T(128)} %bitcast.2.here, bf16[200,1024]{1,0:T(8,128)(2,1)} %pack.1.refs_0_, bf16[384,1024]{1,0:T(8,128)(2,1)S(1)} %bitcast.26, ...), custom_call_target="tpu_custom_call" | custom-call | flops 1048576 | bytes 16384 | tf_op jit(solution)/shard_map/dispatch/pallas_call | solution.py:162
  22.7 3.1 %dispatch.6 = (bf16[1152,1024]{1,0:T(8,128)(2,1)S(1)}, bf16[1152,1024]{1,0:T(8,128)(2,1)S(1)}, f32[576,384]{1,0:T(8,128)S(1)}, bf16[288,384]{1,0:T(8,128)(2,1)S(...) custom-call(s32[1]{0:T(128)} %bitcast.2.here, ...), custom_call_target="tpu_custom_call", output_to_operand_aliasing={{0}: (5, {}), {1}: (6, {})} | custom-call | flops 1048576 | bytes 16384 | tf_op jit(solution)/shard_map/dispatch/pallas_call | solution.py:162
  26.3 2.5 %hidden.3.hid = bf16[384,1152]{1,0:T(8,128)(2,1)S(1)} custom-call(s32[1]{0:T(128)} %bitcast.2.here, bf16[2304,384]{1,0:T(8,128)(2,1)} %bitcast.11, bf16[2304,384]{1,0:T(8,128)(2,1)} %bitcast.19), custom_call_target="tpu_custom_call" | custom-call | flops 1048576 | bytes 16384 | tf_op jit(solution)/shard_map/hidden/pallas_call | solution.py:347
  28.9 2.3 %combine.5 = (bf16[1152,768]{1,0:T(8,128)(2,1)S(1)}, bf16[1152,768]{1,0:T(8,128)(2,1)S(1)}, bf16[192,1024]{1,0:T(8,128)(2,1)S(1)}) custom-call(s32[1]{0:T(128)} %bitcast.2.here, f32[288,384]{1,0:T(8,128)S(1)} %get-tuple-element.102.share, bf16[288,384]{1,0:T(8,128)(2,1)S(1)} %collective-permute-done.8.refs_0_, f32[8,192]{1,0:T(8,128)S(1)} %get-tuple-element.104.refs_1_, ...), custom_call_target="tpu_custom_call" | custom-call | flops 1048576 | bytes 16384 | tf_op jit(solution)/shard_map/combine/pallas_call | solution.py:231
  36.7 2.8 %dispatch.7 = (bf16[1152,1024]{1,0:T(8,128)(2,1)S(1)}, bf16[1152,1024]{1,0:T(8,128)(2,1)S(1)}, f32[576,384]{1,0:T(8,128)S(1)}, bf16[288,384]{1,0:T(8,128)(2,1)S(...) custom-call(s32[1]{0:T(128)} %bitcast.2.here, ...), custom_call_target="tpu_custom_call", output_to_operand_aliasing={{0}: (5, {}), {1}: (6, {})} | custom-call | flops 1048576 | bytes 16384 | tf_op jit(solution)/shard_map/dispatch/pallas_call | solution.py:162
  42.0 3.3 %combine.6 = (bf16[1152,768]{1,0:T(8,128)(2,1)S(1)}, bf16[1152,768]{1,0:T(8,128)(2,1)S(1)}, bf16[192,1024]{1,0:T(8,128)(2,1)S(1)}, bf16[192,1024]{1,0:T(8,128)(2,1)S(1)}) custom-call(s32[1]{0:T(128)} %bitcast.2.here, f32[576,384]{1,0:T(8,128)S(1)} %get-tuple-element.116.share, ...), custom_call_target="tpu_custom_call", output_to_operand_aliasing={{0}: (11, {}), {1}: (12, {})} | custom-call | flops 1048576 | bytes 16384 | tf_op jit(solution)/shard_map/combine/pallas_call | solution.py:231
  49.7 2.8 %dispatch.8 = (bf16[1152,1024]{1,0:T(8,128)(2,1)S(1)}, bf16[1152,1024]{1,0:T(8,128)(2,1)S(1)}, f32[576,384]{1,0:T(8,128)S(1)}, bf16[288,384]{1,0:T(8,128)(2,1)S(...) custom-call(s32[1]{0:T(128)} %bitcast.2.here, ...), custom_call_target="tpu_custom_call", output_to_operand_aliasing={{0}: (5, {}), {1}: (6, {})} | custom-call | flops 1048576 | bytes 16384 | tf_op jit(solution)/shard_map/dispatch/pallas_call | solution.py:162
  52.7 2.5 %collective-permute-done.17.refs_1_ = bf16[288,384]{1,0:T(8,128)(2,1)S(1)} collective-permute-done((bf16[288,384]{1,0:T(8,128)(2,1)S(1)}, bf16[288,384]{1,0:T(8,128)(2,1)S(1)}, u32[]{:S(2)}, u32[]{:S(2)}) %collective-permute-start.17) | collective-permute-done | bytes 221216 | tf_op jit(solution)/shard_map/ppermute | solution.py:536
  55.2 3.3 %combine.7 = (bf16[1152,768]{1,0:T(8,128)(2,1)S(1)}, bf16[1152,768]{1,0:T(8,128)(2,1)S(1)}, bf16[192,1024]{1,0:T(8,128)(2,1)S(1)}, bf16[192,1024]{1,0:T(8,128)(2,1)S(1)}) custom-call(s32[1]{0:T(128)} %bitcast.2.here, f32[576,384]{1,0:T(8,128)S(1)} %get-tuple-element.132.share, ...), custom_call_target="tpu_custom_call", output_to_operand_aliasing={{0}: (11, {}), {1}: (12, {})} | custom-call | flops 1048576 | bytes 16384 | tf_op jit(solution)/shard_map/combine/pallas_call | solution.py:231
  58.6 2.0 %collective-permute-start.18 = (bf16[192,1024]{1,0:T(8,128)(2,1)S(1)}, bf16[192,1024]{1,0:T(8,128)(2,1)S(1)}, u32[]{:S(2)}, u32[]{:S(2)}) collective-permute-start(bf16[192,1024]{1,0:T(8,128)(2,1)S(1)} %get-tuple-element.140), channel_id=1, source_target_pairs={{0,4},{1,5},{2,6},{3,7},{4,8},{5,9},{6,10},{7,11},{8,12},{9,13},{1... | collective-permute-start | bytes 1179656 | tf_op jit(solution)/shard_map/ppermute | solution.py:514
  61.2 2.1 %collective-permute-start.21 = (bf16[288,384]{1,0:T(8,128)(2,1)S(1)}, bf16[288,384]{1,0:T(8,128)(2,1)S(1)}, u32[]{:S(2)}, u32[]{:S(2)}) collective-permute-start(bf16[288,384]{1,0:T(8,128)(2,1)S(1)} %get-tuple-element.148), channel_id=1, source_target_pairs={{0,16},{16,0},{1,17},{17,1},{2,18},{18,2},{3,19},{19,3},{4,20},{20... | collective-permute-start | bytes 663560 | tf_op jit(solution)/shard_map/ppermute | solution.py:536
  63.2 2.3 %dispatch.9 = (bf16[1152,1024]{1,0:T(8,128)(2,1)S(1)}, bf16[1152,1024]{1,0:T(8,128)(2,1)S(1)}, f32[288,384]{1,0:T(8,128)S(1)}, bf16[288,384]{1,0:T(8,128)(2,1)S(1)}, f32[8,192]{1,0:T(8,128)S(1)}) custom-call(s32[1]{0:T(128)} %bitcast.2.here, bf16[200,1024]{1,0:T(8,128)(2,1)S(1)} %collective-permute-done.14.refs_0_, ...), custom_call_target="tpu_custom_call", output_to_operand_aliasing={{0}: (4, {}), {1}: (5, {})} | custom-call | flops 1048576 | bytes 16384 | tf_op jit(solution)/shard_map/dispatch/pallas_call | solution.py:162
  65.6 2.5 %collective-permute-done.21.refs_1_ = bf16[288,384]{1,0:T(8,128)(2,1)S(1)} collective-permute-done((bf16[288,384]{1,0:T(8,128)(2,1)S(1)}, bf16[288,384]{1,0:T(8,128)(2,1)S(1)}, u32[]{:S(2)}, u32[]{:S(2)}) %collective-permute-start.21) | collective-permute-done | bytes 221216 | tf_op jit(solution)/shard_map/ppermute | solution.py:536
  68.1 3.3 %combine.8 = (bf16[1152,768]{1,0:T(8,128)(2,1)S(1)}, bf16[1152,768]{1,0:T(8,128)(2,1)S(1)}, bf16[192,1024]{1,0:T(8,128)(2,1)S(1)}, bf16[192,1024]{1,0:T(8,128)(2,1)S(1)}) custom-call(s32[1]{0:T(128)} %bitcast.2.here, f32[576,384]{1,0:T(8,128)S(1)} %get-tuple-element.146.share, ...), custom_call_target="tpu_custom_call", output_to_operand_aliasing={{0}: (11, {}), {1}: (12, {})} | custom-call | flops 1048576 | bytes 16384 | tf_op jit(solution)/shard_map/combine/pallas_call | solution.py:231
  74.3 2.0 %combine.9 = (bf16[1152,768]{1,0:T(8,128)(2,1)S(1)}, bf16[144,768]{1,0:T(8,128)(2,1)S(1)}, bf16[192,512]{1,0:T(8,128)(2,1)S(1)}, bf16[192,512]{1,0:T(8,128)(2,1)S(1)}) custom-call(s32[1]{0:T(128)} %bitcast.2.here, f32[288,384]{1,0:T(8,128)S(1)} %get-tuple-element.158.share, ...), custom_call_target="tpu_custom_call", output_to_operand_aliasing={{0}: (10, {})} | custom-call | flops 1048576 | bytes 16384 | tf_op jit(solution)/shard_map/combine/pallas_call | solution.py:231
  77.9 2.1 %collective-permute-done.28.refs_2_ = bf16[192,512]{1,0:T(8,128)(2,1)S(1)} collective-permute-done((bf16[192,512]{1,0:T(8,128)(2,1)S(1)}, bf16[192,512]{1,0:T(8,128)(2,1)S(1)}, u32[]{:S(2)}, u32[]{:S(2)}) %collective-permute-start.28) | collective-permute-done | bytes 196640 | tf_op jit(solution)/shard_map/ppermute | solution.py:514
  80.1 2.9 %collective-permute-start.29 = (bf16[192,512]{1,0:T(8,128)(2,1)S(1)}, bf16[192,512]{1,0:T(8,128)(2,1)S(1)}, u32[]{:S(2)}, u32[]{:S(2)}) collective-permute-start(bf16[192,512]{1,0:T(8,128)(2,1)S(1)} %add.6), channel_id=1, source_target_pairs={{0,4},{1,5},{2,6},{3,7},{4,8},{5,9},{6,10},{7,11},{8,12},{9,13},{1... | collective-permute-start | bytes 589832 | tf_op jit(solution)/shard_map/ppermute | solution.py:514
  84.3 2.9 %collective-permute-start.25 = (bf16[192,512]{1,0:T(8,128)(2,1)S(1)}, bf16[192,512]{1,0:T(8,128)(2,1)S(1)}, u32[]{:S(2)}, u32[]{:S(2)}) collective-permute-start(bf16[192,512]{1,0:T(8,128)(2,1)S(1)} %add.4), channel_id=1, source_target_pairs={{0,4},{1,5},{2,6},{3,7},{4,8},{5,9},{6,10},{7,11},{8,12},{9,13},{1... | collective-permute-start | bytes 589832 | tf_op jit(solution)/shard_map/ppermute | solution.py:514
  88.1 3.3 %collective-permute-start.30 = (bf16[192,512]{1,0:T(8,128)(2,1)S(1)}, bf16[192,512]{1,0:T(8,128)(2,1)S(1)}, u32[]{:S(2)}, u32[]{:S(2)}) collective-permute-start(bf16[192,512]{1,0:T(8,128)(2,1)S(1)} %add.7), channel_id=1, source_target_pairs={{0,4},{1,5},{2,6},{3,7},{4,8},{5,9},{6,10},{7,11},{8,12},{9,13},{1... | collective-permute-start | bytes 589832 | tf_op jit(solution)/shard_map/ppermute | solution.py:514
  94.9 5.2 %inputs_part.1 = bf16[1,1024,1152]{2,1,0:T(8,128)(2,1)} custom-call(s32[1]{0:T(128)} %bitcast.2.here, bf16[1,1024,1152]{2,1,0:T(8,128)(2,1)} %received_other.1.old, bf16[1024,2304]{1,0:T(8,128)(2,1)S(1)} %turn.1.inputs, bf16[1152,768]{1,0:T(8,128)(2,1)S(1)} %get-tuple-element.183.own, ...), custom_call_target="tpu_custom_call", output_to_operand_aliasing={{}: (1, {})} | custom-call | flops 1048576 | bytes 16384 | tf_op jit(solution)/shard_map/inputs_part/pallas_call | solution.py:482
  100.1 2.5 %collective-permute-done.26.left = bf16[192,512]{1,0:T(8,128)(2,1)S(1)} collective-permute-done((bf16[192,512]{1,0:T(8,128)(2,1)S(1)}, bf16[192,512]{1,0:T(8,128)(2,1)S(1)}, u32[]{:S(2)}, u32[]{:S(2)}) %collective-permute-start.26) | collective-permute-done | bytes 196640 | tf_op jit(solution)/shard_map/ppermute | solution.py:514
  (76 shorter events, 35.7 us)
Async XLA Ops:
  0.6 17.9 %collective-permute-start.3 = (bf16[2304,384]{1,0:T(8,128)(2,1)}, bf16[2304,384]{1,0:T(8,128)(2,1)S(1)}, u32[]{:S(2)}, u32[]{:S(2)}) collective-permute-start(bf16[2304,384]{1,0:T(8,128)(2,1)} %bitcast.9), channel_id=1, source_target_pairs={{0,1},{1,0},{2,3},{3,2},{4,5},{5,4},{6,7},{7,6},{8,9},{9,8},{10,11... | collective-permute-start | bytes 5308424 | tf_op jit(solution)/shard_map/ppermute | solution.py:514
  1.1 17.4 %collective-permute-start.4 = (bf16[2304,384]{1,0:T(8,128)(2,1)}, bf16[2304,384]{1,0:T(8,128)(2,1)S(1)}, u32[]{:S(2)}, u32[]{:S(2)}) collective-permute-start(bf16[2304,384]{1,0:T(8,128)(2,1)} %bitcast.17), channel_id=1, source_target_pairs={{0,1},{1,0},{2,3},{3,2},{4,5},{5,4},{6,7},{7,6},{8,9},{9,8},{10,11... | collective-permute-start | bytes 5308424 | tf_op jit(solution)/shard_map/ppermute | solution.py:514
  1.2 12.7 %collective-permute-start.2 = (bf16[384,1024]{1,0:T(8,128)(2,1)}, bf16[384,1024]{1,0:T(8,128)(2,1)}, u32[]{:S(2)}, u32[]{:S(2)}) collective-permute-start(bf16[384,1024]{1,0:T(8,128)(2,1)} %bitcast.25), channel_id=1, source_target_pairs={{0,1},{1,0},{2,3},{3,2},{4,5},{5,4},{6,7},{7,6},{8,9},{9,8},{10,11... | collective-permute-start | bytes 2359304 | tf_op jit(solution)/shard_map/ppermute | solution.py:514
  3.4 15.1 %collective-permute-start = (bf16[200,1024]{1,0:T(8,128)(2,1)}, bf16[200,1024]{1,0:T(8,128)(2,1)}, u32[]{:S(2)}, u32[]{:S(2)}) collective-permute-start(bf16[200,1024]{1,0:T(8,128)(2,1)} %pack.1.refs_0_), channel_id=1, source_target_pairs={{0,4},{1,5},{2,6},{3,7},{4,8},{5,9},{6,10},{7,11},{8,12},{9,13},{1... | collective-permute-start | bytes 1228808 | tf_op jit(solution)/shard_map/ppermute | solution.py:514
  6.1 12.4 %collective-permute-start.1 = (bf16[200,1024]{1,0:T(8,128)(2,1)}, bf16[200,1024]{1,0:T(8,128)(2,1)}, u32[]{:S(2)}, u32[]{:S(2)}) collective-permute-start(bf16[200,1024]{1,0:T(8,128)(2,1)} %pack.1.refs_0_), channel_id=1, source_target_pairs={{0,2},{1,3},{2,0},{3,1},{4,6},{5,7},{6,4},{7,5},{8,10},{9,11},{10,... | collective-permute-start | bytes 1228808 | tf_op jit(solution)/shard_map/ppermute | solution.py:514
  18.6 10.3 %collective-permute-start.9 = (bf16[1024,768]{1,0:T(8,128)(2,1)S(1)}, bf16[1024,768]{1,0:T(8,128)(2,1)S(1)}, u32[]{:S(2)}, u32[]{:S(2)}) collective-permute-start(bf16[1024,768]{1,0:T(8,128)(2,1)S(1)} %join.1.refs_6_.refs_7_), channel_id=1, source_target_pairs={{0,1},{1,0},{2,3},{3,2},{4,5},{5,4},{6,7},{7,6},{8,9},{9,8},{10,11... | collective-permute-start | bytes 4718600 | tf_op jit(solution)/shard_map/ppermute | solution.py:514
  18.6 14.5 %collective-permute-start.5 = (bf16[200,1024]{1,0:T(8,128)(2,1)}, bf16[200,1024]{1,0:T(8,128)(2,1)S(1)}, u32[]{:S(2)}, u32[]{:S(2)}) collective-permute-start(bf16[200,1024]{1,0:T(8,128)(2,1)} %collective-permute-done.refs_1_), channel_id=1, source_target_pairs={{0,4},{1,5},{2,6},{3,7},{4,8},{5,9},{6,10},{7,11},{8,12},{9,13},{1... | collective-permute-start | bytes 1228808 | tf_op jit(solution)/shard_map/ppermute | solution.py:514
  19.6 13.5 %collective-permute-start.6 = (bf16[200,1024]{1,0:T(8,128)(2,1)}, bf16[200,1024]{1,0:T(8,128)(2,1)S(1)}, u32[]{:S(2)}, u32[]{:S(2)}) collective-permute-start(bf16[200,1024]{1,0:T(8,128)(2,1)} %collective-permute-done.refs_1_), channel_id=1, source_target_pairs={{0,2},{1,3},{2,0},{3,1},{4,6},{5,7},{6,4},{7,5},{8,10},{9,11},{10,... | collective-permute-start | bytes 1228808 | tf_op jit(solution)/shard_map/ppermute | solution.py:514
  21.1 7.7 %collective-permute-start.8 = (bf16[288,384]{1,0:T(8,128)(2,1)S(1)}, bf16[288,384]{1,0:T(8,128)(2,1)S(1)}, u32[]{:S(2)}, u32[]{:S(2)}) collective-permute-start(bf16[288,384]{1,0:T(8,128)(2,1)S(1)} %get-tuple-element.103), channel_id=1, source_target_pairs={{0,16},{16,0},{1,17},{17,1},{2,18},{18,2},{3,19},{19,3},{4,20},{20... | collective-permute-start | bytes 663560 | tf_op jit(solution)/shard_map/ppermute | solution.py:536
  33.1 12.8 %collective-permute-start.10 = (bf16[200,1024]{1,0:T(8,128)(2,1)S(1)}, bf16[200,1024]{1,0:T(8,128)(2,1)S(1)}, u32[]{:S(2)}, u32[]{:S(2)}) collective-permute-start(bf16[200,1024]{1,0:T(8,128)(2,1)S(1)} %collective-permute-done.5.refs_1_), channel_id=1, source_target_pairs={{0,4},{1,5},{2,6},{3,7},{4,8},{5,9},{6,10},{7,11},{8,12},{9,13},{1... | collective-permute-start | bytes 1228808 | tf_op jit(solution)/shard_map/ppermute | solution.py:514
  34.7 11.2 %collective-permute-start.11 = (bf16[200,1024]{1,0:T(8,128)(2,1)S(1)}, bf16[200,1024]{1,0:T(8,128)(2,1)S(1)}, u32[]{:S(2)}, u32[]{:S(2)}) collective-permute-start(bf16[200,1024]{1,0:T(8,128)(2,1)S(1)} %collective-permute-done.5.refs_1_), channel_id=1, source_target_pairs={{0,2},{1,3},{2,0},{3,1},{4,6},{5,7},{6,4},{7,5},{8,10},{9,11},{10,... | collective-permute-start | bytes 1228808 | tf_op jit(solution)/shard_map/ppermute | solution.py:514
  45.9 12.7 %collective-permute-start.14 = (bf16[200,1024]{1,0:T(8,128)(2,1)S(1)}, bf16[200,1024]{1,0:T(8,128)(2,1)S(1)}, u32[]{:S(2)}, u32[]{:S(2)}) collective-permute-start(bf16[200,1024]{1,0:T(8,128)(2,1)S(1)} %collective-permute-done.10.refs_1_), channel_id=1, source_target_pairs={{0,2},{1,3},{2,0},{3,1},{4,6},{5,7},{6,4},{7,5},{8,10},{9,11},{10,... | collective-permute-start | bytes 1228808 | tf_op jit(solution)/shard_map/ppermute | solution.py:514
  47.4 11.2 %collective-permute-start.15 = (bf16[192,1024]{1,0:T(8,128)(2,1)S(1)}, bf16[192,1024]{1,0:T(8,128)(2,1)S(1)}, u32[]{:S(2)}, u32[]{:S(2)}) collective-permute-start(bf16[192,1024]{1,0:T(8,128)(2,1)S(1)} %get-tuple-element.125), channel_id=1, source_target_pairs={{0,4},{1,5},{2,6},{3,7},{4,8},{5,9},{6,10},{7,11},{8,12},{9,13},{1... | collective-permute-start | bytes 1179656 | tf_op jit(solution)/shard_map/ppermute | solution.py:514
  58.6 13.0 %collective-permute-start.18 = (bf16[192,1024]{1,0:T(8,128)(2,1)S(1)}, bf16[192,1024]{1,0:T(8,128)(2,1)S(1)}, u32[]{:S(2)}, u32[]{:S(2)}) collective-permute-start(bf16[192,1024]{1,0:T(8,128)(2,1)S(1)} %get-tuple-element.140), channel_id=1, source_target_pairs={{0,4},{1,5},{2,6},{3,7},{4,8},{5,9},{6,10},{7,11},{8,12},{9,13},{1... | collective-permute-start | bytes 1179656 | tf_op jit(solution)/shard_map/ppermute | solution.py:514
  60.6 10.9 %collective-permute-start.19 = (bf16[192,1024]{1,0:T(8,128)(2,1)S(1)}, bf16[192,1024]{1,0:T(8,128)(2,1)S(1)}, u32[]{:S(2)}, u32[]{:S(2)}) collective-permute-start(bf16[192,1024]{1,0:T(8,128)(2,1)S(1)} %get-tuple-element.141), channel_id=1, source_target_pairs={{0,2},{1,3},{2,0},{3,1},{4,6},{5,7},{6,4},{7,5},{8,10},{9,11},{10,... | collective-permute-start | bytes 1179656 | tf_op jit(solution)/shard_map/ppermute | solution.py:514
  71.6 12.6 %collective-permute-start.24 = (bf16[1152,1024]{1,0:T(8,128)(2,1)S(1)}, bf16[1152,1024]{1,0:T(8,128)(2,1)S(1)}, u32[]{:S(2)}, u32[]{:S(2)}) collective-permute-start(bf16[1152,1024]{1,0:T(8,128)(2,1)S(1)} %get-tuple-element.173), channel_id=1, source_target_pairs={{0,1},{1,0},{2,3},{3,2},{4,5},{5,4},{6,7},{7,6},{8,9},{9,8},{10,11... | collective-permute-start | bytes 7077896 | tf_op jit(solution)/shard_map/ppermute | solution.py:514
  71.6 23.3 %collective-permute-start.31 = (bf16[1152,768]{1,0:T(8,128)(2,1)S(1)}, bf16[1152,768]{1,0:T(8,128)(2,1)S(1)}, u32[]{:S(2)}, u32[]{:S(2)}) collective-permute-start(bf16[1152,768]{1,0:T(8,128)(2,1)S(1)} %get-tuple-element.184), channel_id=1, source_target_pairs={{0,1},{1,0},{2,3},{3,2},{4,5},{5,4},{6,7},{7,6},{8,9},{9,8},{10,11... | collective-permute-start | bytes 5308424 | tf_op jit(solution)/shard_map/ppermute | solution.py:514
  72.2 7.8 %collective-permute-start.28 = (bf16[192,512]{1,0:T(8,128)(2,1)S(1)}, bf16[192,512]{1,0:T(8,128)(2,1)S(1)}, u32[]{:S(2)}, u32[]{:S(2)}) collective-permute-start(bf16[192,512]{1,0:T(8,128)(2,1)S(1)} %get-tuple-element.180), channel_id=1, source_target_pairs={{0,2},{1,3},{2,0},{3,1},{4,6},{5,7},{6,4},{7,5},{8,10},{9,11},{10,... | collective-permute-start | bytes 589832 | tf_op jit(solution)/shard_map/ppermute | solution.py:514
  73.7 10.5 %collective-permute-start.23 = (bf16[192,512]{1,0:T(8,128)(2,1)S(1)}, bf16[192,512]{1,0:T(8,128)(2,1)S(1)}, u32[]{:S(2)}, u32[]{:S(2)}) collective-permute-start(bf16[192,512]{1,0:T(8,128)(2,1)S(1)} %get-tuple-element.170), channel_id=1, source_target_pairs={{0,2},{1,3},{2,0},{3,1},{4,6},{5,7},{6,4},{7,5},{8,10},{9,11},{10,... | collective-permute-start | bytes 589832 | tf_op jit(solution)/shard_map/ppermute | solution.py:514
  76.3 11.2 %collective-permute-start.27 = (bf16[192,512]{1,0:T(8,128)(2,1)S(1)}, bf16[192,512]{1,0:T(8,128)(2,1)S(1)}, u32[]{:S(2)}, u32[]{:S(2)}) collective-permute-start(bf16[192,512]{1,0:T(8,128)(2,1)S(1)} %get-tuple-element.179), channel_id=1, source_target_pairs={{0,2},{1,3},{2,0},{3,1},{4,6},{5,7},{6,4},{7,5},{8,10},{9,11},{10,... | collective-permute-start | bytes 589832 | tf_op jit(solution)/shard_map/ppermute | solution.py:514
  80.1 7.9 %collective-permute-start.29 = (bf16[192,512]{1,0:T(8,128)(2,1)S(1)}, bf16[192,512]{1,0:T(8,128)(2,1)S(1)}, u32[]{:S(2)}, u32[]{:S(2)}) collective-permute-start(bf16[192,512]{1,0:T(8,128)(2,1)S(1)} %add.6), channel_id=1, source_target_pairs={{0,4},{1,5},{2,6},{3,7},{4,8},{5,9},{6,10},{7,11},{8,12},{9,13},{1... | collective-permute-start | bytes 589832 | tf_op jit(solution)/shard_map/ppermute | solution.py:514
  84.3 9.1 %collective-permute-start.25 = (bf16[192,512]{1,0:T(8,128)(2,1)S(1)}, bf16[192,512]{1,0:T(8,128)(2,1)S(1)}, u32[]{:S(2)}, u32[]{:S(2)}) collective-permute-start(bf16[192,512]{1,0:T(8,128)(2,1)S(1)} %add.4), channel_id=1, source_target_pairs={{0,4},{1,5},{2,6},{3,7},{4,8},{5,9},{6,10},{7,11},{8,12},{9,13},{1... | collective-permute-start | bytes 589832 | tf_op jit(solution)/shard_map/ppermute | solution.py:514
  88.1 12.0 %collective-permute-start.30 = (bf16[192,512]{1,0:T(8,128)(2,1)S(1)}, bf16[192,512]{1,0:T(8,128)(2,1)S(1)}, u32[]{:S(2)}, u32[]{:S(2)}) collective-permute-start(bf16[192,512]{1,0:T(8,128)(2,1)S(1)} %add.7), channel_id=1, source_target_pairs={{0,4},{1,5},{2,6},{3,7},{4,8},{5,9},{6,10},{7,11},{8,12},{9,13},{1... | collective-permute-start | bytes 589832 | tf_op jit(solution)/shard_map/ppermute | solution.py:514
  93.5 9.1 %collective-permute-start.26 = (bf16[192,512]{1,0:T(8,128)(2,1)S(1)}, bf16[192,512]{1,0:T(8,128)(2,1)S(1)}, u32[]{:S(2)}, u32[]{:S(2)}) collective-permute-start(bf16[192,512]{1,0:T(8,128)(2,1)S(1)} %add.5), channel_id=1, source_target_pairs={{0,4},{1,5},{2,6},{3,7},{4,8},{5,9},{6,10},{7,11},{8,12},{9,13},{1... | collective-permute-start | bytes 589832 | tf_op jit(solution)/shard_map/ppermute | solution.py:514
  (14 other events, 75.6 us)

commit v14 on v13

--- a/solution.py
+++ b/solution.py
@@ -582,9 +582,9 @@
     part = received_own(hid, recs[0])
     b2[0], _, part, rec_c = together(b2[0], left, part, rec_c)
     w2 = [ring(add([t_r2, w1, b2[k]], k)) for k in range(2)]
+    w2[0], _ = together(w2[0], b3[1])
+    w3 = [ring(add([t_r3, b3[k], w2[k]], k)) for k in range(2)]
     part = received_other(part, hid_c, rec_c)
-    w2[0], part = together(w2[0], part)
-    w3 = [ring(add([t_r3, b3[k], w2[k]], k)) for k in range(2)]
     weight_grads = inputs_part(here, (1, 3), part, inputs, gps[0], gp_c, late, cap)
     w3[1], weight_grads = together(w3[1], weight_grads)
     return (finish(t_r0, b0, *w3), weight_grads)

time: 104 us -> 104 us (level)
  transfers between devices with their start and end apart: 33 -> 33, of which waited for: 13 -> 14; matrix products, arithmetic and copies ran while one was open for 0% -> 0% of each run, Pallas kernels for 45% -> 46%
where the time goes in v14:
time: 104 us; the launch traced here: 103 us
  Pallas kernels  47.9 us (46%)
  starting transfers between devices  38.3 us (37%)
  waiting for transfers between devices  15 us (14%)
    ppermute x25, starting transfers between devices, send(): return lax.ppermute(v, 'expert', perm)  29.9 us
    pallas_call x5, Pallas kernels, combine(): pl.pallas_call(functools.partial(combine_kernel, chunk, cap, len(old), la...  14.2 us
    pallas_call x5, Pallas kernels, dispatch(): pl.pallas_call(functools.partial(dispatch_kernel, chunk, cap, len(old) //...  13.5 us
    ppermute x8, waiting for transfers between devices, exchange(): return lax.ppermute(v, 'dp', [(0, 1), (1, 0)])  9.56 us
    ppermute x8, starting transfers between devices, exchange(): return lax.ppermute(v, 'dp', [(0, 1), (1, 0)])  8.4 us
    ppermute x25, waiting for transfers between devices, send(): return lax.ppermute(v, 'expert', perm)  5.42 us
    pallas_call x1, Pallas kernels, inputs_part(): pl.pallas_call(functools.partial(inputs_kernel, cap, last), out_shape=jax...  5.19 us
    pallas_call x2, Pallas kernels, hidden(): pl.pallas_call(functools.partial(hidden_kernel, cap, k), out_shape=jax.Sh...  4.73 us
  transfers between devices with their start and end apart: 33, of which 14 were waited for; matrix products, arithmetic and copies ran while one was open for 0% of the time, Pallas kernels for 46%

profile of v14, /device:TPU:0, one launch (start us, length us, event | category | flops | bytes accessed | tf_op | source)
XLA Modules:
  0.0 103.1 jit_solution(12851354966119827350)
XLA Ops:
  3.4 2.7 %collective-permute-start = (bf16[200,1024]{1,0:T(8,128)(2,1)}, bf16[200,1024]{1,0:T(8,128)(2,1)}, u32[]{:S(2)}, u32[]{:S(2)}) collective-permute-start(bf16[200,1024]{1,0:T(8,128)(2,1)} %pack.1.refs_0_), channel_id=1, source_target_pairs={{0,4},{1,5},{2,6},{3,7},{4,8},{5,9},{6,10},{7,11},{8,12},{9,13},{1... | collective-permute-start | bytes 1228808 | tf_op jit(solution)/shard_map/ppermute | solution.py:514
  7.6 2.2 %hidden.2.hid = bf16[384,1152]{1,0:T(8,128)(2,1)S(1)} custom-call(s32[1]{0:T(128)} %bitcast.2.here, bf16[2304,384]{1,0:T(8,128)(2,1)} %bitcast.10, bf16[2304,384]{1,0:T(8,128)(2,1)} %bitcast.18), custom_call_target="tpu_custom_call" | custom-call | flops 1048576 | bytes 16384 | tf_op jit(solution)/shard_map/hidden/pallas_call | solution.py:347
  9.9 3.9 %turn.1.inputs = bf16[1024,2304]{1,0:T(8,128)(2,1)S(1)} custom-call(s32[1]{0:T(128)} %bitcast.2.here, bf16[2304,1024]{1,0:T(8,128)(2,1)} %bitcast.33), custom_call_target="tpu_custom_call" | custom-call | flops 1048576 | bytes 16384 | tf_op jit(solution)/shard_map/turn/pallas_call | solution.py:371
  14.9 2.5 %dispatch.5 = (bf16[1152,1024]{1,0:T(8,128)(2,1)S(1)}, bf16[1152,1024]{1,0:T(8,128)(2,1)S(1)}, f32[288,384]{1,0:T(8,128)S(1)}, bf16[288,384]{1,0:T(8,128)(2,1)S(1)}, f32[8,192]{1,0:T(8,128)S(1)}) custom-call(s32[1]{0:T(128)} %bitcast.2.here, bf16[200,1024]{1,0:T(8,128)(2,1)} %pack.1.refs_0_, bf16[384,1024]{1,0:T(8,128)(2,1)S(1)} %bitcast.26, ...), custom_call_target="tpu_custom_call" | custom-call | flops 1048576 | bytes 16384 | tf_op jit(solution)/shard_map/dispatch/pallas_call | solution.py:162
  22.7 3.1 %dispatch.6 = (bf16[1152,1024]{1,0:T(8,128)(2,1)S(1)}, bf16[1152,1024]{1,0:T(8,128)(2,1)S(1)}, f32[576,384]{1,0:T(8,128)S(1)}, bf16[288,384]{1,0:T(8,128)(2,1)S(...) custom-call(s32[1]{0:T(128)} %bitcast.2.here, ...), custom_call_target="tpu_custom_call", output_to_operand_aliasing={{0}: (5, {}), {1}: (6, {})} | custom-call | flops 1048576 | bytes 16384 | tf_op jit(solution)/shard_map/dispatch/pallas_call | solution.py:162
  26.3 2.5 %hidden.3.hid = bf16[384,1152]{1,0:T(8,128)(2,1)S(1)} custom-call(s32[1]{0:T(128)} %bitcast.2.here, bf16[2304,384]{1,0:T(8,128)(2,1)} %bitcast.11, bf16[2304,384]{1,0:T(8,128)(2,1)} %bitcast.19), custom_call_target="tpu_custom_call" | custom-call | flops 1048576 | bytes 16384 | tf_op jit(solution)/shard_map/hidden/pallas_call | solution.py:347
  28.9 2.3 %combine.5 = (bf16[1152,768]{1,0:T(8,128)(2,1)S(1)}, bf16[1152,768]{1,0:T(8,128)(2,1)S(1)}, bf16[192,1024]{1,0:T(8,128)(2,1)S(1)}) custom-call(s32[1]{0:T(128)} %bitcast.2.here, f32[288,384]{1,0:T(8,128)S(1)} %get-tuple-element.101.share, bf16[288,384]{1,0:T(8,128)(2,1)S(1)} %collective-permute-done.8.refs_0_, f32[8,192]{1,0:T(8,128)S(1)} %get-tuple-element.103.refs_1_, ...), custom_call_target="tpu_custom_call" | custom-call | flops 1048576 | bytes 16384 | tf_op jit(solution)/shard_map/combine/pallas_call | solution.py:231
  36.7 2.8 %dispatch.7 = (bf16[1152,1024]{1,0:T(8,128)(2,1)S(1)}, bf16[1152,1024]{1,0:T(8,128)(2,1)S(1)}, f32[576,384]{1,0:T(8,128)S(1)}, bf16[288,384]{1,0:T(8,128)(2,1)S(...) custom-call(s32[1]{0:T(128)} %bitcast.2.here, ...), custom_call_target="tpu_custom_call", output_to_operand_aliasing={{0}: (5, {}), {1}: (6, {})} | custom-call | flops 1048576 | bytes 16384 | tf_op jit(solution)/shard_map/dispatch/pallas_call | solution.py:162
  42.0 3.3 %combine.6 = (bf16[1152,768]{1,0:T(8,128)(2,1)S(1)}, bf16[1152,768]{1,0:T(8,128)(2,1)S(1)}, bf16[192,1024]{1,0:T(8,128)(2,1)S(1)}, bf16[192,1024]{1,0:T(8,128)(2,1)S(1)}) custom-call(s32[1]{0:T(128)} %bitcast.2.here, f32[576,384]{1,0:T(8,128)S(1)} %get-tuple-element.115.share, ...), custom_call_target="tpu_custom_call", output_to_operand_aliasing={{0}: (11, {}), {1}: (12, {})} | custom-call | flops 1048576 | bytes 16384 | tf_op jit(solution)/shard_map/combine/pallas_call | solution.py:231
  49.7 2.8 %dispatch.8 = (bf16[1152,1024]{1,0:T(8,128)(2,1)S(1)}, bf16[1152,1024]{1,0:T(8,128)(2,1)S(1)}, f32[576,384]{1,0:T(8,128)S(1)}, bf16[288,384]{1,0:T(8,128)(2,1)S(...) custom-call(s32[1]{0:T(128)} %bitcast.2.here, ...), custom_call_target="tpu_custom_call", output_to_operand_aliasing={{0}: (5, {}), {1}: (6, {})} | custom-call | flops 1048576 | bytes 16384 | tf_op jit(solution)/shard_map/dispatch/pallas_call | solution.py:162
  52.7 2.5 %collective-permute-done.17.refs_1_ = bf16[288,384]{1,0:T(8,128)(2,1)S(1)} collective-permute-done((bf16[288,384]{1,0:T(8,128)(2,1)S(1)}, bf16[288,384]{1,0:T(8,128)(2,1)S(1)}, u32[]{:S(2)}, u32[]{:S(2)}) %collective-permute-start.17) | collective-permute-done | bytes 221216 | tf_op jit(solution)/shard_map/ppermute | solution.py:536
  55.2 3.3 %combine.7 = (bf16[1152,768]{1,0:T(8,128)(2,1)S(1)}, bf16[1152,768]{1,0:T(8,128)(2,1)S(1)}, bf16[192,1024]{1,0:T(8,128)(2,1)S(1)}, bf16[192,1024]{1,0:T(8,128)(2,1)S(1)}) custom-call(s32[1]{0:T(128)} %bitcast.2.here, f32[576,384]{1,0:T(8,128)S(1)} %get-tuple-element.131.share, ...), custom_call_target="tpu_custom_call", output_to_operand_aliasing={{0}: (11, {}), {1}: (12, {})} | custom-call | flops 1048576 | bytes 16384 | tf_op jit(solution)/shard_map/combine/pallas_call | solution.py:231
  58.6 2.0 %collective-permute-start.18 = (bf16[192,1024]{1,0:T(8,128)(2,1)S(1)}, bf16[192,1024]{1,0:T(8,128)(2,1)S(1)}, u32[]{:S(2)}, u32[]{:S(2)}) collective-permute-start(bf16[192,1024]{1,0:T(8,128)(2,1)S(1)} %get-tuple-element.139), channel_id=1, source_target_pairs={{0,4},{1,5},{2,6},{3,7},{4,8},{5,9},{6,10},{7,11},{8,12},{9,13},{1... | collective-permute-start | bytes 1179656 | tf_op jit(solution)/shard_map/ppermute | solution.py:514
  61.2 2.1 %collective-permute-start.21 = (bf16[288,384]{1,0:T(8,128)(2,1)S(1)}, bf16[288,384]{1,0:T(8,128)(2,1)S(1)}, u32[]{:S(2)}, u32[]{:S(2)}) collective-permute-start(bf16[288,384]{1,0:T(8,128)(2,1)S(1)} %get-tuple-element.147), channel_id=1, source_target_pairs={{0,16},{16,0},{1,17},{17,1},{2,18},{18,2},{3,19},{19,3},{4,20},{20... | collective-permute-start | bytes 663560 | tf_op jit(solution)/shard_map/ppermute | solution.py:536
  63.2 2.3 %dispatch.9 = (bf16[1152,1024]{1,0:T(8,128)(2,1)S(1)}, bf16[1152,1024]{1,0:T(8,128)(2,1)S(1)}, f32[288,384]{1,0:T(8,128)S(1)}, bf16[288,384]{1,0:T(8,128)(2,1)S(1)}, f32[8,192]{1,0:T(8,128)S(1)}) custom-call(s32[1]{0:T(128)} %bitcast.2.here, bf16[200,1024]{1,0:T(8,128)(2,1)S(1)} %collective-permute-done.14.refs_0_, ...), custom_call_target="tpu_custom_call", output_to_operand_aliasing={{0}: (4, {}), {1}: (5, {})} | custom-call | flops 1048576 | bytes 16384 | tf_op jit(solution)/shard_map/dispatch/pallas_call | solution.py:162
  65.6 2.5 %collective-permute-done.21.refs_1_ = bf16[288,384]{1,0:T(8,128)(2,1)S(1)} collective-permute-done((bf16[288,384]{1,0:T(8,128)(2,1)S(1)}, bf16[288,384]{1,0:T(8,128)(2,1)S(1)}, u32[]{:S(2)}, u32[]{:S(2)}) %collective-permute-start.21) | collective-permute-done | bytes 221216 | tf_op jit(solution)/shard_map/ppermute | solution.py:536
  68.1 3.3 %combine.8 = (bf16[1152,768]{1,0:T(8,128)(2,1)S(1)}, bf16[1152,768]{1,0:T(8,128)(2,1)S(1)}, bf16[192,1024]{1,0:T(8,128)(2,1)S(1)}, bf16[192,1024]{1,0:T(8,128)(2,1)S(1)}) custom-call(s32[1]{0:T(128)} %bitcast.2.here, f32[576,384]{1,0:T(8,128)S(1)} %get-tuple-element.145.share, ...), custom_call_target="tpu_custom_call", output_to_operand_aliasing={{0}: (11, {}), {1}: (12, {})} | custom-call | flops 1048576 | bytes 16384 | tf_op jit(solution)/shard_map/combine/pallas_call | solution.py:231
  74.3 2.0 %combine.9 = (bf16[1152,768]{1,0:T(8,128)(2,1)S(1)}, bf16[144,768]{1,0:T(8,128)(2,1)S(1)}, bf16[192,512]{1,0:T(8,128)(2,1)S(1)}, bf16[192,512]{1,0:T(8,128)(2,1)S(1)}) custom-call(s32[1]{0:T(128)} %bitcast.2.here, f32[288,384]{1,0:T(8,128)S(1)} %get-tuple-element.157.share, ...), custom_call_target="tpu_custom_call", output_to_operand_aliasing={{0}: (10, {})} | custom-call | flops 1048576 | bytes 16384 | tf_op jit(solution)/shard_map/combine/pallas_call | solution.py:231
  80.1 2.9 %collective-permute-start.29 = (bf16[192,512]{1,0:T(8,128)(2,1)S(1)}, bf16[192,512]{1,0:T(8,128)(2,1)S(1)}, u32[]{:S(2)}, u32[]{:S(2)}) collective-permute-start(bf16[192,512]{1,0:T(8,128)(2,1)S(1)} %add.6), channel_id=1, source_target_pairs={{0,4},{1,5},{2,6},{3,7},{4,8},{5,9},{6,10},{7,11},{8,12},{9,13},{1... | collective-permute-start | bytes 589832 | tf_op jit(solution)/shard_map/ppermute | solution.py:514
  84.3 2.9 %collective-permute-start.25 = (bf16[192,512]{1,0:T(8,128)(2,1)S(1)}, bf16[192,512]{1,0:T(8,128)(2,1)S(1)}, u32[]{:S(2)}, u32[]{:S(2)}) collective-permute-start(bf16[192,512]{1,0:T(8,128)(2,1)S(1)} %add.4), channel_id=1, source_target_pairs={{0,4},{1,5},{2,6},{3,7},{4,8},{5,9},{6,10},{7,11},{8,12},{9,13},{1... | collective-permute-start | bytes 589832 | tf_op jit(solution)/shard_map/ppermute | solution.py:514
  88.1 3.3 %collective-permute-start.30 = (bf16[192,512]{1,0:T(8,128)(2,1)S(1)}, bf16[192,512]{1,0:T(8,128)(2,1)S(1)}, u32[]{:S(2)}, u32[]{:S(2)}) collective-permute-start(bf16[192,512]{1,0:T(8,128)(2,1)S(1)} %add.7), channel_id=1, source_target_pairs={{0,4},{1,5},{2,6},{3,7},{4,8},{5,9},{6,10},{7,11},{8,12},{9,13},{1... | collective-permute-start | bytes 589832 | tf_op jit(solution)/shard_map/ppermute | solution.py:514
  92.9 2.0 %collective-permute-start.27 = (bf16[192,512]{1,0:T(8,128)(2,1)S(1)}, bf16[192,512]{1,0:T(8,128)(2,1)S(1)}, u32[]{:S(2)}, u32[]{:S(2)}) collective-permute-start(bf16[192,512]{1,0:T(8,128)(2,1)S(1)} %add.5), channel_id=1, source_target_pairs={{0,4},{1,5},{2,6},{3,7},{4,8},{5,9},{6,10},{7,11},{8,12},{9,13},{1... | collective-permute-start | bytes 589832 | tf_op jit(solution)/shard_map/ppermute | solution.py:514
  94.9 2.0 %received_other.1.old = bf16[1,1024,1152]{2,1,0:T(8,128)(2,1)} custom-call(f32[384,1024]{1,0:T(8,128)S(1)} %received_own.1.part, bf16[384,1152]{1,0:T(8,128)(2,1)S(1)} %hidden.3.hid, bf16[1152,1024]{1,0:T(8,128)(2,1)S(1)} %collective-permute-done.24.other), custom_call_target="tpu_custom_call" | custom-call | flops 1048576 | bytes 16384 | tf_op jit(solution)/shard_map/received_other/pallas_call | solution.py:449
  97.0 5.2 %inputs_part.1 = bf16[1,1024,1152]{2,1,0:T(8,128)(2,1)} custom-call(s32[1]{0:T(128)} %bitcast.2.here, bf16[1,1024,1152]{2,1,0:T(8,128)(2,1)} %received_other.1.old, bf16[1024,2304]{1,0:T(8,128)(2,1)S(1)} %turn.1.inputs, bf16[1152,768]{1,0:T(8,128)(2,1)S(1)} %get-tuple-element.181.own, ...), custom_call_target="tpu_custom_call", output_to_operand_aliasing={{}: (1, {})} | custom-call | flops 1048576 | bytes 16384 | tf_op jit(solution)/shard_map/inputs_part/pallas_call | solution.py:482
  (76 shorter events, 35.9 us)
Async XLA Ops:
  0.6 17.9 %collective-permute-start.3 = (bf16[2304,384]{1,0:T(8,128)(2,1)}, bf16[2304,384]{1,0:T(8,128)(2,1)S(1)}, u32[]{:S(2)}, u32[]{:S(2)}) collective-permute-start(bf16[2304,384]{1,0:T(8,128)(2,1)} %bitcast.9), channel_id=1, source_target_pairs={{0,1},{1,0},{2,3},{3,2},{4,5},{5,4},{6,7},{7,6},{8,9},{9,8},{10,11... | collective-permute-start | bytes 5308424 | tf_op jit(solution)/shard_map/ppermute | solution.py:514
  1.1 17.4 %collective-permute-start.4 = (bf16[2304,384]{1,0:T(8,128)(2,1)}, bf16[2304,384]{1,0:T(8,128)(2,1)S(1)}, u32[]{:S(2)}, u32[]{:S(2)}) collective-permute-start(bf16[2304,384]{1,0:T(8,128)(2,1)} %bitcast.17), channel_id=1, source_target_pairs={{0,1},{1,0},{2,3},{3,2},{4,5},{5,4},{6,7},{7,6},{8,9},{9,8},{10,11... | collective-permute-start | bytes 5308424 | tf_op jit(solution)/shard_map/ppermute | solution.py:514
  1.2 12.7 %collective-permute-start.2 = (bf16[384,1024]{1,0:T(8,128)(2,1)}, bf16[384,1024]{1,0:T(8,128)(2,1)}, u32[]{:S(2)}, u32[]{:S(2)}) collective-permute-start(bf16[384,1024]{1,0:T(8,128)(2,1)} %bitcast.25), channel_id=1, source_target_pairs={{0,1},{1,0},{2,3},{3,2},{4,5},{5,4},{6,7},{7,6},{8,9},{9,8},{10,11... | collective-permute-start | bytes 2359304 | tf_op jit(solution)/shard_map/ppermute | solution.py:514
  3.4 15.1 %collective-permute-start = (bf16[200,1024]{1,0:T(8,128)(2,1)}, bf16[200,1024]{1,0:T(8,128)(2,1)}, u32[]{:S(2)}, u32[]{:S(2)}) collective-permute-start(bf16[200,1024]{1,0:T(8,128)(2,1)} %pack.1.refs_0_), channel_id=1, source_target_pairs={{0,4},{1,5},{2,6},{3,7},{4,8},{5,9},{6,10},{7,11},{8,12},{9,13},{1... | collective-permute-start | bytes 1228808 | tf_op jit(solution)/shard_map/ppermute | solution.py:514
  6.1 12.4 %collective-permute-start.1 = (bf16[200,1024]{1,0:T(8,128)(2,1)}, bf16[200,1024]{1,0:T(8,128)(2,1)}, u32[]{:S(2)}, u32[]{:S(2)}) collective-permute-start(bf16[200,1024]{1,0:T(8,128)(2,1)} %pack.1.refs_0_), channel_id=1, source_target_pairs={{0,2},{1,3},{2,0},{3,1},{4,6},{5,7},{6,4},{7,5},{8,10},{9,11},{10,... | collective-permute-start | bytes 1228808 | tf_op jit(solution)/shard_map/ppermute | solution.py:514
  18.6 10.3 %collective-permute-start.9 = (bf16[1024,768]{1,0:T(8,128)(2,1)S(1)}, bf16[1024,768]{1,0:T(8,128)(2,1)S(1)}, u32[]{:S(2)}, u32[]{:S(2)}) collective-permute-start(bf16[1024,768]{1,0:T(8,128)(2,1)S(1)} %join.1.refs_6_.refs_7_), channel_id=1, source_target_pairs={{0,1},{1,0},{2,3},{3,2},{4,5},{5,4},{6,7},{7,6},{8,9},{9,8},{10,11... | collective-permute-start | bytes 4718600 | tf_op jit(solution)/shard_map/ppermute | solution.py:514
  18.6 14.5 %collective-permute-start.5 = (bf16[200,1024]{1,0:T(8,128)(2,1)}, bf16[200,1024]{1,0:T(8,128)(2,1)S(1)}, u32[]{:S(2)}, u32[]{:S(2)}) collective-permute-start(bf16[200,1024]{1,0:T(8,128)(2,1)} %collective-permute-done.refs_1_), channel_id=1, source_target_pairs={{0,4},{1,5},{2,6},{3,7},{4,8},{5,9},{6,10},{7,11},{8,12},{9,13},{1... | collective-permute-start | bytes 1228808 | tf_op jit(solution)/shard_map/ppermute | solution.py:514
  19.6 13.5 %collective-permute-start.6 = (bf16[200,1024]{1,0:T(8,128)(2,1)}, bf16[200,1024]{1,0:T(8,128)(2,1)S(1)}, u32[]{:S(2)}, u32[]{:S(2)}) collective-permute-start(bf16[200,1024]{1,0:T(8,128)(2,1)} %collective-permute-done.refs_1_), channel_id=1, source_target_pairs={{0,2},{1,3},{2,0},{3,1},{4,6},{5,7},{6,4},{7,5},{8,10},{9,11},{10,... | collective-permute-start | bytes 1228808 | tf_op jit(solution)/shard_map/ppermute | solution.py:514
  21.1 7.7 %collective-permute-start.8 = (bf16[288,384]{1,0:T(8,128)(2,1)S(1)}, bf16[288,384]{1,0:T(8,128)(2,1)S(1)}, u32[]{:S(2)}, u32[]{:S(2)}) collective-permute-start(bf16[288,384]{1,0:T(8,128)(2,1)S(1)} %get-tuple-element.102), channel_id=1, source_target_pairs={{0,16},{16,0},{1,17},{17,1},{2,18},{18,2},{3,19},{19,3},{4,20},{20... | collective-permute-start | bytes 663560 | tf_op jit(solution)/shard_map/ppermute | solution.py:536
  33.1 12.8 %collective-permute-start.10 = (bf16[200,1024]{1,0:T(8,128)(2,1)S(1)}, bf16[200,1024]{1,0:T(8,128)(2,1)S(1)}, u32[]{:S(2)}, u32[]{:S(2)}) collective-permute-start(bf16[200,1024]{1,0:T(8,128)(2,1)S(1)} %collective-permute-done.5.refs_1_), channel_id=1, source_target_pairs={{0,4},{1,5},{2,6},{3,7},{4,8},{5,9},{6,10},{7,11},{8,12},{9,13},{1... | collective-permute-start | bytes 1228808 | tf_op jit(solution)/shard_map/ppermute | solution.py:514
  34.7 11.2 %collective-permute-start.11 = (bf16[200,1024]{1,0:T(8,128)(2,1)S(1)}, bf16[200,1024]{1,0:T(8,128)(2,1)S(1)}, u32[]{:S(2)}, u32[]{:S(2)}) collective-permute-start(bf16[200,1024]{1,0:T(8,128)(2,1)S(1)} %collective-permute-done.5.refs_1_), channel_id=1, source_target_pairs={{0,2},{1,3},{2,0},{3,1},{4,6},{5,7},{6,4},{7,5},{8,10},{9,11},{10,... | collective-permute-start | bytes 1228808 | tf_op jit(solution)/shard_map/ppermute | solution.py:514
  45.9 12.7 %collective-permute-start.14 = (bf16[200,1024]{1,0:T(8,128)(2,1)S(1)}, bf16[200,1024]{1,0:T(8,128)(2,1)S(1)}, u32[]{:S(2)}, u32[]{:S(2)}) collective-permute-start(bf16[200,1024]{1,0:T(8,128)(2,1)S(1)} %collective-permute-done.10.refs_1_), channel_id=1, source_target_pairs={{0,2},{1,3},{2,0},{3,1},{4,6},{5,7},{6,4},{7,5},{8,10},{9,11},{10,... | collective-permute-start | bytes 1228808 | tf_op jit(solution)/shard_map/ppermute | solution.py:514
  47.4 11.2 %collective-permute-start.15 = (bf16[192,1024]{1,0:T(8,128)(2,1)S(1)}, bf16[192,1024]{1,0:T(8,128)(2,1)S(1)}, u32[]{:S(2)}, u32[]{:S(2)}) collective-permute-start(bf16[192,1024]{1,0:T(8,128)(2,1)S(1)} %get-tuple-element.124), channel_id=1, source_target_pairs={{0,4},{1,5},{2,6},{3,7},{4,8},{5,9},{6,10},{7,11},{8,12},{9,13},{1... | collective-permute-start | bytes 1179656 | tf_op jit(solution)/shard_map/ppermute | solution.py:514
  58.6 13.0 %collective-permute-start.18 = (bf16[192,1024]{1,0:T(8,128)(2,1)S(1)}, bf16[192,1024]{1,0:T(8,128)(2,1)S(1)}, u32[]{:S(2)}, u32[]{:S(2)}) collective-permute-start(bf16[192,1024]{1,0:T(8,128)(2,1)S(1)} %get-tuple-element.139), channel_id=1, source_target_pairs={{0,4},{1,5},{2,6},{3,7},{4,8},{5,9},{6,10},{7,11},{8,12},{9,13},{1... | collective-permute-start | bytes 1179656 | tf_op jit(solution)/shard_map/ppermute | solution.py:514
  60.6 10.9 %collective-permute-start.19 = (bf16[192,1024]{1,0:T(8,128)(2,1)S(1)}, bf16[192,1024]{1,0:T(8,128)(2,1)S(1)}, u32[]{:S(2)}, u32[]{:S(2)}) collective-permute-start(bf16[192,1024]{1,0:T(8,128)(2,1)S(1)} %get-tuple-element.140), channel_id=1, source_target_pairs={{0,2},{1,3},{2,0},{3,1},{4,6},{5,7},{6,4},{7,5},{8,10},{9,11},{10,... | collective-permute-start | bytes 1179656 | tf_op jit(solution)/shard_map/ppermute | solution.py:514
  71.6 12.6 %collective-permute-start.24 = (bf16[1152,1024]{1,0:T(8,128)(2,1)S(1)}, bf16[1152,1024]{1,0:T(8,128)(2,1)S(1)}, u32[]{:S(2)}, u32[]{:S(2)}) collective-permute-start(bf16[1152,1024]{1,0:T(8,128)(2,1)S(1)} %get-tuple-element.172), channel_id=1, source_target_pairs={{0,1},{1,0},{2,3},{3,2},{4,5},{5,4},{6,7},{7,6},{8,9},{9,8},{10,11... | collective-permute-start | bytes 7077896 | tf_op jit(solution)/shard_map/ppermute | solution.py:514
  71.6 25.4 %collective-permute-start.31 = (bf16[1152,768]{1,0:T(8,128)(2,1)S(1)}, bf16[1152,768]{1,0:T(8,128)(2,1)S(1)}, u32[]{:S(2)}, u32[]{:S(2)}) collective-permute-start(bf16[1152,768]{1,0:T(8,128)(2,1)S(1)} %get-tuple-element.182), channel_id=1, source_target_pairs={{0,1},{1,0},{2,3},{3,2},{4,5},{5,4},{6,7},{7,6},{8,9},{9,8},{10,11... | collective-permute-start | bytes 5308424 | tf_op jit(solution)/shard_map/ppermute | solution.py:514
  72.2 7.8 %collective-permute-start.28 = (bf16[192,512]{1,0:T(8,128)(2,1)S(1)}, bf16[192,512]{1,0:T(8,128)(2,1)S(1)}, u32[]{:S(2)}, u32[]{:S(2)}) collective-permute-start(bf16[192,512]{1,0:T(8,128)(2,1)S(1)} %get-tuple-element.176), channel_id=1, source_target_pairs={{0,2},{1,3},{2,0},{3,1},{4,6},{5,7},{6,4},{7,5},{8,10},{9,11},{10,... | collective-permute-start | bytes 589832 | tf_op jit(solution)/shard_map/ppermute | solution.py:514
  73.7 10.5 %collective-permute-start.23 = (bf16[192,512]{1,0:T(8,128)(2,1)S(1)}, bf16[192,512]{1,0:T(8,128)(2,1)S(1)}, u32[]{:S(2)}, u32[]{:S(2)}) collective-permute-start(bf16[192,512]{1,0:T(8,128)(2,1)S(1)} %get-tuple-element.169), channel_id=1, source_target_pairs={{0,2},{1,3},{2,0},{3,1},{4,6},{5,7},{6,4},{7,5},{8,10},{9,11},{10,... | collective-permute-start | bytes 589832 | tf_op jit(solution)/shard_map/ppermute | solution.py:514
  76.3 11.2 %collective-permute-start.26 = (bf16[192,512]{1,0:T(8,128)(2,1)S(1)}, bf16[192,512]{1,0:T(8,128)(2,1)S(1)}, u32[]{:S(2)}, u32[]{:S(2)}) collective-permute-start(bf16[192,512]{1,0:T(8,128)(2,1)S(1)} %get-tuple-element.174), channel_id=1, source_target_pairs={{0,2},{1,3},{2,0},{3,1},{4,6},{5,7},{6,4},{7,5},{8,10},{9,11},{10,... | collective-permute-start | bytes 589832 | tf_op jit(solution)/shard_map/ppermute | solution.py:514
  80.1 7.9 %collective-permute-start.29 = (bf16[192,512]{1,0:T(8,128)(2,1)S(1)}, bf16[192,512]{1,0:T(8,128)(2,1)S(1)}, u32[]{:S(2)}, u32[]{:S(2)}) collective-permute-start(bf16[192,512]{1,0:T(8,128)(2,1)S(1)} %add.6), channel_id=1, source_target_pairs={{0,4},{1,5},{2,6},{3,7},{4,8},{5,9},{6,10},{7,11},{8,12},{9,13},{1... | collective-permute-start | bytes 589832 | tf_op jit(solution)/shard_map/ppermute | solution.py:514
  87.5 9.4 %collective-permute-start.32 = (bf16[144,768]{1,0:T(8,128)(2,1)S(1)}, bf16[144,768]{1,0:T(8,128)(2,1)S(1)}, u32[]{:S(2)}, u32[]{:S(2)}) collective-permute-start(bf16[144,768]{1,0:T(8,128)(2,1)S(1)} %get-tuple-element.183), channel_id=1, source_target_pairs={{0,1},{1,0},{2,3},{3,2},{4,5},{5,4},{6,7},{7,6},{8,9},{9,8},{10,11... | collective-permute-start | bytes 663560 | tf_op jit(solution)/shard_map/ppermute | solution.py:514
  88.1 14.1 %collective-permute-start.30 = (bf16[192,512]{1,0:T(8,128)(2,1)S(1)}, bf16[192,512]{1,0:T(8,128)(2,1)S(1)}, u32[]{:S(2)}, u32[]{:S(2)}) collective-permute-start(bf16[192,512]{1,0:T(8,128)(2,1)S(1)} %add.7), channel_id=1, source_target_pairs={{0,4},{1,5},{2,6},{3,7},{4,8},{5,9},{6,10},{7,11},{8,12},{9,13},{1... | collective-permute-start | bytes 589832 | tf_op jit(solution)/shard_map/ppermute | solution.py:514
  92.9 9.3 %collective-permute-start.27 = (bf16[192,512]{1,0:T(8,128)(2,1)S(1)}, bf16[192,512]{1,0:T(8,128)(2,1)S(1)}, u32[]{:S(2)}, u32[]{:S(2)}) collective-permute-start(bf16[192,512]{1,0:T(8,128)(2,1)S(1)} %add.5), channel_id=1, source_target_pairs={{0,4},{1,5},{2,6},{3,7},{4,8},{5,9},{6,10},{7,11},{8,12},{9,13},{1... | collective-permute-start | bytes 589832 | tf_op jit(solution)/shard_map/ppermute | solution.py:514
  (14 other events, 75.2 us)

commit v15 on v14

--- a/solution.py
+++ b/solution.py
@@ -180,7 +180,8 @@
     else:
         peer0, peer1, pos, *refs = refs
     saved, ws, refs = refs[:4], refs[4:6], refs[6 + begun :]
-    buffers, backs, (gps, out_sems) = refs[:2], refs[2:-2], refs[-2:]
+    count = 3 if last else 2
+    buffers, backs, (gps, out_sems) = refs[:count], refs[count:-2], refs[-2:]
     h = share.shape[1]
     slot = lax.broadcasted_iota(jnp.int32, (cap, pos.shape[1]), 0).astype(f32)
     leaving = []
@@ -200,7 +201,8 @@
     for c in leaving:
         c.start()
     if last:
-        buffers[1][...] = gps[1]
+        buffers[1][...] = gps[1, :, :h]
+        buffers[2][...] = gps[1, :, h:]
     sums = [None] * n
     for a, w in enumerate(ws):
         slots = contract_cols(gps[a], w[...]).astype(bf16)
@@ -226,13 +228,13 @@
     d = w0.shape[0]
     tok = pos.shape[1]
     old = old[:1] if last else old
-    outs = [(rows, 2 * h), (n * cap if last else rows, 2 * h)] + ([(tok, d // 2)] * 2 if last else [(tok, d)] * n)
+    outs = [(rows, 2 * h)] + ([(n * cap, h)] * 2 if last else [(rows, 2 * h)]) + ([(tok, d // 2)] * 2 if last else [(tok, d)] * n)
     first_old = 2 + len(peers) + 1 + 4 + 2
     return pl.pallas_call(
         functools.partial(combine_kernel, chunk, cap, len(old), last),
         out_shape=[jax.ShapeDtypeStruct(s, bf16) for s in outs],
         in_specs=[on_scalar] + [on_chip] * (2 + len(peers) + 6) + [anywhere] * len(old),
-        out_specs=[anywhere, on_chip if last else anywhere] + [on_chip] * (len(outs) - 2),
+        out_specs=[anywhere] * (1 if last else 2) + [on_chip] * (len(outs) - (1 if last else 2)),
         scratch_shapes=[
             pltpu.VMEM((2, n * cap, 2 * h), bf16),
             pltpu.SemaphoreType.DMA((2 * n,)),
@@ -458,11 +460,13 @@
     )(part, hid, other)
 
 
-def inputs_kernel(cap, last, here, old, inputs, own, other, late, out, held, tiles, sems):
+def inputs_kernel(cap, last, here, old, inputs, own, other, late0, late1, out, held, tiles, sems):
     rows, wide = own.shape
     count, tile, _ = tiles.shape
     held[...] = other[...]
-    held[plane_rows(here[0], *last, cap), :] = late[...]
+    at = plane_rows(here[0], *last, cap)
+    held[at, : wide // 2] = late0[...]
+    held[at, wide // 2 :] = late1[...]
     copies = []
     for i in range(count):
         at = slice(i * tile, (i + 1) * tile)
@@ -475,14 +479,14 @@
         c.wait()
 
 
-def inputs_part(here, last, old, inputs, own, other, late, cap):
+def inputs_part(here, last, old, inputs, own, other, late0, late1, cap):
     d = inputs.shape[0]
     rows, wide = own.shape
     tile = 256
     return pl.pallas_call(
         functools.partial(inputs_kernel, cap, last),
         out_shape=jax.ShapeDtypeStruct(old.shape, bf16),
-        in_specs=[on_scalar, anywhere] + [on_chip] * 4,
+        in_specs=[on_scalar, anywhere] + [on_chip] * 5,
         out_specs=anywhere,
         scratch_shapes=[
             pltpu.VMEM((rows, wide), bf16),
@@ -493,7 +497,7 @@
         cost_estimate=light,
         compiler_params=params(20),
         name="inputs_part",
-    )(here, old, inputs, own, other, late)
+    )(here, old, inputs, own, other, late0, late1)
 
 
 def together(*values):
@@ -576,16 +580,16 @@
     rec_c, gp_c = send(rec_away, to_core), send(gp_away, to_core)
     a0, a1, h4 = together(*add_halves(t_x2, u1), h4)
     b2 = [send(a0, to_x), send(a1, to_x)]
-    left, right = second(c4, h4, last=True)
+    late, left, right = second(c4, h4, last=True)
     b3 = [send(left, to_x), send(right, to_x)]
-    late = send(gps[1], to_core)
+    late = [send(gps[1], to_core), send(late, to_core)]
     part = received_own(hid, recs[0])
     b2[0], _, part, rec_c = together(b2[0], left, part, rec_c)
     w2 = [ring(add([t_r2, w1, b2[k]], k)) for k in range(2)]
     w2[0], _ = together(w2[0], b3[1])
     w3 = [ring(add([t_r3, b3[k], w2[k]], k)) for k in range(2)]
     part = received_other(part, hid_c, rec_c)
-    weight_grads = inputs_part(here, (1, 3), part, inputs, gps[0], gp_c, late, cap)
+    weight_grads = inputs_part(here, (1, 3), part, inputs, gps[0], gp_c, *late, cap)
     w3[1], weight_grads = together(w3[1], weight_grads)
     return (finish(t_r0, b0, *w3), weight_grads)
 

time: 104 us -> 104 us (level)
    ppermute x25 -> x26, starting transfers between devices: 29.9 us -> 30.4 us  [send(): return lax.ppermute(v, 'expert', perm)]
    ppermute x25 -> x26, waiting for transfers between devices: 5.42 us -> 5.43 us  [send(): return lax.ppermute(v, 'expert', perm)]
  transfers between devices with their start and end apart: 33 -> 34, of which waited for: 14 -> 14; matrix products, arithmetic and copies ran while one was open for 0% -> 0% of each run, Pallas kernels for 46% -> 45%
where the time goes in v15:
time: 104 us
  Pallas kernels  47.9 us (46%)
  starting transfers between devices  38.8 us (37%)
  waiting for transfers between devices  15 us (14%)
    ppermute x26, starting transfers between devices, send(): return lax.ppermute(v, 'expert', perm)  30.4 us
    pallas_call x5, Pallas kernels, combine(): pl.pallas_call(functools.partial(combine_kernel, chunk, cap, len(old), la...  14.2 us
    pallas_call x5, Pallas kernels, dispatch(): pl.pallas_call(functools.partial(dispatch_kernel, chunk, cap, len(old) //...  13.5 us
    ppermute x8, waiting for transfers between devices, exchange(): return lax.ppermute(v, 'dp', [(0, 1), (1, 0)])  9.57 us
    ppermute x8, starting transfers between devices, exchange(): return lax.ppermute(v, 'dp', [(0, 1), (1, 0)])  8.4 us
    ppermute x26, waiting for transfers between devices, send(): return lax.ppermute(v, 'expert', perm)  5.43 us
    pallas_call x1, Pallas kernels, inputs_part(): pl.pallas_call(functools.partial(inputs_kernel, cap, last), out_shape=jax...  5.2 us
    pallas_call x2, Pallas kernels, hidden(): pl.pallas_call(functools.partial(hidden_kernel, cap, k), out_shape=jax.Sh...  4.73 us
  transfers between devices with their start and end apart: 34, of which 14 were waited for; matrix products, arithmetic and copies ran while one was open for 0% of the time, Pallas kernels for 45%

profile of v15, /device:TPU:0, one launch (start us, length us, event | category | flops | bytes accessed | tf_op | source)
XLA Modules:
  0.0 103.6 jit_solution(15569153254706790367)
XLA Ops:
  3.4 2.7 %collective-permute-start = (bf16[200,1024]{1,0:T(8,128)(2,1)}, bf16[200,1024]{1,0:T(8,128)(2,1)}, u32[]{:S(2)}, u32[]{:S(2)}) collective-permute-start(bf16[200,1024]{1,0:T(8,128)(2,1)} %pack.1.refs_0_), channel_id=1, source_target_pairs={{0,4},{1,5},{2,6},{3,7},{4,8},{5,9},{6,10},{7,11},{8,12},{9,13},{1... | collective-permute-start | bytes 1228808 | tf_op jit(solution)/shard_map/ppermute | solution.py:518
  7.6 2.2 %hidden.2.hid = bf16[384,1152]{1,0:T(8,128)(2,1)S(1)} custom-call(s32[1]{0:T(128)} %bitcast.2.here, bf16[2304,384]{1,0:T(8,128)(2,1)} %bitcast.10, bf16[2304,384]{1,0:T(8,128)(2,1)} %bitcast.18), custom_call_target="tpu_custom_call" | custom-call | flops 1048576 | bytes 16384 | tf_op jit(solution)/shard_map/hidden/pallas_call | solution.py:349
  9.9 3.9 %turn.1.inputs = bf16[1024,2304]{1,0:T(8,128)(2,1)S(1)} custom-call(s32[1]{0:T(128)} %bitcast.2.here, bf16[2304,1024]{1,0:T(8,128)(2,1)} %bitcast.33), custom_call_target="tpu_custom_call" | custom-call | flops 1048576 | bytes 16384 | tf_op jit(solution)/shard_map/turn/pallas_call | solution.py:373
  14.9 2.5 %dispatch.5 = (bf16[1152,1024]{1,0:T(8,128)(2,1)S(1)}, bf16[1152,1024]{1,0:T(8,128)(2,1)S(1)}, f32[288,384]{1,0:T(8,128)S(1)}, bf16[288,384]{1,0:T(8,128)(2,1)S(1)}, f32[8,192]{1,0:T(8,128)S(1)}) custom-call(s32[1]{0:T(128)} %bitcast.2.here, bf16[200,1024]{1,0:T(8,128)(2,1)} %pack.1.refs_0_, bf16[384,1024]{1,0:T(8,128)(2,1)S(1)} %bitcast.26, ...), custom_call_target="tpu_custom_call" | custom-call | flops 1048576 | bytes 16384 | tf_op jit(solution)/shard_map/dispatch/pallas_call | solution.py:162
  22.7 3.1 %dispatch.6 = (bf16[1152,1024]{1,0:T(8,128)(2,1)S(1)}, bf16[1152,1024]{1,0:T(8,128)(2,1)S(1)}, f32[576,384]{1,0:T(8,128)S(1)}, bf16[288,384]{1,0:T(8,128)(2,1)S(...) custom-call(s32[1]{0:T(128)} %bitcast.2.here, ...), custom_call_target="tpu_custom_call", output_to_operand_aliasing={{0}: (5, {}), {1}: (6, {})} | custom-call | flops 1048576 | bytes 16384 | tf_op jit(solution)/shard_map/dispatch/pallas_call | solution.py:162
  26.3 2.5 %hidden.3.hid = bf16[384,1152]{1,0:T(8,128)(2,1)S(1)} custom-call(s32[1]{0:T(128)} %bitcast.2.here, bf16[2304,384]{1,0:T(8,128)(2,1)} %bitcast.11, bf16[2304,384]{1,0:T(8,128)(2,1)} %bitcast.19), custom_call_target="tpu_custom_call" | custom-call | flops 1048576 | bytes 16384 | tf_op jit(solution)/shard_map/hidden/pallas_call | solution.py:349
  28.9 2.3 %combine.5 = (bf16[1152,768]{1,0:T(8,128)(2,1)S(1)}, bf16[1152,768]{1,0:T(8,128)(2,1)S(1)}, bf16[192,1024]{1,0:T(8,128)(2,1)S(1)}) custom-call(s32[1]{0:T(128)} %bitcast.2.here, f32[288,384]{1,0:T(8,128)S(1)} %get-tuple-element.102.share, bf16[288,384]{1,0:T(8,128)(2,1)S(1)} %collective-permute-done.8.refs_0_, f32[8,192]{1,0:T(8,128)S(1)} %get-tuple-element.104.refs_1_, ...), custom_call_target="tpu_custom_call" | custom-call | flops 1048576 | bytes 16384 | tf_op jit(solution)/shard_map/combine/pallas_call | solution.py:233
  36.7 2.8 %dispatch.7 = (bf16[1152,1024]{1,0:T(8,128)(2,1)S(1)}, bf16[1152,1024]{1,0:T(8,128)(2,1)S(1)}, f32[576,384]{1,0:T(8,128)S(1)}, bf16[288,384]{1,0:T(8,128)(2,1)S(...) custom-call(s32[1]{0:T(128)} %bitcast.2.here, ...), custom_call_target="tpu_custom_call", output_to_operand_aliasing={{0}: (5, {}), {1}: (6, {})} | custom-call | flops 1048576 | bytes 16384 | tf_op jit(solution)/shard_map/dispatch/pallas_call | solution.py:162
  42.0 3.3 %combine.6 = (bf16[1152,768]{1,0:T(8,128)(2,1)S(1)}, bf16[1152,768]{1,0:T(8,128)(2,1)S(1)}, bf16[192,1024]{1,0:T(8,128)(2,1)S(1)}, bf16[192,1024]{1,0:T(8,128)(2,1)S(1)}) custom-call(s32[1]{0:T(128)} %bitcast.2.here, f32[576,384]{1,0:T(8,128)S(1)} %get-tuple-element.116.share, ...), custom_call_target="tpu_custom_call", output_to_operand_aliasing={{0}: (11, {}), {1}: (12, {})} | custom-call | flops 1048576 | bytes 16384 | tf_op jit(solution)/shard_map/combine/pallas_call | solution.py:233
  49.7 2.8 %dispatch.8 = (bf16[1152,1024]{1,0:T(8,128)(2,1)S(1)}, bf16[1152,1024]{1,0:T(8,128)(2,1)S(1)}, f32[576,384]{1,0:T(8,128)S(1)}, bf16[288,384]{1,0:T(8,128)(2,1)S(...) custom-call(s32[1]{0:T(128)} %bitcast.2.here, ...), custom_call_target="tpu_custom_call", output_to_operand_aliasing={{0}: (5, {}), {1}: (6, {})} | custom-call | flops 1048576 | bytes 16384 | tf_op jit(solution)/shard_map/dispatch/pallas_call | solution.py:162
  52.7 2.5 %collective-permute-done.17.refs_1_ = bf16[288,384]{1,0:T(8,128)(2,1)S(1)} collective-permute-done((bf16[288,384]{1,0:T(8,128)(2,1)S(1)}, bf16[288,384]{1,0:T(8,128)(2,1)S(1)}, u32[]{:S(2)}, u32[]{:S(2)}) %collective-permute-start.17) | collective-permute-done | bytes 221216 | tf_op jit(solution)/shard_map/ppermute | solution.py:540
  55.2 3.3 %combine.7 = (bf16[1152,768]{1,0:T(8,128)(2,1)S(1)}, bf16[1152,768]{1,0:T(8,128)(2,1)S(1)}, bf16[192,1024]{1,0:T(8,128)(2,1)S(1)}, bf16[192,1024]{1,0:T(8,128)(2,1)S(1)}) custom-call(s32[1]{0:T(128)} %bitcast.2.here, f32[576,384]{1,0:T(8,128)S(1)} %get-tuple-element.132.share, ...), custom_call_target="tpu_custom_call", output_to_operand_aliasing={{0}: (11, {}), {1}: (12, {})} | custom-call | flops 1048576 | bytes 16384 | tf_op jit(solution)/shard_map/combine/pallas_call | solution.py:233
  58.6 2.0 %collective-permute-start.18 = (bf16[192,1024]{1,0:T(8,128)(2,1)S(1)}, bf16[192,1024]{1,0:T(8,128)(2,1)S(1)}, u32[]{:S(2)}, u32[]{:S(2)}) collective-permute-start(bf16[192,1024]{1,0:T(8,128)(2,1)S(1)} %get-tuple-element.140), channel_id=1, source_target_pairs={{0,4},{1,5},{2,6},{3,7},{4,8},{5,9},{6,10},{7,11},{8,12},{9,13},{1... | collective-permute-start | bytes 1179656 | tf_op jit(solution)/shard_map/ppermute | solution.py:518
  61.2 2.1 %collective-permute-start.21 = (bf16[288,384]{1,0:T(8,128)(2,1)S(1)}, bf16[288,384]{1,0:T(8,128)(2,1)S(1)}, u32[]{:S(2)}, u32[]{:S(2)}) collective-permute-start(bf16[288,384]{1,0:T(8,128)(2,1)S(1)} %get-tuple-element.148), channel_id=1, source_target_pairs={{0,16},{16,0},{1,17},{17,1},{2,18},{18,2},{3,19},{19,3},{4,20},{20... | collective-permute-start | bytes 663560 | tf_op jit(solution)/shard_map/ppermute | solution.py:540
  63.2 2.3 %dispatch.9 = (bf16[1152,1024]{1,0:T(8,128)(2,1)S(1)}, bf16[1152,1024]{1,0:T(8,128)(2,1)S(1)}, f32[288,384]{1,0:T(8,128)S(1)}, bf16[288,384]{1,0:T(8,128)(2,1)S(1)}, f32[8,192]{1,0:T(8,128)S(1)}) custom-call(s32[1]{0:T(128)} %bitcast.2.here, bf16[200,1024]{1,0:T(8,128)(2,1)S(1)} %collective-permute-done.14.refs_0_, ...), custom_call_target="tpu_custom_call", output_to_operand_aliasing={{0}: (4, {}), {1}: (5, {})} | custom-call | flops 1048576 | bytes 16384 | tf_op jit(solution)/shard_map/dispatch/pallas_call | solution.py:162
  65.6 2.5 %collective-permute-done.21.refs_1_ = bf16[288,384]{1,0:T(8,128)(2,1)S(1)} collective-permute-done((bf16[288,384]{1,0:T(8,128)(2,1)S(1)}, bf16[288,384]{1,0:T(8,128)(2,1)S(1)}, u32[]{:S(2)}, u32[]{:S(2)}) %collective-permute-start.21) | collective-permute-done | bytes 221216 | tf_op jit(solution)/shard_map/ppermute | solution.py:540
  68.1 3.3 %combine.8 = (bf16[1152,768]{1,0:T(8,128)(2,1)S(1)}, bf16[1152,768]{1,0:T(8,128)(2,1)S(1)}, bf16[192,1024]{1,0:T(8,128)(2,1)S(1)}, bf16[192,1024]{1,0:T(8,128)(2,1)S(1)}) custom-call(s32[1]{0:T(128)} %bitcast.2.here, f32[576,384]{1,0:T(8,128)S(1)} %get-tuple-element.146.share, ...), custom_call_target="tpu_custom_call", output_to_operand_aliasing={{0}: (11, {}), {1}: (12, {})} | custom-call | flops 1048576 | bytes 16384 | tf_op jit(solution)/shard_map/combine/pallas_call | solution.py:233
  75.4 2.0 %combine.9 = (bf16[1152,768]{1,0:T(8,128)(2,1)S(1)}, bf16[144,384]{1,0:T(8,128)(2,1)S(1)}, bf16[144,384]{1,0:T(8,128)(2,1)S(1)}, bf16[192,512]{1,0:T(8,128)(2,1)S(1)}, bf16[192,512]{1,0:T(8,128)(2,1)S(1)}) custom-call(s32[1]{0:T(128)} %bitcast.2.here, f32[288,384]{1,0:T(8,128)S(1)} %get-tuple-element.158.share, ...), custom_call_target="tpu_custom_call", output_to_operand_aliasing={{0}: (10, {})} | custom-call | flops 1048576 | bytes 16384 | tf_op jit(solution)/shard_map/combine/pallas_call | solution.py:233
  80.1 2.9 %collective-permute-start.29 = (bf16[192,512]{1,0:T(8,128)(2,1)S(1)}, bf16[192,512]{1,0:T(8,128)(2,1)S(1)}, u32[]{:S(2)}, u32[]{:S(2)}) collective-permute-start(bf16[192,512]{1,0:T(8,128)(2,1)S(1)} %add.6), channel_id=1, source_target_pairs={{0,4},{1,5},{2,6},{3,7},{4,8},{5,9},{6,10},{7,11},{8,12},{9,13},{1... | collective-permute-start | bytes 589832 | tf_op jit(solution)/shard_map/ppermute | solution.py:518
  84.3 2.9 %collective-permute-start.25 = (bf16[192,512]{1,0:T(8,128)(2,1)S(1)}, bf16[192,512]{1,0:T(8,128)(2,1)S(1)}, u32[]{:S(2)}, u32[]{:S(2)}) collective-permute-start(bf16[192,512]{1,0:T(8,128)(2,1)S(1)} %add.4), channel_id=1, source_target_pairs={{0,4},{1,5},{2,6},{3,7},{4,8},{5,9},{6,10},{7,11},{8,12},{9,13},{1... | collective-permute-start | bytes 589832 | tf_op jit(solution)/shard_map/ppermute | solution.py:518
  88.1 3.3 %collective-permute-start.30 = (bf16[192,512]{1,0:T(8,128)(2,1)S(1)}, bf16[192,512]{1,0:T(8,128)(2,1)S(1)}, u32[]{:S(2)}, u32[]{:S(2)}) collective-permute-start(bf16[192,512]{1,0:T(8,128)(2,1)S(1)} %add.7), channel_id=1, source_target_pairs={{0,4},{1,5},{2,6},{3,7},{4,8},{5,9},{6,10},{7,11},{8,12},{9,13},{1... | collective-permute-start | bytes 589832 | tf_op jit(solution)/shard_map/ppermute | solution.py:518
  92.9 2.0 %collective-permute-start.27 = (bf16[192,512]{1,0:T(8,128)(2,1)S(1)}, bf16[192,512]{1,0:T(8,128)(2,1)S(1)}, u32[]{:S(2)}, u32[]{:S(2)}) collective-permute-start(bf16[192,512]{1,0:T(8,128)(2,1)S(1)} %add.5), channel_id=1, source_target_pairs={{0,4},{1,5},{2,6},{3,7},{4,8},{5,9},{6,10},{7,11},{8,12},{9,13},{1... | collective-permute-start | bytes 589832 | tf_op jit(solution)/shard_map/ppermute | solution.py:518
  95.4 2.0 %received_other.1.old = bf16[1,1024,1152]{2,1,0:T(8,128)(2,1)} custom-call(f32[384,1024]{1,0:T(8,128)S(1)} %received_own.1.part, bf16[384,1152]{1,0:T(8,128)(2,1)S(1)} %hidden.3.hid, bf16[1152,1024]{1,0:T(8,128)(2,1)S(1)} %collective-permute-done.24.other), custom_call_target="tpu_custom_call" | custom-call | flops 1048576 | bytes 16384 | tf_op jit(solution)/shard_map/received_other/pallas_call | solution.py:451
  97.5 5.2 %inputs_part.1 = bf16[1,1024,1152]{2,1,0:T(8,128)(2,1)} custom-call(s32[1]{0:T(128)} %bitcast.2.here, bf16[1,1024,1152]{2,1,0:T(8,128)(2,1)} %received_other.1.old, bf16[1024,2304]{1,0:T(8,128)(2,1)S(1)} %turn.1.inputs, bf16[1152,768]{1,0:T(8,128)(2,1)S(1)} %get-tuple-element.182.own, ...), custom_call_target="tpu_custom_call", output_to_operand_aliasing={{}: (1, {})} | custom-call | flops 1048576 | bytes 16384 | tf_op jit(solution)/shard_map/inputs_part/pallas_call | solution.py:486
  (78 shorter events, 36.4 us)
Async XLA Ops:
  0.6 17.9 %collective-permute-start.3 = (bf16[2304,384]{1,0:T(8,128)(2,1)}, bf16[2304,384]{1,0:T(8,128)(2,1)S(1)}, u32[]{:S(2)}, u32[]{:S(2)}) collective-permute-start(bf16[2304,384]{1,0:T(8,128)(2,1)} %bitcast.9), channel_id=1, source_target_pairs={{0,1},{1,0},{2,3},{3,2},{4,5},{5,4},{6,7},{7,6},{8,9},{9,8},{10,11... | collective-permute-start | bytes 5308424 | tf_op jit(solution)/shard_map/ppermute | solution.py:518
  1.1 17.4 %collective-permute-start.4 = (bf16[2304,384]{1,0:T(8,128)(2,1)}, bf16[2304,384]{1,0:T(8,128)(2,1)S(1)}, u32[]{:S(2)}, u32[]{:S(2)}) collective-permute-start(bf16[2304,384]{1,0:T(8,128)(2,1)} %bitcast.17), channel_id=1, source_target_pairs={{0,1},{1,0},{2,3},{3,2},{4,5},{5,4},{6,7},{7,6},{8,9},{9,8},{10,11... | collective-permute-start | bytes 5308424 | tf_op jit(solution)/shard_map/ppermute | solution.py:518
  1.2 12.7 %collective-permute-start.2 = (bf16[384,1024]{1,0:T(8,128)(2,1)}, bf16[384,1024]{1,0:T(8,128)(2,1)}, u32[]{:S(2)}, u32[]{:S(2)}) collective-permute-start(bf16[384,1024]{1,0:T(8,128)(2,1)} %bitcast.25), channel_id=1, source_target_pairs={{0,1},{1,0},{2,3},{3,2},{4,5},{5,4},{6,7},{7,6},{8,9},{9,8},{10,11... | collective-permute-start | bytes 2359304 | tf_op jit(solution)/shard_map/ppermute | solution.py:518
  3.4 15.1 %collective-permute-start = (bf16[200,1024]{1,0:T(8,128)(2,1)}, bf16[200,1024]{1,0:T(8,128)(2,1)}, u32[]{:S(2)}, u32[]{:S(2)}) collective-permute-start(bf16[200,1024]{1,0:T(8,128)(2,1)} %pack.1.refs_0_), channel_id=1, source_target_pairs={{0,4},{1,5},{2,6},{3,7},{4,8},{5,9},{6,10},{7,11},{8,12},{9,13},{1... | collective-permute-start | bytes 1228808 | tf_op jit(solution)/shard_map/ppermute | solution.py:518
  6.1 12.4 %collective-permute-start.1 = (bf16[200,1024]{1,0:T(8,128)(2,1)}, bf16[200,1024]{1,0:T(8,128)(2,1)}, u32[]{:S(2)}, u32[]{:S(2)}) collective-permute-start(bf16[200,1024]{1,0:T(8,128)(2,1)} %pack.1.refs_0_), channel_id=1, source_target_pairs={{0,2},{1,3},{2,0},{3,1},{4,6},{5,7},{6,4},{7,5},{8,10},{9,11},{10,... | collective-permute-start | bytes 1228808 | tf_op jit(solution)/shard_map/ppermute | solution.py:518
  18.6 10.3 %collective-permute-start.9 = (bf16[1024,768]{1,0:T(8,128)(2,1)S(1)}, bf16[1024,768]{1,0:T(8,128)(2,1)S(1)}, u32[]{:S(2)}, u32[]{:S(2)}) collective-permute-start(bf16[1024,768]{1,0:T(8,128)(2,1)S(1)} %join.1.refs_6_.refs_7_), channel_id=1, source_target_pairs={{0,1},{1,0},{2,3},{3,2},{4,5},{5,4},{6,7},{7,6},{8,9},{9,8},{10,11... | collective-permute-start | bytes 4718600 | tf_op jit(solution)/shard_map/ppermute | solution.py:518
  18.6 14.5 %collective-permute-start.5 = (bf16[200,1024]{1,0:T(8,128)(2,1)}, bf16[200,1024]{1,0:T(8,128)(2,1)S(1)}, u32[]{:S(2)}, u32[]{:S(2)}) collective-permute-start(bf16[200,1024]{1,0:T(8,128)(2,1)} %collective-permute-done.refs_1_), channel_id=1, source_target_pairs={{0,4},{1,5},{2,6},{3,7},{4,8},{5,9},{6,10},{7,11},{8,12},{9,13},{1... | collective-permute-start | bytes 1228808 | tf_op jit(solution)/shard_map/ppermute | solution.py:518
  19.6 13.5 %collective-permute-start.6 = (bf16[200,1024]{1,0:T(8,128)(2,1)}, bf16[200,1024]{1,0:T(8,128)(2,1)S(1)}, u32[]{:S(2)}, u32[]{:S(2)}) collective-permute-start(bf16[200,1024]{1,0:T(8,128)(2,1)} %collective-permute-done.refs_1_), channel_id=1, source_target_pairs={{0,2},{1,3},{2,0},{3,1},{4,6},{5,7},{6,4},{7,5},{8,10},{9,11},{10,... | collective-permute-start | bytes 1228808 | tf_op jit(solution)/shard_map/ppermute | solution.py:518
  21.1 7.7 %collective-permute-start.8 = (bf16[288,384]{1,0:T(8,128)(2,1)S(1)}, bf16[288,384]{1,0:T(8,128)(2,1)S(1)}, u32[]{:S(2)}, u32[]{:S(2)}) collective-permute-start(bf16[288,384]{1,0:T(8,128)(2,1)S(1)} %get-tuple-element.103), channel_id=1, source_target_pairs={{0,16},{16,0},{1,17},{17,1},{2,18},{18,2},{3,19},{19,3},{4,20},{20... | collective-permute-start | bytes 663560 | tf_op jit(solution)/shard_map/ppermute | solution.py:540
  33.1 12.8 %collective-permute-start.10 = (bf16[200,1024]{1,0:T(8,128)(2,1)S(1)}, bf16[200,1024]{1,0:T(8,128)(2,1)S(1)}, u32[]{:S(2)}, u32[]{:S(2)}) collective-permute-start(bf16[200,1024]{1,0:T(8,128)(2,1)S(1)} %collective-permute-done.5.refs_1_), channel_id=1, source_target_pairs={{0,4},{1,5},{2,6},{3,7},{4,8},{5,9},{6,10},{7,11},{8,12},{9,13},{1... | collective-permute-start | bytes 1228808 | tf_op jit(solution)/shard_map/ppermute | solution.py:518
  34.7 11.2 %collective-permute-start.11 = (bf16[200,1024]{1,0:T(8,128)(2,1)S(1)}, bf16[200,1024]{1,0:T(8,128)(2,1)S(1)}, u32[]{:S(2)}, u32[]{:S(2)}) collective-permute-start(bf16[200,1024]{1,0:T(8,128)(2,1)S(1)} %collective-permute-done.5.refs_1_), channel_id=1, source_target_pairs={{0,2},{1,3},{2,0},{3,1},{4,6},{5,7},{6,4},{7,5},{8,10},{9,11},{10,... | collective-permute-start | bytes 1228808 | tf_op jit(solution)/shard_map/ppermute | solution.py:518
  45.9 12.7 %collective-permute-start.14 = (bf16[200,1024]{1,0:T(8,128)(2,1)S(1)}, bf16[200,1024]{1,0:T(8,128)(2,1)S(1)}, u32[]{:S(2)}, u32[]{:S(2)}) collective-permute-start(bf16[200,1024]{1,0:T(8,128)(2,1)S(1)} %collective-permute-done.10.refs_1_), channel_id=1, source_target_pairs={{0,2},{1,3},{2,0},{3,1},{4,6},{5,7},{6,4},{7,5},{8,10},{9,11},{10,... | collective-permute-start | bytes 1228808 | tf_op jit(solution)/shard_map/ppermute | solution.py:518
  47.4 11.2 %collective-permute-start.15 = (bf16[192,1024]{1,0:T(8,128)(2,1)S(1)}, bf16[192,1024]{1,0:T(8,128)(2,1)S(1)}, u32[]{:S(2)}, u32[]{:S(2)}) collective-permute-start(bf16[192,1024]{1,0:T(8,128)(2,1)S(1)} %get-tuple-element.125), channel_id=1, source_target_pairs={{0,4},{1,5},{2,6},{3,7},{4,8},{5,9},{6,10},{7,11},{8,12},{9,13},{1... | collective-permute-start | bytes 1179656 | tf_op jit(solution)/shard_map/ppermute | solution.py:518
  58.6 13.0 %collective-permute-start.18 = (bf16[192,1024]{1,0:T(8,128)(2,1)S(1)}, bf16[192,1024]{1,0:T(8,128)(2,1)S(1)}, u32[]{:S(2)}, u32[]{:S(2)}) collective-permute-start(bf16[192,1024]{1,0:T(8,128)(2,1)S(1)} %get-tuple-element.140), channel_id=1, source_target_pairs={{0,4},{1,5},{2,6},{3,7},{4,8},{5,9},{6,10},{7,11},{8,12},{9,13},{1... | collective-permute-start | bytes 1179656 | tf_op jit(solution)/shard_map/ppermute | solution.py:518
  60.6 10.9 %collective-permute-start.19 = (bf16[192,1024]{1,0:T(8,128)(2,1)S(1)}, bf16[192,1024]{1,0:T(8,128)(2,1)S(1)}, u32[]{:S(2)}, u32[]{:S(2)}) collective-permute-start(bf16[192,1024]{1,0:T(8,128)(2,1)S(1)} %get-tuple-element.141), channel_id=1, source_target_pairs={{0,2},{1,3},{2,0},{3,1},{4,6},{5,7},{6,4},{7,5},{8,10},{9,11},{10,... | collective-permute-start | bytes 1179656 | tf_op jit(solution)/shard_map/ppermute | solution.py:518
  71.6 12.6 %collective-permute-start.24 = (bf16[1152,1024]{1,0:T(8,128)(2,1)S(1)}, bf16[1152,1024]{1,0:T(8,128)(2,1)S(1)}, u32[]{:S(2)}, u32[]{:S(2)}) collective-permute-start(bf16[1152,1024]{1,0:T(8,128)(2,1)S(1)} %get-tuple-element.173), channel_id=1, source_target_pairs={{0,1},{1,0},{2,3},{3,2},{4,5},{5,4},{6,7},{7,6},{8,9},{9,8},{10,11... | collective-permute-start | bytes 7077896 | tf_op jit(solution)/shard_map/ppermute | solution.py:518
  71.6 25.9 %collective-permute-start.31 = (bf16[1152,768]{1,0:T(8,128)(2,1)S(1)}, bf16[1152,768]{1,0:T(8,128)(2,1)S(1)}, u32[]{:S(2)}, u32[]{:S(2)}) collective-permute-start(bf16[1152,768]{1,0:T(8,128)(2,1)S(1)} %get-tuple-element.183), channel_id=1, source_target_pairs={{0,1},{1,0},{2,3},{3,2},{4,5},{5,4},{6,7},{7,6},{8,9},{9,8},{10,11... | collective-permute-start | bytes 5308424 | tf_op jit(solution)/shard_map/ppermute | solution.py:518
  72.2 7.8 %collective-permute-start.28 = (bf16[192,512]{1,0:T(8,128)(2,1)S(1)}, bf16[192,512]{1,0:T(8,128)(2,1)S(1)}, u32[]{:S(2)}, u32[]{:S(2)}) collective-permute-start(bf16[192,512]{1,0:T(8,128)(2,1)S(1)} %get-tuple-element.177), channel_id=1, source_target_pairs={{0,2},{1,3},{2,0},{3,1},{4,6},{5,7},{6,4},{7,5},{8,10},{9,11},{10,... | collective-permute-start | bytes 589832 | tf_op jit(solution)/shard_map/ppermute | solution.py:518
  73.7 10.5 %collective-permute-start.23 = (bf16[192,512]{1,0:T(8,128)(2,1)S(1)}, bf16[192,512]{1,0:T(8,128)(2,1)S(1)}, u32[]{:S(2)}, u32[]{:S(2)}) collective-permute-start(bf16[192,512]{1,0:T(8,128)(2,1)S(1)} %get-tuple-element.170), channel_id=1, source_target_pairs={{0,2},{1,3},{2,0},{3,1},{4,6},{5,7},{6,4},{7,5},{8,10},{9,11},{10,... | collective-permute-start | bytes 589832 | tf_op jit(solution)/shard_map/ppermute | solution.py:518
  77.5 10.1 %collective-permute-start.26 = (bf16[192,512]{1,0:T(8,128)(2,1)S(1)}, bf16[192,512]{1,0:T(8,128)(2,1)S(1)}, u32[]{:S(2)}, u32[]{:S(2)}) collective-permute-start(bf16[192,512]{1,0:T(8,128)(2,1)S(1)} %get-tuple-element.175), channel_id=1, source_target_pairs={{0,2},{1,3},{2,0},{3,1},{4,6},{5,7},{6,4},{7,5},{8,10},{9,11},{10,... | collective-permute-start | bytes 589832 | tf_op jit(solution)/shard_map/ppermute | solution.py:518
  80.1 7.9 %collective-permute-start.29 = (bf16[192,512]{1,0:T(8,128)(2,1)S(1)}, bf16[192,512]{1,0:T(8,128)(2,1)S(1)}, u32[]{:S(2)}, u32[]{:S(2)}) collective-permute-start(bf16[192,512]{1,0:T(8,128)(2,1)S(1)} %add.6), channel_id=1, source_target_pairs={{0,4},{1,5},{2,6},{3,7},{4,8},{5,9},{6,10},{7,11},{8,12},{9,13},{1... | collective-permute-start | bytes 589832 | tf_op jit(solution)/shard_map/ppermute | solution.py:518
  84.3 7.9 %collective-permute-start.25 = (bf16[192,512]{1,0:T(8,128)(2,1)S(1)}, bf16[192,512]{1,0:T(8,128)(2,1)S(1)}, u32[]{:S(2)}, u32[]{:S(2)}) collective-permute-start(bf16[192,512]{1,0:T(8,128)(2,1)S(1)} %add.4), channel_id=1, source_target_pairs={{0,4},{1,5},{2,6},{3,7},{4,8},{5,9},{6,10},{7,11},{8,12},{9,13},{1... | collective-permute-start | bytes 589832 | tf_op jit(solution)/shard_map/ppermute | solution.py:518
  88.1 14.6 %collective-permute-start.30 = (bf16[192,512]{1,0:T(8,128)(2,1)S(1)}, bf16[192,512]{1,0:T(8,128)(2,1)S(1)}, u32[]{:S(2)}, u32[]{:S(2)}) collective-permute-start(bf16[192,512]{1,0:T(8,128)(2,1)S(1)} %add.7), channel_id=1, source_target_pairs={{0,4},{1,5},{2,6},{3,7},{4,8},{5,9},{6,10},{7,11},{8,12},{9,13},{1... | collective-permute-start | bytes 589832 | tf_op jit(solution)/shard_map/ppermute | solution.py:518
  92.9 9.8 %collective-permute-start.27 = (bf16[192,512]{1,0:T(8,128)(2,1)S(1)}, bf16[192,512]{1,0:T(8,128)(2,1)S(1)}, u32[]{:S(2)}, u32[]{:S(2)}) collective-permute-start(bf16[192,512]{1,0:T(8,128)(2,1)S(1)} %add.5), channel_id=1, source_target_pairs={{0,4},{1,5},{2,6},{3,7},{4,8},{5,9},{6,10},{7,11},{8,12},{9,13},{1... | collective-permute-start | bytes 589832 | tf_op jit(solution)/shard_map/ppermute | solution.py:518
  (15 other events, 72.7 us)
